TPU v7x, 32 devices: a whole 2x2x4 slice. The times are simulated.
32 devices in a mesh: dp: 8 (over z, y), fsdp: 4 (over x, core).
Axes of the slice: x: 2, y: 2, z: 4, core: 2. Of those that a mesh axis runs over, the one named last changes fastest.
Arguments:
- tokens: bfloat16 [8192, 2048], P(('dp', 'fsdp')), may hold values from -6 to 6
- cotangent: bfloat16 [8192, 2048], P(('dp', 'fsdp')), may hold values from -6 to 6
- seq_lengths: int32 [8, 4], P('dp'), may hold values from 1 to 512, as said below
- deal_order: int32 [8, 4], P('dp'), may hold values from 0 to 3, as said below
- attn_gain: bfloat16 [2048], P(('dp', 'fsdp')), may hold values from 0.099609375 to 1.8984375
- w_query: bfloat16 [2048, 1536], P(('dp', 'fsdp')), may hold values from -0.125 to 0.125
- w_key: bfloat16 [2048, 384], P(('dp', 'fsdp')), may hold values from -0.125 to 0.125
- w_value: bfloat16 [2048, 384], P(('dp', 'fsdp')), may hold values from -0.125 to 0.125
- q_gain: bfloat16 [64], replicated, may hold values from 0.796875 to 1.796875
- k_gain: bfloat16 [64], replicated, may hold values from 0.796875 to 1.796875
- w_out: bfloat16 [1536, 2048], P(('dp', 'fsdp')), may hold values from -1.25 to 1.25
- ffn_gain: bfloat16 [2048], P(('dp', 'fsdp')), may hold values from 0.099609375 to 1.8984375
- w_gate: bfloat16 [2048, 4864], P(('dp', 'fsdp')), may hold values from -0.125 to 0.125
- w_up: bfloat16 [2048, 4864], P(('dp', 'fsdp')), may hold values from -0.125 to 0.125
- w_down: bfloat16 [4864, 2048], P(('dp', 'fsdp')), may hold values from -0.078125 to 0.078125
Outputs:
- output: bfloat16 [8192, 2048], P(('dp', 'fsdp'))
- input_grad: bfloat16 [8192, 2048], P(('dp', 'fsdp'))
- attn_gain_grad: float32 [2048], P(('dp', 'fsdp'))
- w_query_grad: float32 [2048, 1536], P(('dp', 'fsdp'))
- w_key_grad: float32 [2048, 384], P(('dp', 'fsdp'))
- w_value_grad: float32 [2048, 384], P(('dp', 'fsdp'))
- q_gain_grad: float32 [64], replicated
- k_gain_grad: float32 [64], replicated
- w_out_grad: float32 [1536, 2048], P(('dp', 'fsdp'))
- ffn_gain_grad: float32 [2048], P(('dp', 'fsdp'))
- w_gate_grad: float32 [2048, 4864], P(('dp', 'fsdp'))
- w_up_grad: float32 [2048, 4864], P(('dp', 'fsdp'))
- w_down_grad: float32 [4864, 2048], P(('dp', 'fsdp'))
Inputs may be any that keep to these rules, and one draw needn't show every extreme that they name: `seq_lengths`: in each group, laid out in the order that deal_order gives, the 4 sequences fill two micro-batch buffers of 512 tokens each exactly; one sequence of each group has 512 tokens. `deal_order`: each group's row is a permutation of 0 to 3.
All inputs are finite; a program needn't handle non-finite values.
Results may differ from a plain program's by a relative error of at most 0.017.
Values may be sent and summed in bfloat16 or wider, within the bound.
No kernel may reach another device: no remote copies, remote signals or barrier semaphores. Data moves between devices by JAX's collectives and lax.ppermute only.
A program may use at most 320 MiB of HBM per device.

v0:
```python
import functools
import math

import jax
import jax.numpy as jnp
from jax import lax
from jax.sharding import PartitionSpec as P

HEADS = 24
KV_HEADS = 6
HD = 64
MB = 2


EPSILON = 1e-06
MASKED = -1e30


def rms_scale(values, gain_row):
    inverse = lax.rsqrt(jnp.mean(values * values, axis=-1, keepdims=True) + EPSILON)
    return values * inverse * gain_row


def rotary(places, head_size):
    halfway = head_size // 2
    frequency = 10000.0 ** (-2.0 * jnp.arange(halfway, dtype=jnp.float32) / head_size)
    angles = places.astype(jnp.float32)[:, None] * frequency[None, :]
    return (jnp.cos(angles), jnp.sin(angles))


def head_part(pre_values, gain_row, cosine, sine_table, head_count):
    row_count = pre_values.shape[0]
    split_heads = pre_values.reshape(row_count, head_count, -1)
    scaled = (
        split_heads
        * lax.rsqrt(jnp.mean(split_heads * split_heads, axis=-1, keepdims=True) + EPSILON)
        * gain_row
    )
    halfway = scaled.shape[-1] // 2
    leading = scaled[..., :halfway]
    trailing = scaled[..., halfway:]
    cos_rows = cosine[:, None, :]
    sin_rows = sine_table[:, None, :]
    turned = jnp.concatenate(
        [leading * cos_rows - trailing * sin_rows, trailing * cos_rows + leading * sin_rows],
        axis=-1,
    )
    return turned.reshape(row_count, -1)


def product(left_side, right_side):
    return jnp.dot(left_side, right_side, preferred_element_type=jnp.float32)


def right_transposed(left_side, right_side):
    return lax.dot_general(
        left_side, right_side, (((1,), (1,)), ((), ())), preferred_element_type=jnp.float32
    )


def left_transposed(left_side, right_side):
    return lax.dot_general(
        left_side, right_side, (((0,), (0,)), ((), ())), preferred_element_type=jnp.float32
    )


def gated(gate_values, up_values):
    return jax.nn.silu(gate_values) * up_values


def locate(wanted, starts, targets, slot_ids):
    sequence = jnp.sum((starts <= wanted[..., None]).astype(jnp.int32), axis=-1) - 1
    matches = sequence[..., None] == slot_ids
    places = wanted - jnp.sum(jnp.where(matches, starts, 0), axis=-1)
    mapped = jnp.sum(jnp.where(matches, targets, 0), axis=-1) + places
    return (sequence, places, mapped)


def attend_head(operands, allowed, score_scale):
    query_head, key_head, value_head = operands
    raw_scores = (
        jnp.einsum("trd,sd->rts", query_head, key_head, preferred_element_type=jnp.float32)
        * score_scale
    )
    scores = jnp.where(allowed[None], raw_scores, MASKED)
    highest = jnp.max(scores, axis=-1, keepdims=True)
    log_total = highest + jnp.log(jnp.sum(jnp.exp(scores - highest), axis=-1, keepdims=True))
    attn_low = jnp.exp(scores - log_total).astype(jnp.bfloat16)
    mixed = jnp.einsum("rts,sd->trd", attn_low, value_head, preferred_element_type=jnp.float32)
    return (mixed, log_total)


def attend_back(operands, allowed, score_scale):
    query_head, key_head, value_head, log_total, grad_mixed = operands
    raw_scores = (
        jnp.einsum("trd,sd->rts", query_head, key_head, preferred_element_type=jnp.float32)
        * score_scale
    )
    scores = jnp.where(allowed[None], raw_scores, MASKED)
    attn_probs = jnp.exp(scores - log_total)
    attn_low = attn_probs.astype(jnp.bfloat16)
    grad_probs = jnp.einsum(
        "trd,sd->rts", grad_mixed, value_head, preferred_element_type=jnp.float32
    )
    weighted = jnp.sum(attn_probs * grad_probs, axis=-1, keepdims=True)
    grad_scores = (attn_probs * (grad_probs - weighted)).astype(jnp.bfloat16)
    grad_query = (
        jnp.einsum("rts,sd->trd", grad_scores, key_head, preferred_element_type=jnp.float32)
        * score_scale
    )
    grad_key = (
        jnp.einsum("rts,trd->sd", grad_scores, query_head, preferred_element_type=jnp.float32)
        * score_scale
    )
    grad_value = jnp.einsum("rts,trd->sd", attn_low, grad_mixed, preferred_element_type=jnp.float32)
    return (grad_query, grad_key, grad_value)


def local(
    tokens,
    cotangent,
    seq_lengths,
    deal_order,
    attn_gain,
    w_query,
    w_key,
    w_value,
    q_gain,
    k_gain,
    w_out,
    ffn_gain,
    w_gate,
    w_up,
    w_down,
):
    tok_dev = tokens.shape[0] // MB
    model_width = tokens.shape[1]
    group_rows = lax.axis_size("fsdp") * tok_dev
    member = lax.axis_index("fsdp")
    lengths = seq_lengths[0]
    deal_slots = deal_order[0]
    slot_ids = jnp.arange(lengths.shape[0], dtype=jnp.int32)
    picked = deal_slots[:, None] == slot_ids[None, :]
    dealt_len = jnp.sum(jnp.where(picked, lengths[None, :], 0), axis=1)
    given_start = jnp.cumsum(lengths) - lengths
    dealt_start = jnp.cumsum(dealt_len) - dealt_len
    source_start = jnp.sum(jnp.where(picked, given_start[None, :], 0), axis=1)
    dealt_of_given = jnp.sum(jnp.where(picked, dealt_start[:, None], 0), axis=0)
    batch_ids = jnp.arange(MB, dtype=jnp.int32)[:, None]
    my_rows = (
        batch_ids * group_rows + member * tok_dev + jnp.arange(tok_dev, dtype=jnp.int32)[None, :]
    )
    my_seq, my_place, my_source = locate(my_rows, dealt_start, source_start, slot_ids)
    key_rows = batch_ids * group_rows + jnp.arange(group_rows, dtype=jnp.int32)[None, :]
    key_seq, key_place = locate(key_rows, dealt_start, source_start, slot_ids)[:2]
    flat_source = my_source.reshape(-1)
    blank_rows = jnp.zeros((MB * tok_dev, model_width), jnp.bfloat16)
    pieces = (
        lax.all_gather(tokens, "fsdp", axis=0, tiled=True),
        lax.all_gather(cotangent, "fsdp", axis=0, tiled=True),
    )
    piece_rows = pieces[0].shape[0]
    inside = (flat_source >= 0) & (flat_source < piece_rows)
    safe_rows = jnp.clip(flat_source, 0, piece_rows - 1)
    dealt_x = jnp.where(inside[:, None], jnp.take(pieces[0], safe_rows, axis=0), blank_rows)
    dealt_dy = jnp.where(inside[:, None], jnp.take(pieces[1], safe_rows, axis=0), blank_rows)
    score_scale = 1.0 / math.sqrt(HD)
    repeat = HEADS // KV_HEADS
    outputs_list = []
    grads_list = []
    totals = None
    gain_totals = None
    for micro_step in range(MB):
        gathered = (
            lax.all_gather(attn_gain, ("dp", "fsdp"), axis=0, tiled=True),
            lax.all_gather(w_query, ("dp", "fsdp"), axis=0, tiled=True),
            lax.all_gather(w_key, ("dp", "fsdp"), axis=0, tiled=True),
            lax.all_gather(w_value, ("dp", "fsdp"), axis=0, tiled=True),
            lax.all_gather(w_out, ("dp", "fsdp"), axis=0, tiled=True),
            lax.all_gather(ffn_gain, ("dp", "fsdp"), axis=0, tiled=True),
            lax.all_gather(w_gate, ("dp", "fsdp"), axis=0, tiled=True),
            lax.all_gather(w_up, ("dp", "fsdp"), axis=0, tiled=True),
            lax.all_gather(w_down, ("dp", "fsdp"), axis=0, tiled=True),
        )
        (
            full_attn,
            full_query,
            full_key,
            full_value,
            full_out,
            full_ffn,
            full_gate,
            full_up,
            full_down,
        ) = gathered
        input_rows = dealt_x[micro_step * tok_dev : (micro_step + 1) * tok_dev]
        upstream_low = dealt_dy[micro_step * tok_dev : (micro_step + 1) * tok_dev]
        input_wide = input_rows.astype(jnp.float32)
        normed_wide, attn_norm_back = jax.vjp(rms_scale, input_wide, full_attn.astype(jnp.float32))
        normed = normed_wide.astype(jnp.bfloat16)
        query_pre = product(normed, full_query)
        key_pre = product(normed, full_key)
        value_low = product(normed, full_value).astype(jnp.bfloat16)
        cosine, sine_table = rotary(my_place[micro_step], HD)

        def query_map(pre_values, gain_row):
            return head_part(pre_values, gain_row, cosine, sine_table, HEADS)

        def key_map(pre_values, gain_row):
            return head_part(pre_values, gain_row, cosine, sine_table, KV_HEADS)

        query_turned, query_back = jax.vjp(query_map, query_pre, q_gain.astype(jnp.float32))
        key_turned, key_back = jax.vjp(key_map, key_pre, k_gain.astype(jnp.float32))
        query_low = query_turned.astype(jnp.bfloat16)
        key_low = key_turned.astype(jnp.bfloat16)
        key_all, value_all = (
            lax.all_gather(key_low, "fsdp", axis=0, tiled=True),
            lax.all_gather(value_low, "fsdp", axis=0, tiled=True),
        )
        allowed = (my_seq[micro_step][:, None] == key_seq[micro_step][None, :]) & (
            key_place[micro_step][None, :] <= my_place[micro_step][:, None]
        )
        query_heads = jnp.moveaxis(query_low.reshape(tok_dev, KV_HEADS, repeat, HD), 1, 0)
        key_heads = jnp.moveaxis(key_all.reshape(group_rows, KV_HEADS, HD), 1, 0)
        value_heads = jnp.moveaxis(value_all.reshape(group_rows, KV_HEADS, HD), 1, 0)
        mixed_heads, log_total = lax.map(
            functools.partial(attend_head, allowed=allowed, score_scale=score_scale),
            (query_heads, key_heads, value_heads),
        )
        mixed_low = (
            jnp.moveaxis(mixed_heads, 0, 1).reshape(tok_dev, HEADS * HD).astype(jnp.bfloat16)
        )
        hidden = input_wide + product(mixed_low, full_out)
        ffn_wide, ffn_norm_back = jax.vjp(rms_scale, hidden, full_ffn.astype(jnp.float32))
        ffn_low = ffn_wide.astype(jnp.bfloat16)
        gate_values = product(ffn_low, full_gate)
        up_values = product(ffn_low, full_up)
        act_wide, gate_back = jax.vjp(gated, gate_values, up_values)
        act_low = act_wide.astype(jnp.bfloat16)
        layer_out = hidden + product(act_low, full_down)
        outputs_list.append(layer_out.astype(jnp.bfloat16))
        gathered = (
            lax.all_gather(attn_gain, ("dp", "fsdp"), axis=0, tiled=True),
            lax.all_gather(w_query, ("dp", "fsdp"), axis=0, tiled=True),
            lax.all_gather(w_key, ("dp", "fsdp"), axis=0, tiled=True),
            lax.all_gather(w_value, ("dp", "fsdp"), axis=0, tiled=True),
            lax.all_gather(w_out, ("dp", "fsdp"), axis=0, tiled=True),
            lax.all_gather(ffn_gain, ("dp", "fsdp"), axis=0, tiled=True),
            lax.all_gather(w_gate, ("dp", "fsdp"), axis=0, tiled=True),
            lax.all_gather(w_up, ("dp", "fsdp"), axis=0, tiled=True),
            lax.all_gather(w_down, ("dp", "fsdp"), axis=0, tiled=True),
        )
        (
            full_attn,
            full_query,
            full_key,
            full_value,
            full_out,
            full_ffn,
            full_gate,
            full_up,
            full_down,
        ) = gathered
        term_down = left_transposed(act_low, upstream_low)
        grad_act = right_transposed(upstream_low, full_down)
        grad_gate, grad_up = gate_back(grad_act)
        grad_gate_low = grad_gate.astype(jnp.bfloat16)
        grad_up_low = grad_up.astype(jnp.bfloat16)
        term_gate = left_transposed(ffn_low, grad_gate_low)
        term_up = left_transposed(ffn_low, grad_up_low)
        grad_ffn = right_transposed(grad_gate_low, full_gate) + right_transposed(
            grad_up_low, full_up
        )
        grad_hidden, term_ffn = ffn_norm_back(grad_ffn)
        grad_hidden = grad_hidden + upstream_low.astype(jnp.float32)
        grad_hidden_low = grad_hidden.astype(jnp.bfloat16)
        term_out = left_transposed(mixed_low, grad_hidden_low)
        grad_mixed = right_transposed(grad_hidden_low, full_out).astype(jnp.bfloat16)
        grad_heads = jnp.moveaxis(grad_mixed.reshape(tok_dev, KV_HEADS, repeat, HD), 1, 0)
        grad_query_heads, grad_key_part, grad_value_part = lax.map(
            functools.partial(attend_back, allowed=allowed, score_scale=score_scale),
            (query_heads, key_heads, value_heads, log_total, grad_heads),
        )
        grad_query_turned = jnp.moveaxis(grad_query_heads, 0, 1).reshape(tok_dev, HEADS * HD)
        grad_key_rows = jnp.moveaxis(grad_key_part, 0, 1).reshape(group_rows, KV_HEADS * HD)
        grad_value_rows = jnp.moveaxis(grad_value_part, 0, 1).reshape(group_rows, KV_HEADS * HD)
        grad_key_mine, grad_value_mine = (
            lax.psum_scatter(
                grad_key_rows.astype(jnp.bfloat16), "fsdp", scatter_dimension=0, tiled=True
            ).astype(jnp.float32),
            lax.psum_scatter(
                grad_value_rows.astype(jnp.bfloat16), "fsdp", scatter_dimension=0, tiled=True
            ).astype(jnp.float32),
        )
        grad_query_pre, term_qgain = query_back(grad_query_turned)
        grad_key_pre, term_kgain = key_back(grad_key_mine)
        grad_query_low = grad_query_pre.astype(jnp.bfloat16)
        grad_key_low = grad_key_pre.astype(jnp.bfloat16)
        grad_value_low = grad_value_mine.astype(jnp.bfloat16)
        term_query = left_transposed(normed, grad_query_low)
        term_key = left_transposed(normed, grad_key_low)
        term_value = left_transposed(normed, grad_value_low)
        grad_normed = (
            right_transposed(grad_query_low, full_query)
            + right_transposed(grad_key_low, full_key)
            + right_transposed(grad_value_low, full_value)
        )
        grad_input, term_attn = attn_norm_back(grad_normed)
        grads_list.append((grad_input + grad_hidden).astype(jnp.bfloat16))
        fresh = (
            term_attn,
            term_query,
            term_key,
            term_value,
            term_out,
            term_ffn,
            term_gate,
            term_up,
            term_down,
        )
        totals = (
            fresh
            if totals is None
            else tuple((earlier + latest for earlier, latest in zip(totals, fresh)))
        )
        gain_terms = (term_qgain, term_kgain)
        gain_totals = (
            gain_terms
            if gain_totals is None
            else tuple((earlier + latest for earlier, latest in zip(gain_totals, gain_terms)))
        )
    totals = (
        lax.psum_scatter(totals[0], ("dp", "fsdp"), scatter_dimension=0, tiled=True),
        lax.psum_scatter(totals[1], ("dp", "fsdp"), scatter_dimension=0, tiled=True),
        lax.psum_scatter(totals[2], ("dp", "fsdp"), scatter_dimension=0, tiled=True),
        lax.psum_scatter(totals[3], ("dp", "fsdp"), scatter_dimension=0, tiled=True),
        lax.psum_scatter(totals[4], ("dp", "fsdp"), scatter_dimension=0, tiled=True),
        lax.psum_scatter(totals[5], ("dp", "fsdp"), scatter_dimension=0, tiled=True),
        lax.psum_scatter(totals[6], ("dp", "fsdp"), scatter_dimension=0, tiled=True),
        lax.psum_scatter(totals[7], ("dp", "fsdp"), scatter_dimension=0, tiled=True),
        lax.psum_scatter(totals[8], ("dp", "fsdp"), scatter_dimension=0, tiled=True),
    )
    q_gain_grad, k_gain_grad = lax.psum((gain_totals[0], gain_totals[1]), ("dp", "fsdp"))
    stacked = jnp.concatenate(
        [jnp.concatenate(outputs_list, axis=0), jnp.concatenate(grads_list, axis=0)], axis=1
    )
    wanted = jnp.arange(MB * tok_dev * lax.axis_size("fsdp"), dtype=jnp.int32)
    dealt_rows = locate(wanted, given_start, dealt_of_given, slot_ids)[2]
    owner = dealt_rows % group_rows // tok_dev
    local_rows = dealt_rows // group_rows * tok_dev + dealt_rows % tok_dev
    fetched = jnp.take(stacked, local_rows, axis=0).astype(jnp.float32)
    restored = lax.psum_scatter(
        jnp.where((owner == member)[:, None], fetched, 0.0).astype(jnp.bfloat16),
        "fsdp",
        scatter_dimension=0,
        tiled=True,
    ).astype(jnp.float32)
    output = restored[:, :model_width].astype(jnp.bfloat16)
    input_grad = restored[:, model_width:].astype(jnp.bfloat16)
    return (
        output,
        input_grad,
        totals[0],
        totals[1],
        totals[2],
        totals[3],
        q_gain_grad,
        k_gain_grad,
        totals[4],
        totals[5],
        totals[6],
        totals[7],
        totals[8],
    )


def solution(mesh):
    in_specs = (
        P(("dp", "fsdp"), None),
        P(("dp", "fsdp"), None),
        P("dp", None),
        P("dp", None),
        P(("dp", "fsdp")),
        P(("dp", "fsdp"), None),
        P(("dp", "fsdp"), None),
        P(("dp", "fsdp"), None),
        P(),
        P(),
        P(("dp", "fsdp"), None),
        P(("dp", "fsdp")),
        P(("dp", "fsdp"), None),
        P(("dp", "fsdp"), None),
        P(("dp", "fsdp"), None),
    )
    out_specs = (
        P(("dp", "fsdp"), None),
        P(("dp", "fsdp"), None),
        P(("dp", "fsdp")),
        P(("dp", "fsdp"), None),
        P(("dp", "fsdp"), None),
        P(("dp", "fsdp"), None),
        P(),
        P(),
        P(("dp", "fsdp"), None),
        P(("dp", "fsdp")),
        P(("dp", "fsdp"), None),
        P(("dp", "fsdp"), None),
        P(("dp", "fsdp"), None),
    )
    return jax.shard_map(local, mesh=mesh, in_specs=in_specs, out_specs=out_specs, check_vma=False)
```

profile of v0, /device:TPU:0, one launch (start us, length us, event | category | flops | bytes accessed | tf_op | source)
XLA Modules:
  0.0 2926.4 jit_solution(16211781882280274303)
XLA Ops:
  14.1 42.3 %all-reduce.13 = (bf16[2048]{0:T(1024)(128)(2,1)S(1)}, bf16[2048]{0:T(1024)(128)(2,1)S(1)}) all-reduce(bf16[2048]{0:T(1024)(128)(2,1)S(1)} %dynamic-update-slice, bf16[2048]{0:T(1024)(128)(2,1)S(1)} %dynamic-update-slice.1), channel_id=1, replica_groups=mesh['dp'=8,'fsdp'=4] {'dp','fsdp'}, use_global_device_ids=true, to_apply=%add.8 | all-reduce | flops 4096 | bytes 16384
  62.4 5.1 gather_fusion.2
  67.6 15.8 all-gather.10.cloned.1.call-done
  83.4 6.1 gather_fusion.1
  89.4 2.5 select_select_fusion
  92.3 48.9 %all-gather.12.cloned.1.call-done = bf16[2048,384]{1,0:T(8,128)(2,1)} async-done(((bf16[64,384]{1,0:T(8,128)(2,1)}), bf16[2048,384]{1,0:T(8,128)(2,1)}) %all-gather.12.cloned.1.call-update) | async-done | bytes 1572880 | tf_op jit(solution)/shard_map/all_gather | solution.py:178
  143.3 6.9 all_gather.33
  152.7 6.9 all_gather.80
  160.5 37.3 %all-gather.14.cloned.1.call-done = bf16[2048,384]{1,0:T(8,128)(2,1)} async-done(((bf16[64,384]{1,0:T(8,128)(2,1)}), bf16[2048,384]{1,0:T(8,128)(2,1)}) %all-gather.14.cloned.1.call-update) | async-done | bytes 1572880 | tf_op jit(solution)/shard_map/all_gather | solution.py:177
  203.1 7.0 all_gather.35
  210.1 7.0 all_gather.81
  217.1 51.8 %all-gather.16.cloned.1.call-done = bf16[2048,1536]{1,0:T(8,128)(2,1)} async-done(((bf16[64,1536]{1,0:T(8,128)(2,1)}), bf16[2048,1536]{1,0:T(8,128)(2,1)}) %all-gather.16.cloned.1.call-update) | async-done | bytes 6291472 | tf_op jit(solution)/shard_map/all_gather | solution.py:176
  268.9 5.6 fusion.166
  274.6 2.7 fusion.174
  278.3 16.9 while.56
  295.4 44.3 %all-gather.18.cloned.1.call-done = bf16[1536,2048]{1,0:T(8,128)(2,1)} async-done(((bf16[48,2048]{1,0:T(8,128)(2,1)}), bf16[1536,2048]{1,0:T(8,128)(2,1)}) %all-gather.18.cloned.1.call-update) | async-done | bytes 6291472 | tf_op jit(solution)/shard_map/all_gather | solution.py:179
  339.8 3.9 multiply_reduce_fusion.7
  344.2 16.4 while.57
  361.4 3.9 multiply_reduce_fusion.6
  366.9 103.7 %all-gather.20.cloned.1.call-done = bf16[2048,4864]{1,0:T(8,128)(2,1)} async-done(((bf16[64,4864]{1,0:T(8,128)(2,1)}), bf16[2048,4864]{1,0:T(8,128)(2,1)}) %all-gather.20.cloned.1.call-update) | async-done | bytes 19922960 | tf_op jit(solution)/shard_map/all_gather | solution.py:181
  470.6 11.1 fusion.186
  481.7 119.4 %all-gather.24.cloned.1.call-done = bf16[4864,2048]{1,0:T(8,128)(2,1)} async-done(((bf16[152,2048]{1,0:T(8,128)(2,1)}), bf16[4864,2048]{1,0:T(8,128)(2,1)}) %all-gather.24.cloned.1.call-update) | async-done | bytes 19922960 | tf_op jit(solution)/shard_map/all_gather | solution.py:183
  601.1 12.2 fusion.129
  613.3 118.3 %all-gather.22.cloned.1.call-done = bf16[2048,4864]{1,0:T(8,128)(2,1)} async-done(((bf16[64,4864]{1,0:T(8,128)(2,1)}), bf16[2048,4864]{1,0:T(8,128)(2,1)}) %all-gather.22.cloned.1.call-update) | async-done | bytes 19922960 | tf_op jit(solution)/shard_map/all_gather | solution.py:182
  731.6 13.6 multiply_convert_fusion.5
  745.2 14.4 fusion.188
  759.6 12.4 multiply_reduce_fusion.3
  772.1 10.7 fusion.125
  782.8 8.7 fusion.187
  791.5 12.3 multiply_convert_fusion.4
  803.8 14.6 fusion.190
  818.4 12.9 multiply_reduce_fusion.2
  831.4 3.0 fusion.112
  835.4 3.0 convolution_convert_fusion.1
  841.3 47.5 %while.58 = (s32[]{:T(128)}, f32[6,128,4,64]{1,3,2,0:T(8,128)S(1)}, bf16[6,512,64]{1,2,0:T(8,128)(2,1)}, bf16[6,512,64]{1,2,0:T(8,128)(2,1)}, bf16[6,512,64]{1,2...) while((s32[]{:T(128)}, f32[6,128,4,64]{1,3,2,0:T(8,128)S(1)}, ...), condition=%wide.region_32.34_spmd.clone, body=%wide.region_30.33_spmd.clone.sunk | while | flops 170393088 | bytes 8867985 | solution.py:280
  888.8 6.0 convolution_convert_fusion
  898.3 39.8 %while.59 = (s32[]{:T(128)}, f32[6,128,4,64]{1,3,2,0:T(8,128)}, bf16[6,512,64]{1,2,0:T(8,128)(2,1)S(1)}, bf16[6,512,64]{1,2,0:T(8,128)(2,1)S(1)}, bf16[6,512,64]...) while((s32[]{:T(128)}, f32[6,128,4,64]{1,3,2,0:T(8,128)}, ...), condition=%wide.region_41.43_spmd.clone, body=%wide.region_39.42_spmd.clone.sunk | while | flops 170393088 | bytes 8867985 | solution.py:280
  949.2 2.5 fusion.122
  952.0 6.3 fusion.191
  958.3 6.1 fusion.189
  964.5 10.6 fusion.103
  975.1 3.6 fusion.102
  989.8 3.5 convolution_add_fusion.7
  994.9 9.8 reduce-scatter.39.cloned.1.call-done
  1004.8 3.7 fusion.111
  1009.9 8.1 gather_fusion
  1018.0 9.2 select_convert_fusion
  1032.8 2.4 convolution_add_fusion.5
  1037.2 7.5 convolution_add_fusion.4
  1047.8 6.7 convolution_add_fusion.3
  1055.9 16.6 fusion.192
  1072.5 29.1 convolution_add_fusion.1
  1102.8 16.0 fusion.193
  1118.9 29.4 %convolution_add_fusion = f32[2048,4864]{1,0:T(8,128)} fusion(f32[2048,4864]{1,0:T(8,128)} %fusion.193, bf16[128,2048]{1,0:T(8,128)(2,1)S(1)} %copy-done.26, bf16[128,4864]{1,0:T(8,128)(2,1)S(1)} %copy-done.24), kind=kOutput, calls=%fused_computation.125 | convolution fusion | flops 2560098304 | bytes 81461248 | tf_op jit(solution)/shard_map/dot_general | solution.py:62
  1149.8 16.2 fusion.127
  1166.0 29.1 convolution_add_fusion.2
  1195.9 40.2 %all-reduce.12 = (f32[2048]{0:T(1024)S(1)}, f32[64]{0:T(128)}, f32[64]{0:T(128)}, f32[2048]{0:T(1024)S(1)}) all-reduce(f32[2048]{0:T(1024)S(1)} %add.497, f32[64]{0:T(128)S(1)} %add.501, f32[64]{0:T(128)S(1)} %add.502, f32[2048]{0:T(1024)S(1)} %add.504), channel_id=7, replica_groups=mesh['dp'=8,'fsdp'=4] {'dp','fsdp'}, use_global_device_ids=true, to_apply=%region_50.52.clone | all-reduce | flops 4224 | bytes 33792
  1237.2 3.1 fusion.182
  1240.4 74.4 %reduce-scatter.27.cloned.1.call-done = f32[64,384]{1,0:T(8,128)} async-done(((f32[2048,384]{1,0:T(8,128)}), f32[64,384]{1,0:T(8,128)}) %reduce-scatter.27.cloned.1.call-update) | async-done | bytes 98320 | tf_op jit(solution)/shard_map/reduce_scatter | solution.py:336
  1314.7 161.9 %reduce-scatter.23.cloned.1.call-done = f32[64,1536]{1,0:T(8,128)} async-done(((f32[2048,1536]{1,0:T(8,128)}), f32[64,1536]{1,0:T(8,128)}) %reduce-scatter.23.cloned.1.call-update) | async-done | bytes 393232 | tf_op jit(solution)/shard_map/reduce_scatter | solution.py:334
  1476.6 161.0 %reduce-scatter.29.cloned.1.call-done = f32[48,2048]{1,0:T(8,128)} async-done(((f32[1536,2048]{1,0:T(8,128)}), f32[48,2048]{1,0:T(8,128)}) %reduce-scatter.29.cloned.1.call-update) | async-done | bytes 393232 | tf_op jit(solution)/shard_map/reduce_scatter | solution.py:337
  1637.6 420.8 %reduce-scatter.31.cloned.1.call-done = f32[64,4864]{1,0:T(8,128)} async-done(((f32[2048,4864]{1,0:T(8,128)}), f32[64,4864]{1,0:T(8,128)}) %reduce-scatter.31.cloned.1.call-update) | async-done | bytes 1245200 | tf_op jit(solution)/shard_map/reduce_scatter | solution.py:339
  2058.4 430.4 %reduce-scatter.33.cloned.1.call-done = f32[64,4864]{1,0:T(8,128)} async-done(((f32[2048,4864]{1,0:T(8,128)}), f32[64,4864]{1,0:T(8,128)}) %reduce-scatter.33.cloned.1.call-update) | async-done | bytes 1245200 | tf_op jit(solution)/shard_map/reduce_scatter | solution.py:340
  2488.8 430.6 %reduce-scatter.35.cloned.1.call-done = f32[152,2048]{1,0:T(8,128)} async-done(((f32[4864,2048]{1,0:T(8,128)}), f32[152,2048]{1,0:T(8,128)}) %reduce-scatter.35.cloned.1.call-update) | async-done | bytes 1245200 | tf_op jit(solution)/shard_map/reduce_scatter | solution.py:341
  (598 shorter events, 195.7 us)
Async XLA Ops:
  7.2 49.2 %copy-start.128 = (s32[1,4]{1,0:T(1,128)S(1)}, s32[1,4]{1,0:T(1,128)}, u32[]{:S(2)}) copy-start(s32[1,4]{1,0:T(1,128)} %param.27) | copy-start | bytes 52
  7.2 49.2 %copy-start.121 = (s32[1,4]{1,0:T(1,128)S(1)}, s32[1,4]{1,0:T(1,128)}, u32[]{:S(2)}) copy-start(s32[1,4]{1,0:T(1,128)} %param.28) | copy-start | bytes 52
  7.2 49.8 %copy-start.126 = (bf16[64]{0:T(256)(128)(2,1)S(1)}, bf16[64]{0:T(256)(128)(2,1)}, u32[]{:S(2)}) copy-start(bf16[64]{0:T(256)(128)(2,1)} %param.34) | copy-start | bytes 388
  7.2 49.8 %copy-start.127 = (bf16[64]{0:T(256)(128)(2,1)S(1)}, bf16[64]{0:T(256)(128)(2,1)}, u32[]{:S(2)}) copy-start(bf16[64]{0:T(256)(128)(2,1)} %param.33) | copy-start | bytes 388
  7.2 55.2 %all-gather.26.cloned.1.call-start = ((), (), s32[]{:S(2)}) async-start(), calls=%async_computation.20 | async-start | bytes 5242880 | tf_op jit(solution)/shard_map/all_gather | solution.py:160
  8.0 75.4 %all-gather.10.cloned.1.call-start = ((), (), s32[]{:S(2)}) async-start(), calls=%async_computation.12 | async-start | bytes 5242880 | tf_op jit(solution)/shard_map/all_gather | solution.py:159
  8.7 132.5 %all-gather.12.cloned.1.call-start = ((), (), s32[]{:S(2)}) async-start(), calls=%async_computation.13 | async-start | bytes 1622016 | tf_op jit(solution)/shard_map/all_gather | solution.py:178
  9.5 188.3 %all-gather.14.cloned.1.call-start = ((), (), s32[]{:S(2)}) async-start(), calls=%async_computation.14 | async-start | bytes 1622016 | tf_op jit(solution)/shard_map/all_gather | solution.py:177
  10.0 258.9 %all-gather.16.cloned.1.call-start = ((), (), s32[]{:S(2)}) async-start(), calls=%async_computation.15 | async-start | bytes 6488064 | tf_op jit(solution)/shard_map/all_gather | solution.py:176
  10.6 329.1 %all-gather.18.cloned.1.call-start = ((), (), s32[]{:S(2)}) async-start(), calls=%async_computation.16 | async-start | bytes 6488064 | tf_op jit(solution)/shard_map/all_gather | solution.py:179
  11.2 459.4 %all-gather.20.cloned.1.call-start = ((), (), s32[]{:S(2)}) async-start(), calls=%async_computation.17 | async-start | bytes 20545536 | tf_op jit(solution)/shard_map/all_gather | solution.py:181
  11.9 589.1 %all-gather.24.cloned.1.call-start = ((), (), s32[]{:S(2)}) async-start(), calls=%async_computation.19 | async-start | bytes 20545536 | tf_op jit(solution)/shard_map/all_gather | solution.py:183
  12.7 718.9 %all-gather.22.cloned.1.call-start = ((), (), s32[]{:S(2)}) async-start(), calls=%async_computation.18 | async-start | bytes 20545536 | tf_op jit(solution)/shard_map/all_gather | solution.py:182
  13.4 965.3 %reduce-scatter.37.cloned.1.call-start = ((), (), s32[]{:S(2)}) async-start(), calls=%async_computation.29 | async-start | bytes 491520
  56.4 218.2 %copy-start.49 = (f32[2048]{0:T(1024)}, f32[2048]{0:T(1024)S(1)}, u32[]{:S(2)}) copy-start(f32[2048]{0:T(1024)S(1)} %convert_element_type.243) | copy-start | bytes 24580
  57.0 145.4 %copy-start.106 = (f32[64]{0:T(128)}, f32[64]{0:T(128)S(1)}, u32[]{:S(2)}) copy-start(f32[64]{0:T(128)S(1)} %convert_element_type.247) | copy-start | bytes 772
  62.4 215.5 %copy-start.57 = (f32[128,32]{0,1:T(8,128)}, f32[128,32]{0,1:T(8,128)S(1)}, u32[]{:S(2)}) copy-start(f32[128,32]{0,1:T(8,128)S(1)} %get-tuple-element.507) | copy-start | bytes 49156
  62.4 215.5 %copy-start.59 = (f32[128,32]{0,1:T(8,128)}, f32[128,32]{0,1:T(8,128)S(1)}, u32[]{:S(2)}) copy-start(f32[128,32]{0,1:T(8,128)S(1)} %get-tuple-element.508) | copy-start | bytes 49156
  62.4 215.7 %copy-start.55 = (f32[128,32]{0,1:T(8,128)}, f32[128,32]{0,1:T(8,128)S(1)}, u32[]{:S(2)}) copy-start(f32[128,32]{0,1:T(8,128)S(1)} %get-tuple-element.524) | copy-start | bytes 49156
  91.9 269.5 %copy-start.1 = (bf16[256,2048]{1,0:T(8,128)(2,1)}, bf16[256,2048]{1,0:T(8,128)(2,1)S(1)}, u32[]{:S(2)}) copy-start(bf16[256,2048]{1,0:T(8,128)(2,1)S(1)} %get-tuple-element.510) | copy-start | bytes 3145732
  92.2 60.4 %copy-start.111 = (f32[128]{0:T(128)}, f32[128]{0:T(128)S(1)}, u32[]{:S(2)}) copy-start(f32[128]{0:T(128)S(1)} %get-tuple-element.338) | copy-start | bytes 1540
  92.2 60.4 %copy-start.113 = (f32[128]{0:T(128)}, f32[128]{0:T(128)S(1)}, u32[]{:S(2)}) copy-start(f32[128]{0:T(128)S(1)} %get-tuple-element.339) | copy-start | bytes 1540
  92.3 105.5 %copy-start.99 = (f32[128]{0:T(128)}, f32[128]{0:T(128)S(1)}, u32[]{:S(2)}) copy-start(f32[128]{0:T(128)S(1)} %fusion.152) | copy-start | bytes 1540
  152.1 47.9 %copy-start.102 = (f32[128]{0:T(128)}, f32[128]{0:T(128)S(1)}, u32[]{:S(2)}) copy-start(f32[128]{0:T(128)S(1)} %fusion.154) | copy-start | bytes 1540
  200.0 74.5 %copy-start.42 = (f32[128,384]{0,1:T(8,128)}, f32[128,384]{0,1:T(8,128)S(1)}, u32[]{:S(2)}) copy-start(f32[128,384]{0,1:T(8,128)S(1)} %fusion.168) | copy-start | bytes 589828
  200.0 68.9 %copy-start.100 = (f32[128]{0:T(128)S(1)}, f32[128]{0:T(128)}, u32[]{:S(2)}) copy-start(f32[128]{0:T(128)} %copy-done.99) | copy-start | bytes 1540
  200.1 74.4 %copy-start.90 = (f32[128,6]{0,1:T(8,128)}, f32[128,6]{0,1:T(8,128)S(1)}, u32[]{:S(2)}) copy-start(f32[128,6]{0,1:T(8,128)S(1)} %multiply_reduce_fusion.19) | copy-start | bytes 9220
  202.3 72.2 %copy-start.43 = (f32[128,384]{0,1:T(8,128)}, f32[128,384]{0,1:T(8,128)S(1)}, u32[]{:S(2)}) copy-start(f32[128,384]{0,1:T(8,128)S(1)} %fusion.176) | copy-start | bytes 589828
  202.3 72.2 %copy-start.89 = (f32[128,6]{0,1:T(8,128)}, f32[128,6]{0,1:T(8,128)S(1)}, u32[]{:S(2)}) copy-start(f32[128,6]{0,1:T(8,128)S(1)} %multiply_reduce_fusion.18) | copy-start | bytes 9220
  217.1 57.5 %copy-start.103 = (f32[128]{0:T(128)S(1)}, f32[128]{0:T(128)}, u32[]{:S(2)}) copy-start(f32[128]{0:T(128)} %copy-done.102) | copy-start | bytes 1540
  295.3 44.4 %copy-start.45 = (bf16[6,128,4,64]{1,3,2,0:T(8,128)(2,1)}, bf16[6,128,4,64]{1,3,2,0:T(8,128)(2,1)S(1)}, u32[]{:S(2)}) copy-start(bf16[6,128,4,64]{1,3,2,0:T(8,128)(2,1)S(1)} %get-tuple-element.1037) | copy-start | bytes 1179652
  295.3 44.4 %copy-start.67 = (s32[512]{0:T(512)}, s32[512]{0:T(512)S(1)}, u32[]{:S(2)}) copy-start(s32[512]{0:T(512)S(1)} %get-tuple-element.1065) | copy-start | bytes 6148
  295.3 44.4 %copy-start.68 = (s32[512]{0:T(512)}, s32[512]{0:T(512)S(1)}, u32[]{:S(2)}) copy-start(s32[512]{0:T(512)S(1)} %get-tuple-element.1066) | copy-start | bytes 6148
  295.3 44.4 %copy-start.85 = (s32[128]{0:T(128)}, s32[128]{0:T(128)S(1)}, u32[]{:S(2)}) copy-start(s32[128]{0:T(128)S(1)} %get-tuple-element.1075) | copy-start | bytes 1540
  295.3 44.4 %copy-start.86 = (s32[128]{0:T(128)}, s32[128]{0:T(128)S(1)}, u32[]{:S(2)}) copy-start(s32[128]{0:T(128)S(1)} %get-tuple-element.1076) | copy-start | bytes 1540
  295.4 44.4 %copy-start.87 = (f32[6,4,128,1]{2,1,3,0:T(4,128)}, f32[6,4,128,1]{2,1,3,0:T(4,128)S(1)}, u32[]{:S(2)}) copy-start(f32[6,4,128,1]{2,1,3,0:T(4,128)S(1)} %get-tuple-element.912) | copy-start | bytes 36868
  295.4 48.3 %copy-start.20 = (bf16[6,128,4,64]{1,3,2,0:T(8,128)(2,1)}, bf16[6,128,4,64]{1,3,2,0:T(8,128)(2,1)S(1)}, u32[]{:S(2)}) copy-start(bf16[6,128,4,64]{1,3,2,0:T(8,128)(2,1)S(1)} %get-tuple-element.198) | copy-start | bytes 1179652
  365.4 394.2 %copy-start.3 = (f32[128,2048]{1,0:T(8,128)}, f32[128,2048]{1,0:T(8,128)S(1)}, u32[]{:S(2)}) copy-start(f32[128,2048]{1,0:T(8,128)S(1)} %get-tuple-element.530) | copy-start | bytes 3145732
  366.9 234.2 %copy-start.6 = (bf16[256,2048]{1,0:T(8,128)(2,1)S(1)}, bf16[256,2048]{1,0:T(8,128)(2,1)}, u32[]{:S(2)}) copy-start(bf16[256,2048]{1,0:T(8,128)(2,1)} %get-tuple-element.509) | copy-start | bytes 3145732
  772.1 19.4 copy-start.25
  803.8 31.6 %slice-start.5 = ((s8[6291456]{0:T(1024)(128)(4,1)}), s8[2097152]{0:T(1024)(128)(4,1)S(1)}, s32[]{:S(2)}) async-start(s8[6291456]{0:T(1024)(128)(4,1)} %bitcast.427), calls=%async_computation.38 | async-start | bytes 4194304
  818.4 17.0 slice-start.6
  841.3 47.5 %copy-start.13 = (f32[128,2048]{1,0:T(8,128)S(1)}, f32[128,2048]{1,0:T(8,128)}, u32[]{:S(2)}) copy-start(f32[128,2048]{1,0:T(8,128)} %get-tuple-element.475) | copy-start | bytes 3145732
  897.1 83.6 %reduce-scatter.41.cloned.1.call-start = ((), (), s32[]{:S(2)}) async-start(), calls=%async_computation.31 | async-start | bytes 491520
  898.3 40.9 %copy-start.105 = (s32[1024,1]{0,1:T(1,128)S(1)}, s32[1024,1]{0,1:T(1,128)}, u32[]{:S(2)}) copy-start(s32[1024,1]{0,1:T(1,128)} %compare_select_fusion) | copy-start | bytes 12292
  898.3 41.5 %copy-start.92 = (s32[1024]{0:T(1024)S(1)}, s32[1024]{0:T(1024)}, u32[]{:S(2)}) copy-start(s32[1024]{0:T(1024)} %copy-done.91) | copy-start | bytes 12292
  898.3 41.5 %copy-start.94 = (s32[1024]{0:T(1024)S(1)}, s32[1024]{0:T(1024)}, u32[]{:S(2)}) copy-start(s32[1024]{0:T(1024)} %copy-done.93) | copy-start | bytes 12292
  898.3 43.1 %copy-start.58 = (f32[128,32]{0,1:T(8,128)S(1)}, f32[128,32]{0,1:T(8,128)}, u32[]{:S(2)}) copy-start(f32[128,32]{0,1:T(8,128)} %copy-done.57) | copy-start | bytes 49156
  898.3 43.0 %copy-start.60 = (f32[128,32]{0,1:T(8,128)S(1)}, f32[128,32]{0,1:T(8,128)}, u32[]{:S(2)}) copy-start(f32[128,32]{0,1:T(8,128)} %copy-done.59) | copy-start | bytes 49156
  939.2 50.6 %reduce-scatter.43.cloned.1.call-start = ((), (), s32[]{:S(2)}) async-start(), calls=%async_computation.32 | async-start | bytes 491520
  944.8 60.0 %reduce-scatter.39.cloned.1.call-start = ((), (), s32[]{:S(2)}) async-start(), calls=%async_computation.30 | async-start | bytes 491520
  951.7 285.5 %reduce-scatter.21.cloned.1.call-start = ((), (), s32[]{:S(2)}) async-start(), calls=%async_computation.21 | async-start | bytes 10485760 | tf_op jit(solution)/shard_map/reduce_scatter | solution.py:352
  958.3 16.8 slice-start.1
  1027.2 213.1 %reduce-scatter.25.cloned.1.call-start = ((), (), s32[]{:S(2)}) async-start(), calls=%async_computation.23 | async-start | bytes 3244032 | tf_op jit(solution)/shard_map/reduce_scatter | solution.py:335
  1031.2 283.5 %reduce-scatter.27.cloned.1.call-start = ((), (), s32[]{:S(2)}) async-start(), calls=%async_computation.24 | async-start | bytes 3244032 | tf_op jit(solution)/shard_map/reduce_scatter | solution.py:336
  1035.2 441.4 %reduce-scatter.23.cloned.1.call-start = ((), (), s32[]{:S(2)}) async-start(), calls=%async_computation.22 | async-start | bytes 12976128 | tf_op jit(solution)/shard_map/reduce_scatter | solution.py:334
  1044.7 592.9 %reduce-scatter.29.cloned.1.call-start = ((), (), s32[]{:S(2)}) async-start(), calls=%async_computation.25 | async-start | bytes 12976128 | tf_op jit(solution)/shard_map/reduce_scatter | solution.py:337
  1054.5 18.0 copy-start.26
  1054.5 18.0 copy-start.36
  1054.5 1003.9 %reduce-scatter.31.cloned.1.call-start = ((), (), s32[]{:S(2)}) async-start(), calls=%async_computation.26 | async-start | bytes 41091072 | tf_op jit(solution)/shard_map/reduce_scatter | solution.py:339
  1101.6 17.3 copy-start.24
  1101.6 1387.2 %reduce-scatter.33.cloned.1.call-start = ((), (), s32[]{:S(2)}) async-start(), calls=%async_computation.27 | async-start | bytes 41091072 | tf_op jit(solution)/shard_map/reduce_scatter | solution.py:340
  1148.3 17.8 copy-start.30
  1148.3 1771.1 %reduce-scatter.35.cloned.1.call-start = ((), (), s32[]{:S(2)}) async-start(), calls=%async_computation.28 | async-start | bytes 41091072 | tf_op jit(solution)/shard_map/reduce_scatter | solution.py:341
  (93 other events, 499.4 us)
Sparse Core Ops, SparseCore 0:
  9.6 37.8 all-gather.25
  49.1 34.2 all-gather.9
  86.2 54.9 all-gather.11
  143.9 53.8 all-gather.13
  200.5 68.3 all-gather.15
  271.6 68.0 all-gather.17
  342.5 128.0 all-gather.19
  473.4 127.5 all-gather.23
  603.9 127.5 all-gather.21
  897.2 18.8 reduce-scatter.36
  939.3 18.8 reduce-scatter.40
  960.6 20.7 reduce-scatter.42
  983.9 20.7 reduce-scatter.38
  1027.4 71.6 reduce-scatter.20
  1105.8 101.5 reduce-scatter.24
  1214.1 100.5 reduce-scatter.26
  1322.2 154.3 reduce-scatter.22
  1483.0 154.4 reduce-scatter.28
  1640.5 417.7 reduce-scatter.30
  2061.2 427.5 reduce-scatter.32
  2491.8 427.5 reduce-scatter.34
where the time goes:
time: 2950 us; the launch traced here: 2930 us
  waiting for transfers between devices  2230 us (76%)
  matrix products  451 us (15%)
  blocking collectives  110 us (4%)
  local copies, waits for them, and re-layouts  61.1 us (2%)
  other arithmetic  51 us (2%)
    reduce_scatter x1, waiting for transfers between devices, local(): lax.psum_scatter(totals[8], ('dp', 'fsdp'), scatter_dimension=0, tiled=True)  431 us
    reduce_scatter x1, waiting for transfers between devices, local(): lax.psum_scatter(totals[7], ('dp', 'fsdp'), scatter_dimension=0, tiled=True)  430 us
    reduce_scatter x1, waiting for transfers between devices, local(): lax.psum_scatter(totals[6], ('dp', 'fsdp'), scatter_dimension=0, tiled=True)  421 us
    reduce_scatter x1, waiting for transfers between devices, local(): lax.psum_scatter(totals[1], ('dp', 'fsdp'), scatter_dimension=0, tiled=True)  162 us
    reduce_scatter x1, waiting for transfers between devices, local(): lax.psum_scatter(totals[4], ('dp', 'fsdp'), scatter_dimension=0, tiled=True)  161 us
    dot_general x14, matrix products, left_transposed(): lax.dot_general(left_side, right_side, (((0,), (0,)), ((), ())), preferre...  160 us
    all_gather x1, waiting for transfers between devices, local(): lax.all_gather(w_down, ('dp', 'fsdp'), axis=0, tiled=True)  119 us
    all_gather x1, waiting for transfers between devices, local(): lax.all_gather(w_up, ('dp', 'fsdp'), axis=0, tiled=True)  118 us
  transfers between devices with their start and end apart: 21, of which 15 were waited for; matrix products, arithmetic and copies ran while one was open for 12% of the time, Pallas kernels for 0%

commit v1 on v0

v1 whole, which is shorter than its diff:
```python
import functools
import math

import jax
import jax.numpy as jnp
from jax import lax
from jax.experimental import pallas as pl
from jax.experimental.pallas import tpu as pltpu
from jax.sharding import PartitionSpec as P

HEADS = 24
KV_HEADS = 6
HD = 64
EPSILON = 1e-06
MASKED = -1e30
LANES = 128
BOTH = ("dp", "fsdp")
F32 = jnp.float32
BF16 = jnp.bfloat16
VMEM_LIMIT = 48 * 1024 * 1024


def product(left, right):
    return jnp.dot(left, right, preferred_element_type=F32)


def right_transposed(left, right):
    return lax.dot_general(left, right, (((1,), (1,)), ((), ())), preferred_element_type=F32)


def left_transposed(left, right):
    return lax.dot_general(left, right, (((0,), (0,)), ((), ())), preferred_element_type=F32)


def half_sums(values):
    rows = lax.broadcasted_iota(jnp.int32, (LANES, LANES), 0) // HD
    cols = lax.broadcasted_iota(jnp.int32, (LANES, LANES), 1) // HD
    same = (rows == cols).astype(F32)
    return jnp.dot(values, same, precision=lax.Precision.HIGHEST, preferred_element_type=F32)


def swapped_halves(values):
    lane = lax.broadcasted_iota(jnp.int32, values.shape, 1) % HD
    return jnp.where(
        lane < HD // 2, pltpu.roll(values, LANES - HD // 2, 1), pltpu.roll(values, HD // 2, 1)
    )


def head_prep_kernel(pre_ref, cos_ref, sin_ref, gain_ref, q_ref, kv_ref):
    q_blocks = HEADS * HD // LANES
    k_blocks = KV_HEADS * HD // LANES
    cosine, sine = cos_ref[...], sin_ref[...]
    for block in range(q_blocks + k_blocks):
        at = pl.ds(block * LANES, LANES)
        u = pre_ref[:, at]
        n = u * lax.rsqrt(half_sums(u * u) / HD + EPSILON) * gain_ref[:1, at]
        turned = n * cosine + swapped_halves(n) * sine
        if block < q_blocks:
            q_ref[:, at] = turned.astype(BF16)
        else:
            kv_ref[0, :, pl.ds((block - q_blocks) * LANES, LANES)] = turned.astype(BF16)
    v_at = (q_blocks + k_blocks) * LANES
    kv_ref[1] = pre_ref[:, v_at : v_at + k_blocks * LANES].astype(BF16)


def head_prep(pre, cosine, sine, gains):
    rows = pre.shape[0]
    return pl.pallas_call(
        head_prep_kernel,
        out_shape=(
            jax.ShapeDtypeStruct((rows, HEADS * HD), BF16),
            jax.ShapeDtypeStruct((2, rows, KV_HEADS * HD), BF16),
        ),
        compiler_params=pltpu.CompilerParams(vmem_limit_bytes=VMEM_LIMIT),
        name="head_prep",
    )(pre, cosine, sine, gains)


def head_back_kernel(
    gq_ref, gkv_ref, one_ref, two_ref, pre_ref, cos_ref, sin_ref, gain_ref, out_ref, sums_ref
):
    q_blocks = HEADS * HD // LANES
    k_blocks = KV_HEADS * HD // LANES
    cosine, sine = cos_ref[...], sin_ref[...]
    sums_ref[...] = jnp.zeros_like(sums_ref)
    for block in range(q_blocks + k_blocks):
        at = pl.ds(block * LANES, LANES)
        if block < q_blocks:
            g = gq_ref[:, at]
        else:
            k_at = pl.ds((block - q_blocks) * LANES, LANES)
            g = gkv_ref[0, :, k_at] + one_ref[0, :, k_at].astype(F32) + two_ref[0, :, k_at].astype(F32)
        g = g * cosine - swapped_halves(g) * sine
        u = pre_ref[:, at]
        inverse = lax.rsqrt(half_sums(u * u) / HD + EPSILON)
        unit = u * inverse
        row = 0 if block < q_blocks else 1
        sums_ref[row : row + 1, :] += jnp.sum(unit * g, axis=0, keepdims=True)
        e = g * gain_ref[:1, at]
        out_ref[:, at] = (inverse * (e - unit * (half_sums(e * unit) / HD))).astype(BF16)
    v_at = (q_blocks + k_blocks) * LANES
    width = k_blocks * LANES
    out_ref[:, v_at : v_at + width] = (
        gkv_ref[1] + one_ref[1].astype(F32) + two_ref[1].astype(F32)
    ).astype(BF16)
    tail = out_ref.shape[1] - v_at - width
    out_ref[:, v_at + width :] = jnp.zeros((out_ref.shape[0], tail), BF16)


def head_back(gq, gkv, one, two, pre, cosine, sine, gains):
    rows, width = pre.shape
    return pl.pallas_call(
        head_back_kernel,
        out_shape=(
            jax.ShapeDtypeStruct((rows, width), BF16),
            jax.ShapeDtypeStruct((8, LANES), F32),
        ),
        compiler_params=pltpu.CompilerParams(vmem_limit_bytes=VMEM_LIMIT),
        name="head_back",
    )(gq, gkv, one, two, pre, cosine, sine, gains)


def stacked_heads(ref, pair, repeat):
    return jnp.concatenate(
        [ref[:, pl.ds((pair * repeat + h) * HD, HD)] for h in range(repeat)], axis=0
    )


def window_probs(q4, keys, rel, repeat):
    rows, span = rel.shape[0], keys.shape[0]
    scores = right_transposed(q4, keys).reshape(repeat, rows, span)
    key_at = lax.broadcasted_iota(jnp.int32, (rows, span), 1) - (span - rows)
    row_at = lax.broadcasted_iota(jnp.int32, (rows, span), 0)
    allowed = (key_at <= row_at) & (key_at >= rel)
    scores = jnp.where(allowed[None], scores, MASKED)
    top = jnp.max(scores, axis=-1, keepdims=True)
    raised = jnp.exp(scores - top)
    return raised * (1.0 / jnp.sum(raised, axis=-1, keepdims=True))


def attend_kernel(q_ref, two_ref, one_ref, kv_ref, rel_ref, out_ref):
    repeat = HEADS // KV_HEADS
    rows = q_ref.shape[0]
    rel = rel_ref[:, :1]
    keys = jnp.concatenate([two_ref[0], one_ref[0], kv_ref[0]], axis=0)
    vals = jnp.concatenate([two_ref[1], one_ref[1], kv_ref[1]], axis=0)
    for pair in range(2):
        part = slice(pair * HD, (pair + 1) * HD)
        q4 = stacked_heads(q_ref, pair, repeat)
        probs = window_probs(q4, keys[:, part], rel, repeat)
        low = probs.astype(BF16).reshape(repeat * rows, -1)
        mixed = product(low, vals[:, part])
        for h in range(repeat):
            out_ref[:, pl.ds((pair * repeat + h) * HD, HD)] = mixed[
                h * rows : (h + 1) * rows
            ].astype(BF16)


def attend_specs(rows):
    q_spec = pl.BlockSpec((rows, HEADS * HD // 3), lambda g: (0, g))
    kv_spec = pl.BlockSpec((2, rows, LANES), lambda g: (0, 0, g))
    rel_spec = pl.BlockSpec((rows, LANES), lambda g: (0, 0))
    return q_spec, kv_spec, rel_spec


def attend(q, two, one, kv, rel):
    rows = q.shape[0]
    q_spec, kv_spec, rel_spec = attend_specs(rows)
    return pl.pallas_call(
        attend_kernel,
        grid=(3,),
        in_specs=[q_spec, kv_spec, kv_spec, kv_spec, rel_spec],
        out_specs=q_spec,
        out_shape=jax.ShapeDtypeStruct((rows, HEADS * HD), BF16),
        compiler_params=pltpu.CompilerParams(vmem_limit_bytes=VMEM_LIMIT),
        name="attend",
    )(q, two, one, kv, rel)


def attend_back_kernel(
    q_ref, two_ref, one_ref, kv_ref, rel_ref, gm_ref, gq_ref, gtwo_ref, gone_ref, gkv_ref
):
    repeat = HEADS // KV_HEADS
    rows = q_ref.shape[0]
    rel = rel_ref[:, :1]
    keys = jnp.concatenate([two_ref[0], one_ref[0], kv_ref[0]], axis=0)
    vals = jnp.concatenate([two_ref[1], one_ref[1], kv_ref[1]], axis=0)
    key_grads, val_grads = [], []
    for pair in range(2):
        part = slice(pair * HD, (pair + 1) * HD)
        q4 = stacked_heads(q_ref, pair, repeat)
        gm4 = stacked_heads(gm_ref, pair, repeat)
        probs = window_probs(q4, keys[:, part], rel, repeat)
        grad_probs = right_transposed(gm4, vals[:, part]).reshape(probs.shape)
        weighted = jnp.sum(probs * grad_probs, axis=-1, keepdims=True)
        span = probs.shape[-1]
        gs = (probs * (grad_probs - weighted)).astype(BF16).reshape(repeat * rows, span)
        low = probs.astype(BF16).reshape(repeat * rows, span)
        gq = product(gs, keys[:, part]) * (1.0 / math.sqrt(HD))
        for h in range(repeat):
            gq_ref[:, pl.ds((pair * repeat + h) * HD, HD)] = gq[h * rows : (h + 1) * rows]
        key_grads.append(product(q4.T, gs).T)
        val_grads.append(product(gm4.T, low).T)
    for at, parts in ((0, key_grads), (1, val_grads)):
        both = jnp.concatenate(parts, axis=1)
        gtwo_ref[at] = both[:rows].astype(gtwo_ref.dtype)
        gone_ref[at] = both[rows : 2 * rows].astype(gone_ref.dtype)
        gkv_ref[at] = both[2 * rows :]


def attend_back(q, two, one, kv, rel, gm):
    rows = q.shape[0]
    q_spec, kv_spec, rel_spec = attend_specs(rows)
    return pl.pallas_call(
        attend_back_kernel,
        grid=(3,),
        in_specs=[q_spec, kv_spec, kv_spec, kv_spec, rel_spec, q_spec],
        out_specs=(q_spec, kv_spec, kv_spec, kv_spec),
        out_shape=(
            jax.ShapeDtypeStruct((rows, HEADS * HD), F32),
            jax.ShapeDtypeStruct((2, rows, KV_HEADS * HD), BF16),
            jax.ShapeDtypeStruct((2, rows, KV_HEADS * HD), BF16),
            jax.ShapeDtypeStruct((2, rows, KV_HEADS * HD), F32),
        ),
        compiler_params=pltpu.CompilerParams(vmem_limit_bytes=VMEM_LIMIT),
        name="attend_back",
    )(q, two, one, kv, rel, gm)


class Ring:
    def __init__(self, depth):
        self.depth = depth
        self.arrived = []

    def send(self, value, axis, pairs):
        if len(self.arrived) >= self.depth:
            value, _ = lax.optimization_barrier((value, self.arrived[-self.depth]))
        out = lax.ppermute(value, axis, pairs)
        self.arrived.append(out)
        return out


def swap_pairs(size, bit):
    return [(i, i ^ bit) for i in range(size)]


def far_pairs(size, shift):
    far = size // 2
    return [(i, (i // 2 + shift) % far * 2 + i % 2) for i in range(size)]


def far_order(far):
    order = []
    for step in range(1, far // 2 + 1):
        order.append(step)
        if far - step != step:
            order.append(far - step)
    return order


def gather_dp(piece, size, ring):
    mine = lax.axis_index("dp")
    far, near = mine // 2, mine % 2
    held = [(0, piece)]
    for shift in far_order(size // 2):
        held.append((shift, ring.send(piece, "dp", far_pairs(size, shift))))
    out = jnp.zeros((size,) + piece.shape, piece.dtype)
    zero = jnp.int32(0)
    for shift, value in held:
        other = lax.ppermute(value, "dp", swap_pairs(size, 1))
        base = (far + size // 2 - shift) % (size // 2) * 2
        out = lax.dynamic_update_slice(out, value[None], (base + near, zero, zero))
        out = lax.dynamic_update_slice(out, other[None], (base + 1 - near, zero, zero))
    return out


def scatter_dp(terms, size, ring):
    mine = lax.axis_index("dp")
    far, near = mine // 2, mine % 2
    total = None
    for shift in far_order(size // 2) + [0]:
        base = (far + shift) % (size // 2) * 2
        other = lax.dynamic_index_in_dim(terms, base + 1 - near, 0, keepdims=False)
        own = lax.dynamic_index_in_dim(terms, base + near, 0, keepdims=False)
        got = lax.ppermute(other, "dp", swap_pairs(size, 1))
        pair = own.astype(F32) + got.astype(F32)
        if shift:
            pair = ring.send(pair.astype(BF16), "dp", far_pairs(size, shift)).astype(F32)
        total = pair if total is None else total + pair
    return total


def gather_rows(rows):
    core, chip = swap_pairs(4, 1), swap_pairs(4, 2)
    near = lax.ppermute(rows, "fsdp", core)
    far = lax.ppermute(rows, "fsdp", chip)
    both = lax.ppermute(far, "fsdp", core)
    return jnp.concatenate([rows, near, far, both], axis=0)


def scatter_rows(partial):
    rows = partial.shape[0] // 4
    core, chip = swap_pairs(4, 1), swap_pairs(4, 2)
    parts = partial.reshape(4, rows, -1)
    far = lax.ppermute(parts[3].astype(BF16), "fsdp", core)
    far = parts[2] + far.astype(F32)
    far = lax.ppermute(far.astype(BF16), "fsdp", chip)
    near = lax.ppermute(parts[1].astype(BF16), "fsdp", core)
    return parts[0] + near.astype(F32) + far.astype(F32)


def sum_all(value, dp_size):
    for axis, size in (("fsdp", 4), ("dp", dp_size)):
        bit = 1
        while bit < size:
            value = value + lax.ppermute(value, axis, swap_pairs(size, bit))
            bit *= 2
    return value


def local(
    tokens,
    cotangent,
    seq_lengths,
    deal_order,
    attn_gain,
    w_query,
    w_key,
    w_value,
    q_gain,
    k_gain,
    w_out,
    ffn_gain,
    w_gate,
    w_up,
    w_down,
):
    rows, width = tokens.shape
    dp_size = lax.axis_size("dp")
    shard = w_gate.shape[0]
    ff_rows = w_down.shape[0]
    member = lax.axis_index("fsdp")

    lengths = seq_lengths[0]
    slots = jnp.arange(lengths.shape[0], dtype=jnp.int32)
    starts = jnp.sum(jnp.where(slots[None, :] < slots[:, None], lengths[None, :], 0), axis=1)
    row_ids = member * rows + jnp.arange(rows, dtype=jnp.int32)
    begun = starts[None, :] <= row_ids[:, None]
    row_start = jnp.max(jnp.where(begun, starts[None, :], 0), axis=1)
    place = row_ids - row_start
    rel = jnp.broadcast_to((row_start - member * rows)[:, None], (rows, LANES))
    frequency = 10000.0 ** (-2.0 * jnp.arange(HD // 2, dtype=F32) / HD)
    angles = place.astype(F32)[:, None] * frequency[None, :]
    cosine, sine = jnp.cos(angles), jnp.sin(angles)
    cosine = jnp.concatenate([cosine] * 4, axis=1)
    sine = jnp.concatenate([-sine, sine, -sine, sine], axis=1)
    head_gains = jnp.concatenate([jnp.tile(q_gain, HEADS), jnp.tile(k_gain, KV_HEADS)])
    head_gains = jnp.broadcast_to(head_gains.astype(F32)[None, :], (8, head_gains.shape[0]))

    gain_columns = jnp.pad(
        jnp.stack([attn_gain, ffn_gain], axis=1), ((0, 0), (0, LANES - 2))
    )
    w_qkv = jnp.concatenate([w_query, w_key, w_value, gain_columns], axis=1)
    full_qkv = lax.all_gather(w_qkv, BOTH, axis=0, tiled=True)
    full_out = lax.all_gather(w_out, BOTH, axis=0, tiled=True)

    def quarters(weight):
        split = weight.reshape(shard, dp_size, 4, ff_rows)
        return jnp.moveaxis(split, 2, 0).reshape(4, shard, dp_size * ff_rows)

    ring = Ring(2)
    gate_piece = lax.all_to_all(quarters(w_gate), "fsdp", 0, 0, tiled=True)
    up_piece = lax.all_to_all(quarters(w_up), "fsdp", 0, 0, tiled=True)
    ff_width = dp_size * ff_rows
    my_gate = gather_dp(gate_piece.reshape(4 * shard, ff_width), dp_size, ring)
    my_up = gather_dp(up_piece.reshape(4 * shard, ff_width), dp_size, ring)
    my_down = gather_dp(w_down, dp_size, ring)
    my_gate = my_gate.reshape(width, ff_width)
    my_up = my_up.reshape(width, ff_width)
    my_down = my_down.reshape(ff_width, width)

    gain_table = full_qkv[:, full_qkv.shape[1] - LANES :]
    pick = (
        lax.broadcasted_iota(jnp.int32, (8, LANES), 0)
        == lax.broadcasted_iota(jnp.int32, (8, LANES), 1)
    ).astype(BF16)
    gain_rows = right_transposed(pick, gain_table)
    attn_row, ffn_row = gain_rows[0:1], gain_rows[1:2]
    x = tokens.astype(F32)
    x_inverse = lax.rsqrt(jnp.mean(x * x, axis=-1, keepdims=True) + EPSILON)
    normed = (x * x_inverse * attn_row).astype(BF16)
    pre = product(normed, full_qkv)
    queries, kv = head_prep(pre, cosine, sine, head_gains)
    queries = queries * jnp.bfloat16(1.0 / math.sqrt(HD))
    ahead_one = [(i, i + 1) for i in range(3)]
    ahead_two = [(i, i + 2) for i in range(2)]
    kv_one = lax.ppermute(kv, "fsdp", ahead_one)
    kv_two = lax.ppermute(kv, "fsdp", ahead_two)
    mixed = attend(queries, kv_two, kv_one, kv, rel)
    hidden = x + product(mixed, full_out)
    h_inverse = lax.rsqrt(jnp.mean(hidden * hidden, axis=-1, keepdims=True) + EPSILON)
    ffn_mine = (hidden * h_inverse * ffn_row).astype(BF16)

    upstream = gather_rows(cotangent)
    ffn_low = gather_rows(ffn_mine)
    gate = product(ffn_low, my_gate)
    up = product(ffn_low, my_up)
    sig = 1.0 / (1.0 + jnp.exp(-gate))
    silu = gate * sig
    act_low = (silu * up).astype(BF16)
    back = Ring(2)
    term_down = left_transposed(act_low, upstream).astype(BF16)
    down_grad = scatter_dp(term_down.reshape(dp_size, ff_rows, width), dp_size, back)
    grad_act = right_transposed(upstream, my_down)
    grad_gate = (grad_act * up * sig * (1.0 + gate * (1.0 - sig))).astype(BF16)
    grad_up = (grad_act * silu).astype(BF16)
    grad_ffn = scatter_rows(right_transposed(grad_gate, my_gate) + right_transposed(grad_up, my_up))
    term_gate = left_transposed(ffn_low, grad_gate).astype(BF16)
    term_up = left_transposed(ffn_low, grad_up).astype(BF16)
    gate_sum = scatter_dp(term_gate.reshape(dp_size, 4 * shard, ff_width), dp_size, back)
    up_sum = scatter_dp(term_up.reshape(dp_size, 4 * shard, ff_width), dp_size, back)
    output = (hidden + scatter_rows(product(act_low, my_down))).astype(BF16)

    def whole_rows(total):
        sent = total.astype(BF16).reshape(4, shard, ff_width)
        got = lax.all_to_all(sent, "fsdp", 0, 0, tiled=True)
        split = jnp.moveaxis(got.reshape(4, shard, dp_size, ff_rows), 0, 2)
        return split.reshape(shard, 4 * ff_width).astype(F32)

    gate_grad = whole_rows(gate_sum)
    up_grad = whole_rows(up_sum)

    e = grad_ffn * ffn_row
    slope = jnp.mean(hidden * e, axis=-1, keepdims=True)
    grad_hidden = cotangent.astype(F32) + h_inverse * e - hidden * (h_inverse**3 * slope)
    ffn_gain_term = jnp.sum(grad_ffn * hidden * h_inverse, axis=0)
    grad_hidden_low = grad_hidden.astype(BF16)
    grad_mixed = right_transposed(grad_hidden_low, full_out).astype(BF16)
    term_out = left_transposed(mixed, grad_hidden_low).astype(BF16)
    out_grad = lax.psum_scatter(term_out, BOTH, scatter_dimension=0, tiled=True).astype(F32)
    gq, gkv_two, gkv_one, gkv = attend_back(queries, kv_two, kv_one, kv, rel, grad_mixed)
    got_one = lax.ppermute(gkv_one, "fsdp", [(b, a) for a, b in ahead_one])
    got_two = lax.ppermute(gkv_two, "fsdp", [(b, a) for a, b in ahead_two])
    grad_pre, head_sums = head_back(gq, gkv, got_one, got_two, pre, cosine, sine, head_gains)
    term_qkv = left_transposed(normed, grad_pre).astype(BF16)
    qkv_grad = lax.psum_scatter(term_qkv, BOTH, scatter_dimension=0, tiled=True).astype(F32)
    grad_normed = right_transposed(grad_pre, full_qkv)
    e = grad_normed * attn_row
    slope = jnp.mean(x * e, axis=-1, keepdims=True)
    input_grad = grad_hidden + x_inverse * e - x * (x_inverse**3 * slope)
    attn_gain_term = jnp.sum(grad_normed * x * x_inverse, axis=0)

    small = jnp.concatenate([attn_gain_term, ffn_gain_term, head_sums.reshape(-1)])
    small = sum_all(small.reshape(-1, LANES), dp_size).reshape(-1)
    mine = (lax.axis_index("dp") * 4 + member) * shard
    attn_gain_grad = lax.dynamic_slice(small, (mine,), (shard,))
    ffn_gain_grad = lax.dynamic_slice(small, (width + mine,), (shard,))
    head_total = small[2 * width : 2 * width + 2 * LANES].reshape(2, 2, HD).sum(axis=1)

    q_end = HEADS * HD
    k_end = q_end + KV_HEADS * HD
    v_end = k_end + KV_HEADS * HD
    return (
        output,
        input_grad.astype(BF16),
        attn_gain_grad,
        qkv_grad[:, :q_end],
        qkv_grad[:, q_end:k_end],
        qkv_grad[:, k_end:v_end],
        head_total[0],
        head_total[1],
        out_grad,
        ffn_gain_grad,
        gate_grad,
        up_grad,
        down_grad,
    )


def solution(mesh):
    rows = P(BOTH, None)
    vector = P(BOTH)
    in_specs = (
        rows,
        rows,
        P("dp", None),
        P("dp", None),
        vector,
        rows,
        rows,
        rows,
        P(),
        P(),
        rows,
        vector,
        rows,
        rows,
        rows,
    )
    out_specs = (rows, rows, vector, rows, rows, rows, P(), P(), rows, vector, rows, rows, rows)
    return jax.shard_map(local, mesh=mesh, in_specs=in_specs, out_specs=out_specs, check_vma=False)
```

time: 2950 us -> 1410 us (0.48)
  waiting for transfers between devices: 2230 us -> 401 us
  local copies, waits for them, and re-layouts: 61.1 us -> 649 us
  matrix products: 451 us -> 118 us
  starting transfers between devices: 1.01 us -> 136 us
  blocking collectives: 110 us -> 0 us
  Pallas kernels: 0 us -> 37 us
    reduce_scatter x8 -> x2, waiting for transfers between devices: 1680 us -> 0.01 us  [the longest x1 0.01 us: local(): lax.psum_scatter(term_out, BOTH, scatter_dimension=0, tiled=True)]
    all_gather x9 -> x2, waiting for transfers between devices: 540 us -> 0.01 us  [the longest x1 0.01 us: local(): full_qkv = lax.all_gather(w_qkv, BOTH, axis=0, tiled=True)]
    dynamic_update_slice x0 -> x24, local copies, waits for them, and re-layouts: none -> 445 us  [the longest x12 223 us: gather_dp(): out = lax.dynamic_update_slice(out, value[None], (base + near, zero, zero))]
    ppermute x0 -> x63, waiting for transfers between devices: none -> 398 us  [the longest x18 204 us: send(): out = lax.ppermute(value, axis, pairs)]
    dot_general x126 -> x16, matrix products: 451 us -> 118 us  [the longest x6 45.6 us: right_transposed(): lax.dot_general(left, right, (((1,), (1,)), ((), ())), preferred_element_...]
    ppermute x0 -> x63, starting transfers between devices: none -> 120 us  [the longest x18 70.4 us: send(): out = lax.ppermute(value, axis, pairs)]
    broadcast_in_dim x0 -> x17, local copies, waits for them, and re-layouts: none -> 84.1 us  [the longest x8 45.2 us: gather_dp(): other[None]]
    unnamed x2 -> x0, blocking collectives: 82.5 us -> none
  transfers between devices with their start and end apart: 21 -> 71, of which waited for: 15 -> 23; matrix products, arithmetic and copies ran while one was open for 12% -> 52% of each run, Pallas kernels for 0% -> 3%
where the time goes in v1:
time: 1410 us; the launch traced here: 1390 us
  local copies, waits for them, and re-layouts  649 us (46%)
  waiting for transfers between devices  401 us (28%)
  starting transfers between devices  136 us (10%)
  matrix products  118 us (8%)
  Pallas kernels  37 us (3%)
  other arithmetic  30.9 us (2%)
  between operations  15.4 us (1%)
    dynamic_update_slice x12, local copies, waits for them, and re-layouts, gather_dp(): out = lax.dynamic_update_slice(out, value[None], (base + near, zero, zero))  223 us
    dynamic_update_slice x12, local copies, waits for them, and re-layouts, gather_dp(): lax.dynamic_update_slice(out, other[None], (base + 1 - near, zero, zero))  222 us
    ppermute x18, waiting for transfers between devices, send(): out = lax.ppermute(value, axis, pairs)  204 us
    ppermute x12, waiting for transfers between devices, scatter_dp(): got = lax.ppermute(other, 'dp', swap_pairs(size, 1))  93 us
    ppermute x18, starting transfers between devices, send(): out = lax.ppermute(value, axis, pairs)  70.4 us
    dot_general x6, matrix products, right_transposed(): lax.dot_general(left, right, (((1,), (1,)), ((), ())), preferred_element_...  45.6 us
    broadcast_in_dim x8, local copies, waits for them, and re-layouts, gather_dp(): other[None]  45.2 us
    ppermute x2, waiting for transfers between devices, scatter_rows(): far = lax.ppermute(far.astype(BF16), 'fsdp', chip)  43 us
  transfers between devices with their start and end apart: 71, of which 23 were waited for; matrix products, arithmetic and copies ran while one was open for 52% of the time, Pallas kernels for 3%

profile of v1, /device:TPU:0, one launch (start us, length us, event | category | flops | bytes accessed | tf_op | source)
XLA Modules:
  0.0 1386.9 jit_solution(15115221655368355070)
XLA Ops:
  42.6 40.9 %collective-permute-done.6 = bf16[256,1216]{0,1:T(8,128)(2,1)} collective-permute-done((bf16[256,1216]{0,1:T(8,128)(2,1)S(1)}, bf16[256,1216]{0,1:T(8,128)(2,1)}, u32[]{:S(2)}, u32[]{:S(2)}) %collective-permute-start.6) | collective-permute-done | bytes 622624 | tf_op jit(solution)/shard_map/ppermute | solution.py:238
  94.1 60.4 %collective-permute-done.10 = bf16[256,1216]{0,1:T(8,128)(2,1)} collective-permute-done((bf16[256,1216]{0,1:T(8,128)(2,1)}, bf16[256,1216]{0,1:T(8,128)(2,1)}, u32[]{:S(2)}, u32[]{:S(2)}) %collective-permute-start.10) | collective-permute-done | bytes 622624 | tf_op jit(solution)/shard_map/ppermute | solution.py:238
  163.9 9.3 collective-permute-done.5
  177.0 25.4 %collective-permute-done.17 = bf16[256,1216]{0,1:T(8,128)(2,1)} collective-permute-done((bf16[256,1216]{0,1:T(8,128)(2,1)}, bf16[256,1216]{0,1:T(8,128)(2,1)}, u32[]{:S(2)}, u32[]{:S(2)}) %collective-permute-start.17) | collective-permute-done | bytes 622624 | tf_op jit(solution)/shard_map/ppermute | solution.py:238
  211.1 26.9 %dynamic_update_slice.72 = bf16[8,256,1216]{1,0,2:T(8,128)(2,1)} dynamic-update-slice(bf16[8,256,1216]{1,0,2:T(8,128)(2,1)} %broadcast.97.clone, bf16[1,256,1216]{1,0,2:T(2,128)(2,1)S(1)} %copy.208, s32[]{:T(128)S(6)} %select_n.173, s32[]{:T(128)} %constant.205.clone.1, s32[]{:T(128)} %constant.205.clone.1) | dynamic-update-slice | bytes 1245188 | tf_op jit(solution)/shard_map/dynamic_update_slice | solution.py:272
  240.4 26.9 %dynamic_update_slice.80 = bf16[8,256,1216]{1,0,2:T(8,128)(2,1)} dynamic-update-slice(bf16[8,256,1216]{1,0,2:T(8,128)(2,1)} %broadcast.97.clone.1, bf16[1,256,1216]{1,0,2:T(2,128)(2,1)S(1)} %copy-done.20, s32[]{:T(128)S(6)} %select_n.173, s32[]{:T(128)} %constant.205.clone.1, s32[]{:T(128)} %constant.205.clone.1) | dynamic-update-slice | bytes 1245188 | tf_op jit(solution)/shard_map/dynamic_update_slice | solution.py:272
  286.4 5.9 copy.210
  297.5 6.0 copy.212
  303.5 6.9 copy.215
  310.4 27.0 %dynamic_update_slice.73 = bf16[8,256,1216]{1,0,2:T(8,128)(2,1)} dynamic-update-slice(bf16[8,256,1216]{1,0,2:T(8,128)(2,1)} %dynamic_update_slice.72, bf16[1,256,1216]{1,0,2:T(2,128)(2,1)} %copy.210, s32[]{:T(128)S(6)} %select_n.174, s32[]{:T(128)} %constant.205.clone.1, s32[]{:T(128)} %constant.205.clone.1) | dynamic-update-slice | bytes 1245188 | tf_op jit(solution)/shard_map/dynamic_update_slice | solution.py:273
  337.4 26.8 %dynamic_update_slice.81 = bf16[8,256,1216]{1,0,2:T(8,128)(2,1)} dynamic-update-slice(bf16[8,256,1216]{1,0,2:T(8,128)(2,1)} %dynamic_update_slice.80, bf16[1,256,1216]{1,0,2:T(2,128)(2,1)S(1)} %copy.223, s32[]{:T(128)S(6)} %select_n.174, s32[]{:T(128)} %constant.205.clone.1, s32[]{:T(128)} %constant.205.clone.1) | dynamic-update-slice | bytes 1245188 | tf_op jit(solution)/shard_map/dynamic_update_slice | solution.py:273
  364.2 27.0 %dynamic_update_slice.74 = bf16[8,256,1216]{1,0,2:T(8,128)(2,1)} dynamic-update-slice(bf16[8,256,1216]{1,0,2:T(8,128)(2,1)} %dynamic_update_slice.73, bf16[1,256,1216]{1,0,2:T(2,128)(2,1)} %copy.212, s32[]{:T(128)S(6)} %select_n.176, s32[]{:T(128)} %constant.205.clone.1, s32[]{:T(128)} %constant.205.clone.1) | dynamic-update-slice | bytes 1245188 | tf_op jit(solution)/shard_map/dynamic_update_slice | solution.py:272
  396.4 6.2 copy.213
  402.5 5.9 copy.225
  414.4 27.0 %dynamic_update_slice.82 = bf16[8,256,1216]{1,0,2:T(8,128)(2,1)} dynamic-update-slice(bf16[8,256,1216]{1,0,2:T(8,128)(2,1)} %dynamic_update_slice.81, bf16[1,256,1216]{1,0,2:T(2,128)(2,1)} %copy.225, s32[]{:T(128)S(6)} %select_n.176, s32[]{:T(128)} %constant.205.clone.1, s32[]{:T(128)} %constant.205.clone.1) | dynamic-update-slice | bytes 1245188 | tf_op jit(solution)/shard_map/dynamic_update_slice | solution.py:272
  441.4 27.0 %dynamic_update_slice.75 = bf16[8,256,1216]{1,0,2:T(8,128)(2,1)} dynamic-update-slice(bf16[8,256,1216]{1,0,2:T(8,128)(2,1)} %dynamic_update_slice.74, bf16[1,256,1216]{1,0,2:T(2,128)(2,1)} %copy.213, s32[]{:T(128)S(6)} %select_n.177, s32[]{:T(128)} %constant.205.clone.1, s32[]{:T(128)} %constant.205.clone.1) | dynamic-update-slice | bytes 1245188 | tf_op jit(solution)/shard_map/dynamic_update_slice | solution.py:273
  468.4 26.9 %dynamic_update_slice.76 = bf16[8,256,1216]{1,0,2:T(8,128)(2,1)} dynamic-update-slice(bf16[8,256,1216]{1,0,2:T(8,128)(2,1)} %dynamic_update_slice.75, bf16[1,256,1216]{1,0,2:T(2,128)(2,1)S(1)} %copy.215, s32[]{:T(128)S(6)} %select_n.179, s32[]{:T(128)} %constant.205.clone.1, s32[]{:T(128)} %constant.205.clone.1) | dynamic-update-slice | bytes 1245188 | tf_op jit(solution)/shard_map/dynamic_update_slice | solution.py:272
  495.2 27.0 %dynamic_update_slice.77 = bf16[8,256,1216]{1,0,2:T(8,128)(2,1)} dynamic-update-slice(bf16[8,256,1216]{1,0,2:T(8,128)(2,1)} %dynamic_update_slice.76, bf16[1,256,1216]{1,0,2:T(2,128)(2,1)S(1)} %copy.216, s32[]{:T(128)S(6)} %select_n.180, s32[]{:T(128)} %constant.205.clone.1, s32[]{:T(128)} %constant.205.clone.1) | dynamic-update-slice | bytes 1245188 | tf_op jit(solution)/shard_map/dynamic_update_slice | solution.py:273
  522.2 26.9 %dynamic_update_slice.78 = bf16[8,256,1216]{1,0,2:T(8,128)(2,1)} dynamic-update-slice(bf16[8,256,1216]{1,0,2:T(8,128)(2,1)} %dynamic_update_slice.77, bf16[1,256,1216]{1,0,2:T(2,128)(2,1)S(1)} %copy-done.17, s32[]{:T(128)S(6)} %select_n.182, s32[]{:T(128)} %constant.205.clone.1, s32[]{:T(128)} %constant.205.clone.1) | dynamic-update-slice | bytes 1245188 | tf_op jit(solution)/shard_map/dynamic_update_slice | solution.py:272
  556.5 6.4 copy.226
  568.0 6.0 copy.228
  574.0 26.9 %dynamic_update_slice.79 = bf16[8,256,1216]{1,0,2:T(8,128)(2,1)} dynamic-update-slice(bf16[8,256,1216]{1,0,2:T(8,128)(2,1)} %dynamic_update_slice.78, bf16[1,256,1216]{1,0,2:T(2,128)(2,1)S(1)} %copy.219, s32[]{:T(128)S(6)} %select_n.183, s32[]{:T(128)} %constant.205.clone.1, s32[]{:T(128)} %constant.205.clone.1) | dynamic-update-slice | bytes 1245188 | tf_op jit(solution)/shard_map/dynamic_update_slice | solution.py:273
  600.8 6.9 copy.270
  607.7 26.9 %dynamic_update_slice.83 = bf16[8,256,1216]{1,0,2:T(8,128)(2,1)} dynamic-update-slice(bf16[8,256,1216]{1,0,2:T(8,128)(2,1)} %dynamic_update_slice.82, bf16[1,256,1216]{1,0,2:T(2,128)(2,1)S(1)} %copy-done.18, s32[]{:T(128)S(6)} %select_n.177, s32[]{:T(128)} %constant.205.clone.1, s32[]{:T(128)} %constant.205.clone.1) | dynamic-update-slice | bytes 1245188 | tf_op jit(solution)/shard_map/dynamic_update_slice | solution.py:273
  634.6 27.0 %dynamic_update_slice.84 = bf16[8,256,1216]{1,0,2:T(8,128)(2,1)} dynamic-update-slice(bf16[8,256,1216]{1,0,2:T(8,128)(2,1)} %dynamic_update_slice.83, bf16[1,256,1216]{1,0,2:T(2,128)(2,1)} %copy.228, s32[]{:T(128)S(6)} %select_n.179, s32[]{:T(128)} %constant.205.clone.1, s32[]{:T(128)} %constant.205.clone.1) | dynamic-update-slice | bytes 1245188 | tf_op jit(solution)/shard_map/dynamic_update_slice | solution.py:272
  667.4 6.0 copy.232
  673.4 26.8 %dynamic_update_slice.85 = bf16[8,256,1216]{1,0,2:T(8,128)(2,1)} dynamic-update-slice(bf16[8,256,1216]{1,0,2:T(8,128)(2,1)} %dynamic_update_slice.84, bf16[1,256,1216]{1,0,2:T(2,128)(2,1)S(1)} %copy.229, s32[]{:T(128)S(6)} %select_n.180, s32[]{:T(128)} %constant.205.clone.1, s32[]{:T(128)} %constant.205.clone.1) | dynamic-update-slice | bytes 1245188 | tf_op jit(solution)/shard_map/dynamic_update_slice | solution.py:273
  700.2 26.9 %dynamic_update_slice.86 = bf16[8,256,1216]{1,0,2:T(8,128)(2,1)} dynamic-update-slice(bf16[8,256,1216]{1,0,2:T(8,128)(2,1)} %dynamic_update_slice.85, bf16[1,256,1216]{1,0,2:T(2,128)(2,1)S(1)} %copy.231, s32[]{:T(128)S(6)} %select_n.182, s32[]{:T(128)} %constant.205.clone.1, s32[]{:T(128)} %constant.205.clone.1) | dynamic-update-slice | bytes 1245188 | tf_op jit(solution)/shard_map/dynamic_update_slice | solution.py:272
  727.2 26.9 %dynamic_update_slice.87 = bf16[8,256,1216]{1,0,2:T(8,128)(2,1)} dynamic-update-slice(bf16[8,256,1216]{1,0,2:T(8,128)(2,1)} %dynamic_update_slice.86, bf16[1,256,1216]{1,0,2:T(2,128)(2,1)S(1)} %copy-done.19, s32[]{:T(128)S(6)} %select_n.183, s32[]{:T(128)} %constant.205.clone.1, s32[]{:T(128)} %constant.205.clone.1) | dynamic-update-slice | bytes 1245188 | tf_op jit(solution)/shard_map/dynamic_update_slice | solution.py:273
  754.0 6.8 copy.271
  764.2 6.1 fusion.36.pre_ref
  777.2 9.4 collective-permute-done.two_ref
  786.8 12.0 attend.1
  817.3 15.9 %collective-permute-done.3 = bf16[256,2048]{1,0:T(8,128)(2,1)S(1)} collective-permute-done((bf16[256,2048]{1,0:T(8,128)(2,1)S(1)}, bf16[256,2048]{1,0:T(8,128)(2,1)S(1)}, u32[]{:S(2)}, u32[]{:S(2)}) %collective-permute-start.3) | collective-permute-done | bytes 1048608 | tf_op jit(solution)/shard_map/ppermute | solution.py:296
  838.7 12.4 fusion.43
  851.1 9.1 fusion.42
  860.3 12.8 multiply_convert_fusion
  873.1 7.8 fusion.51
  881.0 10.2 fusion.49
  891.8 7.9 fusion.50
  905.0 21.9 %collective-permute-done.34 = bf16[256,2048]{1,0:T(8,128)(2,1)S(1)} collective-permute-done((bf16[256,2048]{1,0:T(8,128)(2,1)S(1)}, bf16[256,2048]{1,0:T(8,128)(2,1)S(1)}, u32[]{:S(2)}, u32[]{:S(2)}) %collective-permute-start.34) | collective-permute-done | bytes 1048608 | tf_op jit(solution)/shard_map/ppermute | solution.py:307
  927.9 21.0 %collective-permute-done.28 = bf16[256,2048]{1,0:T(8,128)(2,1)S(1)} collective-permute-done((bf16[256,2048]{1,0:T(8,128)(2,1)S(1)}, bf16[256,2048]{1,0:T(8,128)(2,1)S(1)}, u32[]{:S(2)}, u32[]{:S(2)}) %collective-permute-start.28) | collective-permute-done | bytes 1048608 | tf_op jit(solution)/shard_map/ppermute | solution.py:307
  964.9 17.2 %attend_back.1 = (f32[256,1536]{1,0:T(8,128)S(1)}, bf16[2,256,384]{2,1,0:T(8,128)(2,1)S(1)}, bf16[2,256,384]{2,1,0:T(8,128)(2,1)S(1)}, f32[2,256,384]{2,1,0:T(8,128)S(1)}) custom-call(bf16[256,1536]{1,0:T(8,128)(2,1)S(1)} %broadcast_multiply_fusion.q_ref, bf16[2,256,384]{2,1,0:T(8,128)(2,1)S(1)} %copy-done.8, bf16[2,256,384]{2,1,0:T(8,128)(2,1)S(1)} %copy-done.6, ...), custom_call_target="tpu_custom_call" | custom-call | tf_op jit(solution)/shard_map/attend_back/pallas_call | solution.py:214
  985.7 14.2 %collective-permute-done.36.two_ref = bf16[2,256,384]{2,1,0:T(8,128)(2,1)S(1)} collective-permute-done((bf16[2,256,384]{2,1,0:T(8,128)(2,1)S(1)}, bf16[2,256,384]{2,1,0:T(8,128)(2,1)S(1)}, u32[]{:S(2)}, u32[]{:S(2)}) %collective-permute-start.36) | collective-permute-done | bytes 393248 | tf_op jit(solution)/shard_map/ppermute | solution.py:443
  1005.7 6.1 convolution_convert_fusion
  1011.9 8.2 convolution_convert_fusion.4
  1033.5 7.6 convolution_convert_fusion.2
  1043.3 12.1 constant_dynamic-slice_fusion.1
  1058.2 11.5 constant_dynamic-slice_fusion.9
  1077.3 8.7 collective-permute-done.43
  1088.7 15.2 %collective-permute-done.55 = bf16[256,1216]{0,1:T(8,128)(2,1)} collective-permute-done((bf16[256,1216]{0,1:T(8,128)(2,1)}, bf16[256,1216]{0,1:T(8,128)(2,1)}, u32[]{:S(2)}, u32[]{:S(2)}) %collective-permute-start.55) | collective-permute-done | bytes 622624 | tf_op jit(solution)/shard_map/ppermute | solution.py:285
  1108.2 39.1 %collective-permute-done.57 = bf16[256,1216]{0,1:T(8,128)(2,1)S(1)} collective-permute-done((bf16[256,1216]{0,1:T(8,128)(2,1)S(1)}, bf16[256,1216]{0,1:T(8,128)(2,1)S(1)}, u32[]{:S(2)}, u32[]{:S(2)}) %collective-permute-start.57) | collective-permute-done | bytes 622624 | tf_op jit(solution)/shard_map/ppermute | solution.py:285
  1147.3 8.6 collective-permute-start.49
  1157.0 10.4 collective-permute-done.59
  1174.0 13.9 collective-permute-done.42
  1187.8 11.6 collective-permute-start.50
  1208.1 10.5 collective-permute-start.45
  1218.6 25.1 %collective-permute-done.50 = bf16[152,2048]{1,0:T(8,128)(2,1)S(1)} collective-permute-done((bf16[152,2048]{1,0:T(8,128)(2,1)S(1)}, bf16[152,2048]{1,0:T(8,128)(2,1)S(1)}, u32[]{:S(2)}, u32[]{:S(2)}) %collective-permute-start.50) | collective-permute-done | bytes 622624 | tf_op jit(solution)/shard_map/ppermute | solution.py:238
  1243.7 8.2 fusion.8
  1254.8 7.4 collective-permute-start.53
  1266.4 36.7 %collective-permute-done.53 = bf16[256,1216]{0,1:T(8,128)(2,1)S(1)} collective-permute-done((bf16[256,1216]{0,1:T(8,128)(2,1)S(1)}, bf16[256,1216]{0,1:T(8,128)(2,1)S(1)}, u32[]{:S(2)}, u32[]{:S(2)}) %collective-permute-start.53) | collective-permute-done | bytes 622624 | tf_op jit(solution)/shard_map/ppermute | solution.py:238
  1305.2 13.0 collective-permute-start.60
  1324.0 8.5 collective-permute-done.40
  1332.6 10.3 collective-permute-done.60
  (365 shorter events, 291.3 us)
Async XLA Ops:
  7.2 755.7 %all-gather.3.cloned.1.call-start = ((), (), s32[]{:S(2)}) async-start(), calls=%async_computation.6 | async-start | bytes 10272768 | tf_op jit(solution)/shard_map/all_gather | solution.py:364
  9.8 792.1 %all-gather.5.cloned.1.call-start = ((), (), s32[]{:S(2)}) async-start(), calls=%async_computation.7 | async-start | bytes 6488064 | tf_op jit(solution)/shard_map/all_gather | solution.py:365
  17.0 17.4 %all-to-all-start = ((bf16[4,64,1216]{2,1,0:T(8,128)(2,1)}), bf16[4,64,1216]{2,1,0:T(8,128)(2,1)S(1)}, u32[]{:S(2)}, u32[]{:S(2)}) async-start(bf16[4,64,1216]{2,1,0:T(8,128)(2,1)} %reshape.215), calls=%async_computation | async-start | bytes 1310720 | tf_op jit(solution)/shard_map/all_to_all | solution.py:372
  21.2 142.1 %collective-permute-start.29 = (bf16[256,2048]{1,0:T(8,128)(2,1)}, bf16[256,2048]{1,0:T(8,128)(2,1)}, u32[]{:S(2)}, u32[]{:S(2)}) collective-permute-start(bf16[256,2048]{1,0:T(8,128)(2,1)} %param.16), channel_id=1, source_target_pairs={{0,1},{1,0},{2,3},{3,2},{4,5},{5,4},{6,7},{7,6},{8,9},{9,8},{10,11... | collective-permute-start | bytes 3145736 | tf_op jit(solution)/shard_map/ppermute | solution.py:295
  21.7 136.9 %collective-permute-start.30 = (bf16[256,2048]{1,0:T(8,128)(2,1)}, bf16[256,2048]{1,0:T(8,128)(2,1)}, u32[]{:S(2)}, u32[]{:S(2)}) collective-permute-start(bf16[256,2048]{1,0:T(8,128)(2,1)} %param.16), channel_id=1, source_target_pairs={{0,2},{1,3},{2,0},{3,1},{4,6},{5,7},{6,4},{7,5},{8,10},{9,11},{10,... | collective-permute-start | bytes 3145736 | tf_op jit(solution)/shard_map/ppermute | solution.py:296
  23.5 134.8 %collective-permute-start.19 = (bf16[152,2048]{1,0:T(8,128)(2,1)}, bf16[152,2048]{1,0:T(8,128)(2,1)}, u32[]{:S(2)}, u32[]{:S(2)}) collective-permute-start(bf16[152,2048]{1,0:T(8,128)(2,1)} %param.28), channel_id=1, source_target_pairs={{0,4},{4,0},{8,12},{12,8},{16,20},{20,16},{24,28},{28,24},{1,5},{5... | collective-permute-start | bytes 1867784 | tf_op jit(solution)/shard_map/ppermute | solution.py:270
  34.3 51.0 %all-to-all-start.1 = ((bf16[4,64,1216]{2,1,0:T(8,128)(2,1)}), bf16[4,64,1216]{2,1,0:T(8,128)(2,1)S(1)}, u32[]{:S(2)}, u32[]{:S(2)}) async-start(bf16[4,64,1216]{2,1,0:T(8,128)(2,1)} %reshape.219), calls=%async_computation.1 | async-start | bytes 1310720 | tf_op jit(solution)/shard_map/all_to_all | solution.py:373
  37.8 1337.2 %reduce-scatter.5.cloned.1.call-start = ((), (), s32[]{:S(2)}) async-start(), calls=%async_computation.9 | async-start | bytes 6488064 | tf_op jit(solution)/shard_map/reduce_scatter | solution.py:440
  38.1 47.2 %collective-permute-start.8 = (bf16[256,1216]{0,1:T(8,128)(2,1)S(1)}, bf16[256,1216]{0,1:T(8,128)(2,1)S(1)}, u32[]{:S(2)}, u32[]{:S(2)}) collective-permute-start(bf16[256,1216]{0,1:T(8,128)(2,1)S(1)} %copy.209), channel_id=1, source_target_pairs={{0,24},{4,28},{8,0},{12,4},{16,8},{20,12},{24,16},{28,20},{1,25},{... | collective-permute-start | bytes 1867784 | tf_op jit(solution)/shard_map/ppermute | solution.py:238
  41.8 41.7 %collective-permute-start.6 = (bf16[256,1216]{0,1:T(8,128)(2,1)S(1)}, bf16[256,1216]{0,1:T(8,128)(2,1)}, u32[]{:S(2)}, u32[]{:S(2)}) collective-permute-start(bf16[256,1216]{0,1:T(8,128)(2,1)S(1)} %copy.209), channel_id=1, source_target_pairs={{0,8},{4,12},{8,16},{12,20},{16,24},{20,28},{24,0},{28,4},{1,9},{5... | collective-permute-start | bytes 1867784 | tf_op jit(solution)/shard_map/ppermute | solution.py:238
  84.6 69.9 %collective-permute-start.10 = (bf16[256,1216]{0,1:T(8,128)(2,1)}, bf16[256,1216]{0,1:T(8,128)(2,1)}, u32[]{:S(2)}, u32[]{:S(2)}) collective-permute-start(bf16[256,1216]{0,1:T(8,128)(2,1)} %copy.217), channel_id=1, source_target_pairs={{0,16},{4,20},{8,24},{12,28},{16,0},{20,4},{24,8},{28,12},{1,17},{... | collective-permute-start | bytes 1867784 | tf_op jit(solution)/shard_map/ppermute | solution.py:238
  86.4 70.6 %collective-permute-start.13 = (bf16[256,1216]{0,1:T(8,128)(2,1)}, bf16[256,1216]{0,1:T(8,128)(2,1)}, u32[]{:S(2)}, u32[]{:S(2)}) collective-permute-start(bf16[256,1216]{0,1:T(8,128)(2,1)} %copy.224), channel_id=1, source_target_pairs={{0,8},{4,12},{8,16},{12,20},{16,24},{20,28},{24,0},{28,4},{1,9},{5... | collective-permute-start | bytes 1867784 | tf_op jit(solution)/shard_map/ppermute | solution.py:238
  154.5 18.6 %collective-permute-start.5 = (bf16[256,1216]{0,1:T(8,128)(2,1)}, bf16[256,1216]{0,1:T(8,128)(2,1)}, u32[]{:S(2)}, u32[]{:S(2)}) collective-permute-start(bf16[256,1216]{0,1:T(8,128)(2,1)} %copy-done.33), channel_id=1, source_target_pairs={{0,4},{4,0},{8,12},{12,8},{16,20},{20,16},{24,28},{28,24},{1,5},{5... | collective-permute-start | bytes 1867784 | tf_op jit(solution)/shard_map/ppermute | solution.py:270
  157.0 19.6 %collective-permute-start.15 = (bf16[256,1216]{0,1:T(8,128)(2,1)}, bf16[256,1216]{0,1:T(8,128)(2,1)}, u32[]{:S(2)}, u32[]{:S(2)}) collective-permute-start(bf16[256,1216]{0,1:T(8,128)(2,1)} %copy.227), channel_id=1, source_target_pairs={{0,24},{4,28},{8,0},{12,4},{16,8},{20,12},{24,16},{28,20},{1,25},{... | collective-permute-start | bytes 1867784 | tf_op jit(solution)/shard_map/ppermute | solution.py:238
  158.3 44.1 %collective-permute-start.17 = (bf16[256,1216]{0,1:T(8,128)(2,1)}, bf16[256,1216]{0,1:T(8,128)(2,1)}, u32[]{:S(2)}, u32[]{:S(2)}) collective-permute-start(bf16[256,1216]{0,1:T(8,128)(2,1)} %copy.230), channel_id=1, source_target_pairs={{0,16},{4,20},{8,24},{12,28},{16,0},{20,4},{24,8},{28,12},{1,17},{... | collective-permute-start | bytes 1867784 | tf_op jit(solution)/shard_map/ppermute | solution.py:238
  158.6 121.2 %collective-permute-start.31 = (bf16[256,2048]{1,0:T(8,128)(2,1)}, bf16[256,2048]{1,0:T(8,128)(2,1)}, u32[]{:S(2)}, u32[]{:S(2)}) collective-permute-start(bf16[256,2048]{1,0:T(8,128)(2,1)} %collective-permute-done.30), channel_id=1, source_target_pairs={{0,1},{1,0},{2,3},{3,2},{4,5},{5,4},{6,7},{7,6},{8,9},{9,8},{10,11... | collective-permute-start | bytes 3145736 | tf_op jit(solution)/shard_map/ppermute | solution.py:297
  163.3 105.9 %collective-permute-start.12 = (bf16[256,1216]{0,1:T(8,128)(2,1)}, bf16[256,1216]{0,1:T(8,128)(2,1)}, u32[]{:S(2)}, u32[]{:S(2)}) collective-permute-start(bf16[256,1216]{0,1:T(8,128)(2,1)} %copy.222), channel_id=1, source_target_pairs={{0,4},{4,0},{8,12},{12,8},{16,20},{20,16},{24,28},{28,24},{1,5},{5... | collective-permute-start | bytes 1867784 | tf_op jit(solution)/shard_map/ppermute | solution.py:270
  173.1 98.1 %collective-permute-start.9 = (bf16[256,1216]{0,1:T(8,128)(2,1)S(1)}, bf16[256,1216]{0,1:T(8,128)(2,1)}, u32[]{:S(2)}, u32[]{:S(2)}) collective-permute-start(bf16[256,1216]{0,1:T(8,128)(2,1)S(1)} %collective-permute-done.8), channel_id=1, source_target_pairs={{0,4},{4,0},{8,12},{12,8},{16,20},{20,16},{24,28},{28,24},{1,5},{5... | collective-permute-start | bytes 1867784 | tf_op jit(solution)/shard_map/ppermute | solution.py:270
  176.7 99.8 %collective-permute-start.7 = (bf16[256,1216]{0,1:T(8,128)(2,1)}, bf16[256,1216]{0,1:T(8,128)(2,1)}, u32[]{:S(2)}, u32[]{:S(2)}) collective-permute-start(bf16[256,1216]{0,1:T(8,128)(2,1)} %collective-permute-done.6), channel_id=1, source_target_pairs={{0,4},{4,0},{8,12},{12,8},{16,20},{20,16},{24,28},{28,24},{1,5},{5... | collective-permute-start | bytes 1867784 | tf_op jit(solution)/shard_map/ppermute | solution.py:270
  202.4 77.7 %collective-permute-start.11 = (bf16[256,1216]{0,1:T(8,128)(2,1)}, bf16[256,1216]{0,1:T(8,128)(2,1)}, u32[]{:S(2)}, u32[]{:S(2)}) collective-permute-start(bf16[256,1216]{0,1:T(8,128)(2,1)} %collective-permute-done.10), channel_id=1, source_target_pairs={{0,4},{4,0},{8,12},{12,8},{16,20},{20,16},{24,28},{28,24},{1,5},{5... | collective-permute-start | bytes 1867784 | tf_op jit(solution)/shard_map/ppermute | solution.py:270
  269.2 287.3 %collective-permute-start.14 = (bf16[256,1216]{0,1:T(8,128)(2,1)}, bf16[256,1216]{0,1:T(8,128)(2,1)}, u32[]{:S(2)}, u32[]{:S(2)}) collective-permute-start(bf16[256,1216]{0,1:T(8,128)(2,1)} %collective-permute-done.13), channel_id=1, source_target_pairs={{0,4},{4,0},{8,12},{12,8},{16,20},{20,16},{24,28},{28,24},{1,5},{5... | collective-permute-start | bytes 1867784 | tf_op jit(solution)/shard_map/ppermute | solution.py:270
  271.3 390.2 %collective-permute-start.20 = (bf16[152,2048]{1,0:T(8,128)(2,1)}, bf16[152,2048]{1,0:T(8,128)(2,1)}, u32[]{:S(2)}, u32[]{:S(2)}) collective-permute-start(bf16[152,2048]{1,0:T(8,128)(2,1)} %param.28), channel_id=1, source_target_pairs={{0,8},{4,12},{8,16},{12,20},{16,24},{20,28},{24,0},{28,4},{1,9},{5... | collective-permute-start | bytes 1867784 | tf_op jit(solution)/shard_map/ppermute | solution.py:238
  276.5 484.7 %collective-permute-start.22 = (bf16[152,2048]{1,0:T(8,128)(2,1)}, bf16[152,2048]{1,0:T(8,128)(2,1)}, u32[]{:S(2)}, u32[]{:S(2)}) collective-permute-start(bf16[152,2048]{1,0:T(8,128)(2,1)} %param.28), channel_id=1, source_target_pairs={{0,24},{4,28},{8,0},{12,4},{16,8},{20,12},{24,16},{28,20},{1,25},{... | collective-permute-start | bytes 1867784 | tf_op jit(solution)/shard_map/ppermute | solution.py:238
  279.7 382.4 %collective-permute-start.16 = (bf16[256,1216]{0,1:T(8,128)(2,1)}, bf16[256,1216]{0,1:T(8,128)(2,1)}, u32[]{:S(2)}, u32[]{:S(2)}) collective-permute-start(bf16[256,1216]{0,1:T(8,128)(2,1)} %collective-permute-done.15), channel_id=1, source_target_pairs={{0,4},{4,0},{8,12},{12,8},{16,20},{20,16},{24,28},{28,24},{1,5},{5... | collective-permute-start | bytes 1867784 | tf_op jit(solution)/shard_map/ppermute | solution.py:270
  280.2 387.3 %collective-permute-start.18 = (bf16[256,1216]{0,1:T(8,128)(2,1)}, bf16[256,1216]{0,1:T(8,128)(2,1)}, u32[]{:S(2)}, u32[]{:S(2)}) collective-permute-start(bf16[256,1216]{0,1:T(8,128)(2,1)} %collective-permute-done.17), channel_id=1, source_target_pairs={{0,4},{4,0},{8,12},{12,8},{16,20},{20,16},{24,28},{28,24},{1,5},{5... | collective-permute-start | bytes 1867784 | tf_op jit(solution)/shard_map/ppermute | solution.py:270
  661.5 150.3 %collective-permute-start.24 = (bf16[152,2048]{1,0:T(8,128)(2,1)}, bf16[152,2048]{1,0:T(8,128)(2,1)}, u32[]{:S(2)}, u32[]{:S(2)}) collective-permute-start(bf16[152,2048]{1,0:T(8,128)(2,1)} %param.28), channel_id=1, source_target_pairs={{0,16},{4,20},{8,24},{12,28},{16,0},{20,4},{24,8},{28,12},{1,17},{... | collective-permute-start | bytes 1867784 | tf_op jit(solution)/shard_map/ppermute | solution.py:238
  760.8 51.5 %collective-permute-start.21 = (bf16[152,2048]{1,0:T(8,128)(2,1)}, bf16[152,2048]{1,0:T(8,128)(2,1)}, u32[]{:S(2)}, u32[]{:S(2)}) collective-permute-start(bf16[152,2048]{1,0:T(8,128)(2,1)} %collective-permute-done.20), channel_id=1, source_target_pairs={{0,4},{4,0},{8,12},{12,8},{16,20},{20,16},{24,28},{28,24},{1,5},{5... | collective-permute-start | bytes 1867784 | tf_op jit(solution)/shard_map/ppermute | solution.py:270
  761.3 72.5 %collective-permute-start.23 = (bf16[152,2048]{1,0:T(8,128)(2,1)}, bf16[152,2048]{1,0:T(8,128)(2,1)}, u32[]{:S(2)}, u32[]{:S(2)}) collective-permute-start(bf16[152,2048]{1,0:T(8,128)(2,1)} %collective-permute-done.22), channel_id=1, source_target_pairs={{0,4},{4,0},{8,12},{12,8},{16,20},{20,16},{24,28},{28,24},{1,5},{5... | collective-permute-start | bytes 1867784 | tf_op jit(solution)/shard_map/ppermute | solution.py:270
  773.7 13.0 collective-permute-start
  807.3 25.8 %collective-permute-start.3 = (bf16[256,2048]{1,0:T(8,128)(2,1)S(1)}, bf16[256,2048]{1,0:T(8,128)(2,1)S(1)}, u32[]{:S(2)}, u32[]{:S(2)}) collective-permute-start(bf16[256,2048]{1,0:T(8,128)(2,1)S(1)} %multiply_convert_fusion.3), channel_id=1, source_target_pairs={{0,2},{1,3},{2,0},{3,1},{4,6},{5,7},{6,4},{7,5},{8,10},{9,11},{10,... | collective-permute-start | bytes 3145736 | tf_op jit(solution)/shard_map/ppermute | solution.py:296
  811.8 25.9 %collective-permute-start.25 = (bf16[152,2048]{1,0:T(8,128)(2,1)}, bf16[152,2048]{1,0:T(8,128)(2,1)S(1)}, u32[]{:S(2)}, u32[]{:S(2)}) collective-permute-start(bf16[152,2048]{1,0:T(8,128)(2,1)} %collective-permute-done.24), channel_id=1, source_target_pairs={{0,4},{4,0},{8,12},{12,8},{16,20},{20,16},{24,28},{28,24},{1,5},{5... | collective-permute-start | bytes 1867784 | tf_op jit(solution)/shard_map/ppermute | solution.py:270
  816.3 22.3 %collective-permute-start.2 = (bf16[256,2048]{1,0:T(8,128)(2,1)S(1)}, bf16[256,2048]{1,0:T(8,128)(2,1)S(1)}, u32[]{:S(2)}, u32[]{:S(2)}) collective-permute-start(bf16[256,2048]{1,0:T(8,128)(2,1)S(1)} %multiply_convert_fusion.3), channel_id=1, source_target_pairs={{0,1},{1,0},{2,3},{3,2},{4,5},{5,4},{6,7},{7,6},{8,9},{9,8},{10,11... | collective-permute-start | bytes 3145736 | tf_op jit(solution)/shard_map/ppermute | solution.py:295
  900.9 26.0 %collective-permute-start.34 = (bf16[256,2048]{1,0:T(8,128)(2,1)S(1)}, bf16[256,2048]{1,0:T(8,128)(2,1)S(1)}, u32[]{:S(2)}, u32[]{:S(2)}) collective-permute-start(bf16[256,2048]{1,0:T(8,128)(2,1)S(1)} %fusion.9), channel_id=1, source_target_pairs={{0,2},{1,3},{2,0},{3,1},{4,6},{5,7},{6,4},{7,5},{8,10},{9,11},{10,... | collective-permute-start | bytes 3145736 | tf_op jit(solution)/shard_map/ppermute | solution.py:307
  902.9 25.0 %collective-permute-start.26 = (bf16[256,2048]{1,0:T(8,128)(2,1)S(1)}, bf16[256,2048]{1,0:T(8,128)(2,1)S(1)}, u32[]{:S(2)}, u32[]{:S(2)}) collective-permute-start(bf16[256,2048]{1,0:T(8,128)(2,1)S(1)} %get-tuple-element.89), channel_id=1, source_target_pairs={{0,1},{1,0},{2,3},{3,2},{4,5},{5,4},{6,7},{7,6},{8,9},{9,8},{10,11... | collective-permute-start | bytes 3145736 | tf_op jit(solution)/shard_map/ppermute | solution.py:308
  903.2 45.7 %collective-permute-start.28 = (bf16[256,2048]{1,0:T(8,128)(2,1)S(1)}, bf16[256,2048]{1,0:T(8,128)(2,1)S(1)}, u32[]{:S(2)}, u32[]{:S(2)}) collective-permute-start(bf16[256,2048]{1,0:T(8,128)(2,1)S(1)} %fusion.11), channel_id=1, source_target_pairs={{0,2},{1,3},{2,0},{3,1},{4,6},{5,7},{6,4},{7,5},{8,10},{9,11},{10,... | collective-permute-start | bytes 3145736 | tf_op jit(solution)/shard_map/ppermute | solution.py:307
  959.2 417.5 %reduce-scatter.3.cloned.1.call-start = ((), (), s32[]{:S(2)}) async-start(), calls=%async_computation.8 | async-start | bytes 10272768 | tf_op jit(solution)/shard_map/reduce_scatter | solution.py:446
  983.4 16.5 %collective-permute-start.36 = (bf16[2,256,384]{2,1,0:T(8,128)(2,1)S(1)}, bf16[2,256,384]{2,1,0:T(8,128)(2,1)S(1)}, u32[]{:S(2)}, u32[]{:S(2)}) collective-permute-start(bf16[2,256,384]{2,1,0:T(8,128)(2,1)S(1)} %get-tuple-element.47), channel_id=1, source_target_pairs={{2,0},{3,1},{6,4},{7,5},{10,8},{11,9},{14,12},{15,13},{18,16},{19,... | collective-permute-start | bytes 1179656 | tf_op jit(solution)/shard_map/ppermute | solution.py:443
  1021.7 242.0 %collective-permute-start.62 = (bf16[152,2048]{1,0:T(8,128)(2,1)}, bf16[152,2048]{1,0:T(8,128)(2,1)}, u32[]{:S(2)}, u32[]{:S(2)}) collective-permute-start(bf16[152,2048]{1,0:T(8,128)(2,1)} %get-tuple-element.64), channel_id=1, source_target_pairs={{0,4},{4,0},{8,12},{12,8},{16,20},{20,16},{24,28},{28,24},{1,5},{5... | collective-permute-start | bytes 1867784 | tf_op jit(solution)/shard_map/ppermute | solution.py:285
  1022.2 52.9 %collective-permute-start.48 = (bf16[152,2048]{1,0:T(8,128)(2,1)}, bf16[152,2048]{1,0:T(8,128)(2,1)}, u32[]{:S(2)}, u32[]{:S(2)}) collective-permute-start(bf16[152,2048]{1,0:T(8,128)(2,1)} %get-tuple-element.65), channel_id=1, source_target_pairs={{0,4},{4,0},{8,12},{12,8},{16,20},{20,16},{24,28},{28,24},{1,5},{5... | collective-permute-start | bytes 1867784 | tf_op jit(solution)/shard_map/ppermute | solution.py:285
  1023.7 53.0 %collective-permute-start.47 = (bf16[152,2048]{1,0:T(8,128)(2,1)}, bf16[152,2048]{1,0:T(8,128)(2,1)}, u32[]{:S(2)}, u32[]{:S(2)}) collective-permute-start(bf16[152,2048]{1,0:T(8,128)(2,1)} %get-tuple-element.66), channel_id=1, source_target_pairs={{0,4},{4,0},{8,12},{12,8},{16,20},{20,16},{24,28},{28,24},{1,5},{5... | collective-permute-start | bytes 1867784 | tf_op jit(solution)/shard_map/ppermute | solution.py:285
  1024.3 61.7 %collective-permute-start.43 = (bf16[152,2048]{1,0:T(8,128)(2,1)}, bf16[152,2048]{1,0:T(8,128)(2,1)}, u32[]{:S(2)}, u32[]{:S(2)}) collective-permute-start(bf16[152,2048]{1,0:T(8,128)(2,1)} %get-tuple-element.67), channel_id=1, source_target_pairs={{0,4},{4,0},{8,12},{12,8},{16,20},{20,16},{24,28},{28,24},{1,5},{5... | collective-permute-start | bytes 1867784 | tf_op jit(solution)/shard_map/ppermute | solution.py:285
  1057.6 46.4 %collective-permute-start.55 = (bf16[256,1216]{0,1:T(8,128)(2,1)}, bf16[256,1216]{0,1:T(8,128)(2,1)}, u32[]{:S(2)}, u32[]{:S(2)}) collective-permute-start(bf16[256,1216]{0,1:T(8,128)(2,1)} %bitcast.184), channel_id=1, source_target_pairs={{0,4},{4,0},{8,12},{12,8},{16,20},{20,16},{24,28},{28,24},{1,5},{5... | collective-permute-start | bytes 1867784 | tf_op jit(solution)/shard_map/ppermute | solution.py:285
  1075.2 257.3 %collective-permute-start.61 = (bf16[256,1216]{0,1:T(8,128)(2,1)}, bf16[256,1216]{0,1:T(8,128)(2,1)}, u32[]{:S(2)}, u32[]{:S(2)}) collective-permute-start(bf16[256,1216]{0,1:T(8,128)(2,1)} %bitcast.181), channel_id=1, source_target_pairs={{0,4},{4,0},{8,12},{12,8},{16,20},{20,16},{24,28},{28,24},{1,5},{5... | collective-permute-start | bytes 1867784 | tf_op jit(solution)/shard_map/ppermute | solution.py:285
  1076.7 70.6 %collective-permute-start.57 = (bf16[256,1216]{0,1:T(8,128)(2,1)S(1)}, bf16[256,1216]{0,1:T(8,128)(2,1)S(1)}, u32[]{:S(2)}, u32[]{:S(2)}) collective-permute-start(bf16[256,1216]{0,1:T(8,128)(2,1)S(1)} %bitcast.230), channel_id=1, source_target_pairs={{0,4},{4,0},{8,12},{12,8},{16,20},{20,16},{24,28},{28,24},{1,5},{5... | collective-permute-start | bytes 1867784 | tf_op jit(solution)/shard_map/ppermute | solution.py:285
  1086.0 81.3 %collective-permute-start.59 = (bf16[256,1216]{0,1:T(8,128)(2,1)S(1)}, bf16[256,1216]{0,1:T(8,128)(2,1)S(1)}, u32[]{:S(2)}, u32[]{:S(2)}) collective-permute-start(bf16[256,1216]{0,1:T(8,128)(2,1)S(1)} %bitcast.229), channel_id=1, source_target_pairs={{0,4},{4,0},{8,12},{12,8},{16,20},{20,16},{24,28},{28,24},{1,5},{5... | collective-permute-start | bytes 1867784 | tf_op jit(solution)/shard_map/ppermute | solution.py:285
  1104.0 83.9 %collective-permute-start.42 = (bf16[256,1216]{0,1:T(8,128)(2,1)S(1)}, bf16[256,1216]{0,1:T(8,128)(2,1)S(1)}, u32[]{:S(2)}, u32[]{:S(2)}) collective-permute-start(bf16[256,1216]{0,1:T(8,128)(2,1)S(1)} %bitcast.228), channel_id=1, source_target_pairs={{0,4},{4,0},{8,12},{12,8},{16,20},{20,16},{24,28},{28,24},{1,5},{5... | collective-permute-start | bytes 1867784 | tf_op jit(solution)/shard_map/ppermute | solution.py:285
  1147.3 24.0 %collective-permute-start.49 = (bf16[152,2048]{1,0:T(8,128)(2,1)S(1)}, bf16[152,2048]{1,0:T(8,128)(2,1)S(1)}, u32[]{:S(2)}, u32[]{:S(2)}) collective-permute-start(bf16[152,2048]{1,0:T(8,128)(2,1)S(1)} %get-tuple-element.84), channel_id=1, source_target_pairs={{0,8},{4,12},{8,16},{12,20},{16,24},{20,28},{24,0},{28,4},{1,9},{5... | collective-permute-start | bytes 1867784 | tf_op jit(solution)/shard_map/ppermute | solution.py:238
  1167.3 37.9 %collective-permute-start.46 = (bf16[256,1216]{0,1:T(8,128)(2,1)S(1)}, bf16[256,1216]{0,1:T(8,128)(2,1)S(1)}, u32[]{:S(2)}, u32[]{:S(2)}) collective-permute-start(bf16[256,1216]{0,1:T(8,128)(2,1)S(1)} %bitcast.227), channel_id=1, source_target_pairs={{0,4},{4,0},{8,12},{12,8},{16,20},{20,16},{24,28},{28,24},{1,5},{5... | collective-permute-start | bytes 1867784 | tf_op jit(solution)/shard_map/ppermute | solution.py:285
  1171.3 36.8 %collective-permute-start.44 = (bf16[152,2048]{1,0:T(8,128)(2,1)S(1)}, bf16[152,2048]{1,0:T(8,128)(2,1)S(1)}, u32[]{:S(2)}, u32[]{:S(2)}) collective-permute-start(bf16[152,2048]{1,0:T(8,128)(2,1)S(1)} %get-tuple-element.86), channel_id=1, source_target_pairs={{0,24},{4,28},{8,0},{12,4},{16,8},{20,12},{24,16},{28,20},{1,25},{... | collective-permute-start | bytes 1867784 | tf_op jit(solution)/shard_map/ppermute | solution.py:238
  1187.8 55.8 %collective-permute-start.50 = (bf16[152,2048]{1,0:T(8,128)(2,1)S(1)}, bf16[152,2048]{1,0:T(8,128)(2,1)S(1)}, u32[]{:S(2)}, u32[]{:S(2)}) collective-permute-start(bf16[152,2048]{1,0:T(8,128)(2,1)S(1)} %get-tuple-element.51), channel_id=1, source_target_pairs={{0,16},{4,20},{8,24},{12,28},{16,0},{20,4},{24,8},{28,12},{1,17},{... | collective-permute-start | bytes 1867784 | tf_op jit(solution)/shard_map/ppermute | solution.py:238
  1205.3 46.6 %collective-permute-start.52 = (bf16[256,1216]{0,1:T(8,128)(2,1)S(1)}, bf16[256,1216]{0,1:T(8,128)(2,1)S(1)}, u32[]{:S(2)}, u32[]{:S(2)}) collective-permute-start(bf16[256,1216]{0,1:T(8,128)(2,1)S(1)} %bitcast.226), channel_id=1, source_target_pairs={{0,4},{4,0},{8,12},{12,8},{16,20},{20,16},{24,28},{28,24},{1,5},{5... | collective-permute-start | bytes 1867784 | tf_op jit(solution)/shard_map/ppermute | solution.py:285
  1208.1 44.0 %collective-permute-start.45 = (bf16[256,1216]{0,1:T(8,128)(2,1)S(1)}, bf16[256,1216]{0,1:T(8,128)(2,1)S(1)}, u32[]{:S(2)}, u32[]{:S(2)}) collective-permute-start(bf16[256,1216]{0,1:T(8,128)(2,1)S(1)} %fusion.28), channel_id=1, source_target_pairs={{0,8},{4,12},{8,16},{12,20},{16,24},{20,28},{24,0},{28,4},{1,9},{5... | collective-permute-start | bytes 1867784 | tf_op jit(solution)/shard_map/ppermute | solution.py:238
  1243.6 11.2 collective-permute-start.51
  1252.1 66.2 %collective-permute-start.54 = (bf16[256,1216]{0,1:T(8,128)(2,1)S(1)}, bf16[256,1216]{0,1:T(8,128)(2,1)S(1)}, u32[]{:S(2)}, u32[]{:S(2)}) collective-permute-start(bf16[256,1216]{0,1:T(8,128)(2,1)S(1)} %bitcast.225), channel_id=1, source_target_pairs={{0,4},{4,0},{8,12},{12,8},{16,20},{20,16},{24,28},{28,24},{1,5},{5... | collective-permute-start | bytes 1867784 | tf_op jit(solution)/shard_map/ppermute | solution.py:285
  1254.8 48.3 %collective-permute-start.53 = (bf16[256,1216]{0,1:T(8,128)(2,1)S(1)}, bf16[256,1216]{0,1:T(8,128)(2,1)S(1)}, u32[]{:S(2)}, u32[]{:S(2)}) collective-permute-start(bf16[256,1216]{0,1:T(8,128)(2,1)S(1)} %fusion.23), channel_id=1, source_target_pairs={{0,16},{4,20},{8,24},{12,28},{16,0},{20,4},{24,8},{28,12},{1,17},{... | collective-permute-start | bytes 1867784 | tf_op jit(solution)/shard_map/ppermute | solution.py:238
  1262.3 42.9 %collective-permute-start.56 = (bf16[256,1216]{0,1:T(8,128)(2,1)S(1)}, bf16[256,1216]{0,1:T(8,128)(2,1)S(1)}, u32[]{:S(2)}, u32[]{:S(2)}) collective-permute-start(bf16[256,1216]{0,1:T(8,128)(2,1)S(1)} %fusion.20), channel_id=1, source_target_pairs={{0,8},{4,12},{8,16},{12,20},{16,24},{20,28},{24,0},{28,4},{1,9},{5... | collective-permute-start | bytes 1867784 | tf_op jit(solution)/shard_map/ppermute | solution.py:238
  1263.7 39.4 %collective-permute-start.38 = (f32[40,128]{1,0:T(8,128)S(1)}, f32[40,128]{1,0:T(8,128)S(1)}, u32[]{:S(2)}, u32[]{:S(2)}) collective-permute-start(f32[40,128]{1,0:T(8,128)S(1)} %fusion.41), channel_id=1, source_target_pairs={{0,2},{1,3},{2,0},{3,1},{4,6},{5,7},{6,4},{7,5},{8,10},{9,11},{10,... | collective-permute-start | bytes 61448 | tf_op jit(solution)/shard_map/ppermute | solution.py:316
  1303.1 29.4 %collective-permute-start.58 = (bf16[256,1216]{0,1:T(8,128)(2,1)}, bf16[256,1216]{0,1:T(8,128)(2,1)S(1)}, u32[]{:S(2)}, u32[]{:S(2)}) collective-permute-start(bf16[256,1216]{0,1:T(8,128)(2,1)} %fusion.19), channel_id=1, source_target_pairs={{0,24},{4,28},{8,0},{12,4},{16,8},{20,12},{24,16},{28,20},{1,25},{... | collective-permute-start | bytes 1867784 | tf_op jit(solution)/shard_map/ppermute | solution.py:238
  1303.1 15.1 %collective-permute-start.39 = (f32[40,128]{1,0:T(8,128)S(1)}, f32[40,128]{1,0:T(8,128)S(1)}, u32[]{:S(2)}, u32[]{:S(2)}) collective-permute-start(f32[40,128]{1,0:T(8,128)S(1)} %fusion.74), channel_id=1, source_target_pairs={{0,4},{4,0},{8,12},{12,8},{16,20},{20,16},{24,28},{28,24},{1,5},{5... | collective-permute-start | bytes 61448 | tf_op jit(solution)/shard_map/ppermute | solution.py:316
  1305.2 37.6 %collective-permute-start.60 = (bf16[256,1216]{0,1:T(8,128)(2,1)}, bf16[256,1216]{0,1:T(8,128)(2,1)}, u32[]{:S(2)}, u32[]{:S(2)}) collective-permute-start(bf16[256,1216]{0,1:T(8,128)(2,1)} %fusion.18), channel_id=1, source_target_pairs={{0,16},{4,20},{8,24},{12,28},{16,0},{20,4},{24,8},{28,12},{1,17},{... | collective-permute-start | bytes 1867784 | tf_op jit(solution)/shard_map/ppermute | solution.py:238
  1318.2 14.3 %collective-permute-start.40 = (f32[40,128]{1,0:T(8,128)S(1)}, f32[40,128]{1,0:T(8,128)S(1)}, u32[]{:S(2)}, u32[]{:S(2)}) collective-permute-start(f32[40,128]{1,0:T(8,128)S(1)} %add.427), channel_id=1, source_target_pairs={{0,8},{4,12},{8,0},{12,4},{16,24},{20,28},{24,16},{28,20},{1,9},{5... | collective-permute-start | bytes 61448 | tf_op jit(solution)/shard_map/ppermute | solution.py:316
  1319.9 28.5 %all-to-all-start.2 = ((bf16[4,64,1216]{2,1,0:T(8,128)(2,1)}), bf16[4,64,1216]{2,1,0:T(8,128)(2,1)}, u32[]{:S(2)}, u32[]{:S(2)}) async-start(bf16[4,64,1216]{2,1,0:T(8,128)(2,1)} %bitcast.54), calls=%async_computation.4 | async-start | bytes 1310720 | tf_op jit(solution)/shard_map/all_to_all | solution.py:426
  1332.5 23.4 %collective-permute-start.41 = (f32[40,128]{1,0:T(8,128)S(1)}, f32[40,128]{1,0:T(8,128)S(1)}, u32[]{:S(2)}, u32[]{:S(2)}) collective-permute-start(f32[40,128]{1,0:T(8,128)S(1)} %add.428), channel_id=1, source_target_pairs={{0,16},{4,20},{8,24},{12,28},{16,0},{20,4},{24,8},{28,12},{1,17},{... | collective-permute-start | bytes 61448 | tf_op jit(solution)/shard_map/ppermute | solution.py:316
  1348.4 17.7 %all-to-all-start.3 = ((bf16[4,64,1216]{2,1,0:T(8,128)(2,1)}), bf16[4,64,1216]{2,1,0:T(8,128)(2,1)}, u32[]{:S(2)}, u32[]{:S(2)}) async-start(bf16[4,64,1216]{2,1,0:T(8,128)(2,1)} %bitcast.223), calls=%async_computation.5 | async-start | bytes 1310720 | tf_op jit(solution)/shard_map/all_to_all | solution.py:426
  (68 other events, 1067.7 us)
Sparse Core Ops, SparseCore 0:
  11.4 144.8 all-gather.2
  159.2 88.4 all-gather.4
  959.3 122.0 reduce-scatter.4
  1083.7 160.9 reduce-scatter.2

commit v2 on v1

--- a/solution.py
+++ b/solution.py
@@ -56,7 +56,7 @@
         n = u * lax.rsqrt(half_sums(u * u) / HD + EPSILON) * gain_ref[:1, at]
         turned = n * cosine + swapped_halves(n) * sine
         if block < q_blocks:
-            q_ref[:, at] = turned.astype(BF16)
+            q_ref[:, at] = (turned.astype(BF16).astype(F32) * (1.0 / math.sqrt(HD))).astype(BF16)
         else:
             kv_ref[0, :, pl.ds((block - q_blocks) * LANES, LANES)] = turned.astype(BF16)
     v_at = (q_blocks + k_blocks) * LANES
@@ -227,17 +227,189 @@
     )(q, two, one, kv, rel, gm)
 
 
-class Ring:
-    def __init__(self, depth):
-        self.depth = depth
-        self.arrived = []
-
-    def send(self, value, axis, pairs):
-        if len(self.arrived) >= self.depth:
-            value, _ = lax.optimization_barrier((value, self.arrived[-self.depth]))
-        out = lax.ppermute(value, axis, pairs)
-        self.arrived.append(out)
-        return out
+def feed_kernel(x_ref, gate_ref, up_ref, act_ref, gate_slope_ref, up_slope_ref):
+    x = x_ref[...]
+    gate, up = product(x, gate_ref[...]), product(x, up_ref[...])
+    sig = 1.0 / (1.0 + jnp.exp(-gate))
+    silu = gate * sig
+    act_ref[...] = (silu * up).astype(BF16)
+    gate_slope_ref[...] = (up * sig * (1.0 + gate * (1.0 - sig))).astype(BF16)
+    up_slope_ref[...] = silu.astype(BF16)
+
+
+def feed(x, both):
+    rows, width = x.shape
+    units = both.shape[1] // 2
+    tile = 2 * LANES
+    steps = units // tile
+    out = pl.BlockSpec((rows, tile), lambda j: (0, j))
+    return pl.pallas_call(
+        feed_kernel,
+        grid=(steps,),
+        in_specs=[
+            pl.BlockSpec((rows, width), lambda j: (0, 0)),
+            pl.BlockSpec((width, tile), lambda j: (0, j)),
+            pl.BlockSpec((width, tile), lambda j: (0, j + steps)),
+        ],
+        out_specs=[out] * 3,
+        out_shape=[jax.ShapeDtypeStruct((rows, units), BF16)] * 3,
+        compiler_params=pltpu.CompilerParams(vmem_limit_bytes=VMEM_LIMIT),
+        cost_estimate=pl.CostEstimate(
+            flops=4 * rows * width * units,
+            transcendentals=rows * units,
+            bytes_accessed=2 * (rows * width + 2 * width * units + 3 * rows * units),
+        ),
+        name="feed",
+    )(x, both, both)
+
+
+def feed_slopes_kernel(x_ref, down_ref, gs_ref, us_ref, gg_ref, gu_ref):
+    grad_act = right_transposed(x_ref[...], down_ref[...])
+    gg_ref[...] = (grad_act * gs_ref[...].astype(F32)).astype(BF16)
+    gu_ref[...] = (grad_act * us_ref[...].astype(F32)).astype(BF16)
+
+
+def feed_slopes(upstream, down, gate_slope, up_slope):
+    rows, width = upstream.shape
+    units = down.shape[0]
+    tile = 2 * LANES
+    columns = pl.BlockSpec((rows, tile), lambda j: (0, j))
+    return pl.pallas_call(
+        feed_slopes_kernel,
+        grid=(units // tile,),
+        in_specs=[
+            pl.BlockSpec((rows, width), lambda j: (0, 0)),
+            pl.BlockSpec((tile, width), lambda j: (j, 0)),
+            columns,
+            columns,
+        ],
+        out_specs=[columns, columns],
+        out_shape=[jax.ShapeDtypeStruct((rows, units), BF16)] * 2,
+        compiler_params=pltpu.CompilerParams(vmem_limit_bytes=VMEM_LIMIT),
+        cost_estimate=pl.CostEstimate(
+            flops=2 * rows * width * units,
+            transcendentals=0,
+            bytes_accessed=2 * (rows * width + width * units + 4 * rows * units),
+        ),
+        name="feed_slopes",
+    )(upstream, down, gate_slope, up_slope)
+
+
+def feed_back_kernel(gg_ref, gu_ref, both_ref, own_ref, other_ref):
+    units = gg_ref.shape[1]
+    lot = own_ref.shape[1]
+    total = right_transposed(gg_ref[...], both_ref[:, :units]) + right_transposed(
+        gu_ref[...], both_ref[:, units:]
+    )
+    for half in range(2):
+        own_ref[half] = total[2 * half * lot : (2 * half + 1) * lot]
+        other_ref[half] = total[(2 * half + 1) * lot : (2 * half + 2) * lot].astype(BF16)
+
+
+def feed_back(grad_gate, grad_up, both):
+    rows, units = grad_gate.shape
+    width = both.shape[0]
+    lot = rows // 4
+    tile = 2 * LANES
+    out = pl.BlockSpec((2, lot, tile), lambda j: (0, 0, j))
+    return pl.pallas_call(
+        feed_back_kernel,
+        grid=(width // tile,),
+        in_specs=[
+            pl.BlockSpec((rows, units), lambda j: (0, 0)),
+            pl.BlockSpec((rows, units), lambda j: (0, 0)),
+            pl.BlockSpec((tile, 2 * units), lambda j: (j, 0)),
+        ],
+        out_specs=[out, out],
+        out_shape=[
+            jax.ShapeDtypeStruct((2, lot, width), F32),
+            jax.ShapeDtypeStruct((2, lot, width), BF16),
+        ],
+        compiler_params=pltpu.CompilerParams(vmem_limit_bytes=VMEM_LIMIT),
+        cost_estimate=pl.CostEstimate(
+            flops=4 * rows * width * units,
+            transcendentals=0,
+            bytes_accessed=2 * (2 * rows * units + 2 * width * units + 2 * rows * width),
+        ),
+        name="feed_back",
+    )(grad_gate, grad_up, both)
+
+
+def lane_window(read, tiles, start):
+    tile, shift = start // LANES, start % LANES
+    first = read(min(max(tile, 0), tiles - 1))
+    if shift == 0:
+        return first
+    second = read(min(max(tile + 1, 0), tiles - 1))
+    lane = lax.broadcasted_iota(jnp.int32, first.shape, 1)
+    return jnp.where(
+        lane < LANES - shift,
+        pltpu.roll(first, LANES - shift, 1),
+        pltpu.roll(second, LANES - shift, 1),
+    )
+
+
+def lane_runs(target, runs, source_of):
+    total = None
+    for first, length, source in runs:
+        low, high = max(first, target), min(first + length, target + LANES)
+        if low >= high:
+            continue
+        window = source_of(source, target - first)
+        lane = lax.broadcasted_iota(jnp.int32, window.shape, 1) + target
+        kept = jnp.where((lane >= low) & (lane < high), window, 0.0)
+        total = kept if total is None else total + kept
+    return total
+
+
+def quarters_kernel(dp_size, unit, block, gate_ref, up_ref, out_ref):
+    units = dp_size * block
+    tiles = -(-gate_ref.shape[1] // LANES)
+    for at, ref in ((0, gate_ref), (units, up_ref)):
+        for member in range(4):
+            runs = [(d * block, unit, (4 * d + member) * unit) for d in range(dp_size)]
+
+            def source_of(source, offset):
+                read = lambda t: ref[:, t * LANES : (t + 1) * LANES].astype(F32)
+                return lane_window(read, tiles, source + offset)
+
+            for target in range(0, units, LANES):
+                value = lane_runs(target, runs, source_of)
+                out_ref[member, :, at + target : at + target + LANES] = value.astype(BF16)
+
+
+def quarters_of(gate, up, dp_size, unit, block):
+    return pl.pallas_call(
+        functools.partial(quarters_kernel, dp_size, unit, block),
+        out_shape=jax.ShapeDtypeStruct((4, gate.shape[0], 2 * dp_size * block), BF16),
+        compiler_params=pltpu.CompilerParams(vmem_limit_bytes=VMEM_LIMIT),
+        name="quarters",
+    )(gate, up)
+
+
+def columns_kernel(dp_size, unit, block, got_ref, out_ref):
+    tiles = got_ref.shape[2] // LANES
+    runs = [
+        ((4 * d + member) * unit, unit, (member, d * block))
+        for d in range(dp_size)
+        for member in range(4)
+    ]
+
+    def source_of(source, offset):
+        read = lambda t: got_ref[source[0], :, t * LANES : (t + 1) * LANES].astype(F32)
+        return lane_window(read, tiles, source[1] + offset)
+
+    for target in range(0, out_ref.shape[1], LANES):
+        out_ref[:, target : target + LANES] = lane_runs(target, runs, source_of)
+
+
+def columns_of(got, dp_size, unit, block):
+    return pl.pallas_call(
+        functools.partial(columns_kernel, dp_size, unit, block),
+        out_shape=jax.ShapeDtypeStruct((got.shape[1], 4 * dp_size * unit), F32),
+        compiler_params=pltpu.CompilerParams(vmem_limit_bytes=VMEM_LIMIT),
+        name="columns",
+    )(got)
 
 
 def swap_pairs(size, bit):
@@ -258,63 +430,209 @@
     return order
 
 
-def gather_dp(piece, size, ring):
-    mine = lax.axis_index("dp")
-    far, near = mine // 2, mine % 2
-    held = [(0, piece)]
-    for shift in far_order(size // 2):
-        held.append((shift, ring.send(piece, "dp", far_pairs(size, shift))))
-    out = jnp.zeros((size,) + piece.shape, piece.dtype)
-    zero = jnp.int32(0)
-    for shift, value in held:
-        other = lax.ppermute(value, "dp", swap_pairs(size, 1))
-        base = (far + size // 2 - shift) % (size // 2) * 2
-        out = lax.dynamic_update_slice(out, value[None], (base + near, zero, zero))
-        out = lax.dynamic_update_slice(out, other[None], (base + 1 - near, zero, zero))
+def place_kernel(counts, slots, *refs):
+    pieces, out, held, come, gone = refs[: len(counts)], *refs[len(counts) :]
+    arrivals, departures = [], []
+    for piece, count in zip(pieces, counts):
+        for k in range(count):
+            at = len(arrivals)
+            arrivals.append(pltpu.make_async_copy(piece.at[k], held.at[at], come.at[at]))
+            departures.append(pltpu.make_async_copy(held.at[at], out.at[slots[at]], gone.at[at]))
+    for copy in arrivals:
+        copy.start()
+    for arrival, departure in zip(arrivals, departures):
+        arrival.wait()
+        departure.start()
+    for copy in departures:
+        copy.wait()
+
+
+def place(pieces, slots):
+    counts = [piece.shape[0] for piece in pieces]
+    total = sum(counts)
+    shape = (total,) + pieces[0].shape[1:]
+    moved = 2 * math.prod(shape) * pieces[0].dtype.itemsize
+    return pl.pallas_call(
+        functools.partial(place_kernel, counts),
+        in_specs=[pl.BlockSpec(memory_space=pltpu.SMEM)]
+        + [pl.BlockSpec(memory_space=pl.ANY)] * len(pieces),
+        out_specs=pl.BlockSpec(memory_space=pl.ANY),
+        out_shape=jax.ShapeDtypeStruct(shape, pieces[0].dtype),
+        scratch_shapes=[
+            pltpu.VMEM(shape, pieces[0].dtype),
+            pltpu.SemaphoreType.DMA((total,)),
+            pltpu.SemaphoreType.DMA((total,)),
+        ],
+        compiler_params=pltpu.CompilerParams(vmem_limit_bytes=VMEM_LIMIT),
+        cost_estimate=pl.CostEstimate(flops=0, transcendentals=0, bytes_accessed=moved),
+        name="place",
+    )(slots, *pieces)
+
+
+def pick_kernel(counts, slots, source, *refs):
+    outs, (held, come, gone) = refs[: len(counts)], refs[len(counts) :]
+    arrivals, departures = [], []
+    for out, count in zip(outs, counts):
+        for k in range(count):
+            at = len(arrivals)
+            arrivals.append(pltpu.make_async_copy(source.at[slots[at]], held.at[at], come.at[at]))
+            departures.append(pltpu.make_async_copy(held.at[at], out.at[k], gone.at[at]))
+    for copy in arrivals:
+        copy.start()
+    for arrival, departure in zip(arrivals, departures):
+        arrival.wait()
+        departure.start()
+    for copy in departures:
+        copy.wait()
+
+
+def pick(source, slots, counts):
+    total = sum(counts)
+    block = source.shape[1:]
+    moved = 2 * total * math.prod(block) * source.dtype.itemsize
+    return pl.pallas_call(
+        functools.partial(pick_kernel, counts),
+        in_specs=[pl.BlockSpec(memory_space=pltpu.SMEM), pl.BlockSpec(memory_space=pl.ANY)],
+        out_specs=[pl.BlockSpec(memory_space=pl.ANY)] * len(counts),
+        out_shape=[jax.ShapeDtypeStruct((n,) + block, source.dtype) for n in counts],
+        scratch_shapes=[
+            pltpu.VMEM((total,) + block, source.dtype),
+            pltpu.SemaphoreType.DMA((total,)),
+            pltpu.SemaphoreType.DMA((total,)),
+        ],
+        compiler_params=pltpu.CompilerParams(vmem_limit_bytes=VMEM_LIMIT),
+        cost_estimate=pl.CostEstimate(flops=0, transcendentals=0, bytes_accessed=moved),
+        name="pick",
+    )(slots, source)
+
+
+class Places:
+    def __init__(self, dp_size):
+        self.size, self.far = dp_size, dp_size // 2
+        self.dp, self.member = lax.axis_index("dp"), lax.axis_index("fsdp")
+
+    def near_block(self, shift, near):
+        return (self.dp // 2 + self.far + shift) % self.far * 2 + self.dp % 2 * (1 - near) + (
+            1 - self.dp % 2
+        ) * near
+
+    def block(self, shift, near, member):
+        return self.near_block(shift, near) * 4 + (self.member ^ member)
+
+
+def gather_dp(piece, places, far_gate=None, near_gate=None):
+    piece = gated(piece, far_gate)
+    held = [piece]
+    for r in far_order(places.far):
+        held.append(lax.ppermute(piece, "dp", far_pairs(places.size, r)))
+    mine = jnp.stack(held)
+    return jnp.concatenate([mine, near_swap(gated(mine, near_gate), places)])
+
+
+def gather_group(pair, across, places, gate=None):
+    pair, across = gated((pair, across), gate)
+    beside, both = member_swap(pair, 1), member_swap(across, 1)
+    slots = [
+        places.block(-r, near, member)
+        for member in (0, 2, 1, 3)
+        for near in (0, 1)
+        for r in [0] + far_order(places.far)
+    ]
+    return place([pair, across, beside, both], jnp.stack(slots))
+
+
+def gated(value, gate):
+    return value if gate is None else lax.optimization_barrier((value, gate))[0]
+
+
+def gather_quarters(quarters, places):
+    mine = [
+        lax.dynamic_index_in_dim(quarters, places.member ^ k, 0, keepdims=False) for k in range(4)
+    ]
+    across = member_swap(jnp.stack([mine[2], mine[3]]), 2)
+    beside = member_swap(jnp.stack([mine[1], across[1]]), 1)
+    out = jnp.zeros_like(quarters)
+    for k, value in ((0, mine[0]), (1, beside[0]), (2, across[0]), (3, beside[1])):
+        out = lax.dynamic_update_index_in_dim(out, value, places.member ^ k, 0)
     return out
 
 
-def scatter_dp(terms, size, ring):
-    mine = lax.axis_index("dp")
-    far, near = mine // 2, mine % 2
-    total = None
-    for shift in far_order(size // 2) + [0]:
-        base = (far + shift) % (size // 2) * 2
-        other = lax.dynamic_index_in_dim(terms, base + 1 - near, 0, keepdims=False)
-        own = lax.dynamic_index_in_dim(terms, base + near, 0, keepdims=False)
-        got = lax.ppermute(other, "dp", swap_pairs(size, 1))
-        pair = own.astype(F32) + got.astype(F32)
-        if shift:
-            pair = ring.send(pair.astype(BF16), "dp", far_pairs(size, shift)).astype(F32)
-        total = pair if total is None else total + pair
+def gather_rows(rows, gate=None):
+    if gate is not None:
+        rows, _ = lax.optimization_barrier((rows, gate))
+    near = member_swap(rows, 1)
+    far = member_swap(rows, 2)
+    both = member_swap(far, 1)
+    return jnp.concatenate([rows, near, far, both], axis=0)
+
+
+def split_order(far):
+    order = far_order(far) + [0]
+    return order[: far // 2], order[far // 2 :]
+
+
+def feed_parts(term, places):
+    lots = split_order(places.far)
+    slots = [places.near_block(r, near) for near in (1, 0) for lot in lots for r in lot]
+    return pick(term, jnp.stack(slots), [len(lot) for _ in range(2) for lot in lots])
+
+
+def whole_parts(term, places):
+    order = sum(split_order(places.far), [])
+    slots = [
+        places.block(r, near, core + chip)
+        for core in (1, 0)
+        for chip in (2, 0)
+        for near in (1, 0)
+        for r in order
+    ]
+    return pick(term, jnp.stack(slots), [4 * len(order)] * 2)
+
+
+def near_swap(value, places):
+    return lax.ppermute(value, "dp", swap_pairs(places.size, 1))
+
+
+def member_swap(value, bit):
+    return lax.ppermute(value, "fsdp", swap_pairs(4, bit))
+
+
+def added(own, got):
+    return (own.astype(F32) + got.astype(F32)).astype(BF16)
+
+
+def far_sends(lot, blocks, places):
+    return [
+        lax.ppermute(blocks[k], "dp", far_pairs(places.size, r)) if r else blocks[k]
+        for k, r in enumerate(lot)
+    ]
+
+
+def total_of(parts):
+    total = parts[0].astype(F32)
+    for part in parts[1:]:
+        total = total + part.astype(F32)
     return total
 
 
-def gather_rows(rows):
-    core, chip = swap_pairs(4, 1), swap_pairs(4, 2)
-    near = lax.ppermute(rows, "fsdp", core)
-    far = lax.ppermute(rows, "fsdp", chip)
-    both = lax.ppermute(far, "fsdp", core)
-    return jnp.concatenate([rows, near, far, both], axis=0)
-
-
-def scatter_rows(partial):
-    rows = partial.shape[0] // 4
-    core, chip = swap_pairs(4, 1), swap_pairs(4, 2)
-    parts = partial.reshape(4, rows, -1)
-    far = lax.ppermute(parts[3].astype(BF16), "fsdp", core)
-    far = parts[2] + far.astype(F32)
-    far = lax.ppermute(far.astype(BF16), "fsdp", chip)
-    near = lax.ppermute(parts[1].astype(BF16), "fsdp", core)
-    return parts[0] + near.astype(F32) + far.astype(F32)
-
-
-def sum_all(value, dp_size):
-    for axis, size in (("fsdp", 4), ("dp", dp_size)):
-        bit = 1
-        while bit < size:
-            value = value + lax.ppermute(value, axis, swap_pairs(size, bit))
-            bit *= 2
+class Rounds:
+    def __init__(self):
+        self.results = ()
+
+    def enter(self, *values):
+        kept = lax.optimization_barrier((values, self.results))[0]
+        self.results = ()
+        return kept
+
+    def leave(self, *values):
+        self.results += values
+        return list(values) if len(values) > 1 else values[0]
+
+
+def sum_steps(value, axis, size, bit=1, end=None):
+    while bit < (end or size):
+        value = value + lax.ppermute(value, axis, swap_pairs(size, bit))
+        bit *= 2
     return value
 
 
@@ -357,27 +675,25 @@
     head_gains = jnp.concatenate([jnp.tile(q_gain, HEADS), jnp.tile(k_gain, KV_HEADS)])
     head_gains = jnp.broadcast_to(head_gains.astype(F32)[None, :], (8, head_gains.shape[0]))
 
+    places = Places(dp_size)
     gain_columns = jnp.pad(
         jnp.stack([attn_gain, ffn_gain], axis=1), ((0, 0), (0, LANES - 2))
     )
     w_qkv = jnp.concatenate([w_query, w_key, w_value, gain_columns], axis=1)
-    full_qkv = lax.all_gather(w_qkv, BOTH, axis=0, tiled=True)
-    full_out = lax.all_gather(w_out, BOTH, axis=0, tiled=True)
-
-    def quarters(weight):
-        split = weight.reshape(shard, dp_size, 4, ff_rows)
-        return jnp.moveaxis(split, 2, 0).reshape(4, shard, dp_size * ff_rows)
-
-    ring = Ring(2)
-    gate_piece = lax.all_to_all(quarters(w_gate), "fsdp", 0, 0, tiled=True)
-    up_piece = lax.all_to_all(quarters(w_up), "fsdp", 0, 0, tiled=True)
-    ff_width = dp_size * ff_rows
-    my_gate = gather_dp(gate_piece.reshape(4 * shard, ff_width), dp_size, ring)
-    my_up = gather_dp(up_piece.reshape(4 * shard, ff_width), dp_size, ring)
-    my_down = gather_dp(w_down, dp_size, ring)
-    my_gate = my_gate.reshape(width, ff_width)
-    my_up = my_up.reshape(width, ff_width)
-    my_down = my_down.reshape(ff_width, width)
+    qkv_pair = gather_dp(w_qkv, places)
+    out_pair = gather_dp(w_out, places, qkv_pair)
+    qkv_across = member_swap(qkv_pair, 2)
+    out_across = member_swap(gated(out_pair, qkv_across), 2)
+    full_qkv = gather_group(qkv_pair, qkv_across, places).reshape(width, -1)
+
+    ff_block = -(-ff_rows * dp_size // LANES) * LANES // dp_size
+    ff_width = dp_size * ff_block
+
+    both_low = quarters_of(w_gate, w_up, dp_size, ff_rows, ff_block)
+    both_piece = gather_quarters(gated(both_low, qkv_pair), places).reshape(4 * shard, 2 * ff_width)
+    down_piece = jnp.pad(w_down, ((0, ff_block - ff_rows), (0, 0)))
+    my_down = lax.all_gather(down_piece, "dp", axis=0, tiled=True)
+    my_both = lax.all_gather(both_piece, "dp", axis=0, tiled=True)
 
     gain_table = full_qkv[:, full_qkv.shape[1] - LANES :]
     pick = (
@@ -391,67 +707,148 @@
     normed = (x * x_inverse * attn_row).astype(BF16)
     pre = product(normed, full_qkv)
     queries, kv = head_prep(pre, cosine, sine, head_gains)
-    queries = queries * jnp.bfloat16(1.0 / math.sqrt(HD))
     ahead_one = [(i, i + 1) for i in range(3)]
     ahead_two = [(i, i + 2) for i in range(2)]
     kv_one = lax.ppermute(kv, "fsdp", ahead_one)
     kv_two = lax.ppermute(kv, "fsdp", ahead_two)
     mixed = attend(queries, kv_two, kv_one, kv, rel)
+    full_out = gather_group(out_pair, out_across, places, kv_one).reshape(-1, width)
     hidden = x + product(mixed, full_out)
     h_inverse = lax.rsqrt(jnp.mean(hidden * hidden, axis=-1, keepdims=True) + EPSILON)
     ffn_mine = (hidden * h_inverse * ffn_row).astype(BF16)
 
-    upstream = gather_rows(cotangent)
+    upstream = gather_rows(cotangent, kv_one)
     ffn_low = gather_rows(ffn_mine)
-    gate = product(ffn_low, my_gate)
-    up = product(ffn_low, my_up)
-    sig = 1.0 / (1.0 + jnp.exp(-gate))
-    silu = gate * sig
-    act_low = (silu * up).astype(BF16)
-    back = Ring(2)
-    term_down = left_transposed(act_low, upstream).astype(BF16)
-    down_grad = scatter_dp(term_down.reshape(dp_size, ff_rows, width), dp_size, back)
-    grad_act = right_transposed(upstream, my_down)
-    grad_gate = (grad_act * up * sig * (1.0 + gate * (1.0 - sig))).astype(BF16)
-    grad_up = (grad_act * silu).astype(BF16)
-    grad_ffn = scatter_rows(right_transposed(grad_gate, my_gate) + right_transposed(grad_up, my_up))
-    term_gate = left_transposed(ffn_low, grad_gate).astype(BF16)
-    term_up = left_transposed(ffn_low, grad_up).astype(BF16)
-    gate_sum = scatter_dp(term_gate.reshape(dp_size, 4 * shard, ff_width), dp_size, back)
-    up_sum = scatter_dp(term_up.reshape(dp_size, 4 * shard, ff_width), dp_size, back)
-    output = (hidden + scatter_rows(product(act_low, my_down))).astype(BF16)
-
-    def whole_rows(total):
-        sent = total.astype(BF16).reshape(4, shard, ff_width)
-        got = lax.all_to_all(sent, "fsdp", 0, 0, tiled=True)
-        split = jnp.moveaxis(got.reshape(4, shard, dp_size, ff_rows), 0, 2)
-        return split.reshape(shard, 4 * ff_width).astype(F32)
-
-    gate_grad = whole_rows(gate_sum)
-    up_grad = whole_rows(up_sum)
-
+    act_low, gate_slope, up_slope = feed(ffn_low, my_both)
+    lot_a, lot_b = split_order(places.far)
+
+    def parts_of(left, right):
+        term = left_transposed(left, right).astype(BF16)
+        return feed_parts(term.reshape(dp_size, -1, term.shape[1]), places)
+
+    rounds = Rounds()
+
+    d_oa, d_ob, d_wa, d_wb, upstream, my_down = rounds.enter(
+        *parts_of(act_low, upstream), upstream, my_down
+    )
+    d_ga = rounds.leave(near_swap(d_oa, places))
+    grad_gate, grad_up = feed_slopes(upstream, my_down, gate_slope, up_slope)
+    grad_gate, grad_up, ffn_own, ffn_other = rounds.leave(
+        grad_gate, grad_up, *feed_back(grad_gate, grad_up, my_both)
+    )
+
+    d_sa = added(d_wa, d_ga)
+    d_sa, d_ob, grad_gate, grad_up, ffn_own, ffn_other = rounds.enter(
+        d_sa, d_ob, grad_gate, grad_up, ffn_own, ffn_other
+    )
+    ffn_got = rounds.leave(member_swap(ffn_other, 1))
+    far_got = rounds.leave(member_swap(added(ffn_own[1], ffn_got[1]), 2))
+    d_za = rounds.leave(*far_sends(lot_a, d_sa, places))
+    d_gb = rounds.leave(near_swap(d_ob, places))
+    g_oa, g_ob, g_wa, g_wb = rounds.leave(*parts_of(ffn_low, grad_gate))
+    u_oa, u_ob, u_wa, u_wb = rounds.leave(*parts_of(ffn_low, grad_up))
+
+    d_sb = added(d_wb, d_gb)
+    g_oa, d_sb, ffn_own, ffn_got, far_got = rounds.enter(g_oa, d_sb, ffn_own, ffn_got, far_got)
+    g_ga = rounds.leave(near_swap(g_oa, places))
+    d_zb = rounds.leave(*far_sends(lot_b, d_sb, places))
+    grad_ffn = ffn_own[0] + ffn_got[0].astype(F32) + far_got.astype(F32)
     e = grad_ffn * ffn_row
     slope = jnp.mean(hidden * e, axis=-1, keepdims=True)
     grad_hidden = cotangent.astype(F32) + h_inverse * e - hidden * (h_inverse**3 * slope)
     ffn_gain_term = jnp.sum(grad_ffn * hidden * h_inverse, axis=0)
     grad_hidden_low = grad_hidden.astype(BF16)
     grad_mixed = right_transposed(grad_hidden_low, full_out).astype(BF16)
+    gq, gkv_two, gkv_one, gkv = rounds.leave(
+        *attend_back(queries, kv_two, kv_one, kv, rel, grad_mixed)
+    )
     term_out = left_transposed(mixed, grad_hidden_low).astype(BF16)
-    out_grad = lax.psum_scatter(term_out, BOTH, scatter_dimension=0, tiled=True).astype(F32)
-    gq, gkv_two, gkv_one, gkv = attend_back(queries, kv_two, kv_one, kv, rel, grad_mixed)
+    o_other, o_own = rounds.leave(
+        *whole_parts(term_out.reshape(4 * dp_size, -1, width), places)
+    )
+
+    g_sa = added(g_wa, g_ga)
+    g_sa, g_ob, gkv_one, gkv_two, o_other, o_own, gq, gkv = rounds.enter(
+        g_sa, g_ob, gkv_one, gkv_two, o_other, o_own, gq, gkv
+    )
+    g_za = rounds.leave(*far_sends(lot_a, g_sa, places))
+    g_gb = rounds.leave(near_swap(g_ob, places))
     got_one = lax.ppermute(gkv_one, "fsdp", [(b, a) for a, b in ahead_one])
     got_two = lax.ppermute(gkv_two, "fsdp", [(b, a) for a, b in ahead_two])
+    o_sum = added(o_own, member_swap(o_other, 1))
+    half = o_sum.shape[0] // 2
+    quarter, lot = half // 2, half // 2
+    o_across = rounds.leave(member_swap(gated(o_sum[:half], got_two), 2))
+    o_sum = rounds.leave(o_sum[half:])
     grad_pre, head_sums = head_back(gq, gkv, got_one, got_two, pre, cosine, sine, head_gains)
     term_qkv = left_transposed(normed, grad_pre).astype(BF16)
-    qkv_grad = lax.psum_scatter(term_qkv, BOTH, scatter_dimension=0, tiled=True).astype(F32)
+    q_other, q_own = rounds.leave(
+        *whole_parts(term_qkv.reshape(4 * dp_size, shard, -1), places)
+    )
+
+    g_sb = added(g_wb, g_gb)
+    o_sum = added(o_sum, o_across)
+    u_oa, g_sb, q_other, q_own, grad_pre, o_sum = rounds.enter(
+        u_oa, g_sb, q_other, q_own, grad_pre, o_sum
+    )
+    o_got = rounds.leave(near_swap(o_sum[:quarter], places))
+    o_sum = o_sum[quarter:]
+    q_sum = rounds.leave(added(q_own, member_swap(q_other, 1)))
+    q_xa = rounds.leave(member_swap(q_sum[:lot], 2))
+    u_ga = rounds.leave(near_swap(u_oa, places))
+    g_zb = rounds.leave(*far_sends(lot_b, g_sb, places))
+    u_sa = added(u_wa, u_ga)
+    o_sum = added(o_sum, o_got)
+    u_sa, u_ob, q_xb, grad_pre, act_low, o_sum = rounds.enter(
+        u_sa, u_ob, q_sum[lot:half], grad_pre, act_low, o_sum
+    )
+    o_parts = rounds.leave(*far_sends(lot_a + lot_b, o_sum, places))
+    q_xb = rounds.leave(member_swap(q_xb, 2))
     grad_normed = right_transposed(grad_pre, full_qkv)
+    out_part = product(act_low, my_down).reshape(2, 2, rows, width)
+    out_own, out_other = rounds.leave(out_part[:, 0], out_part[:, 1].astype(BF16))
+    u_za = rounds.leave(*far_sends(lot_a, u_sa, places))
+    u_gb = rounds.leave(near_swap(u_ob, places))
+    gate_low = total_of(g_za + g_zb).astype(BF16).reshape(4, shard, ff_width)
+    gate_low = rounds.leave(gate_low)
+    down_grad = rounds.leave(total_of(d_za + d_zb)[:ff_rows])
     e = grad_normed * attn_row
     slope = jnp.mean(x * e, axis=-1, keepdims=True)
     input_grad = grad_hidden + x_inverse * e - x * (x_inverse**3 * slope)
-    attn_gain_term = jnp.sum(grad_normed * x * x_inverse, axis=0)
+    input_grad = rounds.leave(input_grad.astype(BF16))
+    attn_gain_term = rounds.leave(jnp.sum(grad_normed * x * x_inverse, axis=0))
 
     small = jnp.concatenate([attn_gain_term, ffn_gain_term, head_sums.reshape(-1)])
-    small = sum_all(small.reshape(-1, LANES), dp_size).reshape(-1)
+    small = rounds.leave(small.reshape(-1, LANES))
+
+    u_sb = added(u_wb, u_gb)
+    q_y = added(q_sum[half:], jnp.concatenate([q_xa, q_xb]))
+    u_sb, q_yo, q_yw, gate_low, out_own, out_other = rounds.enter(
+        u_sb, q_y[:quarter], q_y[quarter:], gate_low, out_own, out_other
+    )
+    out_got = member_swap(out_other, 1)
+    out_far = added(out_own[1], out_got[1])
+    u_zb = rounds.leave(*far_sends(lot_b, u_sb, places))
+    q_yo = rounds.leave(near_swap(q_yo, places))
+    out_far = rounds.leave(member_swap(out_far, 2))
+    gate_got = rounds.leave(lax.all_to_all(gate_low, "fsdp", 0, 0, tiled=True))
+    out_grad = rounds.leave(total_of(o_parts))
+
+    q_z = added(q_yw, q_yo)
+    up_low = total_of(u_za + u_zb).astype(BF16).reshape(4, shard, ff_width)
+    q_z, up_low, gate_got, out_far, small = rounds.enter(q_z, up_low, gate_got, out_far, small)
+    small = sum_steps(sum_steps(small, "fsdp", 4), "dp", dp_size, 1, 2)
+    q_parts = rounds.leave(*far_sends(lot_a + lot_b, q_z, places))
+    up_got = rounds.leave(lax.all_to_all(up_low, "fsdp", 0, 0, tiled=True))
+    gate_grad = rounds.leave(columns_of(gate_got, dp_size, ff_rows, ff_block))
+
+    small, up_got = rounds.enter(small, up_got)
+    small = sum_steps(small, "dp", dp_size, 2).reshape(-1)
+    qkv_grad = total_of(q_parts)
+
+    up_grad = columns_of(up_got, dp_size, ff_rows, ff_block)
+    output = (hidden + out_own[0] + out_got[0].astype(F32) + out_far.astype(F32)).astype(BF16)
+
     mine = (lax.axis_index("dp") * 4 + member) * shard
     attn_gain_grad = lax.dynamic_slice(small, (mine,), (shard,))
     ffn_gain_grad = lax.dynamic_slice(small, (width + mine,), (shard,))

time: 1410 us -> 782 us (0.55); the launches traced: 1390 us -> 774 us
  local copies, waits for them, and re-layouts: 649 us -> 50.9 us
  Pallas kernels: 37 us -> 130 us
  matrix products: 118 us -> 65 us
  waiting for transfers between devices: 401 us -> 350 us
  starting transfers between devices: 136 us -> 101 us
  other arithmetic: 30.9 us -> 62.4 us
    dynamic_update_slice x24 -> x3, local copies, waits for them, and re-layouts: 445 us -> 2.26 us  [gather_quarters(): out = lax.dynamic_update_index_in_dim(out, value, places.member ^ k, 0)]
    pallas_call x0 -> x13, Pallas kernels: none -> 92.6 us  [the longest x5 25.6 us: pick(): pl.pallas_call(functools.partial(pick_kernel, counts), in_specs=[pl.Block...]
    broadcast_in_dim x15 -> x1, local copies, waits for them, and re-layouts: 84 us -> 1.2 us  [gather_quarters(): out = jnp.zeros_like(quarters)]
    ppermute x59, waiting for transfers between devices: 373 us -> 334 us  [the longest x23 134 us: member_swap(): return lax.ppermute(value, 'fsdp', swap_pairs(4, bit))]
    dot_general x6 -> x3, matrix products: 45.6 us -> 11.4 us  [right_transposed(): lax.dot_general(left, right, (((1,), (1,)), ((), ())), preferred_element_...]
    ppermute x59, starting transfers between devices: 112 us -> 84.9 us  [the longest x15 29.9 us: far_sends(): lax.ppermute(blocks[k], 'dp', far_pairs(places.size, r))]
    convert_element_type x13 -> x18, other arithmetic: 15.3 us -> 39.6 us  [the longest x14 29.7 us: added(): return (own.astype(F32) + got.astype(F32)).astype(BF16)]
    dynamic_slice x2 -> x1, local copies, waits for them, and re-layouts: 23.6 us -> 0.85 us  [gather_quarters(): lax.dynamic_index_in_dim(quarters, places.member ^ k, 0, keepdims=False)]
  transfers between devices with their start and end apart: 71 -> 67, of which waited for: 23 -> 30; matrix products, arithmetic and copies ran while one was open for 52% -> 17% of each run, Pallas kernels for 3% -> 17%
where the time goes in v2:
time: 782 us; the launch traced here: 774 us
  waiting for transfers between devices  350 us (45%)
  Pallas kernels  130 us (17%)
  starting transfers between devices  101 us (13%)
  matrix products  65 us (8%)
  other arithmetic  62.4 us (8%)
  local copies, waits for them, and re-layouts  50.9 us (7%)
  between operations  15.6 us (2%)
    ppermute x23, waiting for transfers between devices, member_swap(): return lax.ppermute(value, 'fsdp', swap_pairs(4, bit))  134 us
    ppermute x10, waiting for transfers between devices, near_swap(): return lax.ppermute(value, 'dp', swap_pairs(places.size, 1))  99.9 us
    ppermute x15, waiting for transfers between devices, far_sends(): lax.ppermute(blocks[k], 'dp', far_pairs(places.size, r))  57 us
    ppermute x6, waiting for transfers between devices, gather_dp(): held.append(lax.ppermute(piece, 'dp', far_pairs(places.size, r)))  40 us
    dot_general x5, matrix products, left_transposed(): lax.dot_general(left, right, (((0,), (0,)), ((), ())), preferred_element_...  35.1 us
    ppermute x15, starting transfers between devices, far_sends(): lax.ppermute(blocks[k], 'dp', far_pairs(places.size, r))  29.9 us
    convert_element_type x14, other arithmetic, added(): return (own.astype(F32) + got.astype(F32)).astype(BF16)  29.7 us
    unnamed x174, local copies, waits for them, and re-layouts  26.7 us
  transfers between devices with their start and end apart: 67, of which 30 were waited for; matrix products, arithmetic and copies ran while one was open for 17% of the time, Pallas kernels for 17%

profile of v2, /device:TPU:0, one launch (start us, length us, event | category | flops | bytes accessed | tf_op | source)
XLA Modules:
  0.0 773.9 jit_solution(11902372049707726227)
XLA Ops:
  9.1 4.1 collective-permute-start.2
  18.4 10.6 %collective-permute-done.2 = bf16[64,2432]{1,0:T(8,128)(2,1)S(1)} collective-permute-done((bf16[64,2432]{1,0:T(8,128)(2,1)S(1)}, bf16[64,2432]{1,0:T(8,128)(2,1)S(1)}, u32[]{:S(2)}, u32[]{:S(2)}) %collective-permute-start.2) | collective-permute-done | bytes 311328 | tf_op jit(solution)/shard_map/ppermute | solution.py:527
  28.9 6.2 collective-permute-done
  39.0 25.6 %collective-permute-done.3 = bf16[4,64,2432]{2,1,0:T(8,128)(2,1)S(1)} collective-permute-done((bf16[4,64,2432]{2,1,0:T(8,128)(2,1)S(1)}, bf16[4,64,2432]{2,1,0:T(8,128)(2,1)S(1)}, u32[]{:S(2)}, u32[]{:S(2)}) %collective-permute-start.3) | collective-permute-done | bytes 1245216 | tf_op jit(solution)/shard_map/ppermute | solution.py:593
  68.4 13.2 %collective-permute-done.19 = bf16[2,64,2560]{2,1,0:T(8,128)(2,1)S(1)} collective-permute-done((bf16[2,64,2560]{2,1,0:T(8,128)(2,1)S(1)}, bf16[2,64,2560]{2,1,0:T(8,128)(2,1)S(1)}, u32[]{:S(2)}, u32[]{:S(2)}) %collective-permute-start.19) | collective-permute-done | bytes 655392 | tf_op jit(solution)/shard_map/ppermute | solution.py:597
  91.8 50.7 %collective-permute-done.4.refs_1_ = bf16[8,64,2432]{2,1,0:T(8,128)(2,1)} collective-permute-done((bf16[8,64,2432]{2,1,0:T(8,128)(2,1)S(1)}, bf16[8,64,2432]{2,1,0:T(8,128)(2,1)}, u32[]{:S(2)}, u32[]{:S(2)}) %collective-permute-start.4) | collective-permute-done | bytes 2490400 | tf_op jit(solution)/shard_map/ppermute | solution.py:597
  143.6 10.4 %collective-permute-start.11 = (bf16[48,2048]{1,0:T(8,128)(2,1)}, bf16[48,2048]{1,0:T(8,128)(2,1)S(1)}, u32[]{:S(2)}, u32[]{:S(2)}) collective-permute-start(bf16[48,2048]{1,0:T(8,128)(2,1)} %param.24), channel_id=1, source_target_pairs={{0,16},{4,20},{8,24},{12,28},{16,0},{20,4},{24,8},{28,12},{1,17},{... | collective-permute-start | bytes 589832 | tf_op jit(solution)/shard_map/ppermute | solution.py:527
  157.0 22.6 %collective-permute-done.11 = bf16[48,2048]{1,0:T(8,128)(2,1)S(1)} collective-permute-done((bf16[48,2048]{1,0:T(8,128)(2,1)}, bf16[48,2048]{1,0:T(8,128)(2,1)S(1)}, u32[]{:S(2)}, u32[]{:S(2)}) %collective-permute-start.11) | collective-permute-done | bytes 196640 | tf_op jit(solution)/shard_map/ppermute | solution.py:527
  182.9 35.2 %collective-permute-done.12 = bf16[4,48,2048]{2,1,0:T(8,128)(2,1)S(1)} collective-permute-done((bf16[4,48,2048]{2,1,0:T(8,128)(2,1)S(1)}, bf16[4,48,2048]{2,1,0:T(8,128)(2,1)S(1)}, u32[]{:S(2)}, u32[]{:S(2)}) %collective-permute-start.12) | collective-permute-done | bytes 786464 | tf_op jit(solution)/shard_map/ppermute | solution.py:593
  219.9 8.4 %place.2 = bf16[32,64,2432]{2,1,0:T(8,128)(2,1)} custom-call(s32[32]{0:T(128)S(1)} %stack.373.slots, bf16[8,64,2432]{2,1,0:T(8,128)(2,1)S(1)} %constant_dynamic-update-slice_fusion.refs_0_, bf16[8,64,2432]{2,1,0:T(8,128)(2,1)} %collective-permute-done.4.refs_1_, bf16[8,64,2432]{2,1,0:T(8,128)(2,1)} %collective-permute-done.5.refs_2_, ...), custom_call_target="tpu_custom_call" | custom-call | bytes 19922944 | tf_op jit(solution)/shard_map/place/pallas_call | solution.py:455
  229.7 6.1 fusion.20.pre_ref
  239.2 15.6 %collective-permute-done.13.refs_1_ = bf16[8,48,2048]{2,1,0:T(8,128)(2,1)S(1)} collective-permute-done((bf16[8,48,2048]{2,1,0:T(8,128)(2,1)S(1)}, bf16[8,48,2048]{2,1,0:T(8,128)(2,1)S(1)}, u32[]{:S(2)}, u32[]{:S(2)}) %collective-permute-start.13) | collective-permute-done | bytes 1572896 | tf_op jit(solution)/shard_map/ppermute | solution.py:597
  254.8 2.6 collective-permute-start.14
  257.4 5.0 collective-permute-start.7
  262.4 9.2 %collective-permute-done.7.two_ref = bf16[2,256,384]{2,1,0:T(8,128)(2,1)S(1)} collective-permute-done((bf16[2,256,384]{2,1,0:T(8,128)(2,1)S(1)}, bf16[2,256,384]{2,1,0:T(8,128)(2,1)S(1)}, u32[]{:S(2)}, u32[]{:S(2)}) %collective-permute-start.7) | collective-permute-done | bytes 393248 | tf_op jit(solution)/shard_map/ppermute | solution.py:713
  271.8 11.8 %attend.1 = bf16[256,1536]{1,0:T(8,128)(2,1)S(1)} custom-call(bf16[256,1536]{1,0:T(8,128)(2,1)S(1)} %get-tuple-element.101.q_ref, bf16[2,256,384]{2,1,0:T(8,128)(2,1)S(1)} %collective-permute-done.7.two_ref, bf16[2,256,384]{2,1,0:T(8,128)(2,1)S(1)} %collective-permute-done.8.one_ref, bf16[2,256,384]{2,1,0:T(8,128)(2,1)S(1)} %get-tuple-element.102.kv_ref, ...), custom_call_target="tpu_custom_call" | custom-call | tf_op jit(solution)/shard_map/attend/pallas_call | solution.py:169
  284.9 10.7 %place.3 = bf16[32,48,2048]{2,1,0:T(8,128)(2,1)} custom-call(s32[32]{0:T(128)S(1)} %stack.373.slots, bf16[8,48,2048]{2,1,0:T(8,128)(2,1)S(1)} %constant_dynamic-update-slice_fusion.5.refs_0_, bf16[8,48,2048]{2,1,0:T(8,128)(2,1)S(1)} %collective-permute-done.13.refs_1_, bf16[8,48,2048]{2,1,0:T(8,128)(2,1)S(1)} %collective-permute-done.14.refs_2_, ...), custom_call_target="tpu_custom_call" | custom-call | bytes 12582912 | tf_op jit(solution)/shard_map/place/pallas_call | solution.py:455
  295.6 4.7 multiply_reduce_fusion.2
  302.0 2.5 collective-permute-start.17
  305.1 21.1 %collective-permute-done.17 = bf16[256,2048]{1,0:T(8,128)(2,1)} collective-permute-done((bf16[256,2048]{1,0:T(8,128)(2,1)S(1)}, bf16[256,2048]{1,0:T(8,128)(2,1)}, u32[]{:S(2)}, u32[]{:S(2)}) %collective-permute-start.17) | collective-permute-done | bytes 1048608 | tf_op jit(solution)/shard_map/ppermute | solution.py:597
  332.4 3.6 pad_maximum_fusion.x_ref
  336.0 17.7 %feed.1 = (bf16[1024,1280]{1,0:T(8,128)(2,1)S(1)}, bf16[1024,1280]{1,0:T(8,128)(2,1)S(1)}, bf16[1024,1280]{1,0:T(8,128)(2,1)}) custom-call(bf16[1024,2048]{1,0:T(8,128)(2,1)} %pad_maximum_fusion.x_ref, bf16[2048,2560]{1,0:T(8,128)(2,1)} %all-gather.3.cloned.1.call-done.gate_ref.up_ref.both_ref, ...), custom_call_target="tpu_custom_call" | custom-call | flops 10737418240 | bytes 22544384 | tf_op jit(solution)/shard_map/feed/pallas_call | solution.py:246
  353.7 7.4 convolution_convert_fusion.4
  361.1 3.4 pick.5
  369.2 10.4 %feed_slopes.1 = (bf16[1024,1280]{1,0:T(8,128)(2,1)S(1)}, bf16[1024,1280]{1,0:T(8,128)(2,1)S(1)}) custom-call(bf16[1024,2048]{1,0:T(8,128)(2,1)} %copy-done.70, bf16[1280,2048]{1,0:T(8,128)(2,1)} %all-gather.5.cloned.1.call-done.down_ref, bf16[1024,1280]{1,0:T(8,128)(2,1)} %copy-done.32, bf16[1024,1280]{1,0:T(8,128)(2,1)} %get-tuple-element.120.us_ref), custom_call_target="tpu_custom_call" | custom-call | flops 5368709120 | bytes 19922944 | tf_op jit(solution)/shard_map/feed_slopes/pallas_call | solution.py:277
  381.1 15.6 %feed_back.1 = (f32[2,256,2048]{2,1,0:T(8,128)}, bf16[2,256,2048]{2,1,0:T(8,128)(2,1)S(1)}) custom-call(bf16[1024,1280]{1,0:T(8,128)(2,1)S(1)} %get-tuple-element.129.gg_ref, bf16[1024,1280]{1,0:T(8,128)(2,1)} %copy-done.30, bf16[2048,2560]{1,0:T(8,128)(2,1)} %all-gather.3.cloned.1.call-done.gate_ref.up_ref.both_ref), custom_call_target="tpu_custom_call" | custom-call | flops 10737418240 | bytes 24117248 | tf_op jit(solution)/shard_map/feed_back/pallas_call | solution.py:315
  396.7 2.4 collective-permute-done.24
  401.0 13.5 %collective-permute-start.28 = (bf16[160,2048]{1,0:T(8,128)(2,1)}, bf16[160,2048]{1,0:T(8,128)(2,1)}, u32[]{:S(2)}, u32[]{:S(2)}) collective-permute-start(bf16[160,2048]{1,0:T(8,128)(2,1)} %get-tuple-element.206), channel_id=1, source_target_pairs={{0,8},{4,12},{8,16},{12,20},{16,24},{20,28},{24,0},{28,4},{1,9},{5... | collective-permute-start | bytes 1966088 | tf_op jit(solution)/shard_map/ppermute | solution.py:606
  415.1 8.8 %convolution_convert_fusion.3 = bf16[2048,1280]{1,0:T(8,128)(2,1)} fusion(bf16[1024,1280]{1,0:T(8,128)(2,1)S(1)} %copy-done.31, bf16[256,2048]{1,0:T(8,128)(2,1)} %collective-permute-done.18, bf16[256,2048]{1,0:T(8,128)(2,1)} %collective-permute-done.17, bf16[256,2048]{1,0:T(8,128)(2,1)} %collective-permute-done.16, ...), kind=kOutput, calls=%fused_computation.4 | convolution fusion | flops 5388107776 | bytes 12058624 | tf_op jit(solution)/shard_map/dot_general | solution.py:32
  427.4 8.7 %convolution_convert_fusion.2 = bf16[2048,1280]{1,0:T(8,128)(2,1)} fusion(bf16[1024,1280]{1,0:T(8,128)(2,1)S(1)} %get-tuple-element.129.gg_ref, bf16[256,2048]{1,0:T(8,128)(2,1)} %collective-permute-done.18, bf16[256,2048]{1,0:T(8,128)(2,1)} %collective-permute-done.17, bf16[256,2048]{1,0:T(8,128)(2,1)} %collective-permute-done.16, ...), kind=kOutput, calls=%fused_computation.3 | convolution fusion | flops 5388107776 | bytes 12058624 | tf_op jit(solution)/shard_map/dot_general | solution.py:32
  436.1 3.4 pick.6
  441.8 4.3 pick.7
  446.1 2.8 add_convert_fusion.8
  450.9 3.5 multiply_reduce_fusion
  454.5 2.4 multiply_subtract_fusion
  463.7 4.4 convolution_convert_fusion.1
  468.1 7.8 %pick.8 = (bf16[16,48,2048]{2,1,0:T(8,128)(2,1)S(1)}, bf16[16,48,2048]{2,1,0:T(8,128)(2,1)}) custom-call(s32[32]{0:T(128)S(1)} %stack.422.slots, bf16[32,48,2048]{2,1,0:T(8,128)(2,1)} %bitcast.193), custom_call_target="tpu_custom_call" | custom-call | bytes 12582912 | tf_op jit(solution)/shard_map/pick/pallas_call | solution.py:493
  477.7 17.4 %attend_back.1 = (f32[256,1536]{1,0:T(8,128)S(1)}, bf16[2,256,384]{2,1,0:T(8,128)(2,1)S(1)}, bf16[2,256,384]{2,1,0:T(8,128)(2,1)S(1)}, f32[2,256,384]{2,1,0:T(8,128)S(1)}) custom-call(bf16[256,1536]{1,0:T(8,128)(2,1)S(1)} %copy-done.2, bf16[2,256,384]{2,1,0:T(8,128)(2,1)S(1)} %copy-done.8, bf16[2,256,384]{2,1,0:T(8,128)(2,1)S(1)} %copy-done.6, ...), custom_call_target="tpu_custom_call" | custom-call | tf_op jit(solution)/shard_map/attend_back/pallas_call | solution.py:214
  503.0 3.2 add_convert_fusion.1
  509.3 6.3 collective-permute-done.34.two_ref
  518.7 5.7 head_back.1
  524.5 5.8 convolution_convert_fusion
  530.2 6.7 pick.9
  538.8 10.8 %collective-permute-done.36 = bf16[8,48,2048]{2,1,0:T(8,128)(2,1)} collective-permute-done((bf16[8,48,2048]{2,1,0:T(8,128)(2,1)}, bf16[8,48,2048]{2,1,0:T(8,128)(2,1)}, u32[]{:S(2)}, u32[]{:S(2)}) %collective-permute-start.36) | collective-permute-done | bytes 1572896 | tf_op jit(solution)/shard_map/ppermute | solution.py:597
  551.7 3.8 convert_add_fusion.2
  560.1 5.3 add_convert_fusion
  567.0 19.9 %collective-permute-done.43 = bf16[256,1280]{1,0:T(8,128)(2,1)} collective-permute-done((bf16[256,1280]{1,0:T(8,128)(2,1)S(1)}, bf16[256,1280]{1,0:T(8,128)(2,1)}, u32[]{:S(2)}, u32[]{:S(2)}) %collective-permute-start.43) | collective-permute-done | bytes 655392 | tf_op jit(solution)/shard_map/ppermute | solution.py:606
  590.7 12.8 %collective-permute-done.39 = bf16[2,256,1280]{2,1,0:T(8,128)(2,1)} collective-permute-done((bf16[2,256,1280]{2,1,0:T(8,128)(2,1)S(1)}, bf16[2,256,1280]{2,1,0:T(8,128)(2,1)}, u32[]{:S(2)}, u32[]{:S(2)}) %collective-permute-start.39) | collective-permute-done | bytes 1310752 | tf_op jit(solution)/shard_map/ppermute | solution.py:593
  605.1 8.2 %fusion.8 = (f32[2048]{0:T(1024)S(1)}, f32[256]{0:T(256)S(1)}, f32[256,2048]{1,0:T(8,128)}) fusion(bf16[256,2048]{1,0:T(8,128)(2,1)S(1)} %copy-done.45, f32[256]{0:T(256)S(1)} %add_rsqrt_fusion.1, f32[2048]{0:T(1024)S(1)} %bitcast.217, bf16[256,2432]{1,0:T(8,128)(2,1)S(1)} %get-tuple-element.174, bf16[2048,2432]{1,0:T(8,128)(2,1)} %bitcast.196), kind=kOutput, calls=%fused_computation.34 | convolution fusion | flops 2553804544 | bytes 14370816 | tf_op jit(solution)/shard_map/dot_general | solution.py:28
  620.1 7.7 %fusion.31 = f32[1024,2048]{1,0:T(8,128)S(1)} fusion(bf16[1024,1280]{1,0:T(8,128)(2,1)S(1)} %copy-done.34, bf16[1280,2048]{1,0:T(8,128)(2,1)} %all-gather.5.cloned.1.call-done.down_ref), kind=kOutput, calls=%fused_computation.138 | convolution fusion | flops 5368709120 | bytes 16252928 | tf_op jit(solution)/shard_map/dot_general | solution.py:24
  633.4 11.5 %collective-permute-done.45 = bf16[4,64,2432]{2,1,0:T(8,128)(2,1)S(1)} collective-permute-done((bf16[4,64,2432]{2,1,0:T(8,128)(2,1)}, bf16[4,64,2432]{2,1,0:T(8,128)(2,1)S(1)}, u32[]{:S(2)}, u32[]{:S(2)}) %collective-permute-start.45) | collective-permute-done | bytes 1245216 | tf_op jit(solution)/shard_map/ppermute | solution.py:597
  648.8 23.7 %collective-permute-done.44 = bf16[2,256,1280]{2,1,0:T(8,128)(2,1)S(1)} collective-permute-done((bf16[2,256,1280]{2,1,0:T(8,128)(2,1)S(1)}, bf16[2,256,1280]{2,1,0:T(8,128)(2,1)S(1)}, u32[]{:S(2)}, u32[]{:S(2)}) %collective-permute-start.44) | collective-permute-done | bytes 1310752 | tf_op jit(solution)/shard_map/ppermute | solution.py:593
  672.9 7.0 collective-permute-done.46
  685.1 3.5 all-to-all-start
  688.6 3.2 fusion.12
  693.8 18.9 %collective-permute-done.53 = bf16[256,1280]{1,0:T(8,128)(2,1)} collective-permute-done((bf16[256,1280]{1,0:T(8,128)(2,1)}, bf16[256,1280]{1,0:T(8,128)(2,1)}, u32[]{:S(2)}, u32[]{:S(2)}) %collective-permute-start.53) | collective-permute-done | bytes 655392 | tf_op jit(solution)/shard_map/ppermute | solution.py:606
  715.0 2.6 add_convert_fusion.10
  717.6 3.7 collective-permute-done.54
  721.3 3.5 all-to-all-start.1
  728.1 3.0 collective-permute-start.60
  736.8 3.7 fusion.10
  742.1 3.5 collective-permute-done.60
  745.7 7.5 collective-permute-done.59
  753.9 5.2 collective-permute-start.61
  (367 shorter events, 147.2 us)
Async XLA Ops:
  7.2 328.8 %all-gather.3.cloned.1.call-start = ((), (), s32[]{:S(2)}) async-start(), calls=%async_computation.2 | async-start | bytes 11796480 | tf_op jit(solution)/shard_map/all_gather | solution.py:696
  9.1 19.9 %collective-permute-start.2 = (bf16[64,2432]{1,0:T(8,128)(2,1)S(1)}, bf16[64,2432]{1,0:T(8,128)(2,1)S(1)}, u32[]{:S(2)}, u32[]{:S(2)}) collective-permute-start(bf16[64,2432]{1,0:T(8,128)(2,1)S(1)} %get-tuple-element.194), channel_id=1, source_target_pairs={{0,16},{4,20},{8,24},{12,28},{16,0},{20,4},{24,8},{28,12},{1,17},{... | collective-permute-start | bytes 933896 | tf_op jit(solution)/shard_map/ppermute | solution.py:527
  13.2 15.8 %collective-permute-start.1 = (bf16[64,2432]{1,0:T(8,128)(2,1)S(1)}, bf16[64,2432]{1,0:T(8,128)(2,1)S(1)}, u32[]{:S(2)}, u32[]{:S(2)}) collective-permute-start(bf16[64,2432]{1,0:T(8,128)(2,1)S(1)} %get-tuple-element.194), channel_id=1, source_target_pairs={{0,24},{4,28},{8,0},{12,4},{16,8},{20,12},{24,16},{28,20},{1,25},{... | collective-permute-start | bytes 933896 | tf_op jit(solution)/shard_map/ppermute | solution.py:527
  14.5 20.7 %collective-permute-start = (bf16[64,2432]{1,0:T(8,128)(2,1)S(1)}, bf16[64,2432]{1,0:T(8,128)(2,1)}, u32[]{:S(2)}, u32[]{:S(2)}) collective-permute-start(bf16[64,2432]{1,0:T(8,128)(2,1)S(1)} %get-tuple-element.194), channel_id=1, source_target_pairs={{0,8},{4,12},{8,16},{12,20},{16,24},{20,28},{24,0},{28,4},{1,9},{5... | collective-permute-start | bytes 933896 | tf_op jit(solution)/shard_map/ppermute | solution.py:527
  36.3 28.3 %collective-permute-start.3 = (bf16[4,64,2432]{2,1,0:T(8,128)(2,1)S(1)}, bf16[4,64,2432]{2,1,0:T(8,128)(2,1)S(1)}, u32[]{:S(2)}, u32[]{:S(2)}) collective-permute-start(bf16[4,64,2432]{2,1,0:T(8,128)(2,1)S(1)} %pad_maximum_fusion.1), channel_id=1, source_target_pairs={{0,4},{4,0},{8,12},{12,8},{16,20},{20,16},{24,28},{28,24},{1,5},{5... | collective-permute-start | bytes 3735560 | tf_op jit(solution)/shard_map/ppermute | solution.py:593
  66.9 14.7 %collective-permute-start.19 = (bf16[2,64,2560]{2,1,0:T(8,128)(2,1)S(1)}, bf16[2,64,2560]{2,1,0:T(8,128)(2,1)S(1)}, u32[]{:S(2)}, u32[]{:S(2)}) collective-permute-start(bf16[2,64,2560]{2,1,0:T(8,128)(2,1)S(1)} %pad_maximum_fusion.3), channel_id=1, source_target_pairs={{0,2},{1,3},{2,0},{3,1},{4,6},{5,7},{6,4},{7,5},{8,10},{9,11},{10,... | collective-permute-start | bytes 1966088 | tf_op jit(solution)/shard_map/ppermute | solution.py:597
  86.2 281.6 %all-gather.5.cloned.1.call-start = ((), (), s32[]{:S(2)}) async-start(), calls=%async_computation.3 | async-start | bytes 5898240 | tf_op jit(solution)/shard_map/all_gather | solution.py:695
  86.2 56.3 %collective-permute-start.4 = (bf16[8,64,2432]{2,1,0:T(8,128)(2,1)S(1)}, bf16[8,64,2432]{2,1,0:T(8,128)(2,1)}, u32[]{:S(2)}, u32[]{:S(2)}) collective-permute-start(bf16[8,64,2432]{2,1,0:T(8,128)(2,1)S(1)} %constant_dynamic-update-slice_fusion.refs_0_), channel_id=1, source_target_pairs={{0,2},{1,3},{2,0},{3,1},{4,6},{5,7},{6,4},{7,5},{8,10},{9,11},{10,... | collective-permute-start | bytes 7471112 | tf_op jit(solution)/shard_map/ppermute | solution.py:597
  91.7 128.2 %collective-permute-start.5 = (bf16[8,64,2432]{2,1,0:T(8,128)(2,1)S(1)}, bf16[8,64,2432]{2,1,0:T(8,128)(2,1)}, u32[]{:S(2)}, u32[]{:S(2)}) collective-permute-start(bf16[8,64,2432]{2,1,0:T(8,128)(2,1)S(1)} %constant_dynamic-update-slice_fusion.refs_0_), channel_id=1, source_target_pairs={{0,1},{1,0},{2,3},{3,2},{4,5},{5,4},{6,7},{7,6},{8,9},{9,8},{10,11... | collective-permute-start | bytes 7471112 | tf_op jit(solution)/shard_map/ppermute | solution.py:597
  142.5 77.4 %collective-permute-start.6 = (bf16[8,64,2432]{2,1,0:T(8,128)(2,1)}, bf16[8,64,2432]{2,1,0:T(8,128)(2,1)}, u32[]{:S(2)}, u32[]{:S(2)}) collective-permute-start(bf16[8,64,2432]{2,1,0:T(8,128)(2,1)} %collective-permute-done.4.refs_1_), channel_id=1, source_target_pairs={{0,1},{1,0},{2,3},{3,2},{4,5},{5,4},{6,7},{7,6},{8,9},{9,8},{10,11... | collective-permute-start | bytes 7471112 | tf_op jit(solution)/shard_map/ppermute | solution.py:597
  143.6 36.0 %collective-permute-start.11 = (bf16[48,2048]{1,0:T(8,128)(2,1)}, bf16[48,2048]{1,0:T(8,128)(2,1)S(1)}, u32[]{:S(2)}, u32[]{:S(2)}) collective-permute-start(bf16[48,2048]{1,0:T(8,128)(2,1)} %param.24), channel_id=1, source_target_pairs={{0,16},{4,20},{8,24},{12,28},{16,0},{20,4},{24,8},{28,12},{1,17},{... | collective-permute-start | bytes 589832 | tf_op jit(solution)/shard_map/ppermute | solution.py:527
  154.0 25.6 %collective-permute-start.10 = (bf16[48,2048]{1,0:T(8,128)(2,1)}, bf16[48,2048]{1,0:T(8,128)(2,1)S(1)}, u32[]{:S(2)}, u32[]{:S(2)}) collective-permute-start(bf16[48,2048]{1,0:T(8,128)(2,1)} %param.24), channel_id=1, source_target_pairs={{0,24},{4,28},{8,0},{12,4},{16,8},{20,12},{24,16},{28,20},{1,25},{... | collective-permute-start | bytes 589832 | tf_op jit(solution)/shard_map/ppermute | solution.py:527
  154.3 25.8 %collective-permute-start.9 = (bf16[48,2048]{1,0:T(8,128)(2,1)}, bf16[48,2048]{1,0:T(8,128)(2,1)S(1)}, u32[]{:S(2)}, u32[]{:S(2)}) collective-permute-start(bf16[48,2048]{1,0:T(8,128)(2,1)} %param.24), channel_id=1, source_target_pairs={{0,8},{4,12},{8,16},{12,20},{16,24},{20,28},{24,0},{28,4},{1,9},{5... | collective-permute-start | bytes 589832 | tf_op jit(solution)/shard_map/ppermute | solution.py:527
  181.2 37.0 %collective-permute-start.12 = (bf16[4,48,2048]{2,1,0:T(8,128)(2,1)S(1)}, bf16[4,48,2048]{2,1,0:T(8,128)(2,1)S(1)}, u32[]{:S(2)}, u32[]{:S(2)}) collective-permute-start(bf16[4,48,2048]{2,1,0:T(8,128)(2,1)S(1)} %pad_maximum_fusion.2), channel_id=1, source_target_pairs={{0,4},{4,0},{8,12},{12,8},{16,20},{20,16},{24,28},{28,24},{1,5},{5... | collective-permute-start | bytes 2359304 | tf_op jit(solution)/shard_map/ppermute | solution.py:593
  218.2 36.5 %collective-permute-start.13 = (bf16[8,48,2048]{2,1,0:T(8,128)(2,1)S(1)}, bf16[8,48,2048]{2,1,0:T(8,128)(2,1)S(1)}, u32[]{:S(2)}, u32[]{:S(2)}) collective-permute-start(bf16[8,48,2048]{2,1,0:T(8,128)(2,1)S(1)} %constant_dynamic-update-slice_fusion.5.refs_0_), channel_id=1, source_target_pairs={{0,2},{1,3},{2,0},{3,1},{4,6},{5,7},{6,4},{7,5},{8,10},{9,11},{10,... | collective-permute-start | bytes 4718600 | tf_op jit(solution)/shard_map/ppermute | solution.py:597
  237.8 16.9 %collective-permute-start.8 = (bf16[2,256,384]{2,1,0:T(8,128)(2,1)S(1)}, bf16[2,256,384]{2,1,0:T(8,128)(2,1)S(1)}, u32[]{:S(2)}, u32[]{:S(2)}) collective-permute-start(bf16[2,256,384]{2,1,0:T(8,128)(2,1)S(1)} %get-tuple-element.102.kv_ref), channel_id=1, source_target_pairs={{0,1},{1,2},{2,3},{4,5},{5,6},{6,7},{8,9},{9,10},{10,11},{12,13},{... | collective-permute-start | bytes 1179656 | tf_op jit(solution)/shard_map/ppermute | solution.py:712
  254.8 28.8 %collective-permute-start.14 = (bf16[8,48,2048]{2,1,0:T(8,128)(2,1)S(1)}, bf16[8,48,2048]{2,1,0:T(8,128)(2,1)S(1)}, u32[]{:S(2)}, u32[]{:S(2)}) collective-permute-start(bf16[8,48,2048]{2,1,0:T(8,128)(2,1)S(1)} %constant_dynamic-update-slice_fusion.5.refs_0_), channel_id=1, source_target_pairs={{0,1},{1,0},{2,3},{3,2},{4,5},{5,4},{6,7},{7,6},{8,9},{9,8},{10,11... | collective-permute-start | bytes 4718600 | tf_op jit(solution)/shard_map/ppermute | solution.py:597
  257.4 26.3 %collective-permute-start.15 = (bf16[8,48,2048]{2,1,0:T(8,128)(2,1)S(1)}, bf16[8,48,2048]{2,1,0:T(8,128)(2,1)S(1)}, u32[]{:S(2)}, u32[]{:S(2)}) collective-permute-start(bf16[8,48,2048]{2,1,0:T(8,128)(2,1)S(1)} %collective-permute-done.13.refs_1_), channel_id=1, source_target_pairs={{0,1},{1,0},{2,3},{3,2},{4,5},{5,4},{6,7},{7,6},{8,9},{9,8},{10,11... | collective-permute-start | bytes 4718600 | tf_op jit(solution)/shard_map/ppermute | solution.py:597
  257.4 14.3 %collective-permute-start.7 = (bf16[2,256,384]{2,1,0:T(8,128)(2,1)S(1)}, bf16[2,256,384]{2,1,0:T(8,128)(2,1)S(1)}, u32[]{:S(2)}, u32[]{:S(2)}) collective-permute-start(bf16[2,256,384]{2,1,0:T(8,128)(2,1)S(1)} %get-tuple-element.102.kv_ref), channel_id=1, source_target_pairs={{0,2},{1,3},{4,6},{5,7},{8,10},{9,11},{12,14},{13,15},{16,18},{17,... | collective-permute-start | bytes 1179656 | tf_op jit(solution)/shard_map/ppermute | solution.py:713
  262.3 42.2 %collective-permute-start.22 = (bf16[256,2048]{1,0:T(8,128)(2,1)}, bf16[256,2048]{1,0:T(8,128)(2,1)}, u32[]{:S(2)}, u32[]{:S(2)}) collective-permute-start(bf16[256,2048]{1,0:T(8,128)(2,1)} %param.16), channel_id=1, source_target_pairs={{0,2},{1,3},{2,0},{3,1},{4,6},{5,7},{6,4},{7,5},{8,10},{9,11},{10,... | collective-permute-start | bytes 3145736 | tf_op jit(solution)/shard_map/ppermute | solution.py:597
  302.0 24.2 %collective-permute-start.17 = (bf16[256,2048]{1,0:T(8,128)(2,1)S(1)}, bf16[256,2048]{1,0:T(8,128)(2,1)}, u32[]{:S(2)}, u32[]{:S(2)}) collective-permute-start(bf16[256,2048]{1,0:T(8,128)(2,1)S(1)} %multiply_convert_fusion), channel_id=1, source_target_pairs={{0,2},{1,3},{2,0},{3,1},{4,6},{5,7},{6,4},{7,5},{8,10},{9,11},{10,... | collective-permute-start | bytes 3145736 | tf_op jit(solution)/shard_map/ppermute | solution.py:597
  304.6 23.1 %collective-permute-start.21 = (bf16[256,2048]{1,0:T(8,128)(2,1)}, bf16[256,2048]{1,0:T(8,128)(2,1)}, u32[]{:S(2)}, u32[]{:S(2)}) collective-permute-start(bf16[256,2048]{1,0:T(8,128)(2,1)} %param.16), channel_id=1, source_target_pairs={{0,1},{1,0},{2,3},{3,2},{4,5},{5,4},{6,7},{7,6},{8,9},{9,8},{10,11... | collective-permute-start | bytes 3145736 | tf_op jit(solution)/shard_map/ppermute | solution.py:597
  304.6 25.7 %collective-permute-start.23 = (bf16[256,2048]{1,0:T(8,128)(2,1)}, bf16[256,2048]{1,0:T(8,128)(2,1)S(1)}, u32[]{:S(2)}, u32[]{:S(2)}) collective-permute-start(bf16[256,2048]{1,0:T(8,128)(2,1)} %collective-permute-done.22), channel_id=1, source_target_pairs={{0,1},{1,0},{2,3},{3,2},{4,5},{5,4},{6,7},{7,6},{8,9},{9,8},{10,11... | collective-permute-start | bytes 3145736 | tf_op jit(solution)/shard_map/ppermute | solution.py:597
  305.1 25.3 %collective-permute-start.16 = (bf16[256,2048]{1,0:T(8,128)(2,1)S(1)}, bf16[256,2048]{1,0:T(8,128)(2,1)}, u32[]{:S(2)}, u32[]{:S(2)}) collective-permute-start(bf16[256,2048]{1,0:T(8,128)(2,1)S(1)} %multiply_convert_fusion), channel_id=1, source_target_pairs={{0,1},{1,0},{2,3},{3,2},{4,5},{5,4},{6,7},{7,6},{8,9},{9,8},{10,11... | collective-permute-start | bytes 3145736 | tf_op jit(solution)/shard_map/ppermute | solution.py:597
  326.2 6.2 collective-permute-start.18
  367.8 31.4 %collective-permute-start.24 = (bf16[2,160,2048]{2,1,0:T(8,128)(2,1)}, bf16[2,160,2048]{2,1,0:T(8,128)(2,1)S(1)}, u32[]{:S(2)}, u32[]{:S(2)}) collective-permute-start(bf16[2,160,2048]{2,1,0:T(8,128)(2,1)} %copy-done.29), channel_id=1, source_target_pairs={{0,4},{4,0},{8,12},{12,8},{16,20},{20,16},{24,28},{28,24},{1,5},{5... | collective-permute-start | bytes 3932168 | tf_op jit(solution)/shard_map/ppermute | solution.py:593
  399.7 24.3 %collective-permute-start.26 = (bf16[2,256,2048]{2,1,0:T(8,128)(2,1)S(1)}, bf16[2,256,2048]{2,1,0:T(8,128)(2,1)S(1)}, u32[]{:S(2)}, u32[]{:S(2)}) collective-permute-start(bf16[2,256,2048]{2,1,0:T(8,128)(2,1)S(1)} %get-tuple-element.136), channel_id=1, source_target_pairs={{0,1},{1,0},{2,3},{3,2},{4,5},{5,4},{6,7},{7,6},{8,9},{9,8},{10,11... | collective-permute-start | bytes 6291464 | tf_op jit(solution)/shard_map/ppermute | solution.py:597
  401.0 47.9 %collective-permute-start.29 = (bf16[160,2048]{1,0:T(8,128)(2,1)}, bf16[160,2048]{1,0:T(8,128)(2,1)}, u32[]{:S(2)}, u32[]{:S(2)}) collective-permute-start(bf16[160,2048]{1,0:T(8,128)(2,1)} %get-tuple-element.205), channel_id=1, source_target_pairs={{0,24},{4,28},{8,0},{12,4},{16,8},{20,12},{24,16},{28,20},{1,25},{... | collective-permute-start | bytes 1966088 | tf_op jit(solution)/shard_map/ppermute | solution.py:606
  401.0 47.9 %collective-permute-start.28 = (bf16[160,2048]{1,0:T(8,128)(2,1)}, bf16[160,2048]{1,0:T(8,128)(2,1)}, u32[]{:S(2)}, u32[]{:S(2)}) collective-permute-start(bf16[160,2048]{1,0:T(8,128)(2,1)} %get-tuple-element.206), channel_id=1, source_target_pairs={{0,8},{4,12},{8,16},{12,20},{16,24},{20,28},{24,0},{28,4},{1,9},{5... | collective-permute-start | bytes 1966088 | tf_op jit(solution)/shard_map/ppermute | solution.py:606
  414.5 31.6 %collective-permute-start.25 = (bf16[2,160,2048]{2,1,0:T(8,128)(2,1)S(1)}, bf16[2,160,2048]{2,1,0:T(8,128)(2,1)}, u32[]{:S(2)}, u32[]{:S(2)}) collective-permute-start(bf16[2,160,2048]{2,1,0:T(8,128)(2,1)S(1)} %copy-done.28), channel_id=1, source_target_pairs={{0,4},{4,0},{8,12},{12,8},{16,20},{20,16},{24,28},{28,24},{1,5},{5... | collective-permute-start | bytes 3932168 | tf_op jit(solution)/shard_map/ppermute | solution.py:593
  425.7 25.2 %collective-permute-start.27 = (bf16[256,2048]{1,0:T(8,128)(2,1)}, bf16[256,2048]{1,0:T(8,128)(2,1)S(1)}, u32[]{:S(2)}, u32[]{:S(2)}) collective-permute-start(bf16[256,2048]{1,0:T(8,128)(2,1)} %fusion.11), channel_id=1, source_target_pairs={{0,2},{1,3},{2,0},{3,1},{4,6},{5,7},{6,4},{7,5},{8,10},{9,11},{10,... | collective-permute-start | bytes 3145736 | tf_op jit(solution)/shard_map/ppermute | solution.py:597
  456.9 38.2 %collective-permute-start.30 = (bf16[2,256,1280]{2,1,0:T(8,128)(2,1)}, bf16[2,256,1280]{2,1,0:T(8,128)(2,1)}, u32[]{:S(2)}, u32[]{:S(2)}) collective-permute-start(bf16[2,256,1280]{2,1,0:T(8,128)(2,1)} %get-tuple-element.140), channel_id=1, source_target_pairs={{0,4},{4,0},{8,12},{12,8},{16,20},{20,16},{24,28},{28,24},{1,5},{5... | collective-permute-start | bytes 3932168 | tf_op jit(solution)/shard_map/ppermute | solution.py:593
  459.5 37.3 %collective-permute-start.31 = (bf16[160,2048]{1,0:T(8,128)(2,1)}, bf16[160,2048]{1,0:T(8,128)(2,1)}, u32[]{:S(2)}, u32[]{:S(2)}) collective-permute-start(bf16[160,2048]{1,0:T(8,128)(2,1)} %get-tuple-element.204), channel_id=1, source_target_pairs={{0,16},{4,20},{8,24},{12,28},{16,0},{20,4},{24,8},{28,12},{1,17},{... | collective-permute-start | bytes 1966088 | tf_op jit(solution)/shard_map/ppermute | solution.py:606
  497.4 5.7 collective-permute-start.35
  497.4 21.4 %collective-permute-start.33 = (bf16[2,256,384]{2,1,0:T(8,128)(2,1)S(1)}, bf16[2,256,384]{2,1,0:T(8,128)(2,1)S(1)}, u32[]{:S(2)}, u32[]{:S(2)}) collective-permute-start(bf16[2,256,384]{2,1,0:T(8,128)(2,1)S(1)} %get-tuple-element.154), channel_id=1, source_target_pairs={{1,0},{2,1},{3,2},{5,4},{6,5},{7,6},{9,8},{10,9},{11,10},{13,12},{... | collective-permute-start | bytes 1179656 | tf_op jit(solution)/shard_map/ppermute | solution.py:776
  498.6 16.9 %collective-permute-start.34 = (bf16[2,256,384]{2,1,0:T(8,128)(2,1)S(1)}, bf16[2,256,384]{2,1,0:T(8,128)(2,1)S(1)}, u32[]{:S(2)}, u32[]{:S(2)}) collective-permute-start(bf16[2,256,384]{2,1,0:T(8,128)(2,1)S(1)} %get-tuple-element.155), channel_id=1, source_target_pairs={{2,0},{3,1},{6,4},{7,5},{10,8},{11,9},{14,12},{15,13},{18,16},{19,... | collective-permute-start | bytes 1179656 | tf_op jit(solution)/shard_map/ppermute | solution.py:777
  500.0 37.0 %collective-permute-start.32 = (bf16[2,256,1280]{2,1,0:T(8,128)(2,1)S(1)}, bf16[2,256,1280]{2,1,0:T(8,128)(2,1)}, u32[]{:S(2)}, u32[]{:S(2)}) collective-permute-start(bf16[2,256,1280]{2,1,0:T(8,128)(2,1)S(1)} %copy-done.26), channel_id=1, source_target_pairs={{0,4},{4,0},{8,12},{12,8},{16,20},{20,16},{24,28},{28,24},{1,5},{5... | collective-permute-start | bytes 3932168 | tf_op jit(solution)/shard_map/ppermute | solution.py:593
  515.6 34.0 %collective-permute-start.36 = (bf16[8,48,2048]{2,1,0:T(8,128)(2,1)}, bf16[8,48,2048]{2,1,0:T(8,128)(2,1)}, u32[]{:S(2)}, u32[]{:S(2)}) collective-permute-start(bf16[8,48,2048]{2,1,0:T(8,128)(2,1)} %slice.223), channel_id=1, source_target_pairs={{0,2},{1,3},{2,0},{3,1},{4,6},{5,7},{6,4},{7,5},{8,10},{9,11},{10,... | collective-permute-start | bytes 4718600 | tf_op jit(solution)/shard_map/ppermute | solution.py:597
  516.7 34.9 %collective-permute-start.38 = (bf16[256,1280]{1,0:T(8,128)(2,1)}, bf16[256,1280]{1,0:T(8,128)(2,1)S(1)}, u32[]{:S(2)}, u32[]{:S(2)}) collective-permute-start(bf16[256,1280]{1,0:T(8,128)(2,1)} %get-tuple-element.201), channel_id=1, source_target_pairs={{0,24},{4,28},{8,0},{12,4},{16,8},{20,12},{24,16},{28,20},{1,25},{... | collective-permute-start | bytes 1966088 | tf_op jit(solution)/shard_map/ppermute | solution.py:606
  518.6 33.0 %collective-permute-start.37 = (bf16[256,1280]{1,0:T(8,128)(2,1)}, bf16[256,1280]{1,0:T(8,128)(2,1)S(1)}, u32[]{:S(2)}, u32[]{:S(2)}) collective-permute-start(bf16[256,1280]{1,0:T(8,128)(2,1)} %get-tuple-element.202), channel_id=1, source_target_pairs={{0,8},{4,12},{8,16},{12,20},{16,24},{20,28},{24,0},{28,4},{1,9},{5... | collective-permute-start | bytes 1966088 | tf_op jit(solution)/shard_map/ppermute | solution.py:606
  551.7 8.5 %collective-permute-start.40 = (bf16[16,64,2432]{2,1,0:T(8,128)(2,1)S(1)}, bf16[16,64,2432]{2,1,0:T(8,128)(2,1)}, u32[]{:S(2)}, u32[]{:S(2)}) collective-permute-start(bf16[16,64,2432]{2,1,0:T(8,128)(2,1)S(1)} %get-tuple-element.165), channel_id=1, source_target_pairs={{0,1},{1,0},{2,3},{3,2},{4,5},{5,4},{6,7},{7,6},{8,9},{9,8},{10,11... | collective-permute-start | bytes 14942216 | tf_op jit(solution)/shard_map/ppermute | solution.py:597
  555.6 31.3 %collective-permute-start.43 = (bf16[256,1280]{1,0:T(8,128)(2,1)S(1)}, bf16[256,1280]{1,0:T(8,128)(2,1)}, u32[]{:S(2)}, u32[]{:S(2)}) collective-permute-start(bf16[256,1280]{1,0:T(8,128)(2,1)S(1)} %slice_bitcast_fusion.6), channel_id=1, source_target_pairs={{0,16},{4,20},{8,24},{12,28},{16,0},{20,4},{24,8},{28,12},{1,17},{... | collective-permute-start | bytes 1966088 | tf_op jit(solution)/shard_map/ppermute | solution.py:606
  556.5 32.7 %collective-permute-start.41 = (bf16[4,48,2048]{2,1,0:T(8,128)(2,1)S(1)}, bf16[4,48,2048]{2,1,0:T(8,128)(2,1)}, u32[]{:S(2)}, u32[]{:S(2)}) collective-permute-start(bf16[4,48,2048]{2,1,0:T(8,128)(2,1)S(1)} %slice.182), channel_id=1, source_target_pairs={{0,4},{4,0},{8,12},{12,8},{16,20},{20,16},{24,28},{28,24},{1,5},{5... | collective-permute-start | bytes 2359304 | tf_op jit(solution)/shard_map/ppermute | solution.py:593
  557.3 46.2 %collective-permute-start.39 = (bf16[2,256,1280]{2,1,0:T(8,128)(2,1)S(1)}, bf16[2,256,1280]{2,1,0:T(8,128)(2,1)}, u32[]{:S(2)}, u32[]{:S(2)}) collective-permute-start(bf16[2,256,1280]{2,1,0:T(8,128)(2,1)S(1)} %copy-done.24), channel_id=1, source_target_pairs={{0,4},{4,0},{8,12},{12,8},{16,20},{20,16},{24,28},{28,24},{1,5},{5... | collective-permute-start | bytes 3932168 | tf_op jit(solution)/shard_map/ppermute | solution.py:593
  566.7 38.4 %collective-permute-start.42 = (bf16[4,64,2432]{2,1,0:T(8,128)(2,1)S(1)}, bf16[4,64,2432]{2,1,0:T(8,128)(2,1)}, u32[]{:S(2)}, u32[]{:S(2)}) collective-permute-start(bf16[4,64,2432]{2,1,0:T(8,128)(2,1)S(1)} %get-tuple-element.195), channel_id=1, source_target_pairs={{0,2},{1,3},{2,0},{3,1},{4,6},{5,7},{6,4},{7,5},{8,10},{9,11},{10,... | collective-permute-start | bytes 3735560 | tf_op jit(solution)/shard_map/ppermute | solution.py:597
  613.4 59.5 %collective-permute-start.48 = (bf16[48,2048]{1,0:T(8,128)(2,1)S(1)}, bf16[48,2048]{1,0:T(8,128)(2,1)S(1)}, u32[]{:S(2)}, u32[]{:S(2)}) collective-permute-start(bf16[48,2048]{1,0:T(8,128)(2,1)S(1)} %get-tuple-element.214), channel_id=1, source_target_pairs={{0,16},{4,20},{8,24},{12,28},{16,0},{20,4},{24,8},{28,12},{1,17},{... | collective-permute-start | bytes 589832 | tf_op jit(solution)/shard_map/ppermute | solution.py:606
  615.7 57.2 %collective-permute-start.47 = (bf16[48,2048]{1,0:T(8,128)(2,1)S(1)}, bf16[48,2048]{1,0:T(8,128)(2,1)S(1)}, u32[]{:S(2)}, u32[]{:S(2)}) collective-permute-start(bf16[48,2048]{1,0:T(8,128)(2,1)S(1)} %get-tuple-element.215), channel_id=1, source_target_pairs={{0,24},{4,28},{8,0},{12,4},{16,8},{20,12},{24,16},{28,20},{1,25},{... | collective-permute-start | bytes 589832 | tf_op jit(solution)/shard_map/ppermute | solution.py:606
  617.6 27.3 %collective-permute-start.45 = (bf16[4,64,2432]{2,1,0:T(8,128)(2,1)}, bf16[4,64,2432]{2,1,0:T(8,128)(2,1)S(1)}, u32[]{:S(2)}, u32[]{:S(2)}) collective-permute-start(bf16[4,64,2432]{2,1,0:T(8,128)(2,1)} %get-tuple-element.170), channel_id=1, source_target_pairs={{0,2},{1,3},{2,0},{3,1},{4,6},{5,7},{6,4},{7,5},{8,10},{9,11},{10,... | collective-permute-start | bytes 3735560 | tf_op jit(solution)/shard_map/ppermute | solution.py:597
  618.0 62.0 %collective-permute-start.50 = (bf16[256,1280]{1,0:T(8,128)(2,1)S(1)}, bf16[256,1280]{1,0:T(8,128)(2,1)S(1)}, u32[]{:S(2)}, u32[]{:S(2)}) collective-permute-start(bf16[256,1280]{1,0:T(8,128)(2,1)S(1)} %get-tuple-element.199), channel_id=1, source_target_pairs={{0,24},{4,28},{8,0},{12,4},{16,8},{20,12},{24,16},{28,20},{1,25},{... | collective-permute-start | bytes 1966088 | tf_op jit(solution)/shard_map/ppermute | solution.py:606
  618.3 61.7 %collective-permute-start.49 = (bf16[256,1280]{1,0:T(8,128)(2,1)S(1)}, bf16[256,1280]{1,0:T(8,128)(2,1)S(1)}, u32[]{:S(2)}, u32[]{:S(2)}) collective-permute-start(bf16[256,1280]{1,0:T(8,128)(2,1)S(1)} %get-tuple-element.200), channel_id=1, source_target_pairs={{0,8},{4,12},{8,16},{12,20},{16,24},{20,28},{24,0},{28,4},{1,9},{5... | collective-permute-start | bytes 1966088 | tf_op jit(solution)/shard_map/ppermute | solution.py:606
  644.9 27.6 %collective-permute-start.44 = (bf16[2,256,1280]{2,1,0:T(8,128)(2,1)S(1)}, bf16[2,256,1280]{2,1,0:T(8,128)(2,1)S(1)}, u32[]{:S(2)}, u32[]{:S(2)}) collective-permute-start(bf16[2,256,1280]{2,1,0:T(8,128)(2,1)S(1)} %copy-done.22), channel_id=1, source_target_pairs={{0,4},{4,0},{8,12},{12,8},{16,20},{20,16},{24,28},{28,24},{1,5},{5... | collective-permute-start | bytes 3932168 | tf_op jit(solution)/shard_map/ppermute | solution.py:593
  672.5 7.5 collective-permute-start.46
  681.6 6.9 collective-permute-start.51
  682.6 30.1 %collective-permute-start.53 = (bf16[256,1280]{1,0:T(8,128)(2,1)}, bf16[256,1280]{1,0:T(8,128)(2,1)}, u32[]{:S(2)}, u32[]{:S(2)}) collective-permute-start(bf16[256,1280]{1,0:T(8,128)(2,1)} %slice_bitcast_fusion.2), channel_id=1, source_target_pairs={{0,16},{4,20},{8,24},{12,28},{16,0},{20,4},{24,8},{28,12},{1,17},{... | collective-permute-start | bytes 1966088 | tf_op jit(solution)/shard_map/ppermute | solution.py:606
  682.6 32.4 %collective-permute-start.52 = (bf16[4,64,2432]{2,1,0:T(8,128)(2,1)}, bf16[4,64,2432]{2,1,0:T(8,128)(2,1)}, u32[]{:S(2)}, u32[]{:S(2)}) collective-permute-start(bf16[4,64,2432]{2,1,0:T(8,128)(2,1)} %get-tuple-element.179), channel_id=1, source_target_pairs={{0,4},{4,0},{8,12},{12,8},{16,20},{20,16},{24,28},{28,24},{1,5},{5... | collective-permute-start | bytes 3735560 | tf_op jit(solution)/shard_map/ppermute | solution.py:593
  685.1 32.6 %all-to-all-start = ((bf16[4,64,1280]{2,1,0:T(8,128)(2,1)}), bf16[4,64,1280]{2,1,0:T(8,128)(2,1)S(1)}, u32[]{:S(2)}, u32[]{:S(2)}) async-start(bf16[4,64,1280]{2,1,0:T(8,128)(2,1)} %bitcast.206), calls=%async_computation | async-start | bytes 1310720 | tf_op jit(solution)/shard_map/all_to_all | solution.py:834
  691.8 29.5 %collective-permute-start.54 = (bf16[256,2048]{1,0:T(8,128)(2,1)}, bf16[256,2048]{1,0:T(8,128)(2,1)}, u32[]{:S(2)}, u32[]{:S(2)}) collective-permute-start(bf16[256,2048]{1,0:T(8,128)(2,1)} %fusion.12), channel_id=1, source_target_pairs={{0,2},{1,3},{2,0},{3,1},{4,6},{5,7},{6,4},{7,5},{8,10},{9,11},{10,... | collective-permute-start | bytes 3145736 | tf_op jit(solution)/shard_map/ppermute | solution.py:597
  721.3 32.6 %all-to-all-start.1 = ((bf16[4,64,1280]{2,1,0:T(8,128)(2,1)}), bf16[4,64,1280]{2,1,0:T(8,128)(2,1)S(1)}, u32[]{:S(2)}, u32[]{:S(2)}) async-start(bf16[4,64,1280]{2,1,0:T(8,128)(2,1)} %bitcast.207), calls=%async_computation.1 | async-start | bytes 1310720 | tf_op jit(solution)/shard_map/all_to_all | solution.py:842
  724.9 10.6 %collective-permute-start.56 = (f32[40,128]{1,0:T(8,128)S(1)}, f32[40,128]{1,0:T(8,128)S(1)}, u32[]{:S(2)}, u32[]{:S(2)}) collective-permute-start(f32[40,128]{1,0:T(8,128)S(1)} %add.1361), channel_id=1, source_target_pairs={{0,2},{1,3},{2,0},{3,1},{4,6},{5,7},{6,4},{7,5},{8,10},{9,11},{10,... | collective-permute-start | bytes 61448 | tf_op jit(solution)/shard_map/ppermute | solution.py:634
  728.1 17.5 %collective-permute-start.60 = (bf16[64,2432]{1,0:T(8,128)(2,1)S(1)}, bf16[64,2432]{1,0:T(8,128)(2,1)S(1)}, u32[]{:S(2)}, u32[]{:S(2)}) collective-permute-start(bf16[64,2432]{1,0:T(8,128)(2,1)S(1)} %get-tuple-element.211), channel_id=1, source_target_pairs={{0,16},{4,20},{8,24},{12,28},{16,0},{20,4},{24,8},{28,12},{1,17},{... | collective-permute-start | bytes 933896 | tf_op jit(solution)/shard_map/ppermute | solution.py:606
  731.1 22.1 %collective-permute-start.59 = (bf16[64,2432]{1,0:T(8,128)(2,1)S(1)}, bf16[64,2432]{1,0:T(8,128)(2,1)S(1)}, u32[]{:S(2)}, u32[]{:S(2)}) collective-permute-start(bf16[64,2432]{1,0:T(8,128)(2,1)S(1)} %get-tuple-element.212), channel_id=1, source_target_pairs={{0,24},{4,28},{8,0},{12,4},{16,8},{20,12},{24,16},{28,20},{1,25},{... | collective-permute-start | bytes 933896 | tf_op jit(solution)/shard_map/ppermute | solution.py:606
  731.1 22.8 %collective-permute-start.58 = (bf16[64,2432]{1,0:T(8,128)(2,1)S(1)}, bf16[64,2432]{1,0:T(8,128)(2,1)}, u32[]{:S(2)}, u32[]{:S(2)}) collective-permute-start(bf16[64,2432]{1,0:T(8,128)(2,1)S(1)} %get-tuple-element.213), channel_id=1, source_target_pairs={{0,8},{4,12},{8,16},{12,20},{16,24},{20,28},{24,0},{28,4},{1,9},{5... | collective-permute-start | bytes 933896 | tf_op jit(solution)/shard_map/ppermute | solution.py:606
  735.5 6.6 collective-permute-start.57
  753.9 6.9 collective-permute-start.61
  (85 other events, 1156.6 us)
Sparse Core Ops, SparseCore 0:
  86.3 175.5 all-gather.2
  264.6 84.6 all-gather.4

commit v3 on v2

--- a/solution.py
+++ b/solution.py
@@ -227,32 +227,35 @@
     )(q, two, one, kv, rel, gm)
 
 
-def feed_kernel(x_ref, gate_ref, up_ref, act_ref, gate_slope_ref, up_slope_ref):
-    x = x_ref[...]
-    gate, up = product(x, gate_ref[...]), product(x, up_ref[...])
+def feed_kernel(x_ref, both_ref, act_ref, slopes_ref):
+    units = act_ref.shape[1]
+    mixed = product(x_ref[...], both_ref[...])
+    gate, up = mixed[:, :units], mixed[:, units:]
     sig = 1.0 / (1.0 + jnp.exp(-gate))
     silu = gate * sig
     act_ref[...] = (silu * up).astype(BF16)
-    gate_slope_ref[...] = (up * sig * (1.0 + gate * (1.0 - sig))).astype(BF16)
-    up_slope_ref[...] = silu.astype(BF16)
-
-
-def feed(x, both):
+    slopes_ref[:, :units] = (up * sig * (1.0 + gate * (1.0 - sig))).astype(BF16)
+    slopes_ref[:, units:] = silu.astype(BF16)
+
+
+def feed(x, both, tile):
     rows, width = x.shape
     units = both.shape[1] // 2
-    tile = 2 * LANES
-    steps = units // tile
-    out = pl.BlockSpec((rows, tile), lambda j: (0, j))
     return pl.pallas_call(
         feed_kernel,
-        grid=(steps,),
+        grid=(rows // tile,),
         in_specs=[
-            pl.BlockSpec((rows, width), lambda j: (0, 0)),
-            pl.BlockSpec((width, tile), lambda j: (0, j)),
-            pl.BlockSpec((width, tile), lambda j: (0, j + steps)),
-        ],
-        out_specs=[out] * 3,
-        out_shape=[jax.ShapeDtypeStruct((rows, units), BF16)] * 3,
+            pl.BlockSpec((tile, width), lambda i: (i, 0)),
+            pl.BlockSpec((width, 2 * units), lambda i: (0, 0)),
+        ],
+        out_specs=[
+            pl.BlockSpec((tile, units), lambda i: (i, 0)),
+            pl.BlockSpec((tile, 2 * units), lambda i: (i, 0)),
+        ],
+        out_shape=[
+            jax.ShapeDtypeStruct((rows, units), BF16),
+            jax.ShapeDtypeStruct((rows, 2 * units), BF16),
+        ],
         compiler_params=pltpu.CompilerParams(vmem_limit_bytes=VMEM_LIMIT),
         cost_estimate=pl.CostEstimate(
             flops=4 * rows * width * units,
@@ -260,79 +263,63 @@
             bytes_accessed=2 * (rows * width + 2 * width * units + 3 * rows * units),
         ),
         name="feed",
-    )(x, both, both)
-
-
-def feed_slopes_kernel(x_ref, down_ref, gs_ref, us_ref, gg_ref, gu_ref):
+    )(x, both)
+
+
+def feed_back_kernel(x_ref, down_ref, slopes_ref, both_ref, grads_ref, own_ref, other_ref):
+    step, steps = pl.program_id(0), pl.num_programs(0)
+    lots = own_ref.shape[0]
     grad_act = right_transposed(x_ref[...], down_ref[...])
-    gg_ref[...] = (grad_act * gs_ref[...].astype(F32)).astype(BF16)
-    gu_ref[...] = (grad_act * us_ref[...].astype(F32)).astype(BF16)
-
-
-def feed_slopes(upstream, down, gate_slope, up_slope):
+    both_act = jnp.concatenate([grad_act, grad_act], axis=1)
+    grads = (both_act * slopes_ref[...].astype(F32)).astype(BF16)
+    grads_ref[...] = grads
+    total = right_transposed(grads, both_ref[...])
+    total = total.reshape(lots, -1, total.shape[1])
+
+    total = total.astype(BF16)
+
+    @pl.when(step < steps // 2)
+    def _():
+        own_ref[...] = total
+
+    @pl.when(step >= steps // 2)
+    def _():
+        other_ref[...] = total
+
+
+def feed_back(upstream, down, slopes, both, lot, tile):
     rows, width = upstream.shape
     units = down.shape[0]
-    tile = 2 * LANES
-    columns = pl.BlockSpec((rows, tile), lambda j: (0, j))
-    return pl.pallas_call(
-        feed_slopes_kernel,
-        grid=(units // tile,),
+    steps = rows // tile
+    lots = rows // lot
+    per = tile // lot
+    return pl.pallas_call(
+        feed_back_kernel,
+        grid=(steps,),
         in_specs=[
-            pl.BlockSpec((rows, width), lambda j: (0, 0)),
-            pl.BlockSpec((tile, width), lambda j: (j, 0)),
-            columns,
-            columns,
-        ],
-        out_specs=[columns, columns],
-        out_shape=[jax.ShapeDtypeStruct((rows, units), BF16)] * 2,
+            pl.BlockSpec((tile, width), lambda i: (i, 0)),
+            pl.BlockSpec((units, width), lambda i: (0, 0)),
+            pl.BlockSpec((tile, 2 * units), lambda i: (i, 0)),
+            pl.BlockSpec((width, 2 * units), lambda i: (0, 0)),
+        ],
+        out_specs=[
+            pl.BlockSpec((tile, 2 * units), lambda i: (i, 0)),
+            pl.BlockSpec((per, lot, width), lambda i: (jnp.minimum(i, steps // 2 - 1), 0, 0)),
+            pl.BlockSpec((per, lot, width), lambda i: (jnp.maximum(i - steps // 2, 0), 0, 0)),
+        ],
+        out_shape=[
+            jax.ShapeDtypeStruct((rows, 2 * units), BF16),
+            jax.ShapeDtypeStruct((lots // 2, lot, width), BF16),
+            jax.ShapeDtypeStruct((lots // 2, lot, width), BF16),
+        ],
         compiler_params=pltpu.CompilerParams(vmem_limit_bytes=VMEM_LIMIT),
         cost_estimate=pl.CostEstimate(
-            flops=2 * rows * width * units,
+            flops=6 * rows * width * units,
             transcendentals=0,
-            bytes_accessed=2 * (rows * width + width * units + 4 * rows * units),
-        ),
-        name="feed_slopes",
-    )(upstream, down, gate_slope, up_slope)
-
-
-def feed_back_kernel(gg_ref, gu_ref, both_ref, own_ref, other_ref):
-    units = gg_ref.shape[1]
-    lot = own_ref.shape[1]
-    total = right_transposed(gg_ref[...], both_ref[:, :units]) + right_transposed(
-        gu_ref[...], both_ref[:, units:]
-    )
-    for half in range(2):
-        own_ref[half] = total[2 * half * lot : (2 * half + 1) * lot]
-        other_ref[half] = total[(2 * half + 1) * lot : (2 * half + 2) * lot].astype(BF16)
-
-
-def feed_back(grad_gate, grad_up, both):
-    rows, units = grad_gate.shape
-    width = both.shape[0]
-    lot = rows // 4
-    tile = 2 * LANES
-    out = pl.BlockSpec((2, lot, tile), lambda j: (0, 0, j))
-    return pl.pallas_call(
-        feed_back_kernel,
-        grid=(width // tile,),
-        in_specs=[
-            pl.BlockSpec((rows, units), lambda j: (0, 0)),
-            pl.BlockSpec((rows, units), lambda j: (0, 0)),
-            pl.BlockSpec((tile, 2 * units), lambda j: (j, 0)),
-        ],
-        out_specs=[out, out],
-        out_shape=[
-            jax.ShapeDtypeStruct((2, lot, width), F32),
-            jax.ShapeDtypeStruct((2, lot, width), BF16),
-        ],
-        compiler_params=pltpu.CompilerParams(vmem_limit_bytes=VMEM_LIMIT),
-        cost_estimate=pl.CostEstimate(
-            flops=4 * rows * width * units,
-            transcendentals=0,
-            bytes_accessed=2 * (2 * rows * units + 2 * width * units + 2 * rows * width),
+            bytes_accessed=2 * (3 * rows * width + 3 * width * units + 4 * rows * units),
         ),
         name="feed_back",
-    )(grad_gate, grad_up, both)
+    )(upstream, down, slopes, both)
 
 
 def lane_window(read, tiles, start):
@@ -362,12 +349,12 @@
     return total
 
 
-def quarters_kernel(dp_size, unit, block, gate_ref, up_ref, out_ref):
-    units = dp_size * block
+def split_kernel(far, unit, block, me_ref, gate_ref, up_ref, out_ref):
+    units = far * block
     tiles = -(-gate_ref.shape[1] // LANES)
     for at, ref in ((0, gate_ref), (units, up_ref)):
-        for member in range(4):
-            runs = [(d * block, unit, (4 * d + member) * unit) for d in range(dp_size)]
+        for part in range(8):
+            runs = [(d * block, unit, (8 * d + part) * unit) for d in range(far)]
 
             def source_of(source, offset):
                 read = lambda t: ref[:, t * LANES : (t + 1) * LANES].astype(F32)
@@ -375,41 +362,55 @@
 
             for target in range(0, units, LANES):
                 value = lane_runs(target, runs, source_of)
-                out_ref[member, :, at + target : at + target + LANES] = value.astype(BF16)
-
-
-def quarters_of(gate, up, dp_size, unit, block):
-    return pl.pallas_call(
-        functools.partial(quarters_kernel, dp_size, unit, block),
-        out_shape=jax.ShapeDtypeStruct((4, gate.shape[0], 2 * dp_size * block), BF16),
-        compiler_params=pltpu.CompilerParams(vmem_limit_bytes=VMEM_LIMIT),
-        name="quarters",
-    )(gate, up)
-
-
-def columns_kernel(dp_size, unit, block, got_ref, out_ref):
+                to = pl.ds(at + target, LANES)
+                turned = part // 2 % 2 * 4 + part // 4 * 2 + part % 2
+                out_ref[turned ^ me_ref[0], :, to] = value.astype(BF16)
+
+
+def split_units(gate, up, me, far, unit, block):
+    return pl.pallas_call(
+        functools.partial(split_kernel, far, unit, block),
+        in_specs=[
+            pl.BlockSpec(memory_space=pltpu.SMEM),
+            pl.BlockSpec(memory_space=pltpu.VMEM),
+            pl.BlockSpec(memory_space=pltpu.VMEM),
+        ],
+        out_shape=jax.ShapeDtypeStruct((8, gate.shape[0], 2 * far * block), BF16),
+        compiler_params=pltpu.CompilerParams(vmem_limit_bytes=VMEM_LIMIT),
+        name="split_units",
+    )(me, gate, up)
+
+
+def join_kernel(far, unit, block, me_ref, got_ref, gate_ref, up_ref):
+    units = far * block
     tiles = got_ref.shape[2] // LANES
     runs = [
-        ((4 * d + member) * unit, unit, (member, d * block))
-        for d in range(dp_size)
-        for member in range(4)
+        ((8 * d + part) * unit, unit, (part, d * block)) for d in range(far) for part in range(8)
     ]
-
-    def source_of(source, offset):
-        read = lambda t: got_ref[source[0], :, t * LANES : (t + 1) * LANES].astype(F32)
-        return lane_window(read, tiles, source[1] + offset)
-
-    for target in range(0, out_ref.shape[1], LANES):
-        out_ref[:, target : target + LANES] = lane_runs(target, runs, source_of)
-
-
-def columns_of(got, dp_size, unit, block):
-    return pl.pallas_call(
-        functools.partial(columns_kernel, dp_size, unit, block),
-        out_shape=jax.ShapeDtypeStruct((got.shape[1], 4 * dp_size * unit), F32),
-        compiler_params=pltpu.CompilerParams(vmem_limit_bytes=VMEM_LIMIT),
-        name="columns",
-    )(got)
+    for at, ref in ((0, gate_ref), (units, up_ref)):
+
+        def source_of(source, offset):
+            read = lambda t: got_ref[
+                source[0] ^ me_ref[0], :, t * LANES : (t + 1) * LANES
+            ].astype(F32)
+            return lane_window(read, tiles, at + source[1] + offset)
+
+        for target in range(0, ref.shape[1], LANES):
+            ref[:, target : target + LANES] = lane_runs(target, runs, source_of)
+
+
+def join_units(got, me, far, unit, block):
+    out = jax.ShapeDtypeStruct((got.shape[1], 8 * far * unit), F32)
+    return pl.pallas_call(
+        functools.partial(join_kernel, far, unit, block),
+        in_specs=[
+            pl.BlockSpec(memory_space=pltpu.SMEM),
+            pl.BlockSpec(memory_space=pltpu.VMEM),
+        ],
+        out_shape=[out, out],
+        compiler_params=pltpu.CompilerParams(vmem_limit_bytes=VMEM_LIMIT),
+        name="join_units",
+    )(me, got)
 
 
 def swap_pairs(size, bit):
@@ -510,6 +511,8 @@
     def __init__(self, dp_size):
         self.size, self.far = dp_size, dp_size // 2
         self.dp, self.member = lax.axis_index("dp"), lax.axis_index("fsdp")
+        self.me = self.dp % 2 * 4 + self.member
+        self.groups = [[2 * z + y for z in range(self.far)] for y in range(2)]
 
     def near_block(self, shift, near):
         return (self.dp // 2 + self.far + shift) % self.far * 2 + self.dp % 2 * (1 - near) + (
@@ -520,50 +523,158 @@
         return self.near_block(shift, near) * 4 + (self.member ^ member)
 
 
-def gather_dp(piece, places, far_gate=None, near_gate=None):
-    piece = gated(piece, far_gate)
-    held = [piece]
+def far_gather(piece, places):
+    held = {0: piece}
     for r in far_order(places.far):
-        held.append(lax.ppermute(piece, "dp", far_pairs(places.size, r)))
-    mine = jnp.stack(held)
-    return jnp.concatenate([mine, near_swap(gated(mine, near_gate), places)])
-
-
-def gather_group(pair, across, places, gate=None):
-    pair, across = gated((pair, across), gate)
-    beside, both = member_swap(pair, 1), member_swap(across, 1)
-    slots = [
-        places.block(-r, near, member)
-        for member in (0, 2, 1, 3)
-        for near in (0, 1)
-        for r in [0] + far_order(places.far)
-    ]
-    return place([pair, across, beside, both], jnp.stack(slots))
+        held[r] = lax.ppermute(piece, "dp", far_pairs(places.size, r))
+    return held
+
+
+def whole_slots(lots, places):
+    return jnp.stack(
+        [
+            places.block(-r, near, member)
+            for lot in lots
+            for member in (0, 2, 1, 3)
+            for near in (0, 1)
+            for r in lot
+        ]
+    )
 
 
 def gated(value, gate):
     return value if gate is None else lax.optimization_barrier((value, gate))[0]
 
 
-def gather_quarters(quarters, places):
-    mine = [
-        lax.dynamic_index_in_dim(quarters, places.member ^ k, 0, keepdims=False) for k in range(4)
+def exchange_units(parts, places):
+    across = member_swap(parts[4:], 2)
+    parts = jnp.stack([parts[:4], across])
+    near = near_swap(parts[:, 2:], places)
+    parts = jnp.stack([parts[:, :2], near])
+    beside = member_swap(parts[:, :, 1], 1)
+    own = parts[:, :, 0]
+    blocks = [own.reshape(4, *own.shape[2:]), beside.reshape(4, *own.shape[2:])]
+    slots = [
+        places.me ^ (4 * near + 2 * chip + core)
+        for core in (0, 1)
+        for near in (0, 1)
+        for chip in (0, 1)
     ]
-    across = member_swap(jnp.stack([mine[2], mine[3]]), 2)
-    beside = member_swap(jnp.stack([mine[1], across[1]]), 1)
-    out = jnp.zeros_like(quarters)
-    for k, value in ((0, mine[0]), (1, beside[0]), (2, across[0]), (3, beside[1])):
-        out = lax.dynamic_update_index_in_dim(out, value, places.member ^ k, 0)
-    return out
-
-
-def gather_rows(rows, gate=None):
-    if gate is not None:
-        rows, _ = lax.optimization_barrier((rows, gate))
-    near = member_swap(rows, 1)
-    far = member_swap(rows, 2)
-    both = member_swap(far, 1)
-    return jnp.concatenate([rows, near, far, both], axis=0)
+    return place(blocks, jnp.stack(slots)), beside
+
+
+def return_units(blocks, places):
+    slots = [
+        places.me ^ (4 * near + 2 * chip + core)
+        for core in (1, 0)
+        for chip in (1, 0)
+        for near in (1, 0)
+    ]
+    other, own = pick(blocks, jnp.stack(slots), [4, 4])
+    beside = member_swap(other, 1)
+    held = jnp.stack([own, beside])
+    across = member_swap(held[:, :2], 2)
+    held = jnp.stack([held[:, 2:], across])
+    near = near_swap(held[:, :, 0], places)
+    held = jnp.stack([held[:, :, 1], near])
+    return held.reshape(8, *blocks.shape[1:])
+
+
+def assemble_kernel(*refs):
+    pieces, (out, held, come, gone) = refs[:-4], refs[-4:]
+    half = out.shape[2] // 2
+    arrivals, departures = [], []
+    for k, piece in enumerate(pieces):
+        core, at = k // 5, k % 5
+        columns = pl.ds(0, 2 * half) if at < 3 else pl.ds((at - 3) * half, half)
+        spot = (core * 4 + min(at, 3), slice(None), columns)
+        arrivals.append(pltpu.make_async_copy(piece, held.at[spot], come.at[k]))
+        departures.append(pltpu.make_async_copy(held.at[spot], out.at[spot], gone.at[k]))
+    for copy in arrivals:
+        copy.start()
+    for arrival, departure in zip(arrivals, departures):
+        arrival.wait()
+        departure.start()
+    for copy in departures:
+        copy.wait()
+
+
+def assemble(pieces):
+    rows, width = pieces[0].shape
+    shape = (8, rows, width)
+    return pl.pallas_call(
+        assemble_kernel,
+        in_specs=[pl.BlockSpec(memory_space=pl.ANY)] * len(pieces),
+        out_specs=pl.BlockSpec(memory_space=pl.ANY),
+        out_shape=jax.ShapeDtypeStruct(shape, BF16),
+        scratch_shapes=[
+            pltpu.VMEM(shape, BF16),
+            pltpu.SemaphoreType.DMA((len(pieces),)),
+            pltpu.SemaphoreType.DMA((len(pieces),)),
+        ],
+        compiler_params=pltpu.CompilerParams(vmem_limit_bytes=VMEM_LIMIT),
+        cost_estimate=pl.CostEstimate(
+            flops=0, transcendentals=0, bytes_accessed=4 * math.prod(shape)
+        ),
+        name="assemble",
+    )(*pieces)
+
+
+def gather_rows(rows, places, gate=None):
+    rows = gated(rows, gate)
+    half = rows.shape[1] // 2
+    across, near = member_swap(rows, 2), near_swap(rows, places)
+    left = near_swap(across[:, :half], places)
+    right = member_swap(near[:, half:], 2)
+    pieces = [rows, across, near, left, right]
+    out = assemble(pieces + [member_swap(piece, 1) for piece in pieces])
+    return out.reshape(8 * rows.shape[0], rows.shape[1])
+
+
+def merge_kernel(own_ref, got_ref, near_ref, across_ref, left_ref, right_ref):
+    half = own_ref.shape[2] // 2
+    left, right = pl.ds(0, half), pl.ds(half, half)
+
+    def total(lot, columns):
+        return own_ref[lot, :, columns].astype(F32) + got_ref[lot, :, columns].astype(F32)
+
+    for k, lot in enumerate((2, 3)):
+        near_ref[k] = total(lot, left).astype(BF16)
+    for k, lot in enumerate((1, 3)):
+        across_ref[k] = total(lot, right).astype(BF16)
+    for k, lot in enumerate((0, 1)):
+        left_ref[k] = total(lot, left)
+    for k, lot in enumerate((0, 2)):
+        right_ref[k] = total(lot, right)
+
+
+def merge(own, got):
+    shape = (2, own.shape[1], own.shape[2] // 2)
+    low, wide = jax.ShapeDtypeStruct(shape, BF16), jax.ShapeDtypeStruct(shape, F32)
+    return pl.pallas_call(
+        merge_kernel,
+        out_shape=[low, low, wide, wide],
+        compiler_params=pltpu.CompilerParams(vmem_limit_bytes=VMEM_LIMIT),
+        cost_estimate=pl.CostEstimate(
+            flops=own.size, transcendentals=0, bytes_accessed=7 * own.size
+        ),
+        name="merge",
+    )(own, got)
+
+
+def scatter_first(own, other, places):
+    near, across, left, right = merge(own, member_swap(other, 1))
+    near, across = near_swap(near, places), member_swap(across, 2)
+    return left, near, right, across
+
+
+def scatter_second(left, near, right, across, places):
+    left_out = (left[1] + near[1].astype(F32)).astype(BF16)
+    right_out = (right[1] + across[1].astype(F32)).astype(BF16)
+    left_got, right_got = member_swap(left_out, 2), near_swap(right_out, places)
+    left = left[0] + near[0].astype(F32) + left_got.astype(F32)
+    right = right[0] + across[0].astype(F32) + right_got.astype(F32)
+    return jnp.concatenate([left, right], axis=1)
 
 
 def split_order(far):
@@ -571,22 +682,19 @@
     return order[: far // 2], order[far // 2 :]
 
 
-def feed_parts(term, places):
+def far_parts(term, places):
+    order = sum(split_order(places.far), [])
+    slots = [(places.dp // 2 + r) % places.far for r in order]
+    return pick(term, jnp.stack(slots), [1] * len(order))
+
+
+def whole_parts(term, places):
     lots = split_order(places.far)
-    slots = [places.near_block(r, near) for near in (1, 0) for lot in lots for r in lot]
-    return pick(term, jnp.stack(slots), [len(lot) for _ in range(2) for lot in lots])
-
-
-def whole_parts(term, places):
-    order = sum(split_order(places.far), [])
-    slots = [
-        places.block(r, near, core + chip)
-        for core in (1, 0)
-        for chip in (2, 0)
-        for near in (1, 0)
-        for r in order
-    ]
-    return pick(term, jnp.stack(slots), [4 * len(order)] * 2)
+    slots = []
+    for core in (1, 0):
+        slots += [places.block(r, n, core + c) for c in (2, 0) for n in (1, 0) for r in lots[0]]
+        slots += [places.block(r, n, core + c) for n in (1, 0) for c in (2, 0) for r in lots[1]]
+    return pick(term, jnp.stack(slots), [4 * places.far] * 2)
 
 
 def near_swap(value, places):
@@ -665,10 +773,10 @@
     row_ids = member * rows + jnp.arange(rows, dtype=jnp.int32)
     begun = starts[None, :] <= row_ids[:, None]
     row_start = jnp.max(jnp.where(begun, starts[None, :], 0), axis=1)
-    place = row_ids - row_start
+    row_place = row_ids - row_start
     rel = jnp.broadcast_to((row_start - member * rows)[:, None], (rows, LANES))
     frequency = 10000.0 ** (-2.0 * jnp.arange(HD // 2, dtype=F32) / HD)
-    angles = place.astype(F32)[:, None] * frequency[None, :]
+    angles = row_place.astype(F32)[:, None] * frequency[None, :]
     cosine, sine = jnp.cos(angles), jnp.sin(angles)
     cosine = jnp.concatenate([cosine] * 4, axis=1)
     sine = jnp.concatenate([-sine, sine, -sine, sine], axis=1)
@@ -680,20 +788,41 @@
         jnp.stack([attn_gain, ffn_gain], axis=1), ((0, 0), (0, LANES - 2))
     )
     w_qkv = jnp.concatenate([w_query, w_key, w_value, gain_columns], axis=1)
-    qkv_pair = gather_dp(w_qkv, places)
-    out_pair = gather_dp(w_out, places, qkv_pair)
-    qkv_across = member_swap(qkv_pair, 2)
-    out_across = member_swap(gated(out_pair, qkv_across), 2)
-    full_qkv = gather_group(qkv_pair, qkv_across, places).reshape(width, -1)
-
-    ff_block = -(-ff_rows * dp_size // LANES) * LANES // dp_size
-    ff_width = dp_size * ff_block
-
-    both_low = quarters_of(w_gate, w_up, dp_size, ff_rows, ff_block)
-    both_piece = gather_quarters(gated(both_low, qkv_pair), places).reshape(4 * shard, 2 * ff_width)
+    far = places.far
+    ff_block = -(-ff_rows * far // LANES) * LANES // far
+    ff_width = far * ff_block
+    me = places.me.reshape(1)
+    turned = places.member // 2 * 4 + places.dp % 2 * 2 + places.member % 2
+    units = split_units(w_gate, w_up, turned.reshape(1), far, ff_rows, ff_block)
+    both_piece, last_units = exchange_units(units, places)
+    both_piece = both_piece.reshape(8 * shard, 2 * ff_width)
+    sends = far_order(far)
+    lots = ([0] + sends[: far // 2 - 1], sends[far // 2 - 1 :])
+    qkv_held = far_gather(w_qkv, places)
+    out_held = far_gather(gated(w_out, qkv_held[sends[-1]]), places)
+    out_mine = jnp.stack([out_held[r] for r in [0] + sends])
+    mine_a, mine_b = (jnp.stack([qkv_held[r] for r in lot]) for lot in lots)
+    pair_a = jnp.concatenate([mine_a, near_swap(mine_a, places)])
+    pair_b = jnp.concatenate([mine_b, near_swap(gated(mine_b, out_mine), places)])
+    across_a = member_swap(gated(pair_a, last_units), 2)
+    out_pair = jnp.concatenate([out_mine, near_swap(gated(out_mine, pair_b), places)])
+    across_b = member_swap(pair_b, 2)
+    out_across = member_swap(gated(out_pair, across_b), 2)
+    full_qkv = place(
+        [
+            blocks
+            for pair, across in ((pair_a, across_a), (pair_b, across_b))
+            for blocks in (pair, across, member_swap(pair, 1), member_swap(across, 1))
+        ],
+        whole_slots(lots, places),
+    ).reshape(width, -1)
+
     down_piece = jnp.pad(w_down, ((0, ff_block - ff_rows), (0, 0)))
-    my_down = lax.all_gather(down_piece, "dp", axis=0, tiled=True)
-    my_both = lax.all_gather(both_piece, "dp", axis=0, tiled=True)
+    gather_far = functools.partial(
+        lax.all_gather, axis_name="dp", axis=0, tiled=True, axis_index_groups=places.groups
+    )
+    my_down = gather_far(gated(down_piece, qkv_held[sends[-1]]))
+    my_both = gather_far(gated(both_piece, my_down))
 
     gain_table = full_qkv[:, full_qkv.shape[1] - LANES :]
     pick = (
@@ -709,50 +838,64 @@
     queries, kv = head_prep(pre, cosine, sine, head_gains)
     ahead_one = [(i, i + 1) for i in range(3)]
     ahead_two = [(i, i + 2) for i in range(2)]
+    kv = gated(kv, out_across)
     kv_one = lax.ppermute(kv, "fsdp", ahead_one)
     kv_two = lax.ppermute(kv, "fsdp", ahead_two)
     mixed = attend(queries, kv_two, kv_one, kv, rel)
-    full_out = gather_group(out_pair, out_across, places, kv_one).reshape(-1, width)
+    out_pair, out_across = gated((out_pair, out_across), kv_one)
+    full_out = place(
+        [out_pair, out_across, member_swap(out_pair, 1), member_swap(out_across, 1)],
+        whole_slots([[0] + sends], places),
+    ).reshape(-1, width)
     hidden = x + product(mixed, full_out)
     h_inverse = lax.rsqrt(jnp.mean(hidden * hidden, axis=-1, keepdims=True) + EPSILON)
     ffn_mine = (hidden * h_inverse * ffn_row).astype(BF16)
 
-    upstream = gather_rows(cotangent, kv_one)
-    ffn_low = gather_rows(ffn_mine)
-    act_low, gate_slope, up_slope = feed(ffn_low, my_both)
-    lot_a, lot_b = split_order(places.far)
+    upstream = gather_rows(cotangent, places, kv_one)
+    ffn_low = gather_rows(ffn_mine, places)
+    tile = 2 * rows
+    act_low, slopes = feed(ffn_low, my_both, tile)
+    order = sum(split_order(far), [])
 
     def parts_of(left, right):
         term = left_transposed(left, right).astype(BF16)
-        return feed_parts(term.reshape(dp_size, -1, term.shape[1]), places)
-
+        return far_parts(term.reshape(far, -1, term.shape[1]), places)
+
+    def far_sent(blocks, which):
+        return [
+            lax.ppermute(blocks[k], "dp", far_pairs(dp_size, order[k])) if order[k] else blocks[k]
+            for k in which
+        ]
+
+    first, second = range(far // 2), range(far // 2, far)
     rounds = Rounds()
 
-    d_oa, d_ob, d_wa, d_wb, upstream, my_down = rounds.enter(
-        *parts_of(act_low, upstream), upstream, my_down
-    )
-    d_ga = rounds.leave(near_swap(d_oa, places))
-    grad_gate, grad_up = feed_slopes(upstream, my_down, gate_slope, up_slope)
-    grad_gate, grad_up, ffn_own, ffn_other = rounds.leave(
-        grad_gate, grad_up, *feed_back(grad_gate, grad_up, my_both)
-    )
-
-    d_sa = added(d_wa, d_ga)
-    d_sa, d_ob, grad_gate, grad_up, ffn_own, ffn_other = rounds.enter(
-        d_sa, d_ob, grad_gate, grad_up, ffn_own, ffn_other
-    )
-    ffn_got = rounds.leave(member_swap(ffn_other, 1))
-    far_got = rounds.leave(member_swap(added(ffn_own[1], ffn_got[1]), 2))
-    d_za = rounds.leave(*far_sends(lot_a, d_sa, places))
-    d_gb = rounds.leave(near_swap(d_ob, places))
-    g_oa, g_ob, g_wa, g_wb = rounds.leave(*parts_of(ffn_low, grad_gate))
-    u_oa, u_ob, u_wa, u_wb = rounds.leave(*parts_of(ffn_low, grad_up))
-
-    d_sb = added(d_wb, d_gb)
-    g_oa, d_sb, ffn_own, ffn_got, far_got = rounds.enter(g_oa, d_sb, ffn_own, ffn_got, far_got)
-    g_ga = rounds.leave(near_swap(g_oa, places))
-    d_zb = rounds.leave(*far_sends(lot_b, d_sb, places))
-    grad_ffn = ffn_own[0] + ffn_got[0].astype(F32) + far_got.astype(F32)
+    *d_blocks, upstream, my_down, slopes = rounds.enter(
+        *parts_of(act_low, upstream), upstream, my_down, slopes
+    )
+    d_first, d_second = far_sent(d_blocks, first), far_sent(d_blocks, second)
+    rounds.leave(*d_first)
+    grads, ffn_own, ffn_other = rounds.leave(
+        *feed_back(upstream, my_down, slopes, my_both, rows, tile)
+    )
+
+    grads, ffn_own, ffn_other, act_low = rounds.enter(grads, ffn_own, ffn_other, act_low)
+    grad_ffn = scatter_second(*scatter_first(ffn_own, ffn_other, places), places)
+    grad_ffn = rounds.leave(grad_ffn)
+    u_blocks = rounds.leave(*parts_of(ffn_low, grads))
+    out_own, out_other = rounds.leave(
+        *(
+            product(part, my_down).astype(BF16).reshape(4, rows, width)
+            for part in (act_low[: 4 * rows], act_low[4 * rows :])
+        )
+    )
+    rounds.leave(*d_second)
+
+    *u_blocks, grad_ffn, out_own, out_other = rounds.enter(
+        *u_blocks, grad_ffn, out_own, out_other
+    )
+    u_first = far_sent(u_blocks, first)
+    out_steps = rounds.leave(*scatter_first(out_own, out_other, places))
     e = grad_ffn * ffn_row
     slope = jnp.mean(hidden * e, axis=-1, keepdims=True)
     grad_hidden = cotangent.astype(F32) + h_inverse * e - hidden * (h_inverse**3 * slope)
@@ -762,92 +905,60 @@
     gq, gkv_two, gkv_one, gkv = rounds.leave(
         *attend_back(queries, kv_two, kv_one, kv, rel, grad_mixed)
     )
-    term_out = left_transposed(mixed, grad_hidden_low).astype(BF16)
-    o_other, o_own = rounds.leave(
-        *whole_parts(term_out.reshape(4 * dp_size, -1, width), places)
-    )
-
-    g_sa = added(g_wa, g_ga)
-    g_sa, g_ob, gkv_one, gkv_two, o_other, o_own, gq, gkv = rounds.enter(
-        g_sa, g_ob, gkv_one, gkv_two, o_other, o_own, gq, gkv
-    )
-    g_za = rounds.leave(*far_sends(lot_a, g_sa, places))
-    g_gb = rounds.leave(near_swap(g_ob, places))
+    grad_hidden_low = rounds.leave(grad_hidden_low)
+    down_grad = rounds.leave(total_of(d_first + d_second)[0, :ff_rows])
+
+    gkv_one, gkv_two, gq, gkv, grad_hidden_low, *out_steps = rounds.enter(
+        gkv_one, gkv_two, gq, gkv, grad_hidden_low, *out_steps
+    )
     got_one = lax.ppermute(gkv_one, "fsdp", [(b, a) for a, b in ahead_one])
     got_two = lax.ppermute(gkv_two, "fsdp", [(b, a) for a, b in ahead_two])
-    o_sum = added(o_own, member_swap(o_other, 1))
-    half = o_sum.shape[0] // 2
-    quarter, lot = half // 2, half // 2
-    o_across = rounds.leave(member_swap(gated(o_sum[:half], got_two), 2))
-    o_sum = rounds.leave(o_sum[half:])
+    output = rounds.leave((hidden + scatter_second(*out_steps, places)).astype(BF16))
+    term_out = left_transposed(mixed, grad_hidden_low).astype(BF16)
+    out_grad = lax.psum_scatter(term_out, BOTH, scatter_dimension=0, tiled=True).astype(F32)
     grad_pre, head_sums = head_back(gq, gkv, got_one, got_two, pre, cosine, sine, head_gains)
     term_qkv = left_transposed(normed, grad_pre).astype(BF16)
     q_other, q_own = rounds.leave(
         *whole_parts(term_qkv.reshape(4 * dp_size, shard, -1), places)
     )
-
-    g_sb = added(g_wb, g_gb)
-    o_sum = added(o_sum, o_across)
-    u_oa, g_sb, q_other, q_own, grad_pre, o_sum = rounds.enter(
-        u_oa, g_sb, q_other, q_own, grad_pre, o_sum
-    )
-    o_got = rounds.leave(near_swap(o_sum[:quarter], places))
-    o_sum = o_sum[quarter:]
-    q_sum = rounds.leave(added(q_own, member_swap(q_other, 1)))
-    q_xa = rounds.leave(member_swap(q_sum[:lot], 2))
-    u_ga = rounds.leave(near_swap(u_oa, places))
-    g_zb = rounds.leave(*far_sends(lot_b, g_sb, places))
-    u_sa = added(u_wa, u_ga)
-    o_sum = added(o_sum, o_got)
-    u_sa, u_ob, q_xb, grad_pre, act_low, o_sum = rounds.enter(
-        u_sa, u_ob, q_sum[lot:half], grad_pre, act_low, o_sum
-    )
-    o_parts = rounds.leave(*far_sends(lot_a + lot_b, o_sum, places))
-    q_xb = rounds.leave(member_swap(q_xb, 2))
-    grad_normed = right_transposed(grad_pre, full_qkv)
-    out_part = product(act_low, my_down).reshape(2, 2, rows, width)
-    out_own, out_other = rounds.leave(out_part[:, 0], out_part[:, 1].astype(BF16))
-    u_za = rounds.leave(*far_sends(lot_a, u_sa, places))
-    u_gb = rounds.leave(near_swap(u_ob, places))
-    gate_low = total_of(g_za + g_zb).astype(BF16).reshape(4, shard, ff_width)
-    gate_low = rounds.leave(gate_low)
-    down_grad = rounds.leave(total_of(d_za + d_zb)[:ff_rows])
+    grad_pre = rounds.leave(grad_pre)
+    rounds.leave(*u_first)
+
+    u_blocks[far // 2], q_other, q_own, grad_pre = rounds.enter(
+        u_blocks[far // 2], q_other, q_own, grad_pre
+    )
+    q_got = rounds.leave(member_swap(q_other, 1))
+    u_second = far_sent(u_blocks, second)
+    grad_normed = rounds.leave(right_transposed(grad_pre, full_qkv))
+
+    half = 2 * far
+    quarter, eighth = half // 2, half // 4
+    q_a = added(q_own[:half], q_got[:half])
+    q_b = added(q_own[half:], q_got[half:])
+    q_a, q_b, grad_normed = rounds.enter(q_a, q_b, grad_normed)
+    a_got = rounds.leave(member_swap(q_a[:quarter], 2))
+    b_got = rounds.leave(near_swap(q_b[:quarter], places))
     e = grad_normed * attn_row
     slope = jnp.mean(x * e, axis=-1, keepdims=True)
     input_grad = grad_hidden + x_inverse * e - x * (x_inverse**3 * slope)
     input_grad = rounds.leave(input_grad.astype(BF16))
-    attn_gain_term = rounds.leave(jnp.sum(grad_normed * x * x_inverse, axis=0))
-
+    attn_gain_term = jnp.sum(grad_normed * x * x_inverse, axis=0)
     small = jnp.concatenate([attn_gain_term, ffn_gain_term, head_sums.reshape(-1)])
     small = rounds.leave(small.reshape(-1, LANES))
 
-    u_sb = added(u_wb, u_gb)
-    q_y = added(q_sum[half:], jnp.concatenate([q_xa, q_xb]))
-    u_sb, q_yo, q_yw, gate_low, out_own, out_other = rounds.enter(
-        u_sb, q_y[:quarter], q_y[quarter:], gate_low, out_own, out_other
-    )
-    out_got = member_swap(out_other, 1)
-    out_far = added(out_own[1], out_got[1])
-    u_zb = rounds.leave(*far_sends(lot_b, u_sb, places))
-    q_yo = rounds.leave(near_swap(q_yo, places))
-    out_far = rounds.leave(member_swap(out_far, 2))
-    gate_got = rounds.leave(lax.all_to_all(gate_low, "fsdp", 0, 0, tiled=True))
-    out_grad = rounds.leave(total_of(o_parts))
-
-    q_z = added(q_yw, q_yo)
-    up_low = total_of(u_za + u_zb).astype(BF16).reshape(4, shard, ff_width)
-    q_z, up_low, gate_got, out_far, small = rounds.enter(q_z, up_low, gate_got, out_far, small)
-    small = sum_steps(sum_steps(small, "fsdp", 4), "dp", dp_size, 1, 2)
-    q_parts = rounds.leave(*far_sends(lot_a + lot_b, q_z, places))
-    up_got = rounds.leave(lax.all_to_all(up_low, "fsdp", 0, 0, tiled=True))
-    gate_grad = rounds.leave(columns_of(gate_got, dp_size, ff_rows, ff_block))
-
-    small, up_got = rounds.enter(small, up_got)
-    small = sum_steps(small, "dp", dp_size, 2).reshape(-1)
+    q_a, q_b = rounds.enter(added(q_a[quarter:], a_got), added(q_b[quarter:], b_got))
+    a_got = rounds.leave(near_swap(q_a[:eighth], places))
+    b_got = rounds.leave(member_swap(q_b[:eighth], 2))
+    rounds.leave(*u_second)
+
+    unit_sum = total_of(u_first + u_second)[0].astype(BF16).reshape(8, shard, 2 * ff_width)
+    q_a, q_b = added(q_a[eighth:], a_got), added(q_b[eighth:], b_got)
+    q_a, q_b, unit_sum, small = rounds.enter(q_a, q_b, unit_sum, small)
+    q_parts = far_sends(order[: far // 2], q_a, places) + far_sends(order[far // 2 :], q_b, places)
+    unit_all = rounds.leave(return_units(unit_sum, places))
+    small = sum_steps(sum_steps(small, "fsdp", 4), "dp", dp_size).reshape(-1)
     qkv_grad = total_of(q_parts)
-
-    up_grad = columns_of(up_got, dp_size, ff_rows, ff_block)
-    output = (hidden + out_own[0] + out_got[0].astype(F32) + out_far.astype(F32)).astype(BF16)
+    gate_grad, up_grad = join_units(unit_all, me, far, ff_rows, ff_block)
 
     mine = (lax.axis_index("dp") * 4 + member) * shard
     attn_gain_grad = lax.dynamic_slice(small, (mine,), (shard,))

time: 782 us -> 683 us (0.87)
  waiting for transfers between devices: 350 us -> 271 us
  other arithmetic: 62.4 us -> 42.6 us
  local copies, waits for them, and re-layouts: 50.9 us -> 31.2 us
  Pallas kernels: 130 us -> 148 us
    ppermute x15 -> x3, waiting for transfers between devices: 57 us -> 10.7 us  [far_sends(): lax.ppermute(blocks[k], 'dp', far_pairs(places.size, r))]
    ppermute x23 -> x36, waiting for transfers between devices: 134 us -> 95.6 us  [member_swap(): return lax.ppermute(value, 'fsdp', swap_pairs(4, bit))]
    pallas_call x6 -> x8, Pallas kernels: 47.9 us -> 72 us  [the longest x1 29.7 us: feed_back(): pl.pallas_call(feed_back_kernel, grid=(steps,), in_specs=[pl.BlockSpec((t...]
    convert_element_type x14 -> x5, other arithmetic: 29.7 us -> 5.68 us  [added(): return (own.astype(F32) + got.astype(F32)).astype(BF16)]
    ppermute x15 -> x3, starting transfers between devices: 29.9 us -> 6.73 us  [far_sends(): lax.ppermute(blocks[k], 'dp', far_pairs(places.size, r))]
    ppermute x6 -> x12, starting transfers between devices: 18.6 us -> 32.6 us  [the longest x6 23.3 us: far_sent(): lax.ppermute(blocks[k], 'dp', far_pairs(dp_size, order[k]))]
    ppermute x10 -> x15, waiting for transfers between devices: 99.9 us -> 86.2 us  [near_swap(): return lax.ppermute(value, 'dp', swap_pairs(places.size, 1))]
    ppermute x6 -> x12, waiting for transfers between devices: 40 us -> 53.4 us  [the longest x6 28.6 us: far_gather(): held[r] = lax.ppermute(piece, 'dp', far_pairs(places.size, r))]
  transfers between devices with their start and end apart: 67 -> 78, of which waited for: 30 -> 29; matrix products, arithmetic and copies ran while one was open for 17% -> 17% of each run, Pallas kernels for 17% -> 19%
where the time goes in v3:
time: 683 us; the launch traced here: 670 us
  waiting for transfers between devices  271 us (40%)
  Pallas kernels  148 us (22%)
  starting transfers between devices  93.8 us (14%)
  matrix products  67.8 us (10%)
  other arithmetic  42.6 us (6%)
  local copies, waits for them, and re-layouts  31.2 us (5%)
  between operations  15.6 us (2%)
    ppermute x36, waiting for transfers between devices, member_swap(): return lax.ppermute(value, 'fsdp', swap_pairs(4, bit))  95.6 us
    ppermute x15, waiting for transfers between devices, near_swap(): return lax.ppermute(value, 'dp', swap_pairs(places.size, 1))  86.2 us
    dot_general x4, matrix products, left_transposed(): lax.dot_general(left, right, (((0,), (0,)), ((), ())), preferred_element_...  35 us
    pallas_call x1, Pallas kernels, feed_back(): pl.pallas_call(feed_back_kernel, grid=(steps,), in_specs=[pl.BlockSpec((t...  29.7 us
    ppermute x6, waiting for transfers between devices, far_gather(): held[r] = lax.ppermute(piece, 'dp', far_pairs(places.size, r))  28.6 us
    ppermute x6, waiting for transfers between devices, far_sent(): lax.ppermute(blocks[k], 'dp', far_pairs(dp_size, order[k]))  24.8 us
    ppermute x36, starting transfers between devices, member_swap(): return lax.ppermute(value, 'fsdp', swap_pairs(4, bit))  24.6 us
    ppermute x6, starting transfers between devices, far_sent(): lax.ppermute(blocks[k], 'dp', far_pairs(dp_size, order[k]))  23.3 us
  transfers between devices with their start and end apart: 78, of which 29 were waited for; matrix products, arithmetic and copies ran while one was open for 17% of the time, Pallas kernels for 19%

profile of v3, /device:TPU:0, one launch (start us, length us, event | category | flops | bytes accessed | tf_op | source)
XLA Modules:
  0.0 670.5 jit_solution(14856372899983519859)
XLA Ops:
  9.8 5.0 collective-permute-start.8
  25.7 15.8 %collective-permute-done.9 = bf16[64,2432]{1,0:T(8,128)(2,1)S(1)} collective-permute-done((bf16[64,2432]{1,0:T(8,128)(2,1)}, bf16[64,2432]{1,0:T(8,128)(2,1)S(1)}, u32[]{:S(2)}, u32[]{:S(2)}) %collective-permute-start.9) | collective-permute-done | bytes 311328 | tf_op jit(solution)/shard_map/ppermute | solution.py:529
  42.3 2.7 collective-permute-start.11
  49.0 9.4 %collective-permute-done.12 = bf16[48,2048]{1,0:T(8,128)(2,1)S(1)} collective-permute-done((bf16[48,2048]{1,0:T(8,128)(2,1)S(1)}, bf16[48,2048]{1,0:T(8,128)(2,1)S(1)}, u32[]{:S(2)}, u32[]{:S(2)}) %collective-permute-start.12) | collective-permute-done | bytes 196640 | tf_op jit(solution)/shard_map/ppermute | solution.py:529
  58.4 3.3 collective-permute-done.10
  64.7 13.1 %collective-permute-done.1 = bf16[2,64,2432]{2,1,0:T(8,128)(2,1)S(1)} collective-permute-done((bf16[2,64,2432]{2,1,0:T(8,128)(2,1)S(1)}, bf16[2,64,2432]{2,1,0:T(8,128)(2,1)S(1)}, u32[]{:S(2)}, u32[]{:S(2)}) %collective-permute-start.1) | collective-permute-done | bytes 622624 | tf_op jit(solution)/shard_map/ppermute | solution.py:701
  77.9 10.2 %collective-permute-done.13 = bf16[2,64,2432]{2,1,0:T(8,128)(2,1)S(1)} collective-permute-done((bf16[2,64,2432]{2,1,0:T(8,128)(2,1)S(1)}, bf16[2,64,2432]{2,1,0:T(8,128)(2,1)S(1)}, u32[]{:S(2)}, u32[]{:S(2)}) %collective-permute-start.13) | collective-permute-done | bytes 622624 | tf_op jit(solution)/shard_map/ppermute | solution.py:701
  95.8 24.2 %collective-permute-done.14.refs_5_ = bf16[4,64,2432]{2,1,0:T(8,128)(2,1)} collective-permute-done((bf16[4,64,2432]{2,1,0:T(8,128)(2,1)}, bf16[4,64,2432]{2,1,0:T(8,128)(2,1)}, u32[]{:S(2)}, u32[]{:S(2)}) %collective-permute-start.14) | collective-permute-done | bytes 1245216 | tf_op jit(solution)/shard_map/ppermute | solution.py:705
  120.0 22.8 %collective-permute-done.5.refs_1_ = bf16[4,64,2432]{2,1,0:T(8,128)(2,1)S(1)} collective-permute-done((bf16[4,64,2432]{2,1,0:T(8,128)(2,1)S(1)}, bf16[4,64,2432]{2,1,0:T(8,128)(2,1)S(1)}, u32[]{:S(2)}, u32[]{:S(2)}) %collective-permute-start.5) | collective-permute-done | bytes 1245216 | tf_op jit(solution)/shard_map/ppermute | solution.py:705
  143.5 3.5 place.5
  151.0 8.4 %place.3 = bf16[32,64,2432]{2,1,0:T(8,128)(2,1)} custom-call(s32[32]{0:T(128)S(1)} %stack.391.slots, bf16[4,64,2432]{2,1,0:T(8,128)(2,1)S(1)} %pad_maximum_fusion.2.refs_0_, bf16[4,64,2432]{2,1,0:T(8,128)(2,1)S(1)} %collective-permute-done.5.refs_1_, bf16[4,64,2432]{2,1,0:T(8,128)(2,1)} %collective-permute-done.6.refs_2_, ...), custom_call_target="tpu_custom_call" | custom-call | bytes 19922944 | tf_op jit(solution)/shard_map/place/pallas_call | solution.py:456
  161.4 6.4 fusion.29.pre_ref
  167.8 2.7 head_prep.1
  171.4 14.4 %collective-permute-done.18.refs_1_ = bf16[8,48,2048]{2,1,0:T(8,128)(2,1)} collective-permute-done((bf16[8,48,2048]{2,1,0:T(8,128)(2,1)}, bf16[8,48,2048]{2,1,0:T(8,128)(2,1)}, u32[]{:S(2)}, u32[]{:S(2)}) %collective-permute-start.18) | collective-permute-done | bytes 1572896 | tf_op jit(solution)/shard_map/ppermute | solution.py:705
  189.7 5.4 collective-permute-start.21
  195.1 5.6 collective-permute-start.19
  202.4 7.1 %collective-permute-done.19.two_ref = bf16[2,256,384]{2,1,0:T(8,128)(2,1)} collective-permute-done((bf16[2,256,384]{2,1,0:T(8,128)(2,1)}, bf16[2,256,384]{2,1,0:T(8,128)(2,1)}, u32[]{:S(2)}, u32[]{:S(2)}) %collective-permute-start.19) | collective-permute-done | bytes 393248 | tf_op jit(solution)/shard_map/ppermute | solution.py:843
  212.5 12.6 %attend.1 = bf16[256,1536]{1,0:T(8,128)(2,1)S(1)} custom-call(bf16[256,1536]{1,0:T(8,128)(2,1)S(1)} %copy-done.5, bf16[2,256,384]{2,1,0:T(8,128)(2,1)} %collective-permute-done.19.two_ref, bf16[2,256,384]{2,1,0:T(8,128)(2,1)S(1)} %copy-done.12, bf16[2,256,384]{2,1,0:T(8,128)(2,1)} %get-tuple-element.106.kv_ref, s32[256,128]{1,0:T(8,128)S(1)} %broadcast_in_dim.33.rel_ref), custom_call_target="tpu_custom_call" | custom-call | tf_op jit(solution)/shard_map/attend/pallas_call | solution.py:169
  225.2 6.2 place.4
  231.4 4.7 multiply_reduce_fusion.2
  238.0 2.6 collective-permute-start.35
  241.7 11.8 %collective-permute-done.35.refs_4_ = bf16[256,1024]{1,0:T(8,128)(2,1)S(1)} collective-permute-done((bf16[256,1024]{1,0:T(8,128)(2,1)S(1)}, bf16[256,1024]{1,0:T(8,128)(2,1)S(1)}, u32[]{:S(2)}, u32[]{:S(2)}) %collective-permute-start.35) | collective-permute-done | bytes 524320 | tf_op jit(solution)/shard_map/ppermute | solution.py:705
  253.4 17.5 %collective-permute-done.34.refs_3_ = bf16[256,1024]{1,0:T(8,128)(2,1)S(1)} collective-permute-done((bf16[256,1024]{1,0:T(8,128)(2,1)S(1)}, bf16[256,1024]{1,0:T(8,128)(2,1)S(1)}, u32[]{:S(2)}, u32[]{:S(2)}) %collective-permute-start.34) | collective-permute-done | bytes 524320 | tf_op jit(solution)/shard_map/ppermute | solution.py:701
  281.2 9.6 %collective-permute-done.26.refs_4_ = bf16[256,1024]{1,0:T(8,128)(2,1)} collective-permute-done((bf16[256,1024]{1,0:T(8,128)(2,1)S(1)}, bf16[256,1024]{1,0:T(8,128)(2,1)}, u32[]{:S(2)}, u32[]{:S(2)}) %collective-permute-start.26) | collective-permute-done | bytes 524320 | tf_op jit(solution)/shard_map/ppermute | solution.py:705
  290.8 3.2 collective-permute-done.25.refs_3_
  300.7 5.5 assemble.3
  306.3 6.4 assemble.2
  312.7 16.7 %feed.1 = (bf16[2048,640]{1,0:T(8,128)(2,1)S(1)}, bf16[2048,1280]{1,0:T(8,128)(2,1)}) custom-call(bf16[2048,2048]{1,0:T(8,128)(2,1)} %bitcast.183, bf16[2048,1280]{1,0:T(8,128)(2,1)} %all-gather.5.cloned.1.call-done.both_ref), custom_call_target="tpu_custom_call" | custom-call | flops 10737418240 | bytes 21495808 | tf_op jit(solution)/shard_map/feed/pallas_call | solution.py:244
  329.5 8.0 %convolution_convert_fusion.5 = bf16[640,2048]{1,0:T(8,128)(2,1)S(1)} fusion(bf16[2048,640]{1,0:T(8,128)(2,1)S(1)} %get-tuple-element.137, bf16[2048,2048]{1,0:T(8,128)(2,1)} %bitcast.185), kind=kOutput, calls=%fused_computation.13 | convolution fusion | flops 5370019840 | bytes 13631488 | tf_op jit(solution)/shard_map/dot_general | solution.py:32
  339.8 6.2 collective-permute-start.41
  346.0 29.7 %feed_back.1 = (bf16[2048,1280]{1,0:T(8,128)(2,1)}, bf16[4,256,2048]{2,1,0:T(8,128)(2,1)}, bf16[4,256,2048]{2,1,0:T(8,128)(2,1)}) custom-call(bf16[2048,2048]{1,0:T(8,128)(2,1)} %bitcast.186, bf16[640,2048]{1,0:T(8,128)(2,1)S(1)} %copy-done.34, bf16[2048,1280]{1,0:T(8,128)(2,1)} %get-tuple-element.120.slopes_ref, ...), custom_call_target="tpu_custom_call" | custom-call | flops 16106127360 | bytes 43515904 | tf_op jit(solution)/shard_map/feed_back/pallas_call | solution.py:296
  376.1 7.5 %collective-permute-start.48 = (bf16[1,160,2048]{2,1,0:T(8,128)(2,1)S(1)}, bf16[1,160,2048]{2,1,0:T(8,128)(2,1)}, u32[]{:S(2)}, u32[]{:S(2)}) collective-permute-start(bf16[1,160,2048]{2,1,0:T(8,128)(2,1)S(1)} %get-tuple-element.138), channel_id=1, source_target_pairs={{0,16},{4,20},{8,24},{12,28},{16,0},{20,4},{24,8},{28,12},{1,17},{... | collective-permute-start | bytes 1966088 | tf_op jit(solution)/shard_map/ppermute | solution.py:866
  383.5 5.0 merge.2
  390.0 16.7 %convolution_convert_fusion.2 = bf16[2048,1280]{1,0:T(8,128)(2,1)} fusion(bf16[2048,2048]{1,0:T(8,128)(2,1)} %bitcast.184, bf16[2048,1280]{1,0:T(8,128)(2,1)} %get-tuple-element.126), kind=kOutput, calls=%fused_computation.2 | convolution fusion | flops 10740039680 | bytes 18874368 | tf_op jit(solution)/shard_map/dot_general | solution.py:32
  406.7 5.1 convolution_convert_fusion.3
  417.3 4.9 convolution_convert_fusion.4
  422.2 3.8 pick.5
  432.7 2.6 add_bitcast_fusion
  435.3 6.1 collective-permute-start.56
  444.6 5.1 merge.3
  452.9 4.7 convolution_convert_fusion.6.gm_ref
  457.6 18.1 %attend_back.1 = (f32[256,1536]{1,0:T(8,128)S(1)}, bf16[2,256,384]{2,1,0:T(8,128)(2,1)S(1)}, bf16[2,256,384]{2,1,0:T(8,128)(2,1)S(1)}, f32[2,256,384]{2,1,0:T(8,128)S(1)}) custom-call(bf16[256,1536]{1,0:T(8,128)(2,1)S(1)} %copy-done.6, bf16[2,256,384]{2,1,0:T(8,128)(2,1)} %collective-permute-done.19.two_ref, bf16[2,256,384]{2,1,0:T(8,128)(2,1)S(1)} %copy-done.13, ...), custom_call_target="tpu_custom_call" | custom-call | tf_op jit(solution)/shard_map/attend_back/pallas_call | solution.py:214
  478.7 2.3 fusion.24
  482.0 4.8 collective-permute-start.52
  486.8 8.9 %collective-permute-done.55.two_ref = bf16[2,256,384]{2,1,0:T(8,128)(2,1)S(1)} collective-permute-done((bf16[2,256,384]{2,1,0:T(8,128)(2,1)S(1)}, bf16[2,256,384]{2,1,0:T(8,128)(2,1)S(1)}, u32[]{:S(2)}, u32[]{:S(2)}) %collective-permute-start.55) | collective-permute-done | bytes 393248 | tf_op jit(solution)/shard_map/ppermute | solution.py:915
  495.7 5.7 head_back.1
  501.4 5.9 convolution_convert_fusion
  507.3 8.6 %pick.6 = (bf16[16,64,2432]{2,1,0:T(8,128)(2,1)}, bf16[16,64,2432]{2,1,0:T(8,128)(2,1)}) custom-call(s32[32]{0:T(128)S(1)} %stack.451.slots, bf16[32,64,2432]{2,1,0:T(8,128)(2,1)} %bitcast.179), custom_call_target="tpu_custom_call" | custom-call | bytes 19922944 | tf_op jit(solution)/shard_map/pick/pallas_call | solution.py:494
  519.8 4.4 convolution_convert_fusion.1
  524.3 2.6 collective-permute-start.63
  526.9 5.7 fusion.39
  532.7 4.8 add_convert_fusion
  542.4 24.9 %collective-permute-done.60 = bf16[4,64,2432]{2,1,0:T(8,128)(2,1)S(1)} collective-permute-done((bf16[4,64,2432]{2,1,0:T(8,128)(2,1)S(1)}, bf16[4,64,2432]{2,1,0:T(8,128)(2,1)S(1)}, u32[]{:S(2)}, u32[]{:S(2)}) %collective-permute-start.60) | collective-permute-done | bytes 1245216 | tf_op jit(solution)/shard_map/ppermute | solution.py:701
  568.4 24.8 %collective-permute-done.63 = bf16[1,512,1280]{2,1,0:T(8,128)(2,1)S(1)} collective-permute-done((bf16[1,512,1280]{2,1,0:T(8,128)(2,1)}, bf16[1,512,1280]{2,1,0:T(8,128)(2,1)S(1)}, u32[]{:S(2)}, u32[]{:S(2)}) %collective-permute-start.63) | collective-permute-done | bytes 1310752 | tf_op jit(solution)/shard_map/ppermute | solution.py:866
  593.2 2.5 add_convert_fusion.2
  596.8 15.1 %collective-permute-done.61 = bf16[2,64,2432]{2,1,0:T(8,128)(2,1)S(1)} collective-permute-done((bf16[2,64,2432]{2,1,0:T(8,128)(2,1)S(1)}, bf16[2,64,2432]{2,1,0:T(8,128)(2,1)S(1)}, u32[]{:S(2)}, u32[]{:S(2)}) %collective-permute-start.61) | collective-permute-done | bytes 622624 | tf_op jit(solution)/shard_map/ppermute | solution.py:701
  613.3 3.8 collective-permute-done.65
  619.0 4.1 pick.7
  624.1 2.9 collective-permute-done.67
  628.2 2.9 collective-permute-start.71
  631.1 3.8 collective-permute-start.70
  636.1 8.5 %collective-permute-done.73 = bf16[2,2,64,1280]{3,2,1,0:T(8,128)(2,1)S(1)} collective-permute-done((bf16[2,2,64,1280]{3,2,1,0:T(8,128)(2,1)S(1)}, bf16[2,2,64,1280]{3,2,1,0:T(8,128)(2,1)S(1)}, u32[]{:S(2)}, u32[]{:S(2)}) %collective-permute-start.73) | collective-permute-done | bytes 655392 | tf_op jit(solution)/shard_map/ppermute | solution.py:705
  645.7 10.7 %collective-permute-done.71 = bf16[64,2432]{1,0:T(8,128)(2,1)} collective-permute-done((bf16[64,2432]{1,0:T(8,128)(2,1)}, bf16[64,2432]{1,0:T(8,128)(2,1)}, u32[]{:S(2)}, u32[]{:S(2)}) %collective-permute-start.71) | collective-permute-done | bytes 311328 | tf_op jit(solution)/shard_map/ppermute | solution.py:714
  661.0 2.5 join_units.1
  (373 shorter events, 114.2 us)
Async XLA Ops:
  7.2 139.8 %all-gather.3.cloned.1.call-start = ((), (), s32[]{:S(2)}) async-start(), calls=%async_computation.1 | async-start | bytes 3276800 | tf_op jit(solution)/shard_map/all_gather | solution.py:824
  9.8 38.6 %collective-permute-start.8 = (bf16[64,2432]{1,0:T(8,128)(2,1)}, bf16[64,2432]{1,0:T(8,128)(2,1)S(1)}, u32[]{:S(2)}, u32[]{:S(2)}) collective-permute-start(bf16[64,2432]{1,0:T(8,128)(2,1)} %fusion.27), channel_id=1, source_target_pairs={{0,24},{4,28},{8,0},{12,4},{16,8},{20,12},{24,16},{28,20},{1,25},{... | collective-permute-start | bytes 933896 | tf_op jit(solution)/shard_map/ppermute | solution.py:529
  14.8 31.9 %collective-permute-start = (bf16[64,2432]{1,0:T(8,128)(2,1)}, bf16[64,2432]{1,0:T(8,128)(2,1)S(1)}, u32[]{:S(2)}, u32[]{:S(2)}) collective-permute-start(bf16[64,2432]{1,0:T(8,128)(2,1)} %fusion.27), channel_id=1, source_target_pairs={{0,8},{4,12},{8,16},{12,20},{16,24},{20,28},{24,0},{28,4},{1,9},{5... | collective-permute-start | bytes 933896 | tf_op jit(solution)/shard_map/ppermute | solution.py:529
  14.8 26.7 %collective-permute-start.9 = (bf16[64,2432]{1,0:T(8,128)(2,1)}, bf16[64,2432]{1,0:T(8,128)(2,1)S(1)}, u32[]{:S(2)}, u32[]{:S(2)}) collective-permute-start(bf16[64,2432]{1,0:T(8,128)(2,1)} %fusion.27), channel_id=1, source_target_pairs={{0,16},{4,20},{8,24},{12,28},{16,0},{20,4},{24,8},{28,12},{1,17},{... | collective-permute-start | bytes 933896 | tf_op jit(solution)/shard_map/ppermute | solution.py:529
  20.0 25.0 %collective-permute-start.2 = (bf16[4,64,1280]{2,1,0:T(8,128)(2,1)}, bf16[4,64,1280]{2,1,0:T(8,128)(2,1)}, u32[]{:S(2)}, u32[]{:S(2)}) collective-permute-start(bf16[4,64,1280]{2,1,0:T(8,128)(2,1)} %get-tuple-element.199), channel_id=1, source_target_pairs={{0,2},{1,3},{2,0},{3,1},{4,6},{5,7},{6,4},{7,5},{8,10},{9,11},{10,... | collective-permute-start | bytes 1966088 | tf_op jit(solution)/shard_map/ppermute | solution.py:705
  41.6 271.2 %all-gather.5.cloned.1.call-start = ((), (), s32[]{:S(2)}) async-start(), calls=%async_computation.2 | async-start | bytes 6553600 | tf_op jit(solution)/shard_map/all_gather | solution.py:825
  42.2 16.2 %collective-permute-start.12 = (bf16[48,2048]{1,0:T(8,128)(2,1)S(1)}, bf16[48,2048]{1,0:T(8,128)(2,1)S(1)}, u32[]{:S(2)}, u32[]{:S(2)}) collective-permute-start(bf16[48,2048]{1,0:T(8,128)(2,1)S(1)} %copy-done.57), channel_id=1, source_target_pairs={{0,16},{4,20},{8,24},{12,28},{16,0},{20,4},{24,8},{28,12},{1,17},{... | collective-permute-start | bytes 589832 | tf_op jit(solution)/shard_map/ppermute | solution.py:529
  42.3 16.1 %collective-permute-start.11 = (bf16[48,2048]{1,0:T(8,128)(2,1)S(1)}, bf16[48,2048]{1,0:T(8,128)(2,1)S(1)}, u32[]{:S(2)}, u32[]{:S(2)}) collective-permute-start(bf16[48,2048]{1,0:T(8,128)(2,1)S(1)} %copy-done.57), channel_id=1, source_target_pairs={{0,24},{4,28},{8,0},{12,4},{16,8},{20,12},{24,16},{28,20},{1,25},{... | collective-permute-start | bytes 589832 | tf_op jit(solution)/shard_map/ppermute | solution.py:529
  45.0 16.7 %collective-permute-start.10 = (bf16[48,2048]{1,0:T(8,128)(2,1)S(1)}, bf16[48,2048]{1,0:T(8,128)(2,1)S(1)}, u32[]{:S(2)}, u32[]{:S(2)}) collective-permute-start(bf16[48,2048]{1,0:T(8,128)(2,1)S(1)} %copy-done.57), channel_id=1, source_target_pairs={{0,8},{4,12},{8,16},{12,20},{16,24},{20,28},{24,0},{28,4},{1,9},{5... | collective-permute-start | bytes 589832 | tf_op jit(solution)/shard_map/ppermute | solution.py:529
  46.7 17.7 %collective-permute-start.3 = (bf16[2,2,64,1280]{3,2,1,0:T(8,128)(2,1)S(1)}, bf16[2,2,64,1280]{3,2,1,0:T(8,128)(2,1)S(1)}, u32[]{:S(2)}, u32[]{:S(2)}) collective-permute-start(bf16[2,2,64,1280]{3,2,1,0:T(8,128)(2,1)S(1)} %get-tuple-element.197), channel_id=1, source_target_pairs={{0,4},{4,0},{8,12},{12,8},{16,20},{20,16},{24,28},{28,24},{1,5},{5... | collective-permute-start | bytes 1966088 | tf_op jit(solution)/shard_map/ppermute | solution.py:701
  48.3 29.4 %collective-permute-start.1 = (bf16[2,64,2432]{2,1,0:T(8,128)(2,1)S(1)}, bf16[2,64,2432]{2,1,0:T(8,128)(2,1)S(1)}, u32[]{:S(2)}, u32[]{:S(2)}) collective-permute-start(bf16[2,64,2432]{2,1,0:T(8,128)(2,1)S(1)} %pad_maximum_fusion.9), channel_id=1, source_target_pairs={{0,4},{4,0},{8,12},{12,8},{16,20},{20,16},{24,28},{28,24},{1,5},{5... | collective-permute-start | bytes 1867784 | tf_op jit(solution)/shard_map/ppermute | solution.py:701
  62.7 25.4 %collective-permute-start.13 = (bf16[2,64,2432]{2,1,0:T(8,128)(2,1)S(1)}, bf16[2,64,2432]{2,1,0:T(8,128)(2,1)S(1)}, u32[]{:S(2)}, u32[]{:S(2)}) collective-permute-start(bf16[2,64,2432]{2,1,0:T(8,128)(2,1)S(1)} %pad_maximum_fusion.10), channel_id=1, source_target_pairs={{0,4},{4,0},{8,12},{12,8},{16,20},{20,16},{24,28},{28,24},{1,5},{5... | collective-permute-start | bytes 1867784 | tf_op jit(solution)/shard_map/ppermute | solution.py:701
  64.6 26.3 %collective-permute-start.4 = (bf16[2,2,64,1280]{3,2,1,0:T(8,128)(2,1)S(1)}, bf16[2,2,64,1280]{3,2,1,0:T(8,128)(2,1)S(1)}, u32[]{:S(2)}, u32[]{:S(2)}) collective-permute-start(bf16[2,2,64,1280]{3,2,1,0:T(8,128)(2,1)S(1)} %get-tuple-element.196), channel_id=1, source_target_pairs={{0,1},{1,0},{2,3},{3,2},{4,5},{5,4},{6,7},{7,6},{8,9},{9,8},{10,11... | collective-permute-start | bytes 1966088 | tf_op jit(solution)/shard_map/ppermute | solution.py:705
  89.3 30.6 %collective-permute-start.14 = (bf16[4,64,2432]{2,1,0:T(8,128)(2,1)}, bf16[4,64,2432]{2,1,0:T(8,128)(2,1)}, u32[]{:S(2)}, u32[]{:S(2)}) collective-permute-start(bf16[4,64,2432]{2,1,0:T(8,128)(2,1)} %pad_maximum_fusion.3.refs_4_), channel_id=1, source_target_pairs={{0,2},{1,3},{2,0},{3,1},{4,6},{5,7},{6,4},{7,5},{8,10},{9,11},{10,... | collective-permute-start | bytes 3735560 | tf_op jit(solution)/shard_map/ppermute | solution.py:705
  90.8 51.9 %collective-permute-start.5 = (bf16[4,64,2432]{2,1,0:T(8,128)(2,1)S(1)}, bf16[4,64,2432]{2,1,0:T(8,128)(2,1)S(1)}, u32[]{:S(2)}, u32[]{:S(2)}) collective-permute-start(bf16[4,64,2432]{2,1,0:T(8,128)(2,1)S(1)} %pad_maximum_fusion.2.refs_0_), channel_id=1, source_target_pairs={{0,2},{1,3},{2,0},{3,1},{4,6},{5,7},{6,4},{7,5},{8,10},{9,11},{10,... | collective-permute-start | bytes 3735560 | tf_op jit(solution)/shard_map/ppermute | solution.py:705
  93.8 57.2 %collective-permute-start.6 = (bf16[4,64,2432]{2,1,0:T(8,128)(2,1)S(1)}, bf16[4,64,2432]{2,1,0:T(8,128)(2,1)}, u32[]{:S(2)}, u32[]{:S(2)}) collective-permute-start(bf16[4,64,2432]{2,1,0:T(8,128)(2,1)S(1)} %pad_maximum_fusion.2.refs_0_), channel_id=1, source_target_pairs={{0,1},{1,0},{2,3},{3,2},{4,5},{5,4},{6,7},{7,6},{8,9},{9,8},{10,11... | collective-permute-start | bytes 3735560 | tf_op jit(solution)/shard_map/ppermute | solution.py:705
  93.8 57.2 %collective-permute-start.15 = (bf16[4,64,2432]{2,1,0:T(8,128)(2,1)}, bf16[4,64,2432]{2,1,0:T(8,128)(2,1)}, u32[]{:S(2)}, u32[]{:S(2)}) collective-permute-start(bf16[4,64,2432]{2,1,0:T(8,128)(2,1)} %pad_maximum_fusion.3.refs_4_), channel_id=1, source_target_pairs={{0,1},{1,0},{2,3},{3,2},{4,5},{5,4},{6,7},{7,6},{8,9},{9,8},{10,11... | collective-permute-start | bytes 3735560 | tf_op jit(solution)/shard_map/ppermute | solution.py:705
  94.3 53.5 %collective-permute-start.17 = (bf16[4,48,2048]{2,1,0:T(8,128)(2,1)}, bf16[4,48,2048]{2,1,0:T(8,128)(2,1)S(1)}, u32[]{:S(2)}, u32[]{:S(2)}) collective-permute-start(bf16[4,48,2048]{2,1,0:T(8,128)(2,1)} %pad_maximum_fusion.4), channel_id=1, source_target_pairs={{0,4},{4,0},{8,12},{12,8},{16,20},{20,16},{24,28},{28,24},{1,5},{5... | collective-permute-start | bytes 2359304 | tf_op jit(solution)/shard_map/ppermute | solution.py:701
  120.0 31.0 %collective-permute-start.16 = (bf16[4,64,2432]{2,1,0:T(8,128)(2,1)}, bf16[4,64,2432]{2,1,0:T(8,128)(2,1)}, u32[]{:S(2)}, u32[]{:S(2)}) collective-permute-start(bf16[4,64,2432]{2,1,0:T(8,128)(2,1)} %collective-permute-done.14.refs_5_), channel_id=1, source_target_pairs={{0,1},{1,0},{2,3},{3,2},{4,5},{5,4},{6,7},{7,6},{8,9},{9,8},{10,11... | collective-permute-start | bytes 3735560 | tf_op jit(solution)/shard_map/ppermute | solution.py:705
  147.0 512.2 %reduce-scatter.2.cloned.1.call-start = ((), (), s32[]{:S(2)}) async-start(), calls=%async_computation.3 | async-start | bytes 6488064 | tf_op jit(solution)/shard_map/reduce_scatter | solution.py:918
  148.7 37.1 %collective-permute-start.18 = (bf16[8,48,2048]{2,1,0:T(8,128)(2,1)}, bf16[8,48,2048]{2,1,0:T(8,128)(2,1)}, u32[]{:S(2)}, u32[]{:S(2)}) collective-permute-start(bf16[8,48,2048]{2,1,0:T(8,128)(2,1)} %constant_dynamic-update-slice_fusion.refs_0_), channel_id=1, source_target_pairs={{0,2},{1,3},{2,0},{3,1},{4,6},{5,7},{6,4},{7,5},{8,10},{9,11},{10,... | collective-permute-start | bytes 4718600 | tf_op jit(solution)/shard_map/ppermute | solution.py:705
  189.7 35.4 %collective-permute-start.21 = (bf16[8,48,2048]{2,1,0:T(8,128)(2,1)}, bf16[8,48,2048]{2,1,0:T(8,128)(2,1)}, u32[]{:S(2)}, u32[]{:S(2)}) collective-permute-start(bf16[8,48,2048]{2,1,0:T(8,128)(2,1)} %constant_dynamic-update-slice_fusion.refs_0_), channel_id=1, source_target_pairs={{0,1},{1,0},{2,3},{3,2},{4,5},{5,4},{6,7},{7,6},{8,9},{9,8},{10,11... | collective-permute-start | bytes 4718600 | tf_op jit(solution)/shard_map/ppermute | solution.py:705
  195.1 30.1 %collective-permute-start.22 = (bf16[8,48,2048]{2,1,0:T(8,128)(2,1)}, bf16[8,48,2048]{2,1,0:T(8,128)(2,1)}, u32[]{:S(2)}, u32[]{:S(2)}) collective-permute-start(bf16[8,48,2048]{2,1,0:T(8,128)(2,1)} %collective-permute-done.18.refs_1_), channel_id=1, source_target_pairs={{0,1},{1,0},{2,3},{3,2},{4,5},{5,4},{6,7},{7,6},{8,9},{9,8},{10,11... | collective-permute-start | bytes 4718600 | tf_op jit(solution)/shard_map/ppermute | solution.py:705
  195.1 14.5 %collective-permute-start.19 = (bf16[2,256,384]{2,1,0:T(8,128)(2,1)}, bf16[2,256,384]{2,1,0:T(8,128)(2,1)}, u32[]{:S(2)}, u32[]{:S(2)}) collective-permute-start(bf16[2,256,384]{2,1,0:T(8,128)(2,1)} %get-tuple-element.106.kv_ref), channel_id=1, source_target_pairs={{0,2},{1,3},{4,6},{5,7},{8,10},{9,11},{12,14},{13,15},{16,18},{17,... | collective-permute-start | bytes 1179656 | tf_op jit(solution)/shard_map/ppermute | solution.py:843
  200.9 37.1 %collective-permute-start.33 = (bf16[256,2048]{1,0:T(8,128)(2,1)S(1)}, bf16[256,2048]{1,0:T(8,128)(2,1)S(1)}, u32[]{:S(2)}, u32[]{:S(2)}) collective-permute-start(bf16[256,2048]{1,0:T(8,128)(2,1)S(1)} %copy-done.1), channel_id=1, source_target_pairs={{0,4},{4,0},{8,12},{12,8},{16,20},{20,16},{24,28},{28,24},{1,5},{5... | collective-permute-start | bytes 3145736 | tf_op jit(solution)/shard_map/ppermute | solution.py:701
  202.4 38.2 %collective-permute-start.32 = (bf16[256,2048]{1,0:T(8,128)(2,1)S(1)}, bf16[256,2048]{1,0:T(8,128)(2,1)S(1)}, u32[]{:S(2)}, u32[]{:S(2)}) collective-permute-start(bf16[256,2048]{1,0:T(8,128)(2,1)S(1)} %copy-done.1), channel_id=1, source_target_pairs={{0,2},{1,3},{2,0},{3,1},{4,6},{5,7},{6,4},{7,5},{8,10},{9,11},{10,... | collective-permute-start | bytes 3145736 | tf_op jit(solution)/shard_map/ppermute | solution.py:705
  236.4 34.6 %collective-permute-start.24 = (bf16[256,2048]{1,0:T(8,128)(2,1)S(1)}, bf16[256,2048]{1,0:T(8,128)(2,1)}, u32[]{:S(2)}, u32[]{:S(2)}) collective-permute-start(bf16[256,2048]{1,0:T(8,128)(2,1)S(1)} %multiply_convert_fusion.refs_0_), channel_id=1, source_target_pairs={{0,4},{4,0},{8,12},{12,8},{16,20},{20,16},{24,28},{28,24},{1,5},{5... | collective-permute-start | bytes 3145736 | tf_op jit(solution)/shard_map/ppermute | solution.py:701
  238.0 15.4 %collective-permute-start.35 = (bf16[256,1024]{1,0:T(8,128)(2,1)S(1)}, bf16[256,1024]{1,0:T(8,128)(2,1)S(1)}, u32[]{:S(2)}, u32[]{:S(2)}) collective-permute-start(bf16[256,1024]{1,0:T(8,128)(2,1)S(1)} %slice.245), channel_id=1, source_target_pairs={{0,2},{1,3},{2,0},{3,1},{4,6},{5,7},{6,4},{7,5},{8,10},{9,11},{10,... | collective-permute-start | bytes 1572872 | tf_op jit(solution)/shard_map/ppermute | solution.py:705
  240.6 32.6 %collective-permute-start.23 = (bf16[256,2048]{1,0:T(8,128)(2,1)S(1)}, bf16[256,2048]{1,0:T(8,128)(2,1)}, u32[]{:S(2)}, u32[]{:S(2)}) collective-permute-start(bf16[256,2048]{1,0:T(8,128)(2,1)S(1)} %multiply_convert_fusion.refs_0_), channel_id=1, source_target_pairs={{0,2},{1,3},{2,0},{3,1},{4,6},{5,7},{6,4},{7,5},{8,10},{9,11},{10,... | collective-permute-start | bytes 3145736 | tf_op jit(solution)/shard_map/ppermute | solution.py:705
  240.7 30.3 %collective-permute-start.34 = (bf16[256,1024]{1,0:T(8,128)(2,1)S(1)}, bf16[256,1024]{1,0:T(8,128)(2,1)S(1)}, u32[]{:S(2)}, u32[]{:S(2)}) collective-permute-start(bf16[256,1024]{1,0:T(8,128)(2,1)S(1)} %slice.244), channel_id=1, source_target_pairs={{0,4},{4,0},{8,12},{12,8},{16,20},{20,16},{24,28},{28,24},{1,5},{5... | collective-permute-start | bytes 1572872 | tf_op jit(solution)/shard_map/ppermute | solution.py:701
  241.7 33.7 %collective-permute-start.36 = (bf16[256,2048]{1,0:T(8,128)(2,1)S(1)}, bf16[256,2048]{1,0:T(8,128)(2,1)S(1)}, u32[]{:S(2)}, u32[]{:S(2)}) collective-permute-start(bf16[256,2048]{1,0:T(8,128)(2,1)S(1)} %copy-done.1), channel_id=1, source_target_pairs={{0,1},{1,0},{2,3},{3,2},{4,5},{5,4},{6,7},{7,6},{8,9},{9,8},{10,11... | collective-permute-start | bytes 3145736 | tf_op jit(solution)/shard_map/ppermute | solution.py:705
  253.4 25.1 %collective-permute-start.38 = (bf16[256,2048]{1,0:T(8,128)(2,1)S(1)}, bf16[256,2048]{1,0:T(8,128)(2,1)S(1)}, u32[]{:S(2)}, u32[]{:S(2)}) collective-permute-start(bf16[256,2048]{1,0:T(8,128)(2,1)S(1)} %collective-permute-done.33.refs_2_), channel_id=1, source_target_pairs={{0,1},{1,0},{2,3},{3,2},{4,5},{5,4},{6,7},{7,6},{8,9},{9,8},{10,11... | collective-permute-start | bytes 3145736 | tf_op jit(solution)/shard_map/ppermute | solution.py:705
  275.4 30.8 %collective-permute-start.27 = (bf16[256,2048]{1,0:T(8,128)(2,1)S(1)}, bf16[256,2048]{1,0:T(8,128)(2,1)}, u32[]{:S(2)}, u32[]{:S(2)}) collective-permute-start(bf16[256,2048]{1,0:T(8,128)(2,1)S(1)} %multiply_convert_fusion.refs_0_), channel_id=1, source_target_pairs={{0,1},{1,0},{2,3},{3,2},{4,5},{5,4},{6,7},{7,6},{8,9},{9,8},{10,11... | collective-permute-start | bytes 3145736 | tf_op jit(solution)/shard_map/ppermute | solution.py:705
  276.8 14.0 %collective-permute-start.26 = (bf16[256,1024]{1,0:T(8,128)(2,1)S(1)}, bf16[256,1024]{1,0:T(8,128)(2,1)}, u32[]{:S(2)}, u32[]{:S(2)}) collective-permute-start(bf16[256,1024]{1,0:T(8,128)(2,1)S(1)} %slice.243), channel_id=1, source_target_pairs={{0,2},{1,3},{2,0},{3,1},{4,6},{5,7},{6,4},{7,5},{8,10},{9,11},{10,... | collective-permute-start | bytes 1572872 | tf_op jit(solution)/shard_map/ppermute | solution.py:705
  278.5 27.7 %collective-permute-start.29 = (bf16[256,2048]{1,0:T(8,128)(2,1)}, bf16[256,2048]{1,0:T(8,128)(2,1)}, u32[]{:S(2)}, u32[]{:S(2)}) collective-permute-start(bf16[256,2048]{1,0:T(8,128)(2,1)} %collective-permute-done.24.refs_2_), channel_id=1, source_target_pairs={{0,1},{1,0},{2,3},{3,2},{4,5},{5,4},{6,7},{7,6},{8,9},{9,8},{10,11... | collective-permute-start | bytes 3145736 | tf_op jit(solution)/shard_map/ppermute | solution.py:705
  279.5 26.8 %collective-permute-start.28 = (bf16[256,2048]{1,0:T(8,128)(2,1)}, bf16[256,2048]{1,0:T(8,128)(2,1)}, u32[]{:S(2)}, u32[]{:S(2)}) collective-permute-start(bf16[256,2048]{1,0:T(8,128)(2,1)} %collective-permute-done.23.refs_1_), channel_id=1, source_target_pairs={{0,1},{1,0},{2,3},{3,2},{4,5},{5,4},{6,7},{7,6},{8,9},{9,8},{10,11... | collective-permute-start | bytes 3145736 | tf_op jit(solution)/shard_map/ppermute | solution.py:705
  279.9 14.1 %collective-permute-start.25 = (bf16[256,1024]{1,0:T(8,128)(2,1)S(1)}, bf16[256,1024]{1,0:T(8,128)(2,1)}, u32[]{:S(2)}, u32[]{:S(2)}) collective-permute-start(bf16[256,1024]{1,0:T(8,128)(2,1)S(1)} %slice.242), channel_id=1, source_target_pairs={{0,4},{4,0},{8,12},{12,8},{16,20},{20,16},{24,28},{28,24},{1,5},{5... | collective-permute-start | bytes 1572872 | tf_op jit(solution)/shard_map/ppermute | solution.py:701
  290.8 15.5 %collective-permute-start.31 = (bf16[256,1024]{1,0:T(8,128)(2,1)}, bf16[256,1024]{1,0:T(8,128)(2,1)}, u32[]{:S(2)}, u32[]{:S(2)}) collective-permute-start(bf16[256,1024]{1,0:T(8,128)(2,1)} %collective-permute-done.26.refs_4_), channel_id=1, source_target_pairs={{0,1},{1,0},{2,3},{3,2},{4,5},{5,4},{6,7},{7,6},{8,9},{9,8},{10,11... | collective-permute-start | bytes 1572872 | tf_op jit(solution)/shard_map/ppermute | solution.py:705
  294.0 12.3 %collective-permute-start.30 = (bf16[256,1024]{1,0:T(8,128)(2,1)}, bf16[256,1024]{1,0:T(8,128)(2,1)}, u32[]{:S(2)}, u32[]{:S(2)}) collective-permute-start(bf16[256,1024]{1,0:T(8,128)(2,1)} %collective-permute-done.25.refs_3_), channel_id=1, source_target_pairs={{0,1},{1,0},{2,3},{3,2},{4,5},{5,4},{6,7},{7,6},{8,9},{9,8},{10,11... | collective-permute-start | bytes 1572872 | tf_op jit(solution)/shard_map/ppermute | solution.py:705
  339.8 36.0 %collective-permute-start.41 = (bf16[1,160,2048]{2,1,0:T(8,128)(2,1)S(1)}, bf16[1,160,2048]{2,1,0:T(8,128)(2,1)S(1)}, u32[]{:S(2)}, u32[]{:S(2)}) collective-permute-start(bf16[1,160,2048]{2,1,0:T(8,128)(2,1)S(1)} %get-tuple-element.124), channel_id=1, source_target_pairs={{0,8},{4,12},{8,16},{12,20},{16,24},{20,28},{24,0},{28,4},{1,9},{5... | collective-permute-start | bytes 1966088 | tf_op jit(solution)/shard_map/ppermute | solution.py:866
  346.0 29.8 %collective-permute-start.42 = (bf16[1,160,2048]{2,1,0:T(8,128)(2,1)S(1)}, bf16[1,160,2048]{2,1,0:T(8,128)(2,1)S(1)}, u32[]{:S(2)}, u32[]{:S(2)}) collective-permute-start(bf16[1,160,2048]{2,1,0:T(8,128)(2,1)S(1)} %get-tuple-element.125), channel_id=1, source_target_pairs={{0,24},{4,28},{8,0},{12,4},{16,8},{20,12},{24,16},{28,20},{1,25},{... | collective-permute-start | bytes 1966088 | tf_op jit(solution)/shard_map/ppermute | solution.py:866
  376.1 56.5 %collective-permute-start.48 = (bf16[1,160,2048]{2,1,0:T(8,128)(2,1)S(1)}, bf16[1,160,2048]{2,1,0:T(8,128)(2,1)}, u32[]{:S(2)}, u32[]{:S(2)}) collective-permute-start(bf16[1,160,2048]{2,1,0:T(8,128)(2,1)S(1)} %get-tuple-element.138), channel_id=1, source_target_pairs={{0,16},{4,20},{8,24},{12,28},{16,0},{20,4},{24,8},{28,12},{1,17},{... | collective-permute-start | bytes 1966088 | tf_op jit(solution)/shard_map/ppermute | solution.py:866
  388.5 25.2 %collective-permute-start.44 = (bf16[2,256,1024]{2,1,0:T(8,128)(2,1)S(1)}, bf16[2,256,1024]{2,1,0:T(8,128)(2,1)S(1)}, u32[]{:S(2)}, u32[]{:S(2)}) collective-permute-start(bf16[2,256,1024]{2,1,0:T(8,128)(2,1)S(1)} %get-tuple-element.134), channel_id=1, source_target_pairs={{0,4},{4,0},{8,12},{12,8},{16,20},{20,16},{24,28},{28,24},{1,5},{5... | collective-permute-start | bytes 3145736 | tf_op jit(solution)/shard_map/ppermute | solution.py:701
  389.7 25.3 %collective-permute-start.46 = (bf16[2,256,1024]{2,1,0:T(8,128)(2,1)S(1)}, bf16[2,256,1024]{2,1,0:T(8,128)(2,1)S(1)}, u32[]{:S(2)}, u32[]{:S(2)}) collective-permute-start(bf16[2,256,1024]{2,1,0:T(8,128)(2,1)S(1)} %get-tuple-element.136), channel_id=1, source_target_pairs={{0,2},{1,3},{2,0},{3,1},{4,6},{5,7},{6,4},{7,5},{8,10},{9,11},{10,... | collective-permute-start | bytes 3145736 | tf_op jit(solution)/shard_map/ppermute | solution.py:705
  414.9 13.5 %collective-permute-start.45 = (bf16[256,1024]{1,0:T(8,128)(2,1)}, bf16[256,1024]{1,0:T(8,128)(2,1)}, u32[]{:S(2)}, u32[]{:S(2)}) collective-permute-start(bf16[256,1024]{1,0:T(8,128)(2,1)} %fusion.21), channel_id=1, source_target_pairs={{0,2},{1,3},{2,0},{3,1},{4,6},{5,7},{6,4},{7,5},{8,10},{9,11},{10,... | collective-permute-start | bytes 1572872 | tf_op jit(solution)/shard_map/ppermute | solution.py:705
  416.0 13.7 %collective-permute-start.47 = (bf16[256,1024]{1,0:T(8,128)(2,1)}, bf16[256,1024]{1,0:T(8,128)(2,1)}, u32[]{:S(2)}, u32[]{:S(2)}) collective-permute-start(bf16[256,1024]{1,0:T(8,128)(2,1)} %fusion.22), channel_id=1, source_target_pairs={{0,4},{4,0},{8,12},{12,8},{16,20},{20,16},{24,28},{28,24},{1,5},{5... | collective-permute-start | bytes 1572872 | tf_op jit(solution)/shard_map/ppermute | solution.py:701
  435.3 84.5 %collective-permute-start.56 = (bf16[1,512,1280]{2,1,0:T(8,128)(2,1)}, bf16[1,512,1280]{2,1,0:T(8,128)(2,1)}, u32[]{:S(2)}, u32[]{:S(2)}) collective-permute-start(bf16[1,512,1280]{2,1,0:T(8,128)(2,1)} %get-tuple-element.163), channel_id=1, source_target_pairs={{0,8},{4,12},{8,16},{12,20},{16,24},{20,28},{24,0},{28,4},{1,9},{5... | collective-permute-start | bytes 3932168 | tf_op jit(solution)/shard_map/ppermute | solution.py:866
  441.4 78.4 %collective-permute-start.57 = (bf16[1,512,1280]{2,1,0:T(8,128)(2,1)}, bf16[1,512,1280]{2,1,0:T(8,128)(2,1)}, u32[]{:S(2)}, u32[]{:S(2)}) collective-permute-start(bf16[1,512,1280]{2,1,0:T(8,128)(2,1)} %get-tuple-element.164), channel_id=1, source_target_pairs={{0,24},{4,28},{8,0},{12,4},{16,8},{20,12},{24,16},{28,20},{1,25},{... | collective-permute-start | bytes 3932168 | tf_op jit(solution)/shard_map/ppermute | solution.py:866
  449.7 26.1 %collective-permute-start.50 = (bf16[2,256,1024]{2,1,0:T(8,128)(2,1)S(1)}, bf16[2,256,1024]{2,1,0:T(8,128)(2,1)S(1)}, u32[]{:S(2)}, u32[]{:S(2)}) collective-permute-start(bf16[2,256,1024]{2,1,0:T(8,128)(2,1)S(1)} %get-tuple-element.148), channel_id=1, source_target_pairs={{0,4},{4,0},{8,12},{12,8},{16,20},{20,16},{24,28},{28,24},{1,5},{5... | collective-permute-start | bytes 3145736 | tf_op jit(solution)/shard_map/ppermute | solution.py:701
  450.9 25.1 %collective-permute-start.51 = (bf16[2,256,1024]{2,1,0:T(8,128)(2,1)S(1)}, bf16[2,256,1024]{2,1,0:T(8,128)(2,1)}, u32[]{:S(2)}, u32[]{:S(2)}) collective-permute-start(bf16[2,256,1024]{2,1,0:T(8,128)(2,1)S(1)} %get-tuple-element.150), channel_id=1, source_target_pairs={{0,2},{1,3},{2,0},{3,1},{4,6},{5,7},{6,4},{7,5},{8,10},{9,11},{10,... | collective-permute-start | bytes 3145736 | tf_op jit(solution)/shard_map/ppermute | solution.py:705
  477.4 18.3 %collective-permute-start.55 = (bf16[2,256,384]{2,1,0:T(8,128)(2,1)S(1)}, bf16[2,256,384]{2,1,0:T(8,128)(2,1)S(1)}, u32[]{:S(2)}, u32[]{:S(2)}) collective-permute-start(bf16[2,256,384]{2,1,0:T(8,128)(2,1)S(1)} %get-tuple-element.159), channel_id=1, source_target_pairs={{2,0},{3,1},{6,4},{7,5},{10,8},{11,9},{14,12},{15,13},{18,16},{19,... | collective-permute-start | bytes 1179656 | tf_op jit(solution)/shard_map/ppermute | solution.py:915
  481.0 34.8 %collective-permute-start.53 = (bf16[256,1024]{1,0:T(8,128)(2,1)}, bf16[256,1024]{1,0:T(8,128)(2,1)S(1)}, u32[]{:S(2)}, u32[]{:S(2)}) collective-permute-start(bf16[256,1024]{1,0:T(8,128)(2,1)} %fusion.24), channel_id=1, source_target_pairs={{0,4},{4,0},{8,12},{12,8},{16,20},{20,16},{24,28},{28,24},{1,5},{5... | collective-permute-start | bytes 1572872 | tf_op jit(solution)/shard_map/ppermute | solution.py:701
  482.0 35.2 %collective-permute-start.52 = (bf16[256,1024]{1,0:T(8,128)(2,1)S(1)}, bf16[256,1024]{1,0:T(8,128)(2,1)}, u32[]{:S(2)}, u32[]{:S(2)}) collective-permute-start(bf16[256,1024]{1,0:T(8,128)(2,1)S(1)} %fusion.23), channel_id=1, source_target_pairs={{0,2},{1,3},{2,0},{3,1},{4,6},{5,7},{6,4},{7,5},{8,10},{9,11},{10,... | collective-permute-start | bytes 1572872 | tf_op jit(solution)/shard_map/ppermute | solution.py:705
  519.8 12.9 %collective-permute-start.58 = (bf16[16,64,2432]{2,1,0:T(8,128)(2,1)}, bf16[16,64,2432]{2,1,0:T(8,128)(2,1)}, u32[]{:S(2)}, u32[]{:S(2)}) collective-permute-start(bf16[16,64,2432]{2,1,0:T(8,128)(2,1)} %get-tuple-element.166), channel_id=1, source_target_pairs={{0,1},{1,0},{2,3},{3,2},{4,5},{5,4},{6,7},{7,6},{8,9},{9,8},{10,11... | collective-permute-start | bytes 14942216 | tf_op jit(solution)/shard_map/ppermute | solution.py:705
  524.3 68.9 %collective-permute-start.63 = (bf16[1,512,1280]{2,1,0:T(8,128)(2,1)}, bf16[1,512,1280]{2,1,0:T(8,128)(2,1)S(1)}, u32[]{:S(2)}, u32[]{:S(2)}) collective-permute-start(bf16[1,512,1280]{2,1,0:T(8,128)(2,1)} %copy-done.35), channel_id=1, source_target_pairs={{0,16},{4,20},{8,24},{12,28},{16,0},{20,4},{24,8},{28,12},{1,17},{... | collective-permute-start | bytes 3932168 | tf_op jit(solution)/shard_map/ppermute | solution.py:866
  537.7 29.6 %collective-permute-start.60 = (bf16[4,64,2432]{2,1,0:T(8,128)(2,1)S(1)}, bf16[4,64,2432]{2,1,0:T(8,128)(2,1)S(1)}, u32[]{:S(2)}, u32[]{:S(2)}) collective-permute-start(bf16[4,64,2432]{2,1,0:T(8,128)(2,1)S(1)} %slice.214), channel_id=1, source_target_pairs={{0,4},{4,0},{8,12},{12,8},{16,20},{20,16},{24,28},{28,24},{1,5},{5... | collective-permute-start | bytes 3735560 | tf_op jit(solution)/shard_map/ppermute | solution.py:701
  538.5 29.2 %collective-permute-start.59 = (bf16[4,64,2432]{2,1,0:T(8,128)(2,1)S(1)}, bf16[4,64,2432]{2,1,0:T(8,128)(2,1)S(1)}, u32[]{:S(2)}, u32[]{:S(2)}) collective-permute-start(bf16[4,64,2432]{2,1,0:T(8,128)(2,1)S(1)} %slice.212), channel_id=1, source_target_pairs={{0,2},{1,3},{2,0},{3,1},{4,6},{5,7},{6,4},{7,5},{8,10},{9,11},{10,... | collective-permute-start | bytes 3735560 | tf_op jit(solution)/shard_map/ppermute | solution.py:705
  568.1 28.5 %collective-permute-start.62 = (bf16[2,64,2432]{2,1,0:T(8,128)(2,1)S(1)}, bf16[2,64,2432]{2,1,0:T(8,128)(2,1)S(1)}, u32[]{:S(2)}, u32[]{:S(2)}) collective-permute-start(bf16[2,64,2432]{2,1,0:T(8,128)(2,1)S(1)} %slice.218), channel_id=1, source_target_pairs={{0,2},{1,3},{2,0},{3,1},{4,6},{5,7},{6,4},{7,5},{8,10},{9,11},{10,... | collective-permute-start | bytes 1867784 | tf_op jit(solution)/shard_map/ppermute | solution.py:705
  595.7 16.1 %collective-permute-start.61 = (bf16[2,64,2432]{2,1,0:T(8,128)(2,1)S(1)}, bf16[2,64,2432]{2,1,0:T(8,128)(2,1)S(1)}, u32[]{:S(2)}, u32[]{:S(2)}) collective-permute-start(bf16[2,64,2432]{2,1,0:T(8,128)(2,1)S(1)} %slice.216), channel_id=1, source_target_pairs={{0,4},{4,0},{8,12},{12,8},{16,20},{20,16},{24,28},{28,24},{1,5},{5... | collective-permute-start | bytes 1867784 | tf_op jit(solution)/shard_map/ppermute | solution.py:701
  627.2 17.4 %collective-permute-start.73 = (bf16[2,2,64,1280]{3,2,1,0:T(8,128)(2,1)S(1)}, bf16[2,2,64,1280]{3,2,1,0:T(8,128)(2,1)S(1)}, u32[]{:S(2)}, u32[]{:S(2)}) collective-permute-start(bf16[2,2,64,1280]{3,2,1,0:T(8,128)(2,1)S(1)} %get-tuple-element.194), channel_id=1, source_target_pairs={{0,2},{1,3},{2,0},{3,1},{4,6},{5,7},{6,4},{7,5},{8,10},{9,11},{10,... | collective-permute-start | bytes 1966088 | tf_op jit(solution)/shard_map/ppermute | solution.py:705
  628.2 28.2 %collective-permute-start.71 = (bf16[64,2432]{1,0:T(8,128)(2,1)}, bf16[64,2432]{1,0:T(8,128)(2,1)}, u32[]{:S(2)}, u32[]{:S(2)}) collective-permute-start(bf16[64,2432]{1,0:T(8,128)(2,1)} %slice_bitcast_fusion.1), channel_id=1, source_target_pairs={{0,16},{4,20},{8,24},{12,28},{16,0},{20,4},{24,8},{28,12},{1,17},{... | collective-permute-start | bytes 933896 | tf_op jit(solution)/shard_map/ppermute | solution.py:714
  631.1 25.3 %collective-permute-start.69 = (bf16[64,2432]{1,0:T(8,128)(2,1)}, bf16[64,2432]{1,0:T(8,128)(2,1)}, u32[]{:S(2)}, u32[]{:S(2)}) collective-permute-start(bf16[64,2432]{1,0:T(8,128)(2,1)} %get-tuple-element.203), channel_id=1, source_target_pairs={{0,8},{4,12},{8,16},{12,20},{16,24},{20,28},{24,0},{28,4},{1,9},{5... | collective-permute-start | bytes 933896 | tf_op jit(solution)/shard_map/ppermute | solution.py:714
  631.1 25.3 %collective-permute-start.70 = (bf16[64,2432]{1,0:T(8,128)(2,1)}, bf16[64,2432]{1,0:T(8,128)(2,1)}, u32[]{:S(2)}, u32[]{:S(2)}) collective-permute-start(bf16[64,2432]{1,0:T(8,128)(2,1)} %get-tuple-element.204), channel_id=1, source_target_pairs={{0,24},{4,28},{8,0},{12,4},{16,8},{20,12},{24,16},{28,20},{1,25},{... | collective-permute-start | bytes 933896 | tf_op jit(solution)/shard_map/ppermute | solution.py:714
  644.7 16.2 %collective-permute-start.74 = (bf16[2,2,64,1280]{3,2,1,0:T(8,128)(2,1)S(1)}, bf16[2,2,64,1280]{3,2,1,0:T(8,128)(2,1)S(1)}, u32[]{:S(2)}, u32[]{:S(2)}) collective-permute-start(bf16[2,2,64,1280]{3,2,1,0:T(8,128)(2,1)S(1)} %get-tuple-element.192), channel_id=1, source_target_pairs={{0,4},{4,0},{8,12},{12,8},{16,20},{20,16},{24,28},{28,24},{1,5},{5... | collective-permute-start | bytes 1966088 | tf_op jit(solution)/shard_map/ppermute | solution.py:701
  (91 other events, 958.8 us)
Sparse Core Ops, SparseCore 0:
  41.7 62.2 all-gather.2
  147.1 107.6 all-gather.4
  524.4 132.8 reduce-scatter.1

commit v4 on v3

--- a/solution.py
+++ b/solution.py
@@ -530,27 +530,52 @@
     return held
 
 
-def whole_slots(lots, places):
-    return jnp.stack(
-        [
-            places.block(-r, near, member)
-            for lot in lots
-            for member in (0, 2, 1, 3)
-            for near in (0, 1)
-            for r in lot
-        ]
-    )
+def plane_first(mine, places):
+    half = mine.shape[0] // 2
+    first, second = mine[:half], mine[half:]
+    near, across = near_swap(first, places), member_swap(second, 2)
+    return jnp.concatenate([first, near]), jnp.concatenate([second, across])
+
+
+def plane_second(first, second, places):
+    across, near = member_swap(first, 2), near_swap(second, places)
+    return jnp.concatenate([first, across]), jnp.concatenate([second, near])
+
+
+def plane_last(first, second, sends, places):
+    half = places.far // 2
+    lots = [0, *sends][:half], [0, *sends][half:]
+    slots = [
+        places.block(-r, inner, 2 * outer + core)
+        for core in (0, 1)
+        for outer in (0, 1)
+        for inner in (0, 1)
+        for r in lots[0]
+    ]
+    later = [
+        places.block(-r, outer, 2 * inner + core)
+        for core in (0, 1)
+        for outer in (0, 1)
+        for inner in (0, 1)
+        for r in lots[1]
+    ]
+    blocks = [first, member_swap(first, 1), second, member_swap(second, 1)]
+    return place(blocks, jnp.stack(slots + later))
 
 
 def gated(value, gate):
     return value if gate is None else lax.optimization_barrier((value, gate))[0]
 
 
+def exchange_chips(parts):
+    return jnp.stack([parts[:4], member_swap(parts[4:], 2)])
+
+
+def exchange_near(parts, places):
+    return jnp.stack([parts[:, :2], near_swap(parts[:, 2:], places)])
+
+
 def exchange_units(parts, places):
-    across = member_swap(parts[4:], 2)
-    parts = jnp.stack([parts[:4], across])
-    near = near_swap(parts[:, 2:], places)
-    parts = jnp.stack([parts[:, :2], near])
     beside = member_swap(parts[:, :, 1], 1)
     own = parts[:, :, 0]
     blocks = [own.reshape(4, *own.shape[2:]), beside.reshape(4, *own.shape[2:])]
@@ -560,10 +585,10 @@
         for near in (0, 1)
         for chip in (0, 1)
     ]
-    return place(blocks, jnp.stack(slots)), beside
-
-
-def return_units(blocks, places):
+    return place(blocks, jnp.stack(slots))
+
+
+def return_core(blocks, places):
     slots = [
         places.me ^ (4 * near + 2 * chip + core)
         for core in (1, 0)
@@ -571,13 +596,15 @@
         for near in (1, 0)
     ]
     other, own = pick(blocks, jnp.stack(slots), [4, 4])
-    beside = member_swap(other, 1)
-    held = jnp.stack([own, beside])
+    return jnp.stack([own, member_swap(other, 1)])
+
+
+def return_units(held, places):
     across = member_swap(held[:, :2], 2)
     held = jnp.stack([held[:, 2:], across])
     near = near_swap(held[:, :, 0], places)
     held = jnp.stack([held[:, :, 1], near])
-    return held.reshape(8, *blocks.shape[1:])
+    return held.reshape(8, *held.shape[3:])
 
 
 def assemble_kernel(*refs):
@@ -620,15 +647,20 @@
     )(*pieces)
 
 
-def gather_rows(rows, places, gate=None):
-    rows = gated(rows, gate)
+def gather_first(rows, places):
+    return rows, member_swap(rows, 2), near_swap(rows, places)
+
+
+def gather_second(rows, across, near, places):
     half = rows.shape[1] // 2
-    across, near = member_swap(rows, 2), near_swap(rows, places)
     left = near_swap(across[:, :half], places)
     right = member_swap(near[:, half:], 2)
-    pieces = [rows, across, near, left, right]
-    out = assemble(pieces + [member_swap(piece, 1) for piece in pieces])
-    return out.reshape(8 * rows.shape[0], rows.shape[1])
+    return rows, across, near, left, right
+
+
+def gather_last(*pieces):
+    out = assemble([*pieces, *(member_swap(piece, 1) for piece in pieces)])
+    return out.reshape(-1, out.shape[2])
 
 
 def merge_kernel(own_ref, got_ref, near_ref, across_ref, left_ref, right_ref):
@@ -682,10 +714,10 @@
     return order[: far // 2], order[far // 2 :]
 
 
-def far_parts(term, places):
+def far_parts(term, places, cut=1):
     order = sum(split_order(places.far), [])
-    slots = [(places.dp // 2 + r) % places.far for r in order]
-    return pick(term, jnp.stack(slots), [1] * len(order))
+    slots = [(places.dp // 2 + r) % places.far * cut + k for r in order for k in range(cut)]
+    return pick(term, jnp.stack(slots), [1] * len(slots))
 
 
 def whole_parts(term, places):
@@ -707,6 +739,10 @@
 
 def added(own, got):
     return (own.astype(F32) + got.astype(F32)).astype(BF16)
+
+
+def added_parts(own, got, cut):
+    return added(own[:cut], got[:cut]), added(own[cut:], got[cut:])
 
 
 def far_sends(lot, blocks, places):
@@ -788,41 +824,41 @@
         jnp.stack([attn_gain, ffn_gain], axis=1), ((0, 0), (0, LANES - 2))
     )
     w_qkv = jnp.concatenate([w_query, w_key, w_value, gain_columns], axis=1)
+
     far = places.far
     ff_block = -(-ff_rows * far // LANES) * LANES // far
     ff_width = far * ff_block
     me = places.me.reshape(1)
     turned = places.member // 2 * 4 + places.dp % 2 * 2 + places.member % 2
     units = split_units(w_gate, w_up, turned.reshape(1), far, ff_rows, ff_block)
-    both_piece, last_units = exchange_units(units, places)
-    both_piece = both_piece.reshape(8 * shard, 2 * ff_width)
     sends = far_order(far)
-    lots = ([0] + sends[: far // 2 - 1], sends[far // 2 - 1 :])
-    qkv_held = far_gather(w_qkv, places)
-    out_held = far_gather(gated(w_out, qkv_held[sends[-1]]), places)
-    out_mine = jnp.stack([out_held[r] for r in [0] + sends])
-    mine_a, mine_b = (jnp.stack([qkv_held[r] for r in lot]) for lot in lots)
-    pair_a = jnp.concatenate([mine_a, near_swap(mine_a, places)])
-    pair_b = jnp.concatenate([mine_b, near_swap(gated(mine_b, out_mine), places)])
-    across_a = member_swap(gated(pair_a, last_units), 2)
-    out_pair = jnp.concatenate([out_mine, near_swap(gated(out_mine, pair_b), places)])
-    across_b = member_swap(pair_b, 2)
-    out_across = member_swap(gated(out_pair, across_b), 2)
-    full_qkv = place(
-        [
-            blocks
-            for pair, across in ((pair_a, across_a), (pair_b, across_b))
-            for blocks in (pair, across, member_swap(pair, 1), member_swap(across, 1))
-        ],
-        whole_slots(lots, places),
-    ).reshape(width, -1)
-
-    down_piece = jnp.pad(w_down, ((0, ff_block - ff_rows), (0, 0)))
     gather_far = functools.partial(
         lax.all_gather, axis_name="dp", axis=0, tiled=True, axis_index_groups=places.groups
     )
-    my_down = gather_far(gated(down_piece, qkv_held[sends[-1]]))
-    my_both = gather_far(gated(both_piece, my_down))
+
+    rounds = Rounds()
+    qkv_held = far_gather(w_qkv, places)
+    qkv_mine = rounds.leave(jnp.stack([qkv_held[r] for r in [0] + sends]))
+    units = rounds.leave(exchange_near(exchange_chips(units), places))
+
+    qkv_mine, late_out, units, down_piece = rounds.enter(qkv_mine, w_out, units, w_down)
+    out_held = far_gather(late_out, places)
+    out_mine = rounds.leave(jnp.stack([out_held[r] for r in [0] + sends]))
+    qkv_a, qkv_b = plane_first(qkv_mine, places)
+    qkv_a, qkv_b = rounds.leave(qkv_a, qkv_b)
+    down_piece = jnp.pad(down_piece, ((0, ff_block - ff_rows), (0, 0)))
+    my_down = gather_far(down_piece)
+    both_piece = rounds.leave(exchange_units(units, places))
+
+    qkv_a, qkv_b, out_mine, both_piece = rounds.enter(qkv_a, qkv_b, out_mine, both_piece)
+    qkv_a, qkv_b = rounds.leave(*plane_second(qkv_a, qkv_b, places))
+    out_a, out_b = rounds.leave(*plane_first(out_mine, places))
+    my_both = gather_far(both_piece.reshape(8 * shard, 2 * ff_width))
+
+    qkv_a, qkv_b, out_a, out_b = rounds.enter(qkv_a, qkv_b, out_a, out_b)
+    full_qkv = plane_last(qkv_a, qkv_b, sends, places).reshape(width, -1)
+    out_a, out_b = plane_second(*gated((out_a, out_b), full_qkv), places)
+    full_qkv = gated(full_qkv, my_down)
 
     gain_table = full_qkv[:, full_qkv.shape[1] - LANES :]
     pick = (
@@ -838,36 +874,40 @@
     queries, kv = head_prep(pre, cosine, sine, head_gains)
     ahead_one = [(i, i + 1) for i in range(3)]
     ahead_two = [(i, i + 2) for i in range(2)]
-    kv = gated(kv, out_across)
+    kv = gated(kv, (out_a, out_b))
     kv_one = lax.ppermute(kv, "fsdp", ahead_one)
     kv_two = lax.ppermute(kv, "fsdp", ahead_two)
+    pieces = gather_first(gated(cotangent, kv_two), places)
     mixed = attend(queries, kv_two, kv_one, kv, rel)
-    out_pair, out_across = gated((out_pair, out_across), kv_one)
-    full_out = place(
-        [out_pair, out_across, member_swap(out_pair, 1), member_swap(out_across, 1)],
-        whole_slots([[0] + sends], places),
-    ).reshape(-1, width)
+    out_a, out_b, _ = gated((out_a, out_b, kv_one), kv_two)
+    full_out = plane_last(out_a, out_b, sends, places).reshape(-1, width)
+    pieces = gather_second(*gated(pieces, mixed), places)
     hidden = x + product(mixed, full_out)
     h_inverse = lax.rsqrt(jnp.mean(hidden * hidden, axis=-1, keepdims=True) + EPSILON)
     ffn_mine = (hidden * h_inverse * ffn_row).astype(BF16)
 
-    upstream = gather_rows(cotangent, places, kv_one)
-    ffn_low = gather_rows(ffn_mine, places)
+    ffn_pieces = gather_first(gated(ffn_mine, pieces), places)
+    upstream = gather_last(*pieces)
+    ffn_low = gather_last(*gather_second(*gated(ffn_pieces, upstream), places))
     tile = 2 * rows
     act_low, slopes = feed(ffn_low, my_both, tile)
     order = sum(split_order(far), [])
 
-    def parts_of(left, right):
+    def parts_of(left, right, cut=1):
         term = left_transposed(left, right).astype(BF16)
-        return far_parts(term.reshape(far, -1, term.shape[1]), places)
-
-    def far_sent(blocks, which):
+        return far_parts(term.reshape(far * cut, -1, term.shape[1]), places, cut)
+
+    def far_sent(blocks, which, cut=1):
         return [
-            lax.ppermute(blocks[k], "dp", far_pairs(dp_size, order[k])) if order[k] else blocks[k]
+            lax.ppermute(blocks[k], "dp", far_pairs(dp_size, order[k // cut]))
+            if order[k // cut]
+            else blocks[k]
             for k in which
         ]
 
     first, second = range(far // 2), range(far // 2, far)
+    sent = 2 * (far - 1)
+    cut_a = sent // 2
     rounds = Rounds()
 
     *d_blocks, upstream, my_down, slopes = rounds.enter(
@@ -882,7 +922,7 @@
     grads, ffn_own, ffn_other, act_low = rounds.enter(grads, ffn_own, ffn_other, act_low)
     grad_ffn = scatter_second(*scatter_first(ffn_own, ffn_other, places), places)
     grad_ffn = rounds.leave(grad_ffn)
-    u_blocks = rounds.leave(*parts_of(ffn_low, grads))
+    u_blocks = rounds.leave(*parts_of(ffn_low, grads, 2))
     out_own, out_other = rounds.leave(
         *(
             product(part, my_down).astype(BF16).reshape(4, rows, width)
@@ -894,7 +934,7 @@
     *u_blocks, grad_ffn, out_own, out_other = rounds.enter(
         *u_blocks, grad_ffn, out_own, out_other
     )
-    u_first = far_sent(u_blocks, first)
+    u_got = rounds.leave(*far_sent(u_blocks, range(cut_a), 2))
     out_steps = rounds.leave(*scatter_first(out_own, out_other, places))
     e = grad_ffn * ffn_row
     slope = jnp.mean(hidden * e, axis=-1, keepdims=True)
@@ -905,39 +945,45 @@
     gq, gkv_two, gkv_one, gkv = rounds.leave(
         *attend_back(queries, kv_two, kv_one, kv, rel, grad_mixed)
     )
-    grad_hidden_low = rounds.leave(grad_hidden_low)
+    term_out = left_transposed(mixed, grad_hidden_low).astype(BF16)
+    term_out = rounds.leave(term_out)
     down_grad = rounds.leave(total_of(d_first + d_second)[0, :ff_rows])
 
-    gkv_one, gkv_two, gq, gkv, grad_hidden_low, *out_steps = rounds.enter(
-        gkv_one, gkv_two, gq, gkv, grad_hidden_low, *out_steps
-    )
+    u_blocks[sent - 2], gkv_one, gkv_two, gq, gkv, term_out, *out_steps = rounds.enter(
+        u_blocks[sent - 2], gkv_one, gkv_two, gq, gkv, term_out, *out_steps
+    )
+    out_grad = lax.psum_scatter(term_out, BOTH, scatter_dimension=0, tiled=True).astype(F32)
+    u_near = far_sent(u_blocks, [sent - 2], 2)
+    rounds.leave(*u_near)
     got_one = lax.ppermute(gkv_one, "fsdp", [(b, a) for a, b in ahead_one])
     got_two = lax.ppermute(gkv_two, "fsdp", [(b, a) for a, b in ahead_two])
     output = rounds.leave((hidden + scatter_second(*out_steps, places)).astype(BF16))
-    term_out = left_transposed(mixed, grad_hidden_low).astype(BF16)
-    out_grad = lax.psum_scatter(term_out, BOTH, scatter_dimension=0, tiled=True).astype(F32)
+    half = 2 * far
+    quarter, eighth = half // 2, half // 4
     grad_pre, head_sums = head_back(gq, gkv, got_one, got_two, pre, cosine, sine, head_gains)
     term_qkv = left_transposed(normed, grad_pre).astype(BF16)
     q_other, q_own = rounds.leave(
         *whole_parts(term_qkv.reshape(4 * dp_size, shard, -1), places)
     )
     grad_pre = rounds.leave(grad_pre)
-    rounds.leave(*u_first)
-
-    u_blocks[far // 2], q_other, q_own, grad_pre = rounds.enter(
-        u_blocks[far // 2], q_other, q_own, grad_pre
+
+    u_blocks[cut_a], q_other, q_own, grad_pre = rounds.enter(
+        u_blocks[cut_a], q_other, q_own, grad_pre
     )
     q_got = rounds.leave(member_swap(q_other, 1))
-    u_second = far_sent(u_blocks, second)
+    middle = range(cut_a, sent - 2)
+    u_middle = rounds.leave(far_sent(u_blocks, middle, 2))
     grad_normed = rounds.leave(right_transposed(grad_pre, full_qkv))
 
-    half = 2 * far
-    quarter, eighth = half // 2, half // 4
-    q_a = added(q_own[:half], q_got[:half])
-    q_b = added(q_own[half:], q_got[half:])
-    q_a, q_b, grad_normed = rounds.enter(q_a, q_b, grad_normed)
-    a_got = rounds.leave(member_swap(q_a[:quarter], 2))
-    b_got = rounds.leave(near_swap(q_b[:quarter], places))
+    a_out, q_a = added_parts(q_own[:half], q_got[:half], quarter)
+    b_out, q_b = added_parts(q_own[half:], q_got[half:], quarter)
+    u_blocks[sent - 1], a_out, b_out, grad_normed = rounds.enter(
+        u_blocks[sent - 1], a_out, b_out, grad_normed
+    )
+    last = range(sent - 1, sent + 2)
+    u_last = rounds.leave(far_sent(u_blocks, last, 2))
+    a_got = rounds.leave(member_swap(a_out, 2))
+    b_got = rounds.leave(near_swap(b_out, places))
     e = grad_normed * attn_row
     slope = jnp.mean(x * e, axis=-1, keepdims=True)
     input_grad = grad_hidden + x_inverse * e - x * (x_inverse**3 * slope)
@@ -946,18 +992,29 @@
     small = jnp.concatenate([attn_gain_term, ffn_gain_term, head_sums.reshape(-1)])
     small = rounds.leave(small.reshape(-1, LANES))
 
-    q_a, q_b = rounds.enter(added(q_a[quarter:], a_got), added(q_b[quarter:], b_got))
-    a_got = rounds.leave(near_swap(q_a[:eighth], places))
-    b_got = rounds.leave(member_swap(q_b[:eighth], 2))
-    rounds.leave(*u_second)
-
-    unit_sum = total_of(u_first + u_second)[0].astype(BF16).reshape(8, shard, 2 * ff_width)
-    q_a, q_b = added(q_a[eighth:], a_got), added(q_b[eighth:], b_got)
-    q_a, q_b, unit_sum, small = rounds.enter(q_a, q_b, unit_sum, small)
+    u_got = dict(enumerate(u_got)) | {sent - 2: u_near[0]}
+    u_got |= dict(zip(middle, u_middle)) | dict(zip(last, u_last))
+
+    a_out, q_a = added_parts(q_a, a_got, eighth)
+    b_out, q_b = added_parts(q_b, b_got, eighth)
+    unit_sum = jnp.concatenate(
+        [total_of([u_got[2 * r + k] for r in range(far)]) for k in range(2)], axis=1
+    )
+    unit_sum = unit_sum.astype(BF16).reshape(8, shard, 2 * ff_width)
+    a_out, b_out, small, unit_sum = rounds.enter(a_out, b_out, small, unit_sum)
+    a_got = rounds.leave(near_swap(a_out, places))
+    b_got = rounds.leave(member_swap(b_out, 2))
+    small = sum_steps(small, "fsdp", 4, 1, 2)
+    small = rounds.leave(sum_steps(small, "dp", dp_size, 2))
+    units = rounds.leave(return_core(unit_sum, places))
+
+    q_a, q_b = added(q_a, a_got), added(q_b, b_got)
+    q_a, q_b, small, units = rounds.enter(q_a, q_b, small, units)
     q_parts = far_sends(order[: far // 2], q_a, places) + far_sends(order[far // 2 :], q_b, places)
-    unit_all = rounds.leave(return_units(unit_sum, places))
-    small = sum_steps(sum_steps(small, "fsdp", 4), "dp", dp_size).reshape(-1)
+    unit_all = return_units(units, places)
+    small = sum_steps(sum_steps(small, "fsdp", 4, 2), "dp", dp_size, 1, 2).reshape(-1)
     qkv_grad = total_of(q_parts)
+    unit_all = gated(unit_all, out_grad)
     gate_grad, up_grad = join_units(unit_all, me, far, ff_rows, ff_block)
 
     mine = (lax.axis_index("dp") * 4 + member) * shard

time: 683 us -> 640 us (0.937)
  waiting for transfers between devices: 271 us -> 238 us
  starting transfers between devices: 93.8 us -> 84.3 us
    ppermute x15 -> x16, waiting for transfers between devices: 86.2 us -> 43.8 us  [near_swap(): return lax.ppermute(value, 'dp', swap_pairs(places.size, 1))]
    reduce_scatter x1, waiting for transfers between devices: 0.01 us -> 16 us  [local(): lax.psum_scatter(term_out, BOTH, scatter_dimension=0, tiled=True)]
    ppermute x36 -> x35, waiting for transfers between devices: 95.6 us -> 86.1 us  [member_swap(): return lax.ppermute(value, 'fsdp', swap_pairs(4, bit))]
    ppermute x6, waiting for transfers between devices: 28.6 us -> 20.9 us  [far_gather(): held[r] = lax.ppermute(piece, 'dp', far_pairs(places.size, r))]
    ppermute x6 -> x9, waiting for transfers between devices: 24.8 us -> 31.9 us  [far_sent(): lax.ppermute(blocks[k], 'dp', far_pairs(dp_size, order[k // cut]))]
    concatenate x2 -> x7, other arithmetic: 1.34 us -> 8.25 us  [the longest x2 4.98 us: plane_second(): return (jnp.concatenate([first, across]), jnp.concatenate([second, near]))]
    ppermute x6 -> x9, starting transfers between devices: 23.3 us -> 16.8 us  [far_sent(): lax.ppermute(blocks[k], 'dp', far_pairs(dp_size, order[k // cut]))]
    unnamed x158 -> x177, local copies, waits for them, and re-layouts: 18.4 us -> 15.3 us
  transfers between devices with their start and end apart: 78 -> 81, of which waited for: 29 -> 40; matrix products, arithmetic and copies ran while one was open for 17% -> 18% of each run, Pallas kernels for 19% -> 20%
where the time goes in v4:
time: 640 us; the launch traced here: 631 us
  waiting for transfers between devices  238 us (37%)
  Pallas kernels  153 us (24%)
  starting transfers between devices  84.3 us (13%)
  matrix products  68.2 us (11%)
  other arithmetic  46.3 us (7%)
  local copies, waits for them, and re-layouts  25.5 us (4%)
  between operations  15.8 us (2%)
    ppermute x35, waiting for transfers between devices, member_swap(): return lax.ppermute(value, 'fsdp', swap_pairs(4, bit))  86.1 us
    ppermute x16, waiting for transfers between devices, near_swap(): return lax.ppermute(value, 'dp', swap_pairs(places.size, 1))  43.8 us
    dot_general x4, matrix products, left_transposed(): lax.dot_general(left, right, (((0,), (0,)), ((), ())), preferred_element_...  35 us
    ppermute x9, waiting for transfers between devices, far_sent(): lax.ppermute(blocks[k], 'dp', far_pairs(dp_size, order[k // cut]))  31.9 us
    pallas_call x1, Pallas kernels, feed_back(): pl.pallas_call(feed_back_kernel, grid=(steps,), in_specs=[pl.BlockSpec((t...  29.8 us
    ppermute x35, starting transfers between devices, member_swap(): return lax.ppermute(value, 'fsdp', swap_pairs(4, bit))  25.6 us
    pallas_call x3, Pallas kernels, place(): pl.pallas_call(functools.partial(place_kernel, counts), in_specs=[pl.Bloc...  23.2 us
    dot_general x4, matrix products, product(): return jnp.dot(left, right, preferred_element_type=F32)  21.6 us
  transfers between devices with their start and end apart: 81, of which 40 were waited for; matrix products, arithmetic and copies ran while one was open for 18% of the time, Pallas kernels for 20%

profile of v4, /device:TPU:0, one launch (start us, length us, event | category | flops | bytes accessed | tf_op | source)
XLA Modules:
  0.0 630.7 jit_solution(8034255882360680229)
XLA Ops:
  10.6 3.0 collective-permute-start.3
  13.8 3.7 collective-permute-start.1
  18.6 9.8 %collective-permute-done.3 = bf16[4,64,1280]{2,1,0:T(8,128)(2,1)S(1)} collective-permute-done((bf16[4,64,1280]{2,1,0:T(8,128)(2,1)S(1)}, bf16[4,64,1280]{2,1,0:T(8,128)(2,1)S(1)}, u32[]{:S(2)}, u32[]{:S(2)}) %collective-permute-start.3) | collective-permute-done | bytes 655392 | tf_op jit(solution)/shard_map/ppermute | solution.py:737
  30.3 2.6 collective-permute-done
  32.9 10.8 %collective-permute-done.2 = bf16[64,2432]{1,0:T(8,128)(2,1)S(1)} collective-permute-done((bf16[64,2432]{1,0:T(8,128)(2,1)S(1)}, bf16[64,2432]{1,0:T(8,128)(2,1)S(1)}, u32[]{:S(2)}, u32[]{:S(2)}) %collective-permute-start.2) | collective-permute-done | bytes 311328 | tf_op jit(solution)/shard_map/ppermute | solution.py:529
  44.6 2.5 collective-permute-start.9
  52.5 5.4 collective-permute-done.9
  60.1 2.4 collective-permute-done.6
  63.9 4.1 place.3
  74.3 28.7 %collective-permute-done.14 = bf16[2,48,2048]{2,1,0:T(8,128)(2,1)S(1)} collective-permute-done((bf16[2,48,2048]{2,1,0:T(8,128)(2,1)S(1)}, bf16[2,48,2048]{2,1,0:T(8,128)(2,1)S(1)}, u32[]{:S(2)}, u32[]{:S(2)}) %collective-permute-start.14) | collective-permute-done | bytes 393248 | tf_op jit(solution)/shard_map/ppermute | solution.py:737
  108.8 3.0 pad_maximum_fusion.1.refs_2_
  115.9 4.3 collective-permute-done.15.refs_1_
  120.4 8.4 %place.4 = bf16[32,64,2432]{2,1,0:T(8,128)(2,1)} custom-call(s32[32]{0:T(128)S(1)} %stack.408.slots, bf16[8,64,2432]{2,1,0:T(8,128)(2,1)S(1)} %pad_maximum_fusion.refs_0_, bf16[8,64,2432]{2,1,0:T(8,128)(2,1)} %collective-permute-done.15.refs_1_, bf16[8,64,2432]{2,1,0:T(8,128)(2,1)} %pad_maximum_fusion.1.refs_2_, ...), custom_call_target="tpu_custom_call" | custom-call | bytes 19922944 | tf_op jit(solution)/shard_map/place/pallas_call | solution.py:456
  133.4 6.8 %fusion.27.pre_ref = f32[256,2432]{1,0:T(8,128)S(1)} fusion(bf16[2048,2432]{1,0:T(8,128)(2,1)} %bitcast.184, bf16[256,2048]{1,0:T(8,128)(2,1)} %param.15, f32[2048]{0:T(1024)S(1)} %bitcast.204, f32[256]{0:T(256)S(1)} %add_rsqrt_fusion.1), kind=kOutput, calls=%fused_computation.93 | convolution fusion | flops 2552233984 | bytes 13509632 | tf_op jit(solution)/shard_map/dot_general | solution.py:24
  142.7 6.1 collective-permute-done.17
  151.4 3.3 collective-permute-start.19
  154.7 9.3 %collective-permute-done.19.two_ref = bf16[2,256,384]{2,1,0:T(8,128)(2,1)S(1)} collective-permute-done((bf16[2,256,384]{2,1,0:T(8,128)(2,1)S(1)}, bf16[2,256,384]{2,1,0:T(8,128)(2,1)S(1)}, u32[]{:S(2)}, u32[]{:S(2)}) %collective-permute-start.19) | collective-permute-done | bytes 393248 | tf_op jit(solution)/shard_map/ppermute | solution.py:879
  167.3 2.6 collective-permute-start.23
  170.0 11.8 %attend.1 = bf16[256,1536]{1,0:T(8,128)(2,1)S(1)} custom-call(bf16[256,1536]{1,0:T(8,128)(2,1)S(1)} %get-tuple-element.137.q_ref, bf16[2,256,384]{2,1,0:T(8,128)(2,1)S(1)} %collective-permute-done.19.two_ref, bf16[2,256,384]{2,1,0:T(8,128)(2,1)S(1)} %collective-permute-done.20.one_ref, bf16[2,256,384]{2,1,0:T(8,128)(2,1)S(1)} %get-tuple-element.143.kv_ref, ...), custom_call_target="tpu_custom_call" | custom-call | tf_op jit(solution)/shard_map/attend/pallas_call | solution.py:169
  181.9 9.5 %collective-permute-done.24.refs_2_ = bf16[256,2048]{1,0:T(8,128)(2,1)S(1)} collective-permute-done((bf16[256,2048]{1,0:T(8,128)(2,1)S(1)}, bf16[256,2048]{1,0:T(8,128)(2,1)S(1)}, u32[]{:S(2)}, u32[]{:S(2)}) %collective-permute-start.24) | collective-permute-done | bytes 1048608 | tf_op jit(solution)/shard_map/ppermute | solution.py:733
  191.3 2.1 collective-permute-done.23.refs_1_
  198.4 10.7 %place.5 = bf16[32,48,2048]{2,1,0:T(8,128)(2,1)} custom-call(s32[32]{0:T(128)S(1)} %stack.408.slots, bf16[8,48,2048]{2,1,0:T(8,128)(2,1)S(1)} %constant_dynamic-update-slice_fusion.refs_0_, bf16[8,48,2048]{2,1,0:T(8,128)(2,1)S(1)} %collective-permute-done.21.refs_1_, bf16[8,48,2048]{2,1,0:T(8,128)(2,1)S(1)} %constant_dynamic-update-slice_fusion.2.refs_2_, ...), custom_call_target="tpu_custom_call" | custom-call | bytes 12582912 | tf_op jit(solution)/shard_map/place/pallas_call | solution.py:456
  209.1 4.7 multiply_reduce_fusion.2
  218.8 5.5 assemble.2
  224.3 14.6 %collective-permute-done.28.refs_2_ = bf16[256,2048]{1,0:T(8,128)(2,1)} collective-permute-done((bf16[256,2048]{1,0:T(8,128)(2,1)S(1)}, bf16[256,2048]{1,0:T(8,128)(2,1)}, u32[]{:S(2)}, u32[]{:S(2)}) %collective-permute-start.28) | collective-permute-done | bytes 1048608 | tf_op jit(solution)/shard_map/ppermute | solution.py:733
  243.8 13.2 %collective-permute-done.35.refs_4_ = bf16[256,1024]{1,0:T(8,128)(2,1)} collective-permute-done((bf16[256,1024]{1,0:T(8,128)(2,1)S(1)}, bf16[256,1024]{1,0:T(8,128)(2,1)}, u32[]{:S(2)}, u32[]{:S(2)}) %collective-permute-start.35) | collective-permute-done | bytes 524320 | tf_op jit(solution)/shard_map/ppermute | solution.py:737
  260.1 6.4 %assemble.3 = bf16[8,256,2048]{2,1,0:T(8,128)(2,1)} custom-call(bf16[256,2048]{1,0:T(8,128)(2,1)S(1)} %multiply_convert_fusion.refs_0_, bf16[256,2048]{1,0:T(8,128)(2,1)} %collective-permute-done.27.refs_1_, bf16[256,2048]{1,0:T(8,128)(2,1)} %collective-permute-done.28.refs_2_, bf16[256,1024]{1,0:T(8,128)(2,1)} %collective-permute-done.34.refs_3_, ...), custom_call_target="tpu_custom_call" | custom-call | bytes 16777216 | tf_op jit(solution)/shard_map/assemble/pallas_call | solution.py:632
  266.5 16.7 %feed.1 = (bf16[2048,640]{1,0:T(8,128)(2,1)S(1)}, bf16[2048,1280]{1,0:T(8,128)(2,1)}) custom-call(bf16[2048,2048]{1,0:T(8,128)(2,1)} %bitcast.188, bf16[2048,1280]{1,0:T(8,128)(2,1)} %all-gather.5.cloned.1.call-done.both_ref), custom_call_target="tpu_custom_call" | custom-call | flops 10737418240 | bytes 21495808 | tf_op jit(solution)/shard_map/feed/pallas_call | solution.py:244
  284.8 8.0 %convolution_convert_fusion.5 = bf16[640,2048]{1,0:T(8,128)(2,1)S(1)} fusion(bf16[2048,640]{1,0:T(8,128)(2,1)S(1)} %get-tuple-element.184, bf16[2048,2048]{1,0:T(8,128)(2,1)} %bitcast.186), kind=kOutput, calls=%fused_computation.11 | convolution fusion | flops 5370019840 | bytes 13631488 | tf_op jit(solution)/shard_map/dot_general | solution.py:32
  292.8 2.3 pick.4
  295.1 5.1 collective-permute-start.41
  300.2 29.8 %feed_back.1 = (bf16[2048,1280]{1,0:T(8,128)(2,1)}, bf16[4,256,2048]{2,1,0:T(8,128)(2,1)}, bf16[4,256,2048]{2,1,0:T(8,128)(2,1)}) custom-call(bf16[2048,2048]{1,0:T(8,128)(2,1)} %bitcast.187, bf16[640,2048]{1,0:T(8,128)(2,1)S(1)} %copy-done.25, bf16[2048,1280]{1,0:T(8,128)(2,1)} %get-tuple-element.163.slopes_ref, ...), custom_call_target="tpu_custom_call" | custom-call | flops 16106127360 | bytes 43515904 | tf_op jit(solution)/shard_map/feed_back/pallas_call | solution.py:296
  331.8 3.4 collective-permute-start.48
  335.2 4.0 collective-permute-done.43.got_ref
  339.2 5.0 merge.2
  346.4 16.7 %convolution_convert_fusion.2 = bf16[2048,1280]{1,0:T(8,128)(2,1)} fusion(bf16[2048,2048]{1,0:T(8,128)(2,1)} %bitcast.189, bf16[2048,1280]{1,0:T(8,128)(2,1)} %get-tuple-element.169), kind=kOutput, calls=%fused_computation.2 | convolution fusion | flops 10740039680 | bytes 18874368 | tf_op jit(solution)/shard_map/dot_general | solution.py:32
  363.0 5.2 convolution_convert_fusion.3
  373.8 5.0 convolution_convert_fusion.4
  378.8 4.1 pick.5
  384.1 2.5 collective-permute-done.47
  389.7 3.0 add_bitcast_fusion
  398.6 2.8 multiply_reduce_fusion
  402.0 6.5 %merge.3 = (bf16[2,256,1024]{2,1,0:T(8,128)(2,1)}, bf16[2,256,1024]{2,1,0:T(8,128)(2,1)}, f32[2,256,1024]{2,1,0:T(8,128)S(1)}, f32[2,256,1024]{2,1,0:T(8,128)}) custom-call(bf16[4,256,2048]{2,1,0:T(8,128)(2,1)} %bitcast.195, bf16[4,256,2048]{2,1,0:T(8,128)(2,1)} %collective-permute-done.49.got_ref), custom_call_target="tpu_custom_call" | custom-call | flops 2097152 | bytes 14680064 | tf_op jit(solution)/shard_map/merge/pallas_call | solution.py:686
  409.5 4.6 convolution_convert_fusion.6.gm_ref
  414.2 17.4 %attend_back.1 = (f32[256,1536]{1,0:T(8,128)S(1)}, bf16[2,256,384]{2,1,0:T(8,128)(2,1)S(1)}, bf16[2,256,384]{2,1,0:T(8,128)(2,1)S(1)}, f32[2,256,384]{2,1,0:T(8,128)S(1)}) custom-call(bf16[256,1536]{1,0:T(8,128)(2,1)S(1)} %copy-done.4, bf16[2,256,384]{2,1,0:T(8,128)(2,1)S(1)} %copy-done.10, bf16[2,256,384]{2,1,0:T(8,128)(2,1)S(1)} %copy-done.8, ...), custom_call_target="tpu_custom_call" | custom-call | tf_op jit(solution)/shard_map/attend_back/pallas_call | solution.py:214
  435.1 4.5 convolution_convert_fusion.1
  446.8 2.7 collective-permute-start.55
  450.6 9.9 %collective-permute-done.58.two_ref = bf16[2,256,384]{2,1,0:T(8,128)(2,1)S(1)} collective-permute-done((bf16[2,256,384]{2,1,0:T(8,128)(2,1)}, bf16[2,256,384]{2,1,0:T(8,128)(2,1)S(1)}, u32[]{:S(2)}, u32[]{:S(2)}) %collective-permute-start.58) | collective-permute-done | bytes 393248 | tf_op jit(solution)/shard_map/ppermute | solution.py:959
  460.5 5.7 head_back.1
  466.2 5.8 convolution_convert_fusion
  472.1 8.6 %pick.6 = (bf16[16,64,2432]{2,1,0:T(8,128)(2,1)}, bf16[16,64,2432]{2,1,0:T(8,128)(2,1)}) custom-call(s32[32]{0:T(128)S(1)} %stack.475.slots, bf16[32,64,2432]{2,1,0:T(8,128)(2,1)} %bitcast.182), custom_call_target="tpu_custom_call" | custom-call | bytes 19922944 | tf_op jit(solution)/shard_map/pick/pallas_call | solution.py:494
  490.0 5.6 fusion.37
  495.7 3.3 add_convert_fusion
  499.0 4.0 collective-permute-done.61
  506.5 27.5 %collective-permute-done.64 = bf16[1,256,1280]{2,1,0:T(8,128)(2,1)S(1)} collective-permute-done((bf16[1,256,1280]{2,1,0:T(8,128)(2,1)S(1)}, bf16[1,256,1280]{2,1,0:T(8,128)(2,1)S(1)}, u32[]{:S(2)}, u32[]{:S(2)}) %collective-permute-start.64) | collective-permute-done | bytes 655392 | tf_op jit(solution)/shard_map/ppermute | solution.py:902
  540.2 3.8 collective-permute-done.68
  545.5 4.1 pick.7
  549.7 11.6 %collective-permute-done.65 = bf16[2,64,2432]{2,1,0:T(8,128)(2,1)} collective-permute-done((bf16[2,64,2432]{2,1,0:T(8,128)(2,1)}, bf16[2,64,2432]{2,1,0:T(8,128)(2,1)}, u32[]{:S(2)}, u32[]{:S(2)}) %collective-permute-start.65) | collective-permute-done | bytes 622624 | tf_op jit(solution)/shard_map/ppermute | solution.py:733
  568.2 2.7 collective-permute-start.75
  572.4 2.4 collective-permute-start.74
  575.9 8.7 %collective-permute-done.76 = bf16[2,2,64,1280]{3,2,1,0:T(8,128)(2,1)S(1)} collective-permute-done((bf16[2,2,64,1280]{3,2,1,0:T(8,128)(2,1)S(1)}, bf16[2,2,64,1280]{3,2,1,0:T(8,128)(2,1)S(1)}, u32[]{:S(2)}, u32[]{:S(2)}) %collective-permute-start.76) | collective-permute-done | bytes 655392 | tf_op jit(solution)/shard_map/ppermute | solution.py:737
  586.3 13.7 %collective-permute-done.75 = bf16[64,2432]{1,0:T(8,128)(2,1)S(1)} collective-permute-done((bf16[64,2432]{1,0:T(8,128)(2,1)}, bf16[64,2432]{1,0:T(8,128)(2,1)S(1)}, u32[]{:S(2)}, u32[]{:S(2)}) %collective-permute-start.75) | collective-permute-done | bytes 311328 | tf_op jit(solution)/shard_map/ppermute | solution.py:750
  603.4 16.0 %reduce-scatter.2.cloned.1.call-done = bf16[48,2048]{1,0:T(8,128)(2,1)} async-done(((bf16[1536,2048]{1,0:T(8,128)(2,1)}), bf16[48,2048]{1,0:T(8,128)(2,1)}) %reduce-scatter.2.cloned.1.call-update) | async-done | bytes 196624 | tf_op jit(solution)/shard_map/reduce_scatter | solution.py:955
  621.2 2.5 join_units.1
  (405 shorter events, 134.6 us)
Async XLA Ops:
  7.2 121.7 %all-gather.3.cloned.1.call-start = ((), (), s32[]{:S(2)}) async-start(), calls=%async_computation.1 | async-start | bytes 3276800 | tf_op jit(solution)/shard_map/all_gather | solution.py:850
  10.6 17.7 %collective-permute-start.3 = (bf16[4,64,1280]{2,1,0:T(8,128)(2,1)S(1)}, bf16[4,64,1280]{2,1,0:T(8,128)(2,1)S(1)}, u32[]{:S(2)}, u32[]{:S(2)}) collective-permute-start(bf16[4,64,1280]{2,1,0:T(8,128)(2,1)S(1)} %get-tuple-element.258), channel_id=1, source_target_pairs={{0,2},{1,3},{2,0},{3,1},{4,6},{5,7},{6,4},{7,5},{8,10},{9,11},{10,... | collective-permute-start | bytes 1966088 | tf_op jit(solution)/shard_map/ppermute | solution.py:737
  13.8 16.5 %collective-permute-start.1 = (bf16[64,2432]{1,0:T(8,128)(2,1)S(1)}, bf16[64,2432]{1,0:T(8,128)(2,1)S(1)}, u32[]{:S(2)}, u32[]{:S(2)}) collective-permute-start(bf16[64,2432]{1,0:T(8,128)(2,1)S(1)} %fusion.25), channel_id=1, source_target_pairs={{0,24},{4,28},{8,0},{12,4},{16,8},{20,12},{24,16},{28,20},{1,25},{... | collective-permute-start | bytes 933896 | tf_op jit(solution)/shard_map/ppermute | solution.py:529
  17.5 15.5 %collective-permute-start = (bf16[64,2432]{1,0:T(8,128)(2,1)S(1)}, bf16[64,2432]{1,0:T(8,128)(2,1)S(1)}, u32[]{:S(2)}, u32[]{:S(2)}) collective-permute-start(bf16[64,2432]{1,0:T(8,128)(2,1)S(1)} %fusion.25), channel_id=1, source_target_pairs={{0,8},{4,12},{8,16},{12,20},{16,24},{20,28},{24,0},{28,4},{1,9},{5... | collective-permute-start | bytes 933896 | tf_op jit(solution)/shard_map/ppermute | solution.py:529
  17.5 26.2 %collective-permute-start.2 = (bf16[64,2432]{1,0:T(8,128)(2,1)S(1)}, bf16[64,2432]{1,0:T(8,128)(2,1)S(1)}, u32[]{:S(2)}, u32[]{:S(2)}) collective-permute-start(bf16[64,2432]{1,0:T(8,128)(2,1)S(1)} %fusion.25), channel_id=1, source_target_pairs={{0,16},{4,20},{8,24},{12,28},{16,0},{20,4},{24,8},{28,12},{1,17},{... | collective-permute-start | bytes 933896 | tf_op jit(solution)/shard_map/ppermute | solution.py:529
  28.5 16.0 %collective-permute-start.4 = (bf16[2,2,64,1280]{3,2,1,0:T(8,128)(2,1)S(1)}, bf16[2,2,64,1280]{3,2,1,0:T(8,128)(2,1)S(1)}, u32[]{:S(2)}, u32[]{:S(2)}) collective-permute-start(bf16[2,2,64,1280]{3,2,1,0:T(8,128)(2,1)S(1)} %get-tuple-element.256), channel_id=1, source_target_pairs={{0,4},{4,0},{8,12},{12,8},{16,20},{20,16},{24,28},{28,24},{1,5},{5... | collective-permute-start | bytes 1966088 | tf_op jit(solution)/shard_map/ppermute | solution.py:733
  44.6 13.2 %collective-permute-start.9 = (bf16[48,2048]{1,0:T(8,128)(2,1)S(1)}, bf16[48,2048]{1,0:T(8,128)(2,1)S(1)}, u32[]{:S(2)}, u32[]{:S(2)}) collective-permute-start(bf16[48,2048]{1,0:T(8,128)(2,1)S(1)} %copy-done.68), channel_id=1, source_target_pairs={{0,16},{4,20},{8,24},{12,28},{16,0},{20,4},{24,8},{28,12},{1,17},{... | collective-permute-start | bytes 589832 | tf_op jit(solution)/shard_map/ppermute | solution.py:529
  48.5 11.4 %collective-permute-start.7 = (bf16[48,2048]{1,0:T(8,128)(2,1)S(1)}, bf16[48,2048]{1,0:T(8,128)(2,1)S(1)}, u32[]{:S(2)}, u32[]{:S(2)}) collective-permute-start(bf16[48,2048]{1,0:T(8,128)(2,1)S(1)} %copy-done.68), channel_id=1, source_target_pairs={{0,8},{4,12},{8,16},{12,20},{16,24},{20,28},{24,0},{28,4},{1,9},{5... | collective-permute-start | bytes 589832 | tf_op jit(solution)/shard_map/ppermute | solution.py:529
  49.3 13.2 %collective-permute-start.6 = (bf16[2,64,2432]{2,1,0:T(8,128)(2,1)S(1)}, bf16[2,64,2432]{2,1,0:T(8,128)(2,1)S(1)}, u32[]{:S(2)}, u32[]{:S(2)}) collective-permute-start(bf16[2,64,2432]{2,1,0:T(8,128)(2,1)S(1)} %get-tuple-element.259), channel_id=1, source_target_pairs={{0,2},{1,3},{2,0},{3,1},{4,6},{5,7},{6,4},{7,5},{8,10},{9,11},{10,... | collective-permute-start | bytes 1867784 | tf_op jit(solution)/shard_map/ppermute | solution.py:737
  50.9 12.9 %collective-permute-start.5 = (bf16[2,64,2432]{2,1,0:T(8,128)(2,1)S(1)}, bf16[2,64,2432]{2,1,0:T(8,128)(2,1)S(1)}, u32[]{:S(2)}, u32[]{:S(2)}) collective-permute-start(bf16[2,64,2432]{2,1,0:T(8,128)(2,1)S(1)} %get-tuple-element.260), channel_id=1, source_target_pairs={{0,4},{4,0},{8,12},{12,8},{16,20},{20,16},{24,28},{28,24},{1,5},{5... | collective-permute-start | bytes 1867784 | tf_op jit(solution)/shard_map/ppermute | solution.py:733
  69.0 37.7 %collective-permute-start.11 = (bf16[4,64,2432]{2,1,0:T(8,128)(2,1)S(1)}, bf16[4,64,2432]{2,1,0:T(8,128)(2,1)}, u32[]{:S(2)}, u32[]{:S(2)}) collective-permute-start(bf16[4,64,2432]{2,1,0:T(8,128)(2,1)S(1)} %pad_maximum_fusion.8), channel_id=1, source_target_pairs={{0,2},{1,3},{2,0},{3,1},{4,6},{5,7},{6,4},{7,5},{8,10},{9,11},{10,... | collective-permute-start | bytes 3735560 | tf_op jit(solution)/shard_map/ppermute | solution.py:737
  70.5 32.4 %collective-permute-start.14 = (bf16[2,48,2048]{2,1,0:T(8,128)(2,1)S(1)}, bf16[2,48,2048]{2,1,0:T(8,128)(2,1)S(1)}, u32[]{:S(2)}, u32[]{:S(2)}) collective-permute-start(bf16[2,48,2048]{2,1,0:T(8,128)(2,1)S(1)} %get-tuple-element.261), channel_id=1, source_target_pairs={{0,2},{1,3},{2,0},{3,1},{4,6},{5,7},{6,4},{7,5},{8,10},{9,11},{10,... | collective-permute-start | bytes 1179656 | tf_op jit(solution)/shard_map/ppermute | solution.py:737
  72.1 194.4 %all-gather.5.cloned.1.call-start = ((), (), s32[]{:S(2)}) async-start(), calls=%async_computation.2 | async-start | bytes 6553600 | tf_op jit(solution)/shard_map/all_gather | solution.py:856
  72.2 36.6 %collective-permute-start.12 = (bf16[4,64,2432]{2,1,0:T(8,128)(2,1)}, bf16[4,64,2432]{2,1,0:T(8,128)(2,1)S(1)}, u32[]{:S(2)}, u32[]{:S(2)}) collective-permute-start(bf16[4,64,2432]{2,1,0:T(8,128)(2,1)} %pad_maximum_fusion.9), channel_id=1, source_target_pairs={{0,4},{4,0},{8,12},{12,8},{16,20},{20,16},{24,28},{28,24},{1,5},{5... | collective-permute-start | bytes 3735560 | tf_op jit(solution)/shard_map/ppermute | solution.py:733
  73.8 32.1 %collective-permute-start.13 = (bf16[2,48,2048]{2,1,0:T(8,128)(2,1)S(1)}, bf16[2,48,2048]{2,1,0:T(8,128)(2,1)S(1)}, u32[]{:S(2)}, u32[]{:S(2)}) collective-permute-start(bf16[2,48,2048]{2,1,0:T(8,128)(2,1)S(1)} %get-tuple-element.262), channel_id=1, source_target_pairs={{0,4},{4,0},{8,12},{12,8},{16,20},{20,16},{24,28},{28,24},{1,5},{5... | collective-permute-start | bytes 1179656 | tf_op jit(solution)/shard_map/ppermute | solution.py:733
  114.8 504.6 %reduce-scatter.2.cloned.1.call-start = ((), (), s32[]{:S(2)}) async-start(), calls=%async_computation.3 | async-start | bytes 6488064 | tf_op jit(solution)/shard_map/reduce_scatter | solution.py:955
  128.9 19.9 %collective-permute-start.17 = (bf16[4,48,2048]{2,1,0:T(8,128)(2,1)}, bf16[4,48,2048]{2,1,0:T(8,128)(2,1)S(1)}, u32[]{:S(2)}, u32[]{:S(2)}) collective-permute-start(bf16[4,48,2048]{2,1,0:T(8,128)(2,1)} %pad_maximum_fusion.11), channel_id=1, source_target_pairs={{0,2},{1,3},{2,0},{3,1},{4,6},{5,7},{6,4},{7,5},{8,10},{9,11},{10,... | collective-permute-start | bytes 2359304 | tf_op jit(solution)/shard_map/ppermute | solution.py:737
  130.5 19.5 %collective-permute-start.18 = (bf16[4,48,2048]{2,1,0:T(8,128)(2,1)}, bf16[4,48,2048]{2,1,0:T(8,128)(2,1)S(1)}, u32[]{:S(2)}, u32[]{:S(2)}) collective-permute-start(bf16[4,48,2048]{2,1,0:T(8,128)(2,1)} %pad_maximum_fusion.12), channel_id=1, source_target_pairs={{0,4},{4,0},{8,12},{12,8},{16,20},{20,16},{24,28},{28,24},{1,5},{5... | collective-permute-start | bytes 2359304 | tf_op jit(solution)/shard_map/ppermute | solution.py:733
  151.4 12.6 %collective-permute-start.19 = (bf16[2,256,384]{2,1,0:T(8,128)(2,1)S(1)}, bf16[2,256,384]{2,1,0:T(8,128)(2,1)S(1)}, u32[]{:S(2)}, u32[]{:S(2)}) collective-permute-start(bf16[2,256,384]{2,1,0:T(8,128)(2,1)S(1)} %get-tuple-element.143.kv_ref), channel_id=1, source_target_pairs={{0,2},{1,3},{4,6},{5,7},{8,10},{9,11},{12,14},{13,15},{16,18},{17,... | collective-permute-start | bytes 1179656 | tf_op jit(solution)/shard_map/ppermute | solution.py:879
  164.0 32.8 %collective-permute-start.21 = (bf16[8,48,2048]{2,1,0:T(8,128)(2,1)S(1)}, bf16[8,48,2048]{2,1,0:T(8,128)(2,1)S(1)}, u32[]{:S(2)}, u32[]{:S(2)}) collective-permute-start(bf16[8,48,2048]{2,1,0:T(8,128)(2,1)S(1)} %constant_dynamic-update-slice_fusion.refs_0_), channel_id=1, source_target_pairs={{0,1},{1,0},{2,3},{3,2},{4,5},{5,4},{6,7},{7,6},{8,9},{9,8},{10,11... | collective-permute-start | bytes 4718600 | tf_op jit(solution)/shard_map/ppermute | solution.py:737
  165.8 31.5 %collective-permute-start.22 = (bf16[8,48,2048]{2,1,0:T(8,128)(2,1)S(1)}, bf16[8,48,2048]{2,1,0:T(8,128)(2,1)S(1)}, u32[]{:S(2)}, u32[]{:S(2)}) collective-permute-start(bf16[8,48,2048]{2,1,0:T(8,128)(2,1)S(1)} %constant_dynamic-update-slice_fusion.2.refs_2_), channel_id=1, source_target_pairs={{0,1},{1,0},{2,3},{3,2},{4,5},{5,4},{6,7},{7,6},{8,9},{9,8},{10,11... | collective-permute-start | bytes 4718600 | tf_op jit(solution)/shard_map/ppermute | solution.py:737
  165.8 25.6 %collective-permute-start.24 = (bf16[256,2048]{1,0:T(8,128)(2,1)S(1)}, bf16[256,2048]{1,0:T(8,128)(2,1)S(1)}, u32[]{:S(2)}, u32[]{:S(2)}) collective-permute-start(bf16[256,2048]{1,0:T(8,128)(2,1)S(1)} %copy-done.2), channel_id=1, source_target_pairs={{0,4},{4,0},{8,12},{12,8},{16,20},{20,16},{24,28},{28,24},{1,5},{5... | collective-permute-start | bytes 3145736 | tf_op jit(solution)/shard_map/ppermute | solution.py:733
  167.3 26.1 %collective-permute-start.23 = (bf16[256,2048]{1,0:T(8,128)(2,1)S(1)}, bf16[256,2048]{1,0:T(8,128)(2,1)S(1)}, u32[]{:S(2)}, u32[]{:S(2)}) collective-permute-start(bf16[256,2048]{1,0:T(8,128)(2,1)S(1)} %copy-done.2), channel_id=1, source_target_pairs={{0,2},{1,3},{2,0},{3,1},{4,6},{5,7},{6,4},{7,5},{8,10},{9,11},{10,... | collective-permute-start | bytes 3145736 | tf_op jit(solution)/shard_map/ppermute | solution.py:737
  193.5 22.6 %collective-permute-start.30 = (bf16[256,2048]{1,0:T(8,128)(2,1)S(1)}, bf16[256,2048]{1,0:T(8,128)(2,1)}, u32[]{:S(2)}, u32[]{:S(2)}) collective-permute-start(bf16[256,2048]{1,0:T(8,128)(2,1)S(1)} %collective-permute-done.23.refs_1_), channel_id=1, source_target_pairs={{0,1},{1,0},{2,3},{3,2},{4,5},{5,4},{6,7},{7,6},{8,9},{9,8},{10,11... | collective-permute-start | bytes 3145736 | tf_op jit(solution)/shard_map/ppermute | solution.py:737
  194.4 22.2 %collective-permute-start.31 = (bf16[256,2048]{1,0:T(8,128)(2,1)S(1)}, bf16[256,2048]{1,0:T(8,128)(2,1)}, u32[]{:S(2)}, u32[]{:S(2)}) collective-permute-start(bf16[256,2048]{1,0:T(8,128)(2,1)S(1)} %collective-permute-done.24.refs_2_), channel_id=1, source_target_pairs={{0,1},{1,0},{2,3},{3,2},{4,5},{5,4},{6,7},{7,6},{8,9},{9,8},{10,11... | collective-permute-start | bytes 3145736 | tf_op jit(solution)/shard_map/ppermute | solution.py:737
  195.0 19.1 %collective-permute-start.26 = (bf16[256,1024]{1,0:T(8,128)(2,1)}, bf16[256,1024]{1,0:T(8,128)(2,1)S(1)}, u32[]{:S(2)}, u32[]{:S(2)}) collective-permute-start(bf16[256,1024]{1,0:T(8,128)(2,1)} %slice.225), channel_id=1, source_target_pairs={{0,2},{1,3},{2,0},{3,1},{4,6},{5,7},{6,4},{7,5},{8,10},{9,11},{10,... | collective-permute-start | bytes 1572872 | tf_op jit(solution)/shard_map/ppermute | solution.py:737
  196.8 17.4 %collective-permute-start.25 = (bf16[256,1024]{1,0:T(8,128)(2,1)S(1)}, bf16[256,1024]{1,0:T(8,128)(2,1)S(1)}, u32[]{:S(2)}, u32[]{:S(2)}) collective-permute-start(bf16[256,1024]{1,0:T(8,128)(2,1)S(1)} %slice.224), channel_id=1, source_target_pairs={{0,4},{4,0},{8,12},{12,8},{16,20},{20,16},{24,28},{28,24},{1,5},{5... | collective-permute-start | bytes 1572872 | tf_op jit(solution)/shard_map/ppermute | solution.py:733
  197.2 18.9 %collective-permute-start.29 = (bf16[256,2048]{1,0:T(8,128)(2,1)S(1)}, bf16[256,2048]{1,0:T(8,128)(2,1)}, u32[]{:S(2)}, u32[]{:S(2)}) collective-permute-start(bf16[256,2048]{1,0:T(8,128)(2,1)S(1)} %copy-done.2), channel_id=1, source_target_pairs={{0,1},{1,0},{2,3},{3,2},{4,5},{5,4},{6,7},{7,6},{8,9},{9,8},{10,11... | collective-permute-start | bytes 3145736 | tf_op jit(solution)/shard_map/ppermute | solution.py:737
  214.2 24.8 %collective-permute-start.28 = (bf16[256,2048]{1,0:T(8,128)(2,1)S(1)}, bf16[256,2048]{1,0:T(8,128)(2,1)}, u32[]{:S(2)}, u32[]{:S(2)}) collective-permute-start(bf16[256,2048]{1,0:T(8,128)(2,1)S(1)} %multiply_convert_fusion.refs_0_), channel_id=1, source_target_pairs={{0,4},{4,0},{8,12},{12,8},{16,20},{20,16},{24,28},{28,24},{1,5},{5... | collective-permute-start | bytes 3145736 | tf_op jit(solution)/shard_map/ppermute | solution.py:733
  215.8 24.4 %collective-permute-start.27 = (bf16[256,2048]{1,0:T(8,128)(2,1)S(1)}, bf16[256,2048]{1,0:T(8,128)(2,1)}, u32[]{:S(2)}, u32[]{:S(2)}) collective-permute-start(bf16[256,2048]{1,0:T(8,128)(2,1)S(1)} %multiply_convert_fusion.refs_0_), channel_id=1, source_target_pairs={{0,2},{1,3},{2,0},{3,1},{4,6},{5,7},{6,4},{7,5},{8,10},{9,11},{10,... | collective-permute-start | bytes 3145736 | tf_op jit(solution)/shard_map/ppermute | solution.py:737
  241.3 16.6 %collective-permute-start.37 = (bf16[256,2048]{1,0:T(8,128)(2,1)}, bf16[256,2048]{1,0:T(8,128)(2,1)}, u32[]{:S(2)}, u32[]{:S(2)}) collective-permute-start(bf16[256,2048]{1,0:T(8,128)(2,1)} %collective-permute-done.27.refs_1_), channel_id=1, source_target_pairs={{0,1},{1,0},{2,3},{3,2},{4,5},{5,4},{6,7},{7,6},{8,9},{9,8},{10,11... | collective-permute-start | bytes 3145736 | tf_op jit(solution)/shard_map/ppermute | solution.py:737
  242.4 15.5 %collective-permute-start.36 = (bf16[256,2048]{1,0:T(8,128)(2,1)S(1)}, bf16[256,2048]{1,0:T(8,128)(2,1)}, u32[]{:S(2)}, u32[]{:S(2)}) collective-permute-start(bf16[256,2048]{1,0:T(8,128)(2,1)S(1)} %multiply_convert_fusion.refs_0_), channel_id=1, source_target_pairs={{0,1},{1,0},{2,3},{3,2},{4,5},{5,4},{6,7},{7,6},{8,9},{9,8},{10,11... | collective-permute-start | bytes 3145736 | tf_op jit(solution)/shard_map/ppermute | solution.py:737
  243.0 14.0 %collective-permute-start.35 = (bf16[256,1024]{1,0:T(8,128)(2,1)S(1)}, bf16[256,1024]{1,0:T(8,128)(2,1)}, u32[]{:S(2)}, u32[]{:S(2)}) collective-permute-start(bf16[256,1024]{1,0:T(8,128)(2,1)S(1)} %slice.227), channel_id=1, source_target_pairs={{0,2},{1,3},{2,0},{3,1},{4,6},{5,7},{6,4},{7,5},{8,10},{9,11},{10,... | collective-permute-start | bytes 1572872 | tf_op jit(solution)/shard_map/ppermute | solution.py:737
  243.4 14.5 %collective-permute-start.38 = (bf16[256,2048]{1,0:T(8,128)(2,1)}, bf16[256,2048]{1,0:T(8,128)(2,1)}, u32[]{:S(2)}, u32[]{:S(2)}) collective-permute-start(bf16[256,2048]{1,0:T(8,128)(2,1)} %collective-permute-done.28.refs_2_), channel_id=1, source_target_pairs={{0,1},{1,0},{2,3},{3,2},{4,5},{5,4},{6,7},{7,6},{8,9},{9,8},{10,11... | collective-permute-start | bytes 3145736 | tf_op jit(solution)/shard_map/ppermute | solution.py:737
  243.4 14.4 %collective-permute-start.34 = (bf16[256,1024]{1,0:T(8,128)(2,1)S(1)}, bf16[256,1024]{1,0:T(8,128)(2,1)}, u32[]{:S(2)}, u32[]{:S(2)}) collective-permute-start(bf16[256,1024]{1,0:T(8,128)(2,1)S(1)} %slice.226), channel_id=1, source_target_pairs={{0,4},{4,0},{8,12},{12,8},{16,20},{20,16},{24,28},{28,24},{1,5},{5... | collective-permute-start | bytes 1572872 | tf_op jit(solution)/shard_map/ppermute | solution.py:733
  295.1 34.9 %collective-permute-start.41 = (bf16[1,160,2048]{2,1,0:T(8,128)(2,1)S(1)}, bf16[1,160,2048]{2,1,0:T(8,128)(2,1)S(1)}, u32[]{:S(2)}, u32[]{:S(2)}) collective-permute-start(bf16[1,160,2048]{2,1,0:T(8,128)(2,1)S(1)} %get-tuple-element.167), channel_id=1, source_target_pairs={{0,8},{4,12},{8,16},{12,20},{16,24},{20,28},{24,0},{28,4},{1,9},{5... | collective-permute-start | bytes 1966088 | tf_op jit(solution)/shard_map/ppermute | solution.py:902
  300.2 29.8 %collective-permute-start.42 = (bf16[1,160,2048]{2,1,0:T(8,128)(2,1)S(1)}, bf16[1,160,2048]{2,1,0:T(8,128)(2,1)S(1)}, u32[]{:S(2)}, u32[]{:S(2)}) collective-permute-start(bf16[1,160,2048]{2,1,0:T(8,128)(2,1)S(1)} %get-tuple-element.168), channel_id=1, source_target_pairs={{0,24},{4,28},{8,0},{12,4},{16,8},{20,12},{24,16},{28,20},{1,25},{... | collective-permute-start | bytes 1966088 | tf_op jit(solution)/shard_map/ppermute | solution.py:902
  331.8 57.7 %collective-permute-start.48 = (bf16[1,160,2048]{2,1,0:T(8,128)(2,1)}, bf16[1,160,2048]{2,1,0:T(8,128)(2,1)}, u32[]{:S(2)}, u32[]{:S(2)}) collective-permute-start(bf16[1,160,2048]{2,1,0:T(8,128)(2,1)} %copy-done.33), channel_id=1, source_target_pairs={{0,16},{4,20},{8,24},{12,28},{16,0},{20,4},{24,8},{28,12},{1,17},{... | collective-permute-start | bytes 1966088 | tf_op jit(solution)/shard_map/ppermute | solution.py:902
  344.2 25.2 %collective-permute-start.44 = (bf16[2,256,1024]{2,1,0:T(8,128)(2,1)S(1)}, bf16[2,256,1024]{2,1,0:T(8,128)(2,1)S(1)}, u32[]{:S(2)}, u32[]{:S(2)}) collective-permute-start(bf16[2,256,1024]{2,1,0:T(8,128)(2,1)S(1)} %get-tuple-element.181), channel_id=1, source_target_pairs={{0,4},{4,0},{8,12},{12,8},{16,20},{20,16},{24,28},{28,24},{1,5},{5... | collective-permute-start | bytes 3145736 | tf_op jit(solution)/shard_map/ppermute | solution.py:733
  344.7 27.5 %collective-permute-start.46 = (bf16[2,256,1024]{2,1,0:T(8,128)(2,1)S(1)}, bf16[2,256,1024]{2,1,0:T(8,128)(2,1)S(1)}, u32[]{:S(2)}, u32[]{:S(2)}) collective-permute-start(bf16[2,256,1024]{2,1,0:T(8,128)(2,1)S(1)} %get-tuple-element.183), channel_id=1, source_target_pairs={{0,2},{1,3},{2,0},{3,1},{4,6},{5,7},{6,4},{7,5},{8,10},{9,11},{10,... | collective-permute-start | bytes 3145736 | tf_op jit(solution)/shard_map/ppermute | solution.py:737
  370.5 13.3 %collective-permute-start.45 = (bf16[256,1024]{1,0:T(8,128)(2,1)}, bf16[256,1024]{1,0:T(8,128)(2,1)S(1)}, u32[]{:S(2)}, u32[]{:S(2)}) collective-permute-start(bf16[256,1024]{1,0:T(8,128)(2,1)} %fusion.17), channel_id=1, source_target_pairs={{0,2},{1,3},{2,0},{3,1},{4,6},{5,7},{6,4},{7,5},{8,10},{9,11},{10,... | collective-permute-start | bytes 1572872 | tf_op jit(solution)/shard_map/ppermute | solution.py:737
  373.4 13.2 %collective-permute-start.47 = (bf16[256,1024]{1,0:T(8,128)(2,1)}, bf16[256,1024]{1,0:T(8,128)(2,1)}, u32[]{:S(2)}, u32[]{:S(2)}) collective-permute-start(bf16[256,1024]{1,0:T(8,128)(2,1)} %fusion.18), channel_id=1, source_target_pairs={{0,4},{4,0},{8,12},{12,8},{16,20},{20,16},{24,28},{28,24},{1,5},{5... | collective-permute-start | bytes 1572872 | tf_op jit(solution)/shard_map/ppermute | solution.py:733
  389.5 12.5 %collective-permute-start.49 = (bf16[4,256,2048]{2,1,0:T(8,128)(2,1)}, bf16[4,256,2048]{2,1,0:T(8,128)(2,1)}, u32[]{:S(2)}, u32[]{:S(2)}) collective-permute-start(bf16[4,256,2048]{2,1,0:T(8,128)(2,1)} %bitcast.85), channel_id=1, source_target_pairs={{0,1},{1,0},{2,3},{3,2},{4,5},{5,4},{6,7},{7,6},{8,9},{9,8},{10,11... | collective-permute-start | bytes 12582920 | tf_op jit(solution)/shard_map/ppermute | solution.py:737
  392.7 46.9 %collective-permute-start.52 = (bf16[1,256,1280]{2,1,0:T(8,128)(2,1)}, bf16[1,256,1280]{2,1,0:T(8,128)(2,1)}, u32[]{:S(2)}, u32[]{:S(2)}) collective-permute-start(bf16[1,256,1280]{2,1,0:T(8,128)(2,1)} %get-tuple-element.199), channel_id=1, source_target_pairs={{0,8},{4,12},{8,16},{12,20},{16,24},{20,28},{24,0},{28,4},{1,9},{5... | collective-permute-start | bytes 1966088 | tf_op jit(solution)/shard_map/ppermute | solution.py:902
  394.8 44.9 %collective-permute-start.53 = (bf16[1,256,1280]{2,1,0:T(8,128)(2,1)}, bf16[1,256,1280]{2,1,0:T(8,128)(2,1)}, u32[]{:S(2)}, u32[]{:S(2)}) collective-permute-start(bf16[1,256,1280]{2,1,0:T(8,128)(2,1)} %get-tuple-element.200), channel_id=1, source_target_pairs={{0,8},{4,12},{8,16},{12,20},{16,24},{20,28},{24,0},{28,4},{1,9},{5... | collective-permute-start | bytes 1966088 | tf_op jit(solution)/shard_map/ppermute | solution.py:902
  396.7 43.3 %collective-permute-start.54 = (bf16[1,256,1280]{2,1,0:T(8,128)(2,1)}, bf16[1,256,1280]{2,1,0:T(8,128)(2,1)}, u32[]{:S(2)}, u32[]{:S(2)}) collective-permute-start(bf16[1,256,1280]{2,1,0:T(8,128)(2,1)} %get-tuple-element.201), channel_id=1, source_target_pairs={{0,24},{4,28},{8,0},{12,4},{16,8},{20,12},{24,16},{28,20},{1,25},{... | collective-permute-start | bytes 1966088 | tf_op jit(solution)/shard_map/ppermute | solution.py:902
  408.5 31.6 %collective-permute-start.50 = (bf16[2,256,1024]{2,1,0:T(8,128)(2,1)}, bf16[2,256,1024]{2,1,0:T(8,128)(2,1)}, u32[]{:S(2)}, u32[]{:S(2)}) collective-permute-start(bf16[2,256,1024]{2,1,0:T(8,128)(2,1)} %get-tuple-element.196), channel_id=1, source_target_pairs={{0,4},{4,0},{8,12},{12,8},{16,20},{20,16},{24,28},{28,24},{1,5},{5... | collective-permute-start | bytes 3145736 | tf_op jit(solution)/shard_map/ppermute | solution.py:733
  409.0 31.1 %collective-permute-start.51 = (bf16[2,256,1024]{2,1,0:T(8,128)(2,1)}, bf16[2,256,1024]{2,1,0:T(8,128)(2,1)}, u32[]{:S(2)}, u32[]{:S(2)}) collective-permute-start(bf16[2,256,1024]{2,1,0:T(8,128)(2,1)} %get-tuple-element.198), channel_id=1, source_target_pairs={{0,2},{1,3},{2,0},{3,1},{4,6},{5,7},{6,4},{7,5},{8,10},{9,11},{10,... | collective-permute-start | bytes 3145736 | tf_op jit(solution)/shard_map/ppermute | solution.py:737
  441.6 18.9 %collective-permute-start.58 = (bf16[2,256,384]{2,1,0:T(8,128)(2,1)}, bf16[2,256,384]{2,1,0:T(8,128)(2,1)S(1)}, u32[]{:S(2)}, u32[]{:S(2)}) collective-permute-start(bf16[2,256,384]{2,1,0:T(8,128)(2,1)} %copy-done.34), channel_id=1, source_target_pairs={{2,0},{3,1},{6,4},{7,5},{10,8},{11,9},{14,12},{15,13},{18,16},{19,... | collective-permute-start | bytes 1179656 | tf_op jit(solution)/shard_map/ppermute | solution.py:959
  444.5 36.2 %collective-permute-start.56 = (bf16[256,1024]{1,0:T(8,128)(2,1)S(1)}, bf16[256,1024]{1,0:T(8,128)(2,1)S(1)}, u32[]{:S(2)}, u32[]{:S(2)}) collective-permute-start(bf16[256,1024]{1,0:T(8,128)(2,1)S(1)} %fusion.20), channel_id=1, source_target_pairs={{0,4},{4,0},{8,12},{12,8},{16,20},{20,16},{24,28},{28,24},{1,5},{5... | collective-permute-start | bytes 1572872 | tf_op jit(solution)/shard_map/ppermute | solution.py:733
  446.8 35.2 %collective-permute-start.55 = (bf16[256,1024]{1,0:T(8,128)(2,1)S(1)}, bf16[256,1024]{1,0:T(8,128)(2,1)S(1)}, u32[]{:S(2)}, u32[]{:S(2)}) collective-permute-start(bf16[256,1024]{1,0:T(8,128)(2,1)S(1)} %fusion.19), channel_id=1, source_target_pairs={{0,2},{1,3},{2,0},{3,1},{4,6},{5,7},{6,4},{7,5},{8,10},{9,11},{10,... | collective-permute-start | bytes 1572872 | tf_op jit(solution)/shard_map/ppermute | solution.py:737
  449.6 35.4 %collective-permute-start.59 = (bf16[1,256,1280]{2,1,0:T(8,128)(2,1)S(1)}, bf16[1,256,1280]{2,1,0:T(8,128)(2,1)S(1)}, u32[]{:S(2)}, u32[]{:S(2)}) collective-permute-start(bf16[1,256,1280]{2,1,0:T(8,128)(2,1)S(1)} %copy-done.32), channel_id=1, source_target_pairs={{0,16},{4,20},{8,24},{12,28},{16,0},{20,4},{24,8},{28,12},{1,17},{... | collective-permute-start | bytes 1966088 | tf_op jit(solution)/shard_map/ppermute | solution.py:902
  486.9 16.2 %collective-permute-start.61 = (bf16[1,256,1280]{2,1,0:T(8,128)(2,1)S(1)}, bf16[1,256,1280]{2,1,0:T(8,128)(2,1)S(1)}, u32[]{:S(2)}, u32[]{:S(2)}) collective-permute-start(bf16[1,256,1280]{2,1,0:T(8,128)(2,1)S(1)} %copy-done.30), channel_id=1, source_target_pairs={{0,24},{4,28},{8,0},{12,4},{16,8},{20,12},{24,16},{28,20},{1,25},{... | collective-permute-start | bytes 1966088 | tf_op jit(solution)/shard_map/ppermute | solution.py:902
  503.8 30.3 %collective-permute-start.64 = (bf16[1,256,1280]{2,1,0:T(8,128)(2,1)S(1)}, bf16[1,256,1280]{2,1,0:T(8,128)(2,1)S(1)}, u32[]{:S(2)}, u32[]{:S(2)}) collective-permute-start(bf16[1,256,1280]{2,1,0:T(8,128)(2,1)S(1)} %copy-done.28), channel_id=1, source_target_pairs={{0,16},{4,20},{8,24},{12,28},{16,0},{20,4},{24,8},{28,12},{1,17},{... | collective-permute-start | bytes 1966088 | tf_op jit(solution)/shard_map/ppermute | solution.py:902
  503.9 31.8 %collective-permute-start.62 = (bf16[4,64,2432]{2,1,0:T(8,128)(2,1)S(1)}, bf16[4,64,2432]{2,1,0:T(8,128)(2,1)S(1)}, u32[]{:S(2)}, u32[]{:S(2)}) collective-permute-start(bf16[4,64,2432]{2,1,0:T(8,128)(2,1)S(1)} %get-tuple-element.221), channel_id=1, source_target_pairs={{0,2},{1,3},{2,0},{3,1},{4,6},{5,7},{6,4},{7,5},{8,10},{9,11},{10,... | collective-permute-start | bytes 3735560 | tf_op jit(solution)/shard_map/ppermute | solution.py:737
  505.5 31.5 %collective-permute-start.63 = (bf16[4,64,2432]{2,1,0:T(8,128)(2,1)S(1)}, bf16[4,64,2432]{2,1,0:T(8,128)(2,1)S(1)}, u32[]{:S(2)}, u32[]{:S(2)}) collective-permute-start(bf16[4,64,2432]{2,1,0:T(8,128)(2,1)S(1)} %get-tuple-element.222), channel_id=1, source_target_pairs={{0,4},{4,0},{8,12},{12,8},{16,20},{20,16},{24,28},{28,24},{1,5},{5... | collective-permute-start | bytes 3735560 | tf_op jit(solution)/shard_map/ppermute | solution.py:733
  538.2 23.0 %collective-permute-start.65 = (bf16[2,64,2432]{2,1,0:T(8,128)(2,1)}, bf16[2,64,2432]{2,1,0:T(8,128)(2,1)}, u32[]{:S(2)}, u32[]{:S(2)}) collective-permute-start(bf16[2,64,2432]{2,1,0:T(8,128)(2,1)} %add_convert_fusion.10), channel_id=1, source_target_pairs={{0,4},{4,0},{8,12},{12,8},{16,20},{20,16},{24,28},{28,24},{1,5},{5... | collective-permute-start | bytes 1867784 | tf_op jit(solution)/shard_map/ppermute | solution.py:733
  544.4 18.5 %collective-permute-start.66 = (bf16[2,64,2432]{2,1,0:T(8,128)(2,1)S(1)}, bf16[2,64,2432]{2,1,0:T(8,128)(2,1)S(1)}, u32[]{:S(2)}, u32[]{:S(2)}) collective-permute-start(bf16[2,64,2432]{2,1,0:T(8,128)(2,1)S(1)} %add_convert_fusion.9), channel_id=1, source_target_pairs={{0,2},{1,3},{2,0},{3,1},{4,6},{5,7},{6,4},{7,5},{8,10},{9,11},{10,... | collective-permute-start | bytes 1867784 | tf_op jit(solution)/shard_map/ppermute | solution.py:737
  549.6 13.6 %collective-permute-start.70 = (bf16[4,64,1280]{2,1,0:T(8,128)(2,1)S(1)}, bf16[4,64,1280]{2,1,0:T(8,128)(2,1)S(1)}, u32[]{:S(2)}, u32[]{:S(2)}) collective-permute-start(bf16[4,64,1280]{2,1,0:T(8,128)(2,1)S(1)} %get-tuple-element.232), channel_id=1, source_target_pairs={{0,1},{1,0},{2,3},{3,2},{4,5},{5,4},{6,7},{7,6},{8,9},{9,8},{10,11... | collective-permute-start | bytes 1966088 | tf_op jit(solution)/shard_map/ppermute | solution.py:737
  565.8 18.8 %collective-permute-start.76 = (bf16[2,2,64,1280]{3,2,1,0:T(8,128)(2,1)S(1)}, bf16[2,2,64,1280]{3,2,1,0:T(8,128)(2,1)S(1)}, u32[]{:S(2)}, u32[]{:S(2)}) collective-permute-start(bf16[2,2,64,1280]{3,2,1,0:T(8,128)(2,1)S(1)} %get-tuple-element.252), channel_id=1, source_target_pairs={{0,2},{1,3},{2,0},{3,1},{4,6},{5,7},{6,4},{7,5},{8,10},{9,11},{10,... | collective-permute-start | bytes 1966088 | tf_op jit(solution)/shard_map/ppermute | solution.py:737
  568.2 31.9 %collective-permute-start.75 = (bf16[64,2432]{1,0:T(8,128)(2,1)}, bf16[64,2432]{1,0:T(8,128)(2,1)S(1)}, u32[]{:S(2)}, u32[]{:S(2)}) collective-permute-start(bf16[64,2432]{1,0:T(8,128)(2,1)} %slice_bitcast_fusion.3), channel_id=1, source_target_pairs={{0,16},{4,20},{8,24},{12,28},{16,0},{20,4},{24,8},{28,12},{1,17},{... | collective-permute-start | bytes 933896 | tf_op jit(solution)/shard_map/ppermute | solution.py:750
  570.9 29.2 %collective-permute-start.73 = (bf16[64,2432]{1,0:T(8,128)(2,1)}, bf16[64,2432]{1,0:T(8,128)(2,1)S(1)}, u32[]{:S(2)}, u32[]{:S(2)}) collective-permute-start(bf16[64,2432]{1,0:T(8,128)(2,1)} %get-tuple-element.265), channel_id=1, source_target_pairs={{0,8},{4,12},{8,16},{12,20},{16,24},{20,28},{24,0},{28,4},{1,9},{5... | collective-permute-start | bytes 933896 | tf_op jit(solution)/shard_map/ppermute | solution.py:750
  572.4 28.5 %collective-permute-start.74 = (bf16[64,2432]{1,0:T(8,128)(2,1)}, bf16[64,2432]{1,0:T(8,128)(2,1)}, u32[]{:S(2)}, u32[]{:S(2)}) collective-permute-start(bf16[64,2432]{1,0:T(8,128)(2,1)} %get-tuple-element.266), channel_id=1, source_target_pairs={{0,24},{4,28},{8,0},{12,4},{16,8},{20,12},{24,16},{28,20},{1,25},{... | collective-permute-start | bytes 933896 | tf_op jit(solution)/shard_map/ppermute | solution.py:750
  585.6 35.5 %collective-permute-start.77 = (bf16[2,2,64,1280]{3,2,1,0:T(8,128)(2,1)}, bf16[2,2,64,1280]{3,2,1,0:T(8,128)(2,1)S(1)}, u32[]{:S(2)}, u32[]{:S(2)}) collective-permute-start(bf16[2,2,64,1280]{3,2,1,0:T(8,128)(2,1)} %get-tuple-element.250), channel_id=1, source_target_pairs={{0,4},{4,0},{8,12},{12,8},{16,20},{20,16},{24,28},{28,24},{1,5},{5... | collective-permute-start | bytes 1966088 | tf_op jit(solution)/shard_map/ppermute | solution.py:733
  (105 other events, 948.5 us)
Sparse Core Ops, SparseCore 0:
  72.2 55.5 all-gather.2
  129.4 96.8 all-gather.4
  486.0 133.3 reduce-scatter.1

commit v5 on v4

--- a/solution.py
+++ b/solution.py
@@ -841,24 +841,22 @@
     qkv_mine = rounds.leave(jnp.stack([qkv_held[r] for r in [0] + sends]))
     units = rounds.leave(exchange_near(exchange_chips(units), places))
 
-    qkv_mine, late_out, units, down_piece = rounds.enter(qkv_mine, w_out, units, w_down)
-    out_held = far_gather(late_out, places)
-    out_mine = rounds.leave(jnp.stack([out_held[r] for r in [0] + sends]))
+    qkv_mine, units, down_piece = rounds.enter(qkv_mine, units, w_down)
     qkv_a, qkv_b = plane_first(qkv_mine, places)
     qkv_a, qkv_b = rounds.leave(qkv_a, qkv_b)
     down_piece = jnp.pad(down_piece, ((0, ff_block - ff_rows), (0, 0)))
     my_down = gather_far(down_piece)
     both_piece = rounds.leave(exchange_units(units, places))
 
-    qkv_a, qkv_b, out_mine, both_piece = rounds.enter(qkv_a, qkv_b, out_mine, both_piece)
+    qkv_a, qkv_b, late_out, both_piece = rounds.enter(qkv_a, qkv_b, w_out, both_piece)
+    out_held = far_gather(late_out, places)
+    out_mine = rounds.leave(jnp.stack([out_held[r] for r in [0] + sends]))
     qkv_a, qkv_b = rounds.leave(*plane_second(qkv_a, qkv_b, places))
-    out_a, out_b = rounds.leave(*plane_first(out_mine, places))
     my_both = gather_far(both_piece.reshape(8 * shard, 2 * ff_width))
 
-    qkv_a, qkv_b, out_a, out_b = rounds.enter(qkv_a, qkv_b, out_a, out_b)
+    qkv_a, qkv_b, out_mine = rounds.enter(qkv_a, qkv_b, out_mine)
     full_qkv = plane_last(qkv_a, qkv_b, sends, places).reshape(width, -1)
-    out_a, out_b = plane_second(*gated((out_a, out_b), full_qkv), places)
-    full_qkv = gated(full_qkv, my_down)
+    out_first = plane_first(gated(out_mine, full_qkv), places)
 
     gain_table = full_qkv[:, full_qkv.shape[1] - LANES :]
     pick = (
@@ -874,14 +872,14 @@
     queries, kv = head_prep(pre, cosine, sine, head_gains)
     ahead_one = [(i, i + 1) for i in range(3)]
     ahead_two = [(i, i + 2) for i in range(2)]
-    kv = gated(kv, (out_a, out_b))
+    kv = gated(kv, my_down)
     kv_one = lax.ppermute(kv, "fsdp", ahead_one)
     kv_two = lax.ppermute(kv, "fsdp", ahead_two)
-    pieces = gather_first(gated(cotangent, kv_two), places)
+    out_a, out_b = plane_second(*gated(out_first, (kv_one, kv_two)), places)
     mixed = attend(queries, kv_two, kv_one, kv, rel)
-    out_a, out_b, _ = gated((out_a, out_b, kv_one), kv_two)
+    pieces = gather_first(gated(cotangent, (out_a, out_b, mixed)), places)
     full_out = plane_last(out_a, out_b, sends, places).reshape(-1, width)
-    pieces = gather_second(*gated(pieces, mixed), places)
+    pieces = gather_second(*gated(pieces, full_out), places)
     hidden = x + product(mixed, full_out)
     h_inverse = lax.rsqrt(jnp.mean(hidden * hidden, axis=-1, keepdims=True) + EPSILON)
     ffn_mine = (hidden * h_inverse * ffn_row).astype(BF16)
@@ -945,13 +943,14 @@
     gq, gkv_two, gkv_one, gkv = rounds.leave(
         *attend_back(queries, kv_two, kv_one, kv, rel, grad_mixed)
     )
+    grad_hidden_low = rounds.leave(grad_hidden_low)
+    down_grad = rounds.leave(total_of(d_first + d_second)[0, :ff_rows])
+
+    u_blocks[sent - 2], gkv_one, gkv_two, gq, gkv, grad_hidden_low, *out_steps = rounds.enter(
+        u_blocks[sent - 2], gkv_one, gkv_two, gq, gkv, grad_hidden_low, *out_steps
+    )
     term_out = left_transposed(mixed, grad_hidden_low).astype(BF16)
-    term_out = rounds.leave(term_out)
-    down_grad = rounds.leave(total_of(d_first + d_second)[0, :ff_rows])
-
-    u_blocks[sent - 2], gkv_one, gkv_two, gq, gkv, term_out, *out_steps = rounds.enter(
-        u_blocks[sent - 2], gkv_one, gkv_two, gq, gkv, term_out, *out_steps
-    )
+    gq, term_out = lax.optimization_barrier((gq, term_out))
     out_grad = lax.psum_scatter(term_out, BOTH, scatter_dimension=0, tiled=True).astype(F32)
     u_near = far_sent(u_blocks, [sent - 2], 2)
     rounds.leave(*u_near)

time: 640 us -> 652 us (1.019)
  starting transfers between devices: 84.3 us -> 97.3 us
    ppermute x35, waiting for transfers between devices: 86.1 us -> 64.4 us  [member_swap(): return lax.ppermute(value, 'fsdp', swap_pairs(4, bit))]
    ppermute x16, waiting for transfers between devices: 43.8 us -> 58.4 us  [near_swap(): return lax.ppermute(value, 'dp', swap_pairs(places.size, 1))]
    ppermute x9, starting transfers between devices: 16.8 us -> 25.7 us  [far_sent(): lax.ppermute(blocks[k], 'dp', far_pairs(dp_size, order[k // cut]))]
    ppermute x6, waiting for transfers between devices: 20.9 us -> 28.9 us  [far_gather(): held[r] = lax.ppermute(piece, 'dp', far_pairs(places.size, r))]
    ppermute x9, waiting for transfers between devices: 31.9 us -> 38.8 us  [far_sent(): lax.ppermute(blocks[k], 'dp', far_pairs(dp_size, order[k // cut]))]
    ppermute x1, waiting for transfers between devices: 9.94 us -> 3.28 us  [local(): got_two = lax.ppermute(gkv_two, 'fsdp', [(b, a) for a, b in ahead_two])]
    unnamed x177 -> x204, local copies, waits for them, and re-layouts: 15.3 us -> 15.4 us
  transfers between devices with their start and end apart: 81 -> 81, of which waited for: 40 -> 41; matrix products, arithmetic and copies ran while one was open for 18% -> 19% of each run, Pallas kernels for 20% -> 20%
where the time goes in v5:
time: 652 us; the launch traced here: 643 us
  waiting for transfers between devices  235 us (36%)
  Pallas kernels  152 us (23%)
  starting transfers between devices  97.3 us (15%)
  matrix products  67.5 us (10%)
  other arithmetic  49.8 us (8%)
  local copies, waits for them, and re-layouts  25.7 us (4%)
  between operations  15.9 us (2%)
    ppermute x35, waiting for transfers between devices, member_swap(): return lax.ppermute(value, 'fsdp', swap_pairs(4, bit))  64.4 us
    ppermute x16, waiting for transfers between devices, near_swap(): return lax.ppermute(value, 'dp', swap_pairs(places.size, 1))  58.4 us
    ppermute x9, waiting for transfers between devices, far_sent(): lax.ppermute(blocks[k], 'dp', far_pairs(dp_size, order[k // cut]))  38.8 us
    dot_general x4, matrix products, left_transposed(): lax.dot_general(left, right, (((0,), (0,)), ((), ())), preferred_element_...  35.1 us
    pallas_call x1, Pallas kernels, feed_back(): pl.pallas_call(feed_back_kernel, grid=(steps,), in_specs=[pl.BlockSpec((t...  29.7 us
    ppermute x6, waiting for transfers between devices, far_gather(): held[r] = lax.ppermute(piece, 'dp', far_pairs(places.size, r))  28.9 us
    ppermute x35, starting transfers between devices, member_swap(): return lax.ppermute(value, 'fsdp', swap_pairs(4, bit))  27.1 us
    ppermute x9, starting transfers between devices, far_sent(): lax.ppermute(blocks[k], 'dp', far_pairs(dp_size, order[k // cut]))  25.7 us
  transfers between devices with their start and end apart: 81, of which 41 were waited for; matrix products, arithmetic and copies ran while one was open for 19% of the time, Pallas kernels for 20%

profile of v5, /device:TPU:0, one launch (start us, length us, event | category | flops | bytes accessed | tf_op | source)
XLA Modules:
  0.0 643.1 jit_solution(8233285740316795063)
XLA Ops:
  10.6 3.0 collective-permute-start.3
  13.8 3.7 collective-permute-start.1
  18.5 9.9 %collective-permute-done.3 = bf16[4,64,1280]{2,1,0:T(8,128)(2,1)S(1)} collective-permute-done((bf16[4,64,1280]{2,1,0:T(8,128)(2,1)S(1)}, bf16[4,64,1280]{2,1,0:T(8,128)(2,1)S(1)}, u32[]{:S(2)}, u32[]{:S(2)}) %collective-permute-start.3) | collective-permute-done | bytes 655392 | tf_op jit(solution)/shard_map/ppermute | solution.py:737
  30.3 2.6 collective-permute-done
  32.9 10.8 %collective-permute-done.2 = bf16[64,2432]{1,0:T(8,128)(2,1)S(1)} collective-permute-done((bf16[64,2432]{1,0:T(8,128)(2,1)S(1)}, bf16[64,2432]{1,0:T(8,128)(2,1)S(1)}, u32[]{:S(2)}, u32[]{:S(2)}) %collective-permute-start.2) | collective-permute-done | bytes 311328 | tf_op jit(solution)/shard_map/ppermute | solution.py:529
  47.9 11.1 %collective-permute-done.6 = bf16[2,64,2432]{2,1,0:T(8,128)(2,1)S(1)} collective-permute-done((bf16[2,64,2432]{2,1,0:T(8,128)(2,1)S(1)}, bf16[2,64,2432]{2,1,0:T(8,128)(2,1)S(1)}, u32[]{:S(2)}, u32[]{:S(2)}) %collective-permute-start.6) | collective-permute-done | bytes 622624 | tf_op jit(solution)/shard_map/ppermute | solution.py:737
  60.4 4.1 place.3
  69.2 2.7 collective-permute-start.12
  73.8 15.3 %collective-permute-done.12 = bf16[48,2048]{1,0:T(8,128)(2,1)S(1)} collective-permute-done((bf16[48,2048]{1,0:T(8,128)(2,1)S(1)}, bf16[48,2048]{1,0:T(8,128)(2,1)S(1)}, u32[]{:S(2)}, u32[]{:S(2)}) %collective-permute-start.12) | collective-permute-done | bytes 196640 | tf_op jit(solution)/shard_map/ppermute | solution.py:529
  89.5 2.9 collective-permute-done.8
  94.0 3.4 pad_maximum_fusion.1.refs_2_
  102.7 3.1 collective-permute-done.13.refs_1_
  106.0 8.4 %place.4 = bf16[32,64,2432]{2,1,0:T(8,128)(2,1)} custom-call(s32[32]{0:T(128)S(1)} %stack.408.slots, bf16[8,64,2432]{2,1,0:T(8,128)(2,1)S(1)} %pad_maximum_fusion.refs_0_, bf16[8,64,2432]{2,1,0:T(8,128)(2,1)} %collective-permute-done.13.refs_1_, bf16[8,64,2432]{2,1,0:T(8,128)(2,1)} %pad_maximum_fusion.1.refs_2_, ...), custom_call_target="tpu_custom_call" | custom-call | bytes 19922944 | tf_op jit(solution)/shard_map/place/pallas_call | solution.py:456
  119.8 5.8 fusion.25.pre_ref
  130.8 3.0 collective-permute-start.15
  136.3 7.1 %collective-permute-done.15.two_ref = bf16[2,256,384]{2,1,0:T(8,128)(2,1)S(1)} collective-permute-done((bf16[2,256,384]{2,1,0:T(8,128)(2,1)}, bf16[2,256,384]{2,1,0:T(8,128)(2,1)S(1)}, u32[]{:S(2)}, u32[]{:S(2)}) %collective-permute-start.15) | collective-permute-done | bytes 393248 | tf_op jit(solution)/shard_map/ppermute | solution.py:877
  144.4 2.4 collective-permute-start.19
  146.9 16.2 %collective-permute-done.21 = bf16[4,48,2048]{2,1,0:T(8,128)(2,1)S(1)} collective-permute-done((bf16[4,48,2048]{2,1,0:T(8,128)(2,1)S(1)}, bf16[4,48,2048]{2,1,0:T(8,128)(2,1)S(1)}, u32[]{:S(2)}, u32[]{:S(2)}) %collective-permute-start.21) | collective-permute-done | bytes 786464 | tf_op jit(solution)/shard_map/ppermute | solution.py:733
  165.6 11.8 %attend.1 = bf16[256,1536]{1,0:T(8,128)(2,1)S(1)} custom-call(bf16[256,1536]{1,0:T(8,128)(2,1)S(1)} %get-tuple-element.132.q_ref, bf16[2,256,384]{2,1,0:T(8,128)(2,1)S(1)} %collective-permute-done.15.two_ref, bf16[2,256,384]{2,1,0:T(8,128)(2,1)S(1)} %collective-permute-done.16.one_ref, bf16[2,256,384]{2,1,0:T(8,128)(2,1)S(1)} %copy-done.8, ...), custom_call_target="tpu_custom_call" | custom-call | tf_op jit(solution)/shard_map/attend/pallas_call | solution.py:169
  181.9 10.7 %place.5 = bf16[32,48,2048]{2,1,0:T(8,128)(2,1)} custom-call(s32[32]{0:T(128)S(1)} %stack.408.slots, bf16[8,48,2048]{2,1,0:T(8,128)(2,1)S(1)} %constant_dynamic-update-slice_fusion.refs_0_, bf16[8,48,2048]{2,1,0:T(8,128)(2,1)S(1)} %collective-permute-done.20.refs_1_, bf16[8,48,2048]{2,1,0:T(8,128)(2,1)S(1)} %constant_dynamic-update-slice_fusion.2.refs_2_, ...), custom_call_target="tpu_custom_call" | custom-call | bytes 12582912 | tf_op jit(solution)/shard_map/place/pallas_call | solution.py:456
  192.6 10.0 %collective-permute-done.24.refs_2_ = bf16[256,2048]{1,0:T(8,128)(2,1)S(1)} collective-permute-done((bf16[256,2048]{1,0:T(8,128)(2,1)S(1)}, bf16[256,2048]{1,0:T(8,128)(2,1)S(1)}, u32[]{:S(2)}, u32[]{:S(2)}) %collective-permute-start.24) | collective-permute-done | bytes 1048608 | tf_op jit(solution)/shard_map/ppermute | solution.py:733
  207.2 4.7 multiply_reduce_fusion.2
  212.2 6.3 collective-permute-done.26.refs_4_
  223.8 5.6 assemble.2
  229.4 14.7 %collective-permute-done.28.refs_2_ = bf16[256,2048]{1,0:T(8,128)(2,1)} collective-permute-done((bf16[256,2048]{1,0:T(8,128)(2,1)S(1)}, bf16[256,2048]{1,0:T(8,128)(2,1)}, u32[]{:S(2)}, u32[]{:S(2)}) %collective-permute-start.28) | collective-permute-done | bytes 1048608 | tf_op jit(solution)/shard_map/ppermute | solution.py:733
  249.2 12.2 %collective-permute-done.35.refs_4_ = bf16[256,1024]{1,0:T(8,128)(2,1)S(1)} collective-permute-done((bf16[256,1024]{1,0:T(8,128)(2,1)S(1)}, bf16[256,1024]{1,0:T(8,128)(2,1)S(1)}, u32[]{:S(2)}, u32[]{:S(2)}) %collective-permute-start.35) | collective-permute-done | bytes 524320 | tf_op jit(solution)/shard_map/ppermute | solution.py:737
  264.8 6.3 assemble.3
  271.1 16.7 %feed.1 = (bf16[2048,640]{1,0:T(8,128)(2,1)S(1)}, bf16[2048,1280]{1,0:T(8,128)(2,1)}) custom-call(bf16[2048,2048]{1,0:T(8,128)(2,1)} %bitcast.190, bf16[2048,1280]{1,0:T(8,128)(2,1)} %all-gather.5.cloned.1.call-done.both_ref), custom_call_target="tpu_custom_call" | custom-call | flops 10737418240 | bytes 21495808 | tf_op jit(solution)/shard_map/feed/pallas_call | solution.py:244
  289.3 8.0 %convolution_convert_fusion.5 = bf16[640,2048]{1,0:T(8,128)(2,1)S(1)} fusion(bf16[2048,640]{1,0:T(8,128)(2,1)S(1)} %get-tuple-element.178, bf16[2048,2048]{1,0:T(8,128)(2,1)} %bitcast.188), kind=kOutput, calls=%fused_computation.11 | convolution fusion | flops 5370019840 | bytes 13631488 | tf_op jit(solution)/shard_map/dot_general | solution.py:32
  297.4 2.3 pick.4
  299.7 11.5 %collective-permute-start.41 = (bf16[1,160,2048]{2,1,0:T(8,128)(2,1)S(1)}, bf16[1,160,2048]{2,1,0:T(8,128)(2,1)S(1)}, u32[]{:S(2)}, u32[]{:S(2)}) collective-permute-start(bf16[1,160,2048]{2,1,0:T(8,128)(2,1)S(1)} %get-tuple-element.161), channel_id=1, source_target_pairs={{0,8},{4,12},{8,16},{12,20},{16,24},{20,28},{24,0},{28,4},{1,9},{5... | collective-permute-start | bytes 1966088 | tf_op jit(solution)/shard_map/ppermute | solution.py:900
  311.2 29.7 %feed_back.1 = (bf16[2048,1280]{1,0:T(8,128)(2,1)}, bf16[4,256,2048]{2,1,0:T(8,128)(2,1)}, bf16[4,256,2048]{2,1,0:T(8,128)(2,1)}) custom-call(bf16[2048,2048]{1,0:T(8,128)(2,1)} %bitcast.189, bf16[640,2048]{1,0:T(8,128)(2,1)S(1)} %copy-done.30, bf16[2048,1280]{1,0:T(8,128)(2,1)} %get-tuple-element.157.slopes_ref, ...), custom_call_target="tpu_custom_call" | custom-call | flops 16106127360 | bytes 43515904 | tf_op jit(solution)/shard_map/feed_back/pallas_call | solution.py:296
  342.7 3.8 collective-permute-start.48
  346.5 3.6 collective-permute-done.43.got_ref
  350.1 5.0 merge.2
  357.1 16.8 %convolution_convert_fusion.2 = bf16[2048,1280]{1,0:T(8,128)(2,1)} fusion(bf16[2048,2048]{1,0:T(8,128)(2,1)} %bitcast.191, bf16[2048,1280]{1,0:T(8,128)(2,1)} %get-tuple-element.163), kind=kOutput, calls=%fused_computation.2 | convolution fusion | flops 10740039680 | bytes 18874368 | tf_op jit(solution)/shard_map/dot_general | solution.py:32
  373.9 5.2 convolution_convert_fusion.3
  384.6 5.0 convolution_convert_fusion.4
  389.6 4.3 pick.5
  400.2 3.0 add_bitcast_fusion
  403.2 2.4 collective-permute-start.52
  409.5 2.7 multiply_reduce_fusion
  412.2 5.1 merge.3
  419.1 4.7 convolution_convert_fusion.6.gm_ref
  424.0 18.0 %attend_back.1 = (f32[256,1536]{1,0:T(8,128)S(1)}, bf16[2,256,384]{2,1,0:T(8,128)(2,1)}, bf16[2,256,384]{2,1,0:T(8,128)(2,1)}, f32[2,256,384]{2,1,0:T(8,128)S(1)}) custom-call(bf16[256,1536]{1,0:T(8,128)(2,1)S(1)} %copy-done.4, bf16[2,256,384]{2,1,0:T(8,128)(2,1)S(1)} %copy-done.13, bf16[2,256,384]{2,1,0:T(8,128)(2,1)S(1)} %copy-done.11, ...), custom_call_target="tpu_custom_call" | custom-call | tf_op jit(solution)/shard_map/attend_back/pallas_call | solution.py:214
  442.0 8.6 %collective-permute-done.54 = bf16[1,256,1280]{2,1,0:T(8,128)(2,1)} collective-permute-done((bf16[1,256,1280]{2,1,0:T(8,128)(2,1)}, bf16[1,256,1280]{2,1,0:T(8,128)(2,1)}, u32[]{:S(2)}, u32[]{:S(2)}) %collective-permute-start.54) | collective-permute-done | bytes 655392 | tf_op jit(solution)/shard_map/ppermute | solution.py:900
  457.7 3.4 collective-permute-start.55
  463.1 4.5 convolution_convert_fusion.1
  467.6 3.3 collective-permute-done.58.two_ref
  473.7 6.0 head_back.1
  479.8 5.8 convolution_convert_fusion
  485.6 8.5 %pick.6 = (bf16[16,64,2432]{2,1,0:T(8,128)(2,1)}, bf16[16,64,2432]{2,1,0:T(8,128)(2,1)}) custom-call(s32[32]{0:T(128)S(1)} %stack.475.slots, bf16[32,64,2432]{2,1,0:T(8,128)(2,1)} %bitcast.184), custom_call_target="tpu_custom_call" | custom-call | bytes 19922944 | tf_op jit(solution)/shard_map/pick/pallas_call | solution.py:494
  503.7 5.6 fusion.36
  509.4 3.4 add_convert_fusion
  512.9 3.4 collective-permute-done.61
  520.3 26.9 %collective-permute-done.64 = bf16[1,256,1280]{2,1,0:T(8,128)(2,1)S(1)} collective-permute-done((bf16[1,256,1280]{2,1,0:T(8,128)(2,1)S(1)}, bf16[1,256,1280]{2,1,0:T(8,128)(2,1)S(1)}, u32[]{:S(2)}, u32[]{:S(2)}) %collective-permute-start.64) | collective-permute-done | bytes 655392 | tf_op jit(solution)/shard_map/ppermute | solution.py:900
  559.6 4.1 pick.7
  563.8 10.9 %collective-permute-done.65 = bf16[2,64,2432]{2,1,0:T(8,128)(2,1)S(1)} collective-permute-done((bf16[2,64,2432]{2,1,0:T(8,128)(2,1)}, bf16[2,64,2432]{2,1,0:T(8,128)(2,1)S(1)}, u32[]{:S(2)}, u32[]{:S(2)}) %collective-permute-start.65) | collective-permute-done | bytes 622624 | tf_op jit(solution)/shard_map/ppermute | solution.py:733
  581.6 2.7 collective-permute-start.75
  585.7 2.4 collective-permute-start.74
  589.3 8.2 %collective-permute-done.76 = bf16[2,2,64,1280]{3,2,1,0:T(8,128)(2,1)S(1)} collective-permute-done((bf16[2,2,64,1280]{3,2,1,0:T(8,128)(2,1)S(1)}, bf16[2,2,64,1280]{3,2,1,0:T(8,128)(2,1)S(1)}, u32[]{:S(2)}, u32[]{:S(2)}) %collective-permute-start.76) | collective-permute-done | bytes 655392 | tf_op jit(solution)/shard_map/ppermute | solution.py:737
  599.0 14.6 %collective-permute-done.75 = bf16[64,2432]{1,0:T(8,128)(2,1)S(1)} collective-permute-done((bf16[64,2432]{1,0:T(8,128)(2,1)}, bf16[64,2432]{1,0:T(8,128)(2,1)S(1)}, u32[]{:S(2)}, u32[]{:S(2)}) %collective-permute-start.75) | collective-permute-done | bytes 311328 | tf_op jit(solution)/shard_map/ppermute | solution.py:750
  616.5 15.3 %reduce-scatter.2.cloned.1.call-done = bf16[48,2048]{1,0:T(8,128)(2,1)} async-done(((bf16[1536,2048]{1,0:T(8,128)(2,1)}), bf16[48,2048]{1,0:T(8,128)(2,1)}) %reduce-scatter.2.cloned.1.call-update) | async-done | bytes 196624 | tf_op jit(solution)/shard_map/reduce_scatter | solution.py:954
  633.7 2.5 join_units.1
  (432 shorter events, 141.9 us)
Async XLA Ops:
  7.2 121.8 %all-gather.3.cloned.1.call-start = ((), (), s32[]{:S(2)}) async-start(), calls=%async_computation.1 | async-start | bytes 3276800 | tf_op jit(solution)/shard_map/all_gather | solution.py:848
  10.6 17.7 %collective-permute-start.3 = (bf16[4,64,1280]{2,1,0:T(8,128)(2,1)S(1)}, bf16[4,64,1280]{2,1,0:T(8,128)(2,1)S(1)}, u32[]{:S(2)}, u32[]{:S(2)}) collective-permute-start(bf16[4,64,1280]{2,1,0:T(8,128)(2,1)S(1)} %get-tuple-element.254), channel_id=1, source_target_pairs={{0,2},{1,3},{2,0},{3,1},{4,6},{5,7},{6,4},{7,5},{8,10},{9,11},{10,... | collective-permute-start | bytes 1966088 | tf_op jit(solution)/shard_map/ppermute | solution.py:737
  13.8 16.5 %collective-permute-start.1 = (bf16[64,2432]{1,0:T(8,128)(2,1)S(1)}, bf16[64,2432]{1,0:T(8,128)(2,1)S(1)}, u32[]{:S(2)}, u32[]{:S(2)}) collective-permute-start(bf16[64,2432]{1,0:T(8,128)(2,1)S(1)} %fusion.23), channel_id=1, source_target_pairs={{0,24},{4,28},{8,0},{12,4},{16,8},{20,12},{24,16},{28,20},{1,25},{... | collective-permute-start | bytes 933896 | tf_op jit(solution)/shard_map/ppermute | solution.py:529
  17.5 15.5 %collective-permute-start = (bf16[64,2432]{1,0:T(8,128)(2,1)S(1)}, bf16[64,2432]{1,0:T(8,128)(2,1)S(1)}, u32[]{:S(2)}, u32[]{:S(2)}) collective-permute-start(bf16[64,2432]{1,0:T(8,128)(2,1)S(1)} %fusion.23), channel_id=1, source_target_pairs={{0,8},{4,12},{8,16},{12,20},{16,24},{20,28},{24,0},{28,4},{1,9},{5... | collective-permute-start | bytes 933896 | tf_op jit(solution)/shard_map/ppermute | solution.py:529
  17.5 26.2 %collective-permute-start.2 = (bf16[64,2432]{1,0:T(8,128)(2,1)S(1)}, bf16[64,2432]{1,0:T(8,128)(2,1)S(1)}, u32[]{:S(2)}, u32[]{:S(2)}) collective-permute-start(bf16[64,2432]{1,0:T(8,128)(2,1)S(1)} %fusion.23), channel_id=1, source_target_pairs={{0,16},{4,20},{8,24},{12,28},{16,0},{20,4},{24,8},{28,12},{1,17},{... | collective-permute-start | bytes 933896 | tf_op jit(solution)/shard_map/ppermute | solution.py:529
  28.5 16.0 %collective-permute-start.4 = (bf16[2,2,64,1280]{3,2,1,0:T(8,128)(2,1)S(1)}, bf16[2,2,64,1280]{3,2,1,0:T(8,128)(2,1)S(1)}, u32[]{:S(2)}, u32[]{:S(2)}) collective-permute-start(bf16[2,2,64,1280]{3,2,1,0:T(8,128)(2,1)S(1)} %get-tuple-element.252), channel_id=1, source_target_pairs={{0,4},{4,0},{8,12},{12,8},{16,20},{20,16},{24,28},{28,24},{1,5},{5... | collective-permute-start | bytes 1966088 | tf_op jit(solution)/shard_map/ppermute | solution.py:733
  44.7 14.4 %collective-permute-start.6 = (bf16[2,64,2432]{2,1,0:T(8,128)(2,1)S(1)}, bf16[2,64,2432]{2,1,0:T(8,128)(2,1)S(1)}, u32[]{:S(2)}, u32[]{:S(2)}) collective-permute-start(bf16[2,64,2432]{2,1,0:T(8,128)(2,1)S(1)} %get-tuple-element.255), channel_id=1, source_target_pairs={{0,2},{1,3},{2,0},{3,1},{4,6},{5,7},{6,4},{7,5},{8,10},{9,11},{10,... | collective-permute-start | bytes 1867784 | tf_op jit(solution)/shard_map/ppermute | solution.py:737
  46.2 14.0 %collective-permute-start.5 = (bf16[2,64,2432]{2,1,0:T(8,128)(2,1)S(1)}, bf16[2,64,2432]{2,1,0:T(8,128)(2,1)S(1)}, u32[]{:S(2)}, u32[]{:S(2)}) collective-permute-start(bf16[2,64,2432]{2,1,0:T(8,128)(2,1)S(1)} %get-tuple-element.256), channel_id=1, source_target_pairs={{0,4},{4,0},{8,12},{12,8},{16,20},{20,16},{24,28},{28,24},{1,5},{5... | collective-permute-start | bytes 1867784 | tf_op jit(solution)/shard_map/ppermute | solution.py:733
  65.5 26.8 %collective-permute-start.8 = (bf16[4,64,2432]{2,1,0:T(8,128)(2,1)S(1)}, bf16[4,64,2432]{2,1,0:T(8,128)(2,1)}, u32[]{:S(2)}, u32[]{:S(2)}) collective-permute-start(bf16[4,64,2432]{2,1,0:T(8,128)(2,1)S(1)} %pad_maximum_fusion.8), channel_id=1, source_target_pairs={{0,2},{1,3},{2,0},{3,1},{4,6},{5,7},{6,4},{7,5},{8,10},{9,11},{10,... | collective-permute-start | bytes 3735560 | tf_op jit(solution)/shard_map/ppermute | solution.py:737
  66.6 27.3 %collective-permute-start.9 = (bf16[4,64,2432]{2,1,0:T(8,128)(2,1)}, bf16[4,64,2432]{2,1,0:T(8,128)(2,1)}, u32[]{:S(2)}, u32[]{:S(2)}) collective-permute-start(bf16[4,64,2432]{2,1,0:T(8,128)(2,1)} %pad_maximum_fusion.9), channel_id=1, source_target_pairs={{0,4},{4,0},{8,12},{12,8},{16,20},{20,16},{24,28},{28,24},{1,5},{5... | collective-permute-start | bytes 3735560 | tf_op jit(solution)/shard_map/ppermute | solution.py:733
  69.1 202.0 %all-gather.5.cloned.1.call-start = ((), (), s32[]{:S(2)}) async-start(), calls=%async_computation.2 | async-start | bytes 6553600 | tf_op jit(solution)/shard_map/all_gather | solution.py:855
  69.2 20.0 %collective-permute-start.12 = (bf16[48,2048]{1,0:T(8,128)(2,1)S(1)}, bf16[48,2048]{1,0:T(8,128)(2,1)S(1)}, u32[]{:S(2)}, u32[]{:S(2)}) collective-permute-start(bf16[48,2048]{1,0:T(8,128)(2,1)S(1)} %copy-done.76), channel_id=1, source_target_pairs={{0,16},{4,20},{8,24},{12,28},{16,0},{20,4},{24,8},{28,12},{1,17},{... | collective-permute-start | bytes 589832 | tf_op jit(solution)/shard_map/ppermute | solution.py:529
  71.8 17.3 %collective-permute-start.11 = (bf16[48,2048]{1,0:T(8,128)(2,1)S(1)}, bf16[48,2048]{1,0:T(8,128)(2,1)S(1)}, u32[]{:S(2)}, u32[]{:S(2)}) collective-permute-start(bf16[48,2048]{1,0:T(8,128)(2,1)S(1)} %copy-done.76), channel_id=1, source_target_pairs={{0,24},{4,28},{8,0},{12,4},{16,8},{20,12},{24,16},{28,20},{1,25},{... | collective-permute-start | bytes 589832 | tf_op jit(solution)/shard_map/ppermute | solution.py:529
  73.2 16.2 %collective-permute-start.10 = (bf16[48,2048]{1,0:T(8,128)(2,1)S(1)}, bf16[48,2048]{1,0:T(8,128)(2,1)S(1)}, u32[]{:S(2)}, u32[]{:S(2)}) collective-permute-start(bf16[48,2048]{1,0:T(8,128)(2,1)S(1)} %copy-done.76), channel_id=1, source_target_pairs={{0,8},{4,12},{8,16},{12,20},{16,24},{20,28},{24,0},{28,4},{1,9},{5... | collective-permute-start | bytes 589832 | tf_op jit(solution)/shard_map/ppermute | solution.py:529
  102.6 529.3 %reduce-scatter.2.cloned.1.call-start = ((), (), s32[]{:S(2)}) async-start(), calls=%async_computation.3 | async-start | bytes 6488064 | tf_op jit(solution)/shard_map/reduce_scatter | solution.py:954
  117.4 16.5 %collective-permute-start.18 = (bf16[2,48,2048]{2,1,0:T(8,128)(2,1)}, bf16[2,48,2048]{2,1,0:T(8,128)(2,1)}, u32[]{:S(2)}, u32[]{:S(2)}) collective-permute-start(bf16[2,48,2048]{2,1,0:T(8,128)(2,1)} %get-tuple-element.257), channel_id=1, source_target_pairs={{0,2},{1,3},{2,0},{3,1},{4,6},{5,7},{6,4},{7,5},{8,10},{9,11},{10,... | collective-permute-start | bytes 1179656 | tf_op jit(solution)/shard_map/ppermute | solution.py:737
  118.1 17.0 %collective-permute-start.17 = (bf16[2,48,2048]{2,1,0:T(8,128)(2,1)}, bf16[2,48,2048]{2,1,0:T(8,128)(2,1)}, u32[]{:S(2)}, u32[]{:S(2)}) collective-permute-start(bf16[2,48,2048]{2,1,0:T(8,128)(2,1)} %get-tuple-element.258), channel_id=1, source_target_pairs={{0,4},{4,0},{8,12},{12,8},{16,20},{20,16},{24,28},{28,24},{1,5},{5... | collective-permute-start | bytes 1179656 | tf_op jit(solution)/shard_map/ppermute | solution.py:733
  143.5 19.7 %collective-permute-start.21 = (bf16[4,48,2048]{2,1,0:T(8,128)(2,1)S(1)}, bf16[4,48,2048]{2,1,0:T(8,128)(2,1)S(1)}, u32[]{:S(2)}, u32[]{:S(2)}) collective-permute-start(bf16[4,48,2048]{2,1,0:T(8,128)(2,1)S(1)} %pad_maximum_fusion.12), channel_id=1, source_target_pairs={{0,4},{4,0},{8,12},{12,8},{16,20},{20,16},{24,28},{28,24},{1,5},{5... | collective-permute-start | bytes 2359304 | tf_op jit(solution)/shard_map/ppermute | solution.py:733
  144.4 19.9 %collective-permute-start.19 = (bf16[4,48,2048]{2,1,0:T(8,128)(2,1)S(1)}, bf16[4,48,2048]{2,1,0:T(8,128)(2,1)S(1)}, u32[]{:S(2)}, u32[]{:S(2)}) collective-permute-start(bf16[4,48,2048]{2,1,0:T(8,128)(2,1)S(1)} %pad_maximum_fusion.11), channel_id=1, source_target_pairs={{0,2},{1,3},{2,0},{3,1},{4,6},{5,7},{6,4},{7,5},{8,10},{9,11},{10,... | collective-permute-start | bytes 2359304 | tf_op jit(solution)/shard_map/ppermute | solution.py:737
  163.2 17.5 %collective-permute-start.22 = (bf16[8,48,2048]{2,1,0:T(8,128)(2,1)S(1)}, bf16[8,48,2048]{2,1,0:T(8,128)(2,1)S(1)}, u32[]{:S(2)}, u32[]{:S(2)}) collective-permute-start(bf16[8,48,2048]{2,1,0:T(8,128)(2,1)S(1)} %constant_dynamic-update-slice_fusion.2.refs_2_), channel_id=1, source_target_pairs={{0,1},{1,0},{2,3},{3,2},{4,5},{5,4},{6,7},{7,6},{8,9},{9,8},{10,11... | collective-permute-start | bytes 4718600 | tf_op jit(solution)/shard_map/ppermute | solution.py:737
  164.4 16.3 %collective-permute-start.20 = (bf16[8,48,2048]{2,1,0:T(8,128)(2,1)S(1)}, bf16[8,48,2048]{2,1,0:T(8,128)(2,1)S(1)}, u32[]{:S(2)}, u32[]{:S(2)}) collective-permute-start(bf16[8,48,2048]{2,1,0:T(8,128)(2,1)S(1)} %constant_dynamic-update-slice_fusion.refs_0_), channel_id=1, source_target_pairs={{0,1},{1,0},{2,3},{3,2},{4,5},{5,4},{6,7},{7,6},{8,9},{9,8},{10,11... | collective-permute-start | bytes 4718600 | tf_op jit(solution)/shard_map/ppermute | solution.py:737
  177.5 25.2 %collective-permute-start.24 = (bf16[256,2048]{1,0:T(8,128)(2,1)S(1)}, bf16[256,2048]{1,0:T(8,128)(2,1)S(1)}, u32[]{:S(2)}, u32[]{:S(2)}) collective-permute-start(bf16[256,2048]{1,0:T(8,128)(2,1)S(1)} %copy-done.1), channel_id=1, source_target_pairs={{0,4},{4,0},{8,12},{12,8},{16,20},{20,16},{24,28},{28,24},{1,5},{5... | collective-permute-start | bytes 3145736 | tf_op jit(solution)/shard_map/ppermute | solution.py:733
  178.7 25.1 %collective-permute-start.23 = (bf16[256,2048]{1,0:T(8,128)(2,1)S(1)}, bf16[256,2048]{1,0:T(8,128)(2,1)S(1)}, u32[]{:S(2)}, u32[]{:S(2)}) collective-permute-start(bf16[256,2048]{1,0:T(8,128)(2,1)S(1)} %copy-done.1), channel_id=1, source_target_pairs={{0,2},{1,3},{2,0},{3,1},{4,6},{5,7},{6,4},{7,5},{8,10},{9,11},{10,... | collective-permute-start | bytes 3145736 | tf_op jit(solution)/shard_map/ppermute | solution.py:737
  203.8 17.3 %collective-permute-start.30 = (bf16[256,2048]{1,0:T(8,128)(2,1)S(1)}, bf16[256,2048]{1,0:T(8,128)(2,1)S(1)}, u32[]{:S(2)}, u32[]{:S(2)}) collective-permute-start(bf16[256,2048]{1,0:T(8,128)(2,1)S(1)} %collective-permute-done.23.refs_1_), channel_id=1, source_target_pairs={{0,1},{1,0},{2,3},{3,2},{4,5},{5,4},{6,7},{7,6},{8,9},{9,8},{10,11... | collective-permute-start | bytes 3145736 | tf_op jit(solution)/shard_map/ppermute | solution.py:737
  204.0 17.7 %collective-permute-start.31 = (bf16[256,2048]{1,0:T(8,128)(2,1)S(1)}, bf16[256,2048]{1,0:T(8,128)(2,1)S(1)}, u32[]{:S(2)}, u32[]{:S(2)}) collective-permute-start(bf16[256,2048]{1,0:T(8,128)(2,1)S(1)} %collective-permute-done.24.refs_2_), channel_id=1, source_target_pairs={{0,1},{1,0},{2,3},{3,2},{4,5},{5,4},{6,7},{7,6},{8,9},{9,8},{10,11... | collective-permute-start | bytes 3145736 | tf_op jit(solution)/shard_map/ppermute | solution.py:737
  204.5 13.9 %collective-permute-start.26 = (bf16[256,1024]{1,0:T(8,128)(2,1)S(1)}, bf16[256,1024]{1,0:T(8,128)(2,1)S(1)}, u32[]{:S(2)}, u32[]{:S(2)}) collective-permute-start(bf16[256,1024]{1,0:T(8,128)(2,1)S(1)} %slice.225), channel_id=1, source_target_pairs={{0,2},{1,3},{2,0},{3,1},{4,6},{5,7},{6,4},{7,5},{8,10},{9,11},{10,... | collective-permute-start | bytes 1572872 | tf_op jit(solution)/shard_map/ppermute | solution.py:737
  206.3 13.6 %collective-permute-start.25 = (bf16[256,1024]{1,0:T(8,128)(2,1)S(1)}, bf16[256,1024]{1,0:T(8,128)(2,1)S(1)}, u32[]{:S(2)}, u32[]{:S(2)}) collective-permute-start(bf16[256,1024]{1,0:T(8,128)(2,1)S(1)} %slice.224), channel_id=1, source_target_pairs={{0,4},{4,0},{8,12},{12,8},{16,20},{20,16},{24,28},{28,24},{1,5},{5... | collective-permute-start | bytes 1572872 | tf_op jit(solution)/shard_map/ppermute | solution.py:733
  207.2 14.0 %collective-permute-start.29 = (bf16[256,2048]{1,0:T(8,128)(2,1)S(1)}, bf16[256,2048]{1,0:T(8,128)(2,1)S(1)}, u32[]{:S(2)}, u32[]{:S(2)}) collective-permute-start(bf16[256,2048]{1,0:T(8,128)(2,1)S(1)} %copy-done.1), channel_id=1, source_target_pairs={{0,1},{1,0},{2,3},{3,2},{4,5},{5,4},{6,7},{7,6},{8,9},{9,8},{10,11... | collective-permute-start | bytes 3145736 | tf_op jit(solution)/shard_map/ppermute | solution.py:737
  219.9 24.2 %collective-permute-start.28 = (bf16[256,2048]{1,0:T(8,128)(2,1)S(1)}, bf16[256,2048]{1,0:T(8,128)(2,1)}, u32[]{:S(2)}, u32[]{:S(2)}) collective-permute-start(bf16[256,2048]{1,0:T(8,128)(2,1)S(1)} %multiply_convert_fusion.refs_0_), channel_id=1, source_target_pairs={{0,4},{4,0},{8,12},{12,8},{16,20},{20,16},{24,28},{28,24},{1,5},{5... | collective-permute-start | bytes 3145736 | tf_op jit(solution)/shard_map/ppermute | solution.py:733
  220.8 23.9 %collective-permute-start.27 = (bf16[256,2048]{1,0:T(8,128)(2,1)S(1)}, bf16[256,2048]{1,0:T(8,128)(2,1)}, u32[]{:S(2)}, u32[]{:S(2)}) collective-permute-start(bf16[256,2048]{1,0:T(8,128)(2,1)S(1)} %multiply_convert_fusion.refs_0_), channel_id=1, source_target_pairs={{0,2},{1,3},{2,0},{3,1},{4,6},{5,7},{6,4},{7,5},{8,10},{9,11},{10,... | collective-permute-start | bytes 3145736 | tf_op jit(solution)/shard_map/ppermute | solution.py:737
  245.8 16.9 %collective-permute-start.37 = (bf16[256,2048]{1,0:T(8,128)(2,1)}, bf16[256,2048]{1,0:T(8,128)(2,1)}, u32[]{:S(2)}, u32[]{:S(2)}) collective-permute-start(bf16[256,2048]{1,0:T(8,128)(2,1)} %collective-permute-done.27.refs_1_), channel_id=1, source_target_pairs={{0,1},{1,0},{2,3},{3,2},{4,5},{5,4},{6,7},{7,6},{8,9},{9,8},{10,11... | collective-permute-start | bytes 3145736 | tf_op jit(solution)/shard_map/ppermute | solution.py:737
  246.9 15.7 %collective-permute-start.36 = (bf16[256,2048]{1,0:T(8,128)(2,1)S(1)}, bf16[256,2048]{1,0:T(8,128)(2,1)}, u32[]{:S(2)}, u32[]{:S(2)}) collective-permute-start(bf16[256,2048]{1,0:T(8,128)(2,1)S(1)} %multiply_convert_fusion.refs_0_), channel_id=1, source_target_pairs={{0,1},{1,0},{2,3},{3,2},{4,5},{5,4},{6,7},{7,6},{8,9},{9,8},{10,11... | collective-permute-start | bytes 3145736 | tf_op jit(solution)/shard_map/ppermute | solution.py:737
  247.5 13.9 %collective-permute-start.35 = (bf16[256,1024]{1,0:T(8,128)(2,1)S(1)}, bf16[256,1024]{1,0:T(8,128)(2,1)S(1)}, u32[]{:S(2)}, u32[]{:S(2)}) collective-permute-start(bf16[256,1024]{1,0:T(8,128)(2,1)S(1)} %slice.227), channel_id=1, source_target_pairs={{0,2},{1,3},{2,0},{3,1},{4,6},{5,7},{6,4},{7,5},{8,10},{9,11},{10,... | collective-permute-start | bytes 1572872 | tf_op jit(solution)/shard_map/ppermute | solution.py:737
  248.1 14.5 %collective-permute-start.38 = (bf16[256,2048]{1,0:T(8,128)(2,1)}, bf16[256,2048]{1,0:T(8,128)(2,1)}, u32[]{:S(2)}, u32[]{:S(2)}) collective-permute-start(bf16[256,2048]{1,0:T(8,128)(2,1)} %collective-permute-done.28.refs_2_), channel_id=1, source_target_pairs={{0,1},{1,0},{2,3},{3,2},{4,5},{5,4},{6,7},{7,6},{8,9},{9,8},{10,11... | collective-permute-start | bytes 3145736 | tf_op jit(solution)/shard_map/ppermute | solution.py:737
  248.1 14.4 %collective-permute-start.34 = (bf16[256,1024]{1,0:T(8,128)(2,1)S(1)}, bf16[256,1024]{1,0:T(8,128)(2,1)}, u32[]{:S(2)}, u32[]{:S(2)}) collective-permute-start(bf16[256,1024]{1,0:T(8,128)(2,1)S(1)} %slice.226), channel_id=1, source_target_pairs={{0,4},{4,0},{8,12},{12,8},{16,20},{20,16},{24,28},{28,24},{1,5},{5... | collective-permute-start | bytes 1572872 | tf_op jit(solution)/shard_map/ppermute | solution.py:733
  299.7 41.2 %collective-permute-start.41 = (bf16[1,160,2048]{2,1,0:T(8,128)(2,1)S(1)}, bf16[1,160,2048]{2,1,0:T(8,128)(2,1)S(1)}, u32[]{:S(2)}, u32[]{:S(2)}) collective-permute-start(bf16[1,160,2048]{2,1,0:T(8,128)(2,1)S(1)} %get-tuple-element.161), channel_id=1, source_target_pairs={{0,8},{4,12},{8,16},{12,20},{16,24},{20,28},{24,0},{28,4},{1,9},{5... | collective-permute-start | bytes 1966088 | tf_op jit(solution)/shard_map/ppermute | solution.py:900
  311.2 29.7 %collective-permute-start.42 = (bf16[1,160,2048]{2,1,0:T(8,128)(2,1)S(1)}, bf16[1,160,2048]{2,1,0:T(8,128)(2,1)S(1)}, u32[]{:S(2)}, u32[]{:S(2)}) collective-permute-start(bf16[1,160,2048]{2,1,0:T(8,128)(2,1)S(1)} %get-tuple-element.162), channel_id=1, source_target_pairs={{0,24},{4,28},{8,0},{12,4},{16,8},{20,12},{24,16},{28,20},{1,25},{... | collective-permute-start | bytes 1966088 | tf_op jit(solution)/shard_map/ppermute | solution.py:900
  342.7 57.3 %collective-permute-start.48 = (bf16[1,160,2048]{2,1,0:T(8,128)(2,1)S(1)}, bf16[1,160,2048]{2,1,0:T(8,128)(2,1)}, u32[]{:S(2)}, u32[]{:S(2)}) collective-permute-start(bf16[1,160,2048]{2,1,0:T(8,128)(2,1)S(1)} %get-tuple-element.179), channel_id=1, source_target_pairs={{0,16},{4,20},{8,24},{12,28},{16,0},{20,4},{24,8},{28,12},{1,17},{... | collective-permute-start | bytes 1966088 | tf_op jit(solution)/shard_map/ppermute | solution.py:900
  355.1 25.2 %collective-permute-start.44 = (bf16[2,256,1024]{2,1,0:T(8,128)(2,1)S(1)}, bf16[2,256,1024]{2,1,0:T(8,128)(2,1)S(1)}, u32[]{:S(2)}, u32[]{:S(2)}) collective-permute-start(bf16[2,256,1024]{2,1,0:T(8,128)(2,1)S(1)} %get-tuple-element.175), channel_id=1, source_target_pairs={{0,4},{4,0},{8,12},{12,8},{16,20},{20,16},{24,28},{28,24},{1,5},{5... | collective-permute-start | bytes 3145736 | tf_op jit(solution)/shard_map/ppermute | solution.py:733
  355.7 27.1 %collective-permute-start.46 = (bf16[2,256,1024]{2,1,0:T(8,128)(2,1)S(1)}, bf16[2,256,1024]{2,1,0:T(8,128)(2,1)S(1)}, u32[]{:S(2)}, u32[]{:S(2)}) collective-permute-start(bf16[2,256,1024]{2,1,0:T(8,128)(2,1)S(1)} %get-tuple-element.177), channel_id=1, source_target_pairs={{0,2},{1,3},{2,0},{3,1},{4,6},{5,7},{6,4},{7,5},{8,10},{9,11},{10,... | collective-permute-start | bytes 3145736 | tf_op jit(solution)/shard_map/ppermute | solution.py:737
  381.4 13.3 %collective-permute-start.45 = (bf16[256,1024]{1,0:T(8,128)(2,1)}, bf16[256,1024]{1,0:T(8,128)(2,1)S(1)}, u32[]{:S(2)}, u32[]{:S(2)}) collective-permute-start(bf16[256,1024]{1,0:T(8,128)(2,1)} %fusion.17), channel_id=1, source_target_pairs={{0,2},{1,3},{2,0},{3,1},{4,6},{5,7},{6,4},{7,5},{8,10},{9,11},{10,... | collective-permute-start | bytes 1572872 | tf_op jit(solution)/shard_map/ppermute | solution.py:737
  384.0 13.2 %collective-permute-start.47 = (bf16[256,1024]{1,0:T(8,128)(2,1)}, bf16[256,1024]{1,0:T(8,128)(2,1)}, u32[]{:S(2)}, u32[]{:S(2)}) collective-permute-start(bf16[256,1024]{1,0:T(8,128)(2,1)} %fusion.18), channel_id=1, source_target_pairs={{0,4},{4,0},{8,12},{12,8},{16,20},{20,16},{24,28},{28,24},{1,5},{5... | collective-permute-start | bytes 1572872 | tf_op jit(solution)/shard_map/ppermute | solution.py:733
  403.2 38.7 %collective-permute-start.52 = (bf16[1,256,1280]{2,1,0:T(8,128)(2,1)}, bf16[1,256,1280]{2,1,0:T(8,128)(2,1)}, u32[]{:S(2)}, u32[]{:S(2)}) collective-permute-start(bf16[1,256,1280]{2,1,0:T(8,128)(2,1)} %get-tuple-element.193), channel_id=1, source_target_pairs={{0,8},{4,12},{8,16},{12,20},{16,24},{20,28},{24,0},{28,4},{1,9},{5... | collective-permute-start | bytes 1966088 | tf_op jit(solution)/shard_map/ppermute | solution.py:900
  405.6 36.3 %collective-permute-start.53 = (bf16[1,256,1280]{2,1,0:T(8,128)(2,1)}, bf16[1,256,1280]{2,1,0:T(8,128)(2,1)S(1)}, u32[]{:S(2)}, u32[]{:S(2)}) collective-permute-start(bf16[1,256,1280]{2,1,0:T(8,128)(2,1)} %get-tuple-element.194), channel_id=1, source_target_pairs={{0,8},{4,12},{8,16},{12,20},{16,24},{20,28},{24,0},{28,4},{1,9},{5... | collective-permute-start | bytes 1966088 | tf_op jit(solution)/shard_map/ppermute | solution.py:900
  407.6 42.9 %collective-permute-start.54 = (bf16[1,256,1280]{2,1,0:T(8,128)(2,1)}, bf16[1,256,1280]{2,1,0:T(8,128)(2,1)}, u32[]{:S(2)}, u32[]{:S(2)}) collective-permute-start(bf16[1,256,1280]{2,1,0:T(8,128)(2,1)} %get-tuple-element.195), channel_id=1, source_target_pairs={{0,24},{4,28},{8,0},{12,4},{16,8},{20,12},{24,16},{28,20},{1,25},{... | collective-permute-start | bytes 1966088 | tf_op jit(solution)/shard_map/ppermute | solution.py:900
  417.4 33.1 %collective-permute-start.50 = (bf16[2,256,1024]{2,1,0:T(8,128)(2,1)S(1)}, bf16[2,256,1024]{2,1,0:T(8,128)(2,1)}, u32[]{:S(2)}, u32[]{:S(2)}) collective-permute-start(bf16[2,256,1024]{2,1,0:T(8,128)(2,1)S(1)} %get-tuple-element.190), channel_id=1, source_target_pairs={{0,4},{4,0},{8,12},{12,8},{16,20},{20,16},{24,28},{28,24},{1,5},{5... | collective-permute-start | bytes 3145736 | tf_op jit(solution)/shard_map/ppermute | solution.py:733
  418.0 32.5 %collective-permute-start.51 = (bf16[2,256,1024]{2,1,0:T(8,128)(2,1)S(1)}, bf16[2,256,1024]{2,1,0:T(8,128)(2,1)}, u32[]{:S(2)}, u32[]{:S(2)}) collective-permute-start(bf16[2,256,1024]{2,1,0:T(8,128)(2,1)S(1)} %get-tuple-element.192), channel_id=1, source_target_pairs={{0,2},{1,3},{2,0},{3,1},{4,6},{5,7},{6,4},{7,5},{8,10},{9,11},{10,... | collective-permute-start | bytes 3145736 | tf_op jit(solution)/shard_map/ppermute | solution.py:737
  450.5 17.0 %collective-permute-start.57 = (bf16[2,256,384]{2,1,0:T(8,128)(2,1)}, bf16[2,256,384]{2,1,0:T(8,128)(2,1)}, u32[]{:S(2)}, u32[]{:S(2)}) collective-permute-start(bf16[2,256,384]{2,1,0:T(8,128)(2,1)} %get-tuple-element.206), channel_id=1, source_target_pairs={{1,0},{2,1},{3,2},{5,4},{6,5},{7,6},{9,8},{10,9},{11,10},{13,12},{... | collective-permute-start | bytes 1179656 | tf_op jit(solution)/shard_map/ppermute | solution.py:957
  451.8 19.0 %collective-permute-start.58 = (bf16[2,256,384]{2,1,0:T(8,128)(2,1)}, bf16[2,256,384]{2,1,0:T(8,128)(2,1)}, u32[]{:S(2)}, u32[]{:S(2)}) collective-permute-start(bf16[2,256,384]{2,1,0:T(8,128)(2,1)} %get-tuple-element.207), channel_id=1, source_target_pairs={{2,0},{3,1},{6,4},{7,5},{10,8},{11,9},{14,12},{15,13},{18,16},{19,... | collective-permute-start | bytes 1179656 | tf_op jit(solution)/shard_map/ppermute | solution.py:958
  455.1 39.0 %collective-permute-start.56 = (bf16[256,1024]{1,0:T(8,128)(2,1)}, bf16[256,1024]{1,0:T(8,128)(2,1)}, u32[]{:S(2)}, u32[]{:S(2)}) collective-permute-start(bf16[256,1024]{1,0:T(8,128)(2,1)} %fusion.20), channel_id=1, source_target_pairs={{0,4},{4,0},{8,12},{12,8},{16,20},{20,16},{24,28},{28,24},{1,5},{5... | collective-permute-start | bytes 1572872 | tf_op jit(solution)/shard_map/ppermute | solution.py:733
  457.7 38.0 %collective-permute-start.55 = (bf16[256,1024]{1,0:T(8,128)(2,1)}, bf16[256,1024]{1,0:T(8,128)(2,1)}, u32[]{:S(2)}, u32[]{:S(2)}) collective-permute-start(bf16[256,1024]{1,0:T(8,128)(2,1)} %fusion.19), channel_id=1, source_target_pairs={{0,2},{1,3},{2,0},{3,1},{4,6},{5,7},{6,4},{7,5},{8,10},{9,11},{10,... | collective-permute-start | bytes 1572872 | tf_op jit(solution)/shard_map/ppermute | solution.py:737
  461.1 37.9 %collective-permute-start.59 = (bf16[1,256,1280]{2,1,0:T(8,128)(2,1)}, bf16[1,256,1280]{2,1,0:T(8,128)(2,1)}, u32[]{:S(2)}, u32[]{:S(2)}) collective-permute-start(bf16[1,256,1280]{2,1,0:T(8,128)(2,1)} %get-tuple-element.211), channel_id=1, source_target_pairs={{0,16},{4,20},{8,24},{12,28},{16,0},{20,4},{24,8},{28,12},{1,17},{... | collective-permute-start | bytes 1966088 | tf_op jit(solution)/shard_map/ppermute | solution.py:900
  500.1 16.2 %collective-permute-start.61 = (bf16[1,256,1280]{2,1,0:T(8,128)(2,1)S(1)}, bf16[1,256,1280]{2,1,0:T(8,128)(2,1)S(1)}, u32[]{:S(2)}, u32[]{:S(2)}) collective-permute-start(bf16[1,256,1280]{2,1,0:T(8,128)(2,1)S(1)} %copy-done.35), channel_id=1, source_target_pairs={{0,24},{4,28},{8,0},{12,4},{16,8},{20,12},{24,16},{28,20},{1,25},{... | collective-permute-start | bytes 1966088 | tf_op jit(solution)/shard_map/ppermute | solution.py:900
  517.0 30.3 %collective-permute-start.64 = (bf16[1,256,1280]{2,1,0:T(8,128)(2,1)S(1)}, bf16[1,256,1280]{2,1,0:T(8,128)(2,1)S(1)}, u32[]{:S(2)}, u32[]{:S(2)}) collective-permute-start(bf16[1,256,1280]{2,1,0:T(8,128)(2,1)S(1)} %copy-done.33), channel_id=1, source_target_pairs={{0,16},{4,20},{8,24},{12,28},{16,0},{20,4},{24,8},{28,12},{1,17},{... | collective-permute-start | bytes 1966088 | tf_op jit(solution)/shard_map/ppermute | solution.py:900
  517.5 30.2 %collective-permute-start.62 = (bf16[4,64,2432]{2,1,0:T(8,128)(2,1)S(1)}, bf16[4,64,2432]{2,1,0:T(8,128)(2,1)S(1)}, u32[]{:S(2)}, u32[]{:S(2)}) collective-permute-start(bf16[4,64,2432]{2,1,0:T(8,128)(2,1)S(1)} %get-tuple-element.217), channel_id=1, source_target_pairs={{0,2},{1,3},{2,0},{3,1},{4,6},{5,7},{6,4},{7,5},{8,10},{9,11},{10,... | collective-permute-start | bytes 3735560 | tf_op jit(solution)/shard_map/ppermute | solution.py:737
  519.7 29.1 %collective-permute-start.63 = (bf16[4,64,2432]{2,1,0:T(8,128)(2,1)S(1)}, bf16[4,64,2432]{2,1,0:T(8,128)(2,1)S(1)}, u32[]{:S(2)}, u32[]{:S(2)}) collective-permute-start(bf16[4,64,2432]{2,1,0:T(8,128)(2,1)S(1)} %get-tuple-element.218), channel_id=1, source_target_pairs={{0,4},{4,0},{8,12},{12,8},{16,20},{20,16},{24,28},{28,24},{1,5},{5... | collective-permute-start | bytes 3735560 | tf_op jit(solution)/shard_map/ppermute | solution.py:733
  550.8 23.9 %collective-permute-start.65 = (bf16[2,64,2432]{2,1,0:T(8,128)(2,1)}, bf16[2,64,2432]{2,1,0:T(8,128)(2,1)S(1)}, u32[]{:S(2)}, u32[]{:S(2)}) collective-permute-start(bf16[2,64,2432]{2,1,0:T(8,128)(2,1)} %add_convert_fusion.10), channel_id=1, source_target_pairs={{0,4},{4,0},{8,12},{12,8},{16,20},{20,16},{24,28},{28,24},{1,5},{5... | collective-permute-start | bytes 1867784 | tf_op jit(solution)/shard_map/ppermute | solution.py:733
  557.9 18.4 %collective-permute-start.66 = (bf16[2,64,2432]{2,1,0:T(8,128)(2,1)}, bf16[2,64,2432]{2,1,0:T(8,128)(2,1)S(1)}, u32[]{:S(2)}, u32[]{:S(2)}) collective-permute-start(bf16[2,64,2432]{2,1,0:T(8,128)(2,1)} %add_convert_fusion.9), channel_id=1, source_target_pairs={{0,2},{1,3},{2,0},{3,1},{4,6},{5,7},{6,4},{7,5},{8,10},{9,11},{10,... | collective-permute-start | bytes 1867784 | tf_op jit(solution)/shard_map/ppermute | solution.py:737
  563.7 12.8 %collective-permute-start.70 = (bf16[4,64,1280]{2,1,0:T(8,128)(2,1)S(1)}, bf16[4,64,1280]{2,1,0:T(8,128)(2,1)S(1)}, u32[]{:S(2)}, u32[]{:S(2)}) collective-permute-start(bf16[4,64,1280]{2,1,0:T(8,128)(2,1)S(1)} %get-tuple-element.228), channel_id=1, source_target_pairs={{0,1},{1,0},{2,3},{3,2},{4,5},{5,4},{6,7},{7,6},{8,9},{9,8},{10,11... | collective-permute-start | bytes 1966088 | tf_op jit(solution)/shard_map/ppermute | solution.py:737
  579.2 18.3 %collective-permute-start.76 = (bf16[2,2,64,1280]{3,2,1,0:T(8,128)(2,1)S(1)}, bf16[2,2,64,1280]{3,2,1,0:T(8,128)(2,1)S(1)}, u32[]{:S(2)}, u32[]{:S(2)}) collective-permute-start(bf16[2,2,64,1280]{3,2,1,0:T(8,128)(2,1)S(1)} %get-tuple-element.248), channel_id=1, source_target_pairs={{0,2},{1,3},{2,0},{3,1},{4,6},{5,7},{6,4},{7,5},{8,10},{9,11},{10,... | collective-permute-start | bytes 1966088 | tf_op jit(solution)/shard_map/ppermute | solution.py:737
  581.6 32.0 %collective-permute-start.75 = (bf16[64,2432]{1,0:T(8,128)(2,1)}, bf16[64,2432]{1,0:T(8,128)(2,1)S(1)}, u32[]{:S(2)}, u32[]{:S(2)}) collective-permute-start(bf16[64,2432]{1,0:T(8,128)(2,1)} %slice_bitcast_fusion.3), channel_id=1, source_target_pairs={{0,16},{4,20},{8,24},{12,28},{16,0},{20,4},{24,8},{28,12},{1,17},{... | collective-permute-start | bytes 933896 | tf_op jit(solution)/shard_map/ppermute | solution.py:750
  584.3 29.4 %collective-permute-start.73 = (bf16[64,2432]{1,0:T(8,128)(2,1)}, bf16[64,2432]{1,0:T(8,128)(2,1)S(1)}, u32[]{:S(2)}, u32[]{:S(2)}) collective-permute-start(bf16[64,2432]{1,0:T(8,128)(2,1)} %get-tuple-element.261), channel_id=1, source_target_pairs={{0,8},{4,12},{8,16},{12,20},{16,24},{20,28},{24,0},{28,4},{1,9},{5... | collective-permute-start | bytes 933896 | tf_op jit(solution)/shard_map/ppermute | solution.py:750
  585.7 28.2 %collective-permute-start.74 = (bf16[64,2432]{1,0:T(8,128)(2,1)}, bf16[64,2432]{1,0:T(8,128)(2,1)}, u32[]{:S(2)}, u32[]{:S(2)}) collective-permute-start(bf16[64,2432]{1,0:T(8,128)(2,1)} %get-tuple-element.262), channel_id=1, source_target_pairs={{0,24},{4,28},{8,0},{12,4},{16,8},{20,12},{24,16},{28,20},{1,25},{... | collective-permute-start | bytes 933896 | tf_op jit(solution)/shard_map/ppermute | solution.py:750
  598.5 35.1 %collective-permute-start.77 = (bf16[2,2,64,1280]{3,2,1,0:T(8,128)(2,1)}, bf16[2,2,64,1280]{3,2,1,0:T(8,128)(2,1)S(1)}, u32[]{:S(2)}, u32[]{:S(2)}) collective-permute-start(bf16[2,2,64,1280]{3,2,1,0:T(8,128)(2,1)} %get-tuple-element.246), channel_id=1, source_target_pairs={{0,4},{4,0},{8,12},{12,8},{16,20},{20,16},{24,28},{28,24},{1,5},{5... | collective-permute-start | bytes 1966088 | tf_op jit(solution)/shard_map/ppermute | solution.py:733
  (118 other events, 1066.1 us)
Sparse Core Ops, SparseCore 0:
  69.2 59.6 all-gather.2
  130.4 97.2 all-gather.4
  499.2 132.6 reduce-scatter.1

commit v6 on v4

--- a/solution.py
+++ b/solution.py
@@ -881,7 +881,7 @@
     mixed = attend(queries, kv_two, kv_one, kv, rel)
     out_a, out_b, _ = gated((out_a, out_b, kv_one), kv_two)
     full_out = plane_last(out_a, out_b, sends, places).reshape(-1, width)
-    pieces = gather_second(*gated(pieces, mixed), places)
+    pieces = gather_second(*gated(pieces, full_out), places)
     hidden = x + product(mixed, full_out)
     h_inverse = lax.rsqrt(jnp.mean(hidden * hidden, axis=-1, keepdims=True) + EPSILON)
     ffn_mine = (hidden * h_inverse * ffn_row).astype(BF16)

time: 640 us -> 635 us (level)
  waiting for transfers between devices: 238 us -> 231 us
    ppermute x16, waiting for transfers between devices: 43.8 us -> 35 us  [near_swap(): return lax.ppermute(value, 'dp', swap_pairs(places.size, 1))]
    unnamed x177 -> x183, local copies, waits for them, and re-layouts: 15.3 us -> 15.3 us
  transfers between devices with their start and end apart: 81 -> 81, of which waited for: 40 -> 39; matrix products, arithmetic and copies ran while one was open for 18% -> 18% of each run, Pallas kernels for 20% -> 20%
where the time goes in v6:
time: 635 us; the launch traced here: 626 us
  waiting for transfers between devices  231 us (36%)
  Pallas kernels  153 us (24%)
  starting transfers between devices  87.5 us (14%)
  matrix products  68.3 us (11%)
  other arithmetic  46 us (7%)
  local copies, waits for them, and re-layouts  24.6 us (4%)
  between operations  15.9 us (3%)
    ppermute x35, waiting for transfers between devices, member_swap(): return lax.ppermute(value, 'fsdp', swap_pairs(4, bit))  87.7 us
    dot_general x4, matrix products, left_transposed(): lax.dot_general(left, right, (((0,), (0,)), ((), ())), preferred_element_...  35.2 us
    ppermute x16, waiting for transfers between devices, near_swap(): return lax.ppermute(value, 'dp', swap_pairs(places.size, 1))  35 us
    ppermute x9, waiting for transfers between devices, far_sent(): lax.ppermute(blocks[k], 'dp', far_pairs(dp_size, order[k // cut]))  31.8 us
    pallas_call x1, Pallas kernels, feed_back(): pl.pallas_call(feed_back_kernel, grid=(steps,), in_specs=[pl.BlockSpec((t...  29.8 us
    ppermute x35, starting transfers between devices, member_swap(): return lax.ppermute(value, 'fsdp', swap_pairs(4, bit))  25.5 us
    pallas_call x3, Pallas kernels, place(): pl.pallas_call(functools.partial(place_kernel, counts), in_specs=[pl.Bloc...  23.2 us
    dot_general x4, matrix products, product(): return jnp.dot(left, right, preferred_element_type=F32)  21.6 us
  transfers between devices with their start and end apart: 81, of which 39 were waited for; matrix products, arithmetic and copies ran while one was open for 18% of the time, Pallas kernels for 20%

profile of v6, /device:TPU:0, one launch (start us, length us, event | category | flops | bytes accessed | tf_op | source)
XLA Modules:
  0.0 625.8 jit_solution(13622232823754974077)
XLA Ops:
  10.6 3.0 collective-permute-start.3
  13.8 3.7 collective-permute-start.1
  18.6 9.8 %collective-permute-done.3 = bf16[4,64,1280]{2,1,0:T(8,128)(2,1)S(1)} collective-permute-done((bf16[4,64,1280]{2,1,0:T(8,128)(2,1)S(1)}, bf16[4,64,1280]{2,1,0:T(8,128)(2,1)S(1)}, u32[]{:S(2)}, u32[]{:S(2)}) %collective-permute-start.3) | collective-permute-done | bytes 655392 | tf_op jit(solution)/shard_map/ppermute | solution.py:737
  30.3 2.6 collective-permute-done
  32.9 10.8 %collective-permute-done.2 = bf16[64,2432]{1,0:T(8,128)(2,1)S(1)} collective-permute-done((bf16[64,2432]{1,0:T(8,128)(2,1)S(1)}, bf16[64,2432]{1,0:T(8,128)(2,1)S(1)}, u32[]{:S(2)}, u32[]{:S(2)}) %collective-permute-start.2) | collective-permute-done | bytes 311328 | tf_op jit(solution)/shard_map/ppermute | solution.py:529
  44.6 2.5 collective-permute-start.9
  52.5 5.4 collective-permute-done.9
  57.8 2.1 collective-permute-done.7
  60.1 2.4 collective-permute-done.6
  63.9 4.1 place.3
  74.3 28.7 %collective-permute-done.14 = bf16[2,48,2048]{2,1,0:T(8,128)(2,1)S(1)} collective-permute-done((bf16[2,48,2048]{2,1,0:T(8,128)(2,1)S(1)}, bf16[2,48,2048]{2,1,0:T(8,128)(2,1)S(1)}, u32[]{:S(2)}, u32[]{:S(2)}) %collective-permute-start.14) | collective-permute-done | bytes 393248 | tf_op jit(solution)/shard_map/ppermute | solution.py:737
  108.8 3.1 pad_maximum_fusion.1.refs_2_
  115.9 4.3 collective-permute-done.15.refs_1_
  120.5 8.4 %place.4 = bf16[32,64,2432]{2,1,0:T(8,128)(2,1)} custom-call(s32[32]{0:T(128)S(1)} %stack.408.slots, bf16[8,64,2432]{2,1,0:T(8,128)(2,1)S(1)} %pad_maximum_fusion.refs_0_, bf16[8,64,2432]{2,1,0:T(8,128)(2,1)} %collective-permute-done.15.refs_1_, bf16[8,64,2432]{2,1,0:T(8,128)(2,1)} %pad_maximum_fusion.1.refs_2_, ...), custom_call_target="tpu_custom_call" | custom-call | bytes 19922944 | tf_op jit(solution)/shard_map/place/pallas_call | solution.py:456
  133.4 6.8 %fusion.27.pre_ref = f32[256,2432]{1,0:T(8,128)S(1)} fusion(bf16[2048,2432]{1,0:T(8,128)(2,1)} %bitcast.184, bf16[256,2048]{1,0:T(8,128)(2,1)} %param.15, f32[2048]{0:T(1024)S(1)} %bitcast.204, f32[256]{0:T(256)S(1)} %add_rsqrt_fusion.1), kind=kOutput, calls=%fused_computation.93 | convolution fusion | flops 2552233984 | bytes 13509632 | tf_op jit(solution)/shard_map/dot_general | solution.py:24
  142.7 6.1 collective-permute-done.17
  151.4 3.3 collective-permute-start.19
  154.7 9.3 %collective-permute-done.19.two_ref = bf16[2,256,384]{2,1,0:T(8,128)(2,1)S(1)} collective-permute-done((bf16[2,256,384]{2,1,0:T(8,128)(2,1)S(1)}, bf16[2,256,384]{2,1,0:T(8,128)(2,1)S(1)}, u32[]{:S(2)}, u32[]{:S(2)}) %collective-permute-start.19) | collective-permute-done | bytes 393248 | tf_op jit(solution)/shard_map/ppermute | solution.py:879
  167.3 2.6 collective-permute-start.23
  170.0 11.8 %attend.1 = bf16[256,1536]{1,0:T(8,128)(2,1)S(1)} custom-call(bf16[256,1536]{1,0:T(8,128)(2,1)S(1)} %get-tuple-element.137.q_ref, bf16[2,256,384]{2,1,0:T(8,128)(2,1)S(1)} %collective-permute-done.19.two_ref, bf16[2,256,384]{2,1,0:T(8,128)(2,1)S(1)} %collective-permute-done.20.one_ref, bf16[2,256,384]{2,1,0:T(8,128)(2,1)S(1)} %get-tuple-element.143.kv_ref, ...), custom_call_target="tpu_custom_call" | custom-call | tf_op jit(solution)/shard_map/attend/pallas_call | solution.py:169
  183.1 10.7 %place.5 = bf16[32,48,2048]{2,1,0:T(8,128)(2,1)} custom-call(s32[32]{0:T(128)S(1)} %stack.408.slots, bf16[8,48,2048]{2,1,0:T(8,128)(2,1)S(1)} %constant_dynamic-update-slice_fusion.refs_0_, bf16[8,48,2048]{2,1,0:T(8,128)(2,1)S(1)} %collective-permute-done.21.refs_1_, bf16[8,48,2048]{2,1,0:T(8,128)(2,1)S(1)} %constant_dynamic-update-slice_fusion.2.refs_2_, ...), custom_call_target="tpu_custom_call" | custom-call | bytes 12582912 | tf_op jit(solution)/shard_map/place/pallas_call | solution.py:456
  196.4 4.7 multiply_reduce_fusion.2
  201.5 7.0 %collective-permute-done.26.refs_4_ = bf16[256,1024]{1,0:T(8,128)(2,1)S(1)} collective-permute-done((bf16[256,1024]{1,0:T(8,128)(2,1)S(1)}, bf16[256,1024]{1,0:T(8,128)(2,1)S(1)}, u32[]{:S(2)}, u32[]{:S(2)}) %collective-permute-start.26) | collective-permute-done | bytes 524320 | tf_op jit(solution)/shard_map/ppermute | solution.py:737
  213.4 5.5 assemble.2
  219.0 14.8 %collective-permute-done.28.refs_2_ = bf16[256,2048]{1,0:T(8,128)(2,1)} collective-permute-done((bf16[256,2048]{1,0:T(8,128)(2,1)S(1)}, bf16[256,2048]{1,0:T(8,128)(2,1)}, u32[]{:S(2)}, u32[]{:S(2)}) %collective-permute-start.28) | collective-permute-done | bytes 1048608 | tf_op jit(solution)/shard_map/ppermute | solution.py:733
  239.0 11.8 %collective-permute-done.35.refs_4_ = bf16[256,1024]{1,0:T(8,128)(2,1)} collective-permute-done((bf16[256,1024]{1,0:T(8,128)(2,1)S(1)}, bf16[256,1024]{1,0:T(8,128)(2,1)}, u32[]{:S(2)}, u32[]{:S(2)}) %collective-permute-start.35) | collective-permute-done | bytes 524320 | tf_op jit(solution)/shard_map/ppermute | solution.py:737
  254.2 6.4 %assemble.3 = bf16[8,256,2048]{2,1,0:T(8,128)(2,1)} custom-call(bf16[256,2048]{1,0:T(8,128)(2,1)S(1)} %multiply_convert_fusion.refs_0_, bf16[256,2048]{1,0:T(8,128)(2,1)} %collective-permute-done.27.refs_1_, bf16[256,2048]{1,0:T(8,128)(2,1)} %collective-permute-done.28.refs_2_, bf16[256,1024]{1,0:T(8,128)(2,1)} %collective-permute-done.34.refs_3_, ...), custom_call_target="tpu_custom_call" | custom-call | bytes 16777216 | tf_op jit(solution)/shard_map/assemble/pallas_call | solution.py:632
  260.6 16.7 %feed.1 = (bf16[2048,640]{1,0:T(8,128)(2,1)S(1)}, bf16[2048,1280]{1,0:T(8,128)(2,1)}) custom-call(bf16[2048,2048]{1,0:T(8,128)(2,1)} %bitcast.188, bf16[2048,1280]{1,0:T(8,128)(2,1)} %all-gather.5.cloned.1.call-done.both_ref), custom_call_target="tpu_custom_call" | custom-call | flops 10737418240 | bytes 21495808 | tf_op jit(solution)/shard_map/feed/pallas_call | solution.py:244
  278.8 8.0 %convolution_convert_fusion.5 = bf16[640,2048]{1,0:T(8,128)(2,1)S(1)} fusion(bf16[2048,640]{1,0:T(8,128)(2,1)S(1)} %get-tuple-element.184, bf16[2048,2048]{1,0:T(8,128)(2,1)} %bitcast.186), kind=kOutput, calls=%fused_computation.11 | convolution fusion | flops 5370019840 | bytes 13631488 | tf_op jit(solution)/shard_map/dot_general | solution.py:32
  286.9 2.3 pick.4
  289.2 5.0 collective-permute-start.41
  294.2 29.8 %feed_back.1 = (bf16[2048,1280]{1,0:T(8,128)(2,1)}, bf16[4,256,2048]{2,1,0:T(8,128)(2,1)}, bf16[4,256,2048]{2,1,0:T(8,128)(2,1)}) custom-call(bf16[2048,2048]{1,0:T(8,128)(2,1)} %bitcast.187, bf16[640,2048]{1,0:T(8,128)(2,1)S(1)} %copy-done.25, bf16[2048,1280]{1,0:T(8,128)(2,1)} %get-tuple-element.163.slopes_ref, ...), custom_call_target="tpu_custom_call" | custom-call | flops 16106127360 | bytes 43515904 | tf_op jit(solution)/shard_map/feed_back/pallas_call | solution.py:296
  325.8 3.6 collective-permute-start.48
  329.4 3.8 collective-permute-done.43.got_ref
  333.2 5.0 merge.2
  341.2 16.8 %convolution_convert_fusion.2 = bf16[2048,1280]{1,0:T(8,128)(2,1)} fusion(bf16[2048,2048]{1,0:T(8,128)(2,1)} %bitcast.189, bf16[2048,1280]{1,0:T(8,128)(2,1)} %get-tuple-element.169), kind=kOutput, calls=%fused_computation.2 | convolution fusion | flops 10740039680 | bytes 18874368 | tf_op jit(solution)/shard_map/dot_general | solution.py:32
  358.0 5.2 convolution_convert_fusion.3
  368.6 5.0 convolution_convert_fusion.4
  373.6 4.1 pick.5
  378.3 2.1 collective-permute-done.47
  383.5 3.0 add_bitcast_fusion
  392.4 2.8 multiply_reduce_fusion
  395.8 6.5 %merge.3 = (bf16[2,256,1024]{2,1,0:T(8,128)(2,1)}, bf16[2,256,1024]{2,1,0:T(8,128)(2,1)}, f32[2,256,1024]{2,1,0:T(8,128)S(1)}, f32[2,256,1024]{2,1,0:T(8,128)}) custom-call(bf16[4,256,2048]{2,1,0:T(8,128)(2,1)} %bitcast.195, bf16[4,256,2048]{2,1,0:T(8,128)(2,1)} %collective-permute-done.49.got_ref), custom_call_target="tpu_custom_call" | custom-call | flops 2097152 | bytes 14680064 | tf_op jit(solution)/shard_map/merge/pallas_call | solution.py:686
  404.4 4.6 convolution_convert_fusion.6.gm_ref
  409.1 17.4 %attend_back.1 = (f32[256,1536]{1,0:T(8,128)S(1)}, bf16[2,256,384]{2,1,0:T(8,128)(2,1)S(1)}, bf16[2,256,384]{2,1,0:T(8,128)(2,1)S(1)}, f32[2,256,384]{2,1,0:T(8,128)S(1)}) custom-call(bf16[256,1536]{1,0:T(8,128)(2,1)S(1)} %copy-done.4, bf16[2,256,384]{2,1,0:T(8,128)(2,1)S(1)} %copy-done.10, bf16[2,256,384]{2,1,0:T(8,128)(2,1)S(1)} %copy-done.8, ...), custom_call_target="tpu_custom_call" | custom-call | tf_op jit(solution)/shard_map/attend_back/pallas_call | solution.py:214
  430.1 4.5 convolution_convert_fusion.1
  441.0 2.7 collective-permute-start.55
  445.4 9.3 %collective-permute-done.58.two_ref = bf16[2,256,384]{2,1,0:T(8,128)(2,1)S(1)} collective-permute-done((bf16[2,256,384]{2,1,0:T(8,128)(2,1)}, bf16[2,256,384]{2,1,0:T(8,128)(2,1)S(1)}, u32[]{:S(2)}, u32[]{:S(2)}) %collective-permute-start.58) | collective-permute-done | bytes 393248 | tf_op jit(solution)/shard_map/ppermute | solution.py:959
  454.7 5.7 head_back.1
  460.4 5.8 convolution_convert_fusion
  466.2 8.6 %pick.6 = (bf16[16,64,2432]{2,1,0:T(8,128)(2,1)}, bf16[16,64,2432]{2,1,0:T(8,128)(2,1)}) custom-call(s32[32]{0:T(128)S(1)} %stack.475.slots, bf16[32,64,2432]{2,1,0:T(8,128)(2,1)} %bitcast.182), custom_call_target="tpu_custom_call" | custom-call | bytes 19922944 | tf_op jit(solution)/shard_map/pick/pallas_call | solution.py:494
  483.8 5.6 fusion.37
  489.5 3.3 add_convert_fusion
  492.8 4.3 collective-permute-done.61
  500.7 27.4 %collective-permute-done.64 = bf16[1,256,1280]{2,1,0:T(8,128)(2,1)S(1)} collective-permute-done((bf16[1,256,1280]{2,1,0:T(8,128)(2,1)S(1)}, bf16[1,256,1280]{2,1,0:T(8,128)(2,1)S(1)}, u32[]{:S(2)}, u32[]{:S(2)}) %collective-permute-start.64) | collective-permute-done | bytes 655392 | tf_op jit(solution)/shard_map/ppermute | solution.py:902
  534.5 3.8 collective-permute-done.68
  539.6 4.1 pick.7
  543.8 12.1 %collective-permute-done.65 = bf16[2,64,2432]{2,1,0:T(8,128)(2,1)} collective-permute-done((bf16[2,64,2432]{2,1,0:T(8,128)(2,1)}, bf16[2,64,2432]{2,1,0:T(8,128)(2,1)}, u32[]{:S(2)}, u32[]{:S(2)}) %collective-permute-start.65) | collective-permute-done | bytes 622624 | tf_op jit(solution)/shard_map/ppermute | solution.py:733
  562.9 2.8 collective-permute-start.75
  567.1 2.5 collective-permute-start.74
  570.8 8.7 %collective-permute-done.76 = bf16[2,2,64,1280]{3,2,1,0:T(8,128)(2,1)S(1)} collective-permute-done((bf16[2,2,64,1280]{3,2,1,0:T(8,128)(2,1)S(1)}, bf16[2,2,64,1280]{3,2,1,0:T(8,128)(2,1)S(1)}, u32[]{:S(2)}, u32[]{:S(2)}) %collective-permute-start.76) | collective-permute-done | bytes 655392 | tf_op jit(solution)/shard_map/ppermute | solution.py:737
  580.9 14.1 %collective-permute-done.75 = bf16[64,2432]{1,0:T(8,128)(2,1)S(1)} collective-permute-done((bf16[64,2432]{1,0:T(8,128)(2,1)}, bf16[64,2432]{1,0:T(8,128)(2,1)S(1)}, u32[]{:S(2)}, u32[]{:S(2)}) %collective-permute-start.75) | collective-permute-done | bytes 311328 | tf_op jit(solution)/shard_map/ppermute | solution.py:750
  598.1 16.4 %reduce-scatter.2.cloned.1.call-done = bf16[48,2048]{1,0:T(8,128)(2,1)} async-done(((bf16[1536,2048]{1,0:T(8,128)(2,1)}), bf16[48,2048]{1,0:T(8,128)(2,1)}) %reduce-scatter.2.cloned.1.call-update) | async-done | bytes 196624 | tf_op jit(solution)/shard_map/reduce_scatter | solution.py:955
  616.3 2.5 join_units.1
  (411 shorter events, 132.2 us)
Async XLA Ops:
  7.2 121.8 %all-gather.3.cloned.1.call-start = ((), (), s32[]{:S(2)}) async-start(), calls=%async_computation.1 | async-start | bytes 3276800 | tf_op jit(solution)/shard_map/all_gather | solution.py:850
  10.6 17.7 %collective-permute-start.3 = (bf16[4,64,1280]{2,1,0:T(8,128)(2,1)S(1)}, bf16[4,64,1280]{2,1,0:T(8,128)(2,1)S(1)}, u32[]{:S(2)}, u32[]{:S(2)}) collective-permute-start(bf16[4,64,1280]{2,1,0:T(8,128)(2,1)S(1)} %get-tuple-element.258), channel_id=1, source_target_pairs={{0,2},{1,3},{2,0},{3,1},{4,6},{5,7},{6,4},{7,5},{8,10},{9,11},{10,... | collective-permute-start | bytes 1966088 | tf_op jit(solution)/shard_map/ppermute | solution.py:737
  13.8 16.5 %collective-permute-start.1 = (bf16[64,2432]{1,0:T(8,128)(2,1)S(1)}, bf16[64,2432]{1,0:T(8,128)(2,1)S(1)}, u32[]{:S(2)}, u32[]{:S(2)}) collective-permute-start(bf16[64,2432]{1,0:T(8,128)(2,1)S(1)} %fusion.25), channel_id=1, source_target_pairs={{0,24},{4,28},{8,0},{12,4},{16,8},{20,12},{24,16},{28,20},{1,25},{... | collective-permute-start | bytes 933896 | tf_op jit(solution)/shard_map/ppermute | solution.py:529
  17.5 15.5 %collective-permute-start = (bf16[64,2432]{1,0:T(8,128)(2,1)S(1)}, bf16[64,2432]{1,0:T(8,128)(2,1)S(1)}, u32[]{:S(2)}, u32[]{:S(2)}) collective-permute-start(bf16[64,2432]{1,0:T(8,128)(2,1)S(1)} %fusion.25), channel_id=1, source_target_pairs={{0,8},{4,12},{8,16},{12,20},{16,24},{20,28},{24,0},{28,4},{1,9},{5... | collective-permute-start | bytes 933896 | tf_op jit(solution)/shard_map/ppermute | solution.py:529
  17.5 26.2 %collective-permute-start.2 = (bf16[64,2432]{1,0:T(8,128)(2,1)S(1)}, bf16[64,2432]{1,0:T(8,128)(2,1)S(1)}, u32[]{:S(2)}, u32[]{:S(2)}) collective-permute-start(bf16[64,2432]{1,0:T(8,128)(2,1)S(1)} %fusion.25), channel_id=1, source_target_pairs={{0,16},{4,20},{8,24},{12,28},{16,0},{20,4},{24,8},{28,12},{1,17},{... | collective-permute-start | bytes 933896 | tf_op jit(solution)/shard_map/ppermute | solution.py:529
  28.5 16.0 %collective-permute-start.4 = (bf16[2,2,64,1280]{3,2,1,0:T(8,128)(2,1)S(1)}, bf16[2,2,64,1280]{3,2,1,0:T(8,128)(2,1)S(1)}, u32[]{:S(2)}, u32[]{:S(2)}) collective-permute-start(bf16[2,2,64,1280]{3,2,1,0:T(8,128)(2,1)S(1)} %get-tuple-element.256), channel_id=1, source_target_pairs={{0,4},{4,0},{8,12},{12,8},{16,20},{20,16},{24,28},{28,24},{1,5},{5... | collective-permute-start | bytes 1966088 | tf_op jit(solution)/shard_map/ppermute | solution.py:733
  44.6 13.2 %collective-permute-start.9 = (bf16[48,2048]{1,0:T(8,128)(2,1)S(1)}, bf16[48,2048]{1,0:T(8,128)(2,1)S(1)}, u32[]{:S(2)}, u32[]{:S(2)}) collective-permute-start(bf16[48,2048]{1,0:T(8,128)(2,1)S(1)} %copy-done.71), channel_id=1, source_target_pairs={{0,16},{4,20},{8,24},{12,28},{16,0},{20,4},{24,8},{28,12},{1,17},{... | collective-permute-start | bytes 589832 | tf_op jit(solution)/shard_map/ppermute | solution.py:529
  48.5 11.4 %collective-permute-start.7 = (bf16[48,2048]{1,0:T(8,128)(2,1)S(1)}, bf16[48,2048]{1,0:T(8,128)(2,1)S(1)}, u32[]{:S(2)}, u32[]{:S(2)}) collective-permute-start(bf16[48,2048]{1,0:T(8,128)(2,1)S(1)} %copy-done.71), channel_id=1, source_target_pairs={{0,8},{4,12},{8,16},{12,20},{16,24},{20,28},{24,0},{28,4},{1,9},{5... | collective-permute-start | bytes 589832 | tf_op jit(solution)/shard_map/ppermute | solution.py:529
  49.3 13.2 %collective-permute-start.6 = (bf16[2,64,2432]{2,1,0:T(8,128)(2,1)S(1)}, bf16[2,64,2432]{2,1,0:T(8,128)(2,1)S(1)}, u32[]{:S(2)}, u32[]{:S(2)}) collective-permute-start(bf16[2,64,2432]{2,1,0:T(8,128)(2,1)S(1)} %get-tuple-element.259), channel_id=1, source_target_pairs={{0,2},{1,3},{2,0},{3,1},{4,6},{5,7},{6,4},{7,5},{8,10},{9,11},{10,... | collective-permute-start | bytes 1867784 | tf_op jit(solution)/shard_map/ppermute | solution.py:737
  50.9 12.9 %collective-permute-start.5 = (bf16[2,64,2432]{2,1,0:T(8,128)(2,1)S(1)}, bf16[2,64,2432]{2,1,0:T(8,128)(2,1)S(1)}, u32[]{:S(2)}, u32[]{:S(2)}) collective-permute-start(bf16[2,64,2432]{2,1,0:T(8,128)(2,1)S(1)} %get-tuple-element.260), channel_id=1, source_target_pairs={{0,4},{4,0},{8,12},{12,8},{16,20},{20,16},{24,28},{28,24},{1,5},{5... | collective-permute-start | bytes 1867784 | tf_op jit(solution)/shard_map/ppermute | solution.py:733
  69.1 37.7 %collective-permute-start.11 = (bf16[4,64,2432]{2,1,0:T(8,128)(2,1)S(1)}, bf16[4,64,2432]{2,1,0:T(8,128)(2,1)}, u32[]{:S(2)}, u32[]{:S(2)}) collective-permute-start(bf16[4,64,2432]{2,1,0:T(8,128)(2,1)S(1)} %pad_maximum_fusion.8), channel_id=1, source_target_pairs={{0,2},{1,3},{2,0},{3,1},{4,6},{5,7},{6,4},{7,5},{8,10},{9,11},{10,... | collective-permute-start | bytes 3735560 | tf_op jit(solution)/shard_map/ppermute | solution.py:737
  70.6 32.4 %collective-permute-start.14 = (bf16[2,48,2048]{2,1,0:T(8,128)(2,1)S(1)}, bf16[2,48,2048]{2,1,0:T(8,128)(2,1)S(1)}, u32[]{:S(2)}, u32[]{:S(2)}) collective-permute-start(bf16[2,48,2048]{2,1,0:T(8,128)(2,1)S(1)} %get-tuple-element.261), channel_id=1, source_target_pairs={{0,2},{1,3},{2,0},{3,1},{4,6},{5,7},{6,4},{7,5},{8,10},{9,11},{10,... | collective-permute-start | bytes 1179656 | tf_op jit(solution)/shard_map/ppermute | solution.py:737
  72.1 188.5 %all-gather.5.cloned.1.call-start = ((), (), s32[]{:S(2)}) async-start(), calls=%async_computation.2 | async-start | bytes 6553600 | tf_op jit(solution)/shard_map/all_gather | solution.py:856
  72.2 36.6 %collective-permute-start.12 = (bf16[4,64,2432]{2,1,0:T(8,128)(2,1)}, bf16[4,64,2432]{2,1,0:T(8,128)(2,1)S(1)}, u32[]{:S(2)}, u32[]{:S(2)}) collective-permute-start(bf16[4,64,2432]{2,1,0:T(8,128)(2,1)} %pad_maximum_fusion.9), channel_id=1, source_target_pairs={{0,4},{4,0},{8,12},{12,8},{16,20},{20,16},{24,28},{28,24},{1,5},{5... | collective-permute-start | bytes 3735560 | tf_op jit(solution)/shard_map/ppermute | solution.py:733
  73.8 32.1 %collective-permute-start.13 = (bf16[2,48,2048]{2,1,0:T(8,128)(2,1)S(1)}, bf16[2,48,2048]{2,1,0:T(8,128)(2,1)S(1)}, u32[]{:S(2)}, u32[]{:S(2)}) collective-permute-start(bf16[2,48,2048]{2,1,0:T(8,128)(2,1)S(1)} %get-tuple-element.262), channel_id=1, source_target_pairs={{0,4},{4,0},{8,12},{12,8},{16,20},{20,16},{24,28},{28,24},{1,5},{5... | collective-permute-start | bytes 1179656 | tf_op jit(solution)/shard_map/ppermute | solution.py:733
  114.8 499.7 %reduce-scatter.2.cloned.1.call-start = ((), (), s32[]{:S(2)}) async-start(), calls=%async_computation.3 | async-start | bytes 6488064 | tf_op jit(solution)/shard_map/reduce_scatter | solution.py:955
  129.0 19.9 %collective-permute-start.17 = (bf16[4,48,2048]{2,1,0:T(8,128)(2,1)}, bf16[4,48,2048]{2,1,0:T(8,128)(2,1)S(1)}, u32[]{:S(2)}, u32[]{:S(2)}) collective-permute-start(bf16[4,48,2048]{2,1,0:T(8,128)(2,1)} %pad_maximum_fusion.11), channel_id=1, source_target_pairs={{0,2},{1,3},{2,0},{3,1},{4,6},{5,7},{6,4},{7,5},{8,10},{9,11},{10,... | collective-permute-start | bytes 2359304 | tf_op jit(solution)/shard_map/ppermute | solution.py:737
  130.5 19.6 %collective-permute-start.18 = (bf16[4,48,2048]{2,1,0:T(8,128)(2,1)}, bf16[4,48,2048]{2,1,0:T(8,128)(2,1)S(1)}, u32[]{:S(2)}, u32[]{:S(2)}) collective-permute-start(bf16[4,48,2048]{2,1,0:T(8,128)(2,1)} %pad_maximum_fusion.12), channel_id=1, source_target_pairs={{0,4},{4,0},{8,12},{12,8},{16,20},{20,16},{24,28},{28,24},{1,5},{5... | collective-permute-start | bytes 2359304 | tf_op jit(solution)/shard_map/ppermute | solution.py:733
  151.4 12.6 %collective-permute-start.19 = (bf16[2,256,384]{2,1,0:T(8,128)(2,1)S(1)}, bf16[2,256,384]{2,1,0:T(8,128)(2,1)S(1)}, u32[]{:S(2)}, u32[]{:S(2)}) collective-permute-start(bf16[2,256,384]{2,1,0:T(8,128)(2,1)S(1)} %get-tuple-element.143.kv_ref), channel_id=1, source_target_pairs={{0,2},{1,3},{4,6},{5,7},{8,10},{9,11},{12,14},{13,15},{16,18},{17,... | collective-permute-start | bytes 1179656 | tf_op jit(solution)/shard_map/ppermute | solution.py:879
  164.0 17.8 %collective-permute-start.21 = (bf16[8,48,2048]{2,1,0:T(8,128)(2,1)S(1)}, bf16[8,48,2048]{2,1,0:T(8,128)(2,1)S(1)}, u32[]{:S(2)}, u32[]{:S(2)}) collective-permute-start(bf16[8,48,2048]{2,1,0:T(8,128)(2,1)S(1)} %constant_dynamic-update-slice_fusion.refs_0_), channel_id=1, source_target_pairs={{0,1},{1,0},{2,3},{3,2},{4,5},{5,4},{6,7},{7,6},{8,9},{9,8},{10,11... | collective-permute-start | bytes 4718600 | tf_op jit(solution)/shard_map/ppermute | solution.py:737
  165.8 16.1 %collective-permute-start.22 = (bf16[8,48,2048]{2,1,0:T(8,128)(2,1)S(1)}, bf16[8,48,2048]{2,1,0:T(8,128)(2,1)S(1)}, u32[]{:S(2)}, u32[]{:S(2)}) collective-permute-start(bf16[8,48,2048]{2,1,0:T(8,128)(2,1)S(1)} %constant_dynamic-update-slice_fusion.2.refs_2_), channel_id=1, source_target_pairs={{0,1},{1,0},{2,3},{3,2},{4,5},{5,4},{6,7},{7,6},{8,9},{9,8},{10,11... | collective-permute-start | bytes 4718600 | tf_op jit(solution)/shard_map/ppermute | solution.py:737
  165.8 28.0 %collective-permute-start.24 = (bf16[256,2048]{1,0:T(8,128)(2,1)S(1)}, bf16[256,2048]{1,0:T(8,128)(2,1)S(1)}, u32[]{:S(2)}, u32[]{:S(2)}) collective-permute-start(bf16[256,2048]{1,0:T(8,128)(2,1)S(1)} %copy-done.2), channel_id=1, source_target_pairs={{0,4},{4,0},{8,12},{12,8},{16,20},{20,16},{24,28},{28,24},{1,5},{5... | collective-permute-start | bytes 3145736 | tf_op jit(solution)/shard_map/ppermute | solution.py:733
  167.3 26.5 %collective-permute-start.23 = (bf16[256,2048]{1,0:T(8,128)(2,1)S(1)}, bf16[256,2048]{1,0:T(8,128)(2,1)S(1)}, u32[]{:S(2)}, u32[]{:S(2)}) collective-permute-start(bf16[256,2048]{1,0:T(8,128)(2,1)S(1)} %copy-done.2), channel_id=1, source_target_pairs={{0,2},{1,3},{2,0},{3,1},{4,6},{5,7},{6,4},{7,5},{8,10},{9,11},{10,... | collective-permute-start | bytes 3145736 | tf_op jit(solution)/shard_map/ppermute | solution.py:737
  193.9 16.8 %collective-permute-start.30 = (bf16[256,2048]{1,0:T(8,128)(2,1)S(1)}, bf16[256,2048]{1,0:T(8,128)(2,1)S(1)}, u32[]{:S(2)}, u32[]{:S(2)}) collective-permute-start(bf16[256,2048]{1,0:T(8,128)(2,1)S(1)} %collective-permute-done.23.refs_1_), channel_id=1, source_target_pairs={{0,1},{1,0},{2,3},{3,2},{4,5},{5,4},{6,7},{7,6},{8,9},{9,8},{10,11... | collective-permute-start | bytes 3145736 | tf_op jit(solution)/shard_map/ppermute | solution.py:737
  194.0 17.2 %collective-permute-start.31 = (bf16[256,2048]{1,0:T(8,128)(2,1)S(1)}, bf16[256,2048]{1,0:T(8,128)(2,1)S(1)}, u32[]{:S(2)}, u32[]{:S(2)}) collective-permute-start(bf16[256,2048]{1,0:T(8,128)(2,1)S(1)} %collective-permute-done.24.refs_2_), channel_id=1, source_target_pairs={{0,1},{1,0},{2,3},{3,2},{4,5},{5,4},{6,7},{7,6},{8,9},{9,8},{10,11... | collective-permute-start | bytes 3145736 | tf_op jit(solution)/shard_map/ppermute | solution.py:737
  194.6 13.9 %collective-permute-start.26 = (bf16[256,1024]{1,0:T(8,128)(2,1)S(1)}, bf16[256,1024]{1,0:T(8,128)(2,1)S(1)}, u32[]{:S(2)}, u32[]{:S(2)}) collective-permute-start(bf16[256,1024]{1,0:T(8,128)(2,1)S(1)} %slice.225), channel_id=1, source_target_pairs={{0,2},{1,3},{2,0},{3,1},{4,6},{5,7},{6,4},{7,5},{8,10},{9,11},{10,... | collective-permute-start | bytes 1572872 | tf_op jit(solution)/shard_map/ppermute | solution.py:737
  195.9 13.6 %collective-permute-start.25 = (bf16[256,1024]{1,0:T(8,128)(2,1)S(1)}, bf16[256,1024]{1,0:T(8,128)(2,1)S(1)}, u32[]{:S(2)}, u32[]{:S(2)}) collective-permute-start(bf16[256,1024]{1,0:T(8,128)(2,1)S(1)} %slice.224), channel_id=1, source_target_pairs={{0,4},{4,0},{8,12},{12,8},{16,20},{20,16},{24,28},{28,24},{1,5},{5... | collective-permute-start | bytes 1572872 | tf_op jit(solution)/shard_map/ppermute | solution.py:733
  196.4 14.3 %collective-permute-start.29 = (bf16[256,2048]{1,0:T(8,128)(2,1)S(1)}, bf16[256,2048]{1,0:T(8,128)(2,1)S(1)}, u32[]{:S(2)}, u32[]{:S(2)}) collective-permute-start(bf16[256,2048]{1,0:T(8,128)(2,1)S(1)} %copy-done.2), channel_id=1, source_target_pairs={{0,1},{1,0},{2,3},{3,2},{4,5},{5,4},{6,7},{7,6},{8,9},{9,8},{10,11... | collective-permute-start | bytes 3145736 | tf_op jit(solution)/shard_map/ppermute | solution.py:737
  209.6 24.2 %collective-permute-start.28 = (bf16[256,2048]{1,0:T(8,128)(2,1)S(1)}, bf16[256,2048]{1,0:T(8,128)(2,1)}, u32[]{:S(2)}, u32[]{:S(2)}) collective-permute-start(bf16[256,2048]{1,0:T(8,128)(2,1)S(1)} %multiply_convert_fusion.refs_0_), channel_id=1, source_target_pairs={{0,4},{4,0},{8,12},{12,8},{16,20},{20,16},{24,28},{28,24},{1,5},{5... | collective-permute-start | bytes 3145736 | tf_op jit(solution)/shard_map/ppermute | solution.py:733
  210.1 23.9 %collective-permute-start.27 = (bf16[256,2048]{1,0:T(8,128)(2,1)S(1)}, bf16[256,2048]{1,0:T(8,128)(2,1)}, u32[]{:S(2)}, u32[]{:S(2)}) collective-permute-start(bf16[256,2048]{1,0:T(8,128)(2,1)S(1)} %multiply_convert_fusion.refs_0_), channel_id=1, source_target_pairs={{0,2},{1,3},{2,0},{3,1},{4,6},{5,7},{6,4},{7,5},{8,10},{9,11},{10,... | collective-permute-start | bytes 3145736 | tf_op jit(solution)/shard_map/ppermute | solution.py:737
  235.1 16.9 %collective-permute-start.37 = (bf16[256,2048]{1,0:T(8,128)(2,1)}, bf16[256,2048]{1,0:T(8,128)(2,1)}, u32[]{:S(2)}, u32[]{:S(2)}) collective-permute-start(bf16[256,2048]{1,0:T(8,128)(2,1)} %collective-permute-done.27.refs_1_), channel_id=1, source_target_pairs={{0,1},{1,0},{2,3},{3,2},{4,5},{5,4},{6,7},{7,6},{8,9},{9,8},{10,11... | collective-permute-start | bytes 3145736 | tf_op jit(solution)/shard_map/ppermute | solution.py:737
  236.2 15.8 %collective-permute-start.36 = (bf16[256,2048]{1,0:T(8,128)(2,1)S(1)}, bf16[256,2048]{1,0:T(8,128)(2,1)}, u32[]{:S(2)}, u32[]{:S(2)}) collective-permute-start(bf16[256,2048]{1,0:T(8,128)(2,1)S(1)} %multiply_convert_fusion.refs_0_), channel_id=1, source_target_pairs={{0,1},{1,0},{2,3},{3,2},{4,5},{5,4},{6,7},{7,6},{8,9},{9,8},{10,11... | collective-permute-start | bytes 3145736 | tf_op jit(solution)/shard_map/ppermute | solution.py:737
  236.8 14.0 %collective-permute-start.35 = (bf16[256,1024]{1,0:T(8,128)(2,1)S(1)}, bf16[256,1024]{1,0:T(8,128)(2,1)}, u32[]{:S(2)}, u32[]{:S(2)}) collective-permute-start(bf16[256,1024]{1,0:T(8,128)(2,1)S(1)} %slice.227), channel_id=1, source_target_pairs={{0,2},{1,3},{2,0},{3,1},{4,6},{5,7},{6,4},{7,5},{8,10},{9,11},{10,... | collective-permute-start | bytes 1572872 | tf_op jit(solution)/shard_map/ppermute | solution.py:737
  237.5 14.5 %collective-permute-start.38 = (bf16[256,2048]{1,0:T(8,128)(2,1)}, bf16[256,2048]{1,0:T(8,128)(2,1)}, u32[]{:S(2)}, u32[]{:S(2)}) collective-permute-start(bf16[256,2048]{1,0:T(8,128)(2,1)} %collective-permute-done.28.refs_2_), channel_id=1, source_target_pairs={{0,1},{1,0},{2,3},{3,2},{4,5},{5,4},{6,7},{7,6},{8,9},{9,8},{10,11... | collective-permute-start | bytes 3145736 | tf_op jit(solution)/shard_map/ppermute | solution.py:737
  237.5 14.4 %collective-permute-start.34 = (bf16[256,1024]{1,0:T(8,128)(2,1)S(1)}, bf16[256,1024]{1,0:T(8,128)(2,1)}, u32[]{:S(2)}, u32[]{:S(2)}) collective-permute-start(bf16[256,1024]{1,0:T(8,128)(2,1)S(1)} %slice.226), channel_id=1, source_target_pairs={{0,4},{4,0},{8,12},{12,8},{16,20},{20,16},{24,28},{28,24},{1,5},{5... | collective-permute-start | bytes 1572872 | tf_op jit(solution)/shard_map/ppermute | solution.py:733
  289.2 34.8 %collective-permute-start.41 = (bf16[1,160,2048]{2,1,0:T(8,128)(2,1)S(1)}, bf16[1,160,2048]{2,1,0:T(8,128)(2,1)S(1)}, u32[]{:S(2)}, u32[]{:S(2)}) collective-permute-start(bf16[1,160,2048]{2,1,0:T(8,128)(2,1)S(1)} %get-tuple-element.167), channel_id=1, source_target_pairs={{0,8},{4,12},{8,16},{12,20},{16,24},{20,28},{24,0},{28,4},{1,9},{5... | collective-permute-start | bytes 1966088 | tf_op jit(solution)/shard_map/ppermute | solution.py:902
  294.2 29.8 %collective-permute-start.42 = (bf16[1,160,2048]{2,1,0:T(8,128)(2,1)S(1)}, bf16[1,160,2048]{2,1,0:T(8,128)(2,1)S(1)}, u32[]{:S(2)}, u32[]{:S(2)}) collective-permute-start(bf16[1,160,2048]{2,1,0:T(8,128)(2,1)S(1)} %get-tuple-element.168), channel_id=1, source_target_pairs={{0,24},{4,28},{8,0},{12,4},{16,8},{20,12},{24,16},{28,20},{1,25},{... | collective-permute-start | bytes 1966088 | tf_op jit(solution)/shard_map/ppermute | solution.py:902
  325.8 57.5 %collective-permute-start.48 = (bf16[1,160,2048]{2,1,0:T(8,128)(2,1)}, bf16[1,160,2048]{2,1,0:T(8,128)(2,1)}, u32[]{:S(2)}, u32[]{:S(2)}) collective-permute-start(bf16[1,160,2048]{2,1,0:T(8,128)(2,1)} %copy-done.33), channel_id=1, source_target_pairs={{0,16},{4,20},{8,24},{12,28},{16,0},{20,4},{24,8},{28,12},{1,17},{... | collective-permute-start | bytes 1966088 | tf_op jit(solution)/shard_map/ppermute | solution.py:902
  338.2 25.2 %collective-permute-start.44 = (bf16[2,256,1024]{2,1,0:T(8,128)(2,1)S(1)}, bf16[2,256,1024]{2,1,0:T(8,128)(2,1)S(1)}, u32[]{:S(2)}, u32[]{:S(2)}) collective-permute-start(bf16[2,256,1024]{2,1,0:T(8,128)(2,1)S(1)} %get-tuple-element.181), channel_id=1, source_target_pairs={{0,4},{4,0},{8,12},{12,8},{16,20},{20,16},{24,28},{28,24},{1,5},{5... | collective-permute-start | bytes 3145736 | tf_op jit(solution)/shard_map/ppermute | solution.py:733
  339.8 26.1 %collective-permute-start.46 = (bf16[2,256,1024]{2,1,0:T(8,128)(2,1)S(1)}, bf16[2,256,1024]{2,1,0:T(8,128)(2,1)S(1)}, u32[]{:S(2)}, u32[]{:S(2)}) collective-permute-start(bf16[2,256,1024]{2,1,0:T(8,128)(2,1)S(1)} %get-tuple-element.183), channel_id=1, source_target_pairs={{0,2},{1,3},{2,0},{3,1},{4,6},{5,7},{6,4},{7,5},{8,10},{9,11},{10,... | collective-permute-start | bytes 3145736 | tf_op jit(solution)/shard_map/ppermute | solution.py:737
  364.3 13.7 %collective-permute-start.45 = (bf16[256,1024]{1,0:T(8,128)(2,1)}, bf16[256,1024]{1,0:T(8,128)(2,1)S(1)}, u32[]{:S(2)}, u32[]{:S(2)}) collective-permute-start(bf16[256,1024]{1,0:T(8,128)(2,1)} %fusion.17), channel_id=1, source_target_pairs={{0,2},{1,3},{2,0},{3,1},{4,6},{5,7},{6,4},{7,5},{8,10},{9,11},{10,... | collective-permute-start | bytes 1572872 | tf_op jit(solution)/shard_map/ppermute | solution.py:737
  367.0 13.3 %collective-permute-start.47 = (bf16[256,1024]{1,0:T(8,128)(2,1)}, bf16[256,1024]{1,0:T(8,128)(2,1)}, u32[]{:S(2)}, u32[]{:S(2)}) collective-permute-start(bf16[256,1024]{1,0:T(8,128)(2,1)} %fusion.18), channel_id=1, source_target_pairs={{0,4},{4,0},{8,12},{12,8},{16,20},{20,16},{24,28},{28,24},{1,5},{5... | collective-permute-start | bytes 1572872 | tf_op jit(solution)/shard_map/ppermute | solution.py:733
  383.3 12.5 %collective-permute-start.49 = (bf16[4,256,2048]{2,1,0:T(8,128)(2,1)}, bf16[4,256,2048]{2,1,0:T(8,128)(2,1)}, u32[]{:S(2)}, u32[]{:S(2)}) collective-permute-start(bf16[4,256,2048]{2,1,0:T(8,128)(2,1)} %bitcast.85), channel_id=1, source_target_pairs={{0,1},{1,0},{2,3},{3,2},{4,5},{5,4},{6,7},{7,6},{8,9},{9,8},{10,11... | collective-permute-start | bytes 12582920 | tf_op jit(solution)/shard_map/ppermute | solution.py:737
  386.5 48.0 %collective-permute-start.52 = (bf16[1,256,1280]{2,1,0:T(8,128)(2,1)}, bf16[1,256,1280]{2,1,0:T(8,128)(2,1)}, u32[]{:S(2)}, u32[]{:S(2)}) collective-permute-start(bf16[1,256,1280]{2,1,0:T(8,128)(2,1)} %get-tuple-element.199), channel_id=1, source_target_pairs={{0,8},{4,12},{8,16},{12,20},{16,24},{20,28},{24,0},{28,4},{1,9},{5... | collective-permute-start | bytes 1966088 | tf_op jit(solution)/shard_map/ppermute | solution.py:902
  388.5 46.0 %collective-permute-start.53 = (bf16[1,256,1280]{2,1,0:T(8,128)(2,1)}, bf16[1,256,1280]{2,1,0:T(8,128)(2,1)}, u32[]{:S(2)}, u32[]{:S(2)}) collective-permute-start(bf16[1,256,1280]{2,1,0:T(8,128)(2,1)} %get-tuple-element.200), channel_id=1, source_target_pairs={{0,8},{4,12},{8,16},{12,20},{16,24},{20,28},{24,0},{28,4},{1,9},{5... | collective-permute-start | bytes 1966088 | tf_op jit(solution)/shard_map/ppermute | solution.py:902
  390.5 44.0 %collective-permute-start.54 = (bf16[1,256,1280]{2,1,0:T(8,128)(2,1)}, bf16[1,256,1280]{2,1,0:T(8,128)(2,1)}, u32[]{:S(2)}, u32[]{:S(2)}) collective-permute-start(bf16[1,256,1280]{2,1,0:T(8,128)(2,1)} %get-tuple-element.201), channel_id=1, source_target_pairs={{0,24},{4,28},{8,0},{12,4},{16,8},{20,12},{24,16},{28,20},{1,25},{... | collective-permute-start | bytes 1966088 | tf_op jit(solution)/shard_map/ppermute | solution.py:902
  402.2 32.3 %collective-permute-start.50 = (bf16[2,256,1024]{2,1,0:T(8,128)(2,1)}, bf16[2,256,1024]{2,1,0:T(8,128)(2,1)}, u32[]{:S(2)}, u32[]{:S(2)}) collective-permute-start(bf16[2,256,1024]{2,1,0:T(8,128)(2,1)} %get-tuple-element.196), channel_id=1, source_target_pairs={{0,4},{4,0},{8,12},{12,8},{16,20},{20,16},{24,28},{28,24},{1,5},{5... | collective-permute-start | bytes 3145736 | tf_op jit(solution)/shard_map/ppermute | solution.py:733
  403.7 30.8 %collective-permute-start.51 = (bf16[2,256,1024]{2,1,0:T(8,128)(2,1)}, bf16[2,256,1024]{2,1,0:T(8,128)(2,1)}, u32[]{:S(2)}, u32[]{:S(2)}) collective-permute-start(bf16[2,256,1024]{2,1,0:T(8,128)(2,1)} %get-tuple-element.198), channel_id=1, source_target_pairs={{0,2},{1,3},{2,0},{3,1},{4,6},{5,7},{6,4},{7,5},{8,10},{9,11},{10,... | collective-permute-start | bytes 3145736 | tf_op jit(solution)/shard_map/ppermute | solution.py:737
  436.2 18.5 %collective-permute-start.58 = (bf16[2,256,384]{2,1,0:T(8,128)(2,1)}, bf16[2,256,384]{2,1,0:T(8,128)(2,1)S(1)}, u32[]{:S(2)}, u32[]{:S(2)}) collective-permute-start(bf16[2,256,384]{2,1,0:T(8,128)(2,1)} %copy-done.34), channel_id=1, source_target_pairs={{2,0},{3,1},{6,4},{7,5},{10,8},{11,9},{14,12},{15,13},{18,16},{19,... | collective-permute-start | bytes 1179656 | tf_op jit(solution)/shard_map/ppermute | solution.py:959
  439.0 35.8 %collective-permute-start.56 = (bf16[256,1024]{1,0:T(8,128)(2,1)S(1)}, bf16[256,1024]{1,0:T(8,128)(2,1)S(1)}, u32[]{:S(2)}, u32[]{:S(2)}) collective-permute-start(bf16[256,1024]{1,0:T(8,128)(2,1)S(1)} %fusion.20), channel_id=1, source_target_pairs={{0,4},{4,0},{8,12},{12,8},{16,20},{20,16},{24,28},{28,24},{1,5},{5... | collective-permute-start | bytes 1572872 | tf_op jit(solution)/shard_map/ppermute | solution.py:733
  441.0 35.1 %collective-permute-start.55 = (bf16[256,1024]{1,0:T(8,128)(2,1)S(1)}, bf16[256,1024]{1,0:T(8,128)(2,1)S(1)}, u32[]{:S(2)}, u32[]{:S(2)}) collective-permute-start(bf16[256,1024]{1,0:T(8,128)(2,1)S(1)} %fusion.19), channel_id=1, source_target_pairs={{0,2},{1,3},{2,0},{3,1},{4,6},{5,7},{6,4},{7,5},{8,10},{9,11},{10,... | collective-permute-start | bytes 1572872 | tf_op jit(solution)/shard_map/ppermute | solution.py:737
  443.7 35.4 %collective-permute-start.59 = (bf16[1,256,1280]{2,1,0:T(8,128)(2,1)S(1)}, bf16[1,256,1280]{2,1,0:T(8,128)(2,1)S(1)}, u32[]{:S(2)}, u32[]{:S(2)}) collective-permute-start(bf16[1,256,1280]{2,1,0:T(8,128)(2,1)S(1)} %copy-done.32), channel_id=1, source_target_pairs={{0,16},{4,20},{8,24},{12,28},{16,0},{20,4},{24,8},{28,12},{1,17},{... | collective-permute-start | bytes 1966088 | tf_op jit(solution)/shard_map/ppermute | solution.py:902
  481.0 16.2 %collective-permute-start.61 = (bf16[1,256,1280]{2,1,0:T(8,128)(2,1)S(1)}, bf16[1,256,1280]{2,1,0:T(8,128)(2,1)S(1)}, u32[]{:S(2)}, u32[]{:S(2)}) collective-permute-start(bf16[1,256,1280]{2,1,0:T(8,128)(2,1)S(1)} %copy-done.30), channel_id=1, source_target_pairs={{0,24},{4,28},{8,0},{12,4},{16,8},{20,12},{24,16},{28,20},{1,25},{... | collective-permute-start | bytes 1966088 | tf_op jit(solution)/shard_map/ppermute | solution.py:902
  497.9 30.3 %collective-permute-start.64 = (bf16[1,256,1280]{2,1,0:T(8,128)(2,1)S(1)}, bf16[1,256,1280]{2,1,0:T(8,128)(2,1)S(1)}, u32[]{:S(2)}, u32[]{:S(2)}) collective-permute-start(bf16[1,256,1280]{2,1,0:T(8,128)(2,1)S(1)} %copy-done.28), channel_id=1, source_target_pairs={{0,16},{4,20},{8,24},{12,28},{16,0},{20,4},{24,8},{28,12},{1,17},{... | collective-permute-start | bytes 1966088 | tf_op jit(solution)/shard_map/ppermute | solution.py:902
  498.0 31.8 %collective-permute-start.62 = (bf16[4,64,2432]{2,1,0:T(8,128)(2,1)S(1)}, bf16[4,64,2432]{2,1,0:T(8,128)(2,1)S(1)}, u32[]{:S(2)}, u32[]{:S(2)}) collective-permute-start(bf16[4,64,2432]{2,1,0:T(8,128)(2,1)S(1)} %get-tuple-element.221), channel_id=1, source_target_pairs={{0,2},{1,3},{2,0},{3,1},{4,6},{5,7},{6,4},{7,5},{8,10},{9,11},{10,... | collective-permute-start | bytes 3735560 | tf_op jit(solution)/shard_map/ppermute | solution.py:737
  499.6 31.3 %collective-permute-start.63 = (bf16[4,64,2432]{2,1,0:T(8,128)(2,1)S(1)}, bf16[4,64,2432]{2,1,0:T(8,128)(2,1)S(1)}, u32[]{:S(2)}, u32[]{:S(2)}) collective-permute-start(bf16[4,64,2432]{2,1,0:T(8,128)(2,1)S(1)} %get-tuple-element.222), channel_id=1, source_target_pairs={{0,4},{4,0},{8,12},{12,8},{16,20},{20,16},{24,28},{28,24},{1,5},{5... | collective-permute-start | bytes 3735560 | tf_op jit(solution)/shard_map/ppermute | solution.py:733
  532.2 23.8 %collective-permute-start.65 = (bf16[2,64,2432]{2,1,0:T(8,128)(2,1)}, bf16[2,64,2432]{2,1,0:T(8,128)(2,1)}, u32[]{:S(2)}, u32[]{:S(2)}) collective-permute-start(bf16[2,64,2432]{2,1,0:T(8,128)(2,1)} %add_convert_fusion.10), channel_id=1, source_target_pairs={{0,4},{4,0},{8,12},{12,8},{16,20},{20,16},{24,28},{28,24},{1,5},{5... | collective-permute-start | bytes 1867784 | tf_op jit(solution)/shard_map/ppermute | solution.py:733
  538.7 18.9 %collective-permute-start.66 = (bf16[2,64,2432]{2,1,0:T(8,128)(2,1)S(1)}, bf16[2,64,2432]{2,1,0:T(8,128)(2,1)S(1)}, u32[]{:S(2)}, u32[]{:S(2)}) collective-permute-start(bf16[2,64,2432]{2,1,0:T(8,128)(2,1)S(1)} %add_convert_fusion.9), channel_id=1, source_target_pairs={{0,2},{1,3},{2,0},{3,1},{4,6},{5,7},{6,4},{7,5},{8,10},{9,11},{10,... | collective-permute-start | bytes 1867784 | tf_op jit(solution)/shard_map/ppermute | solution.py:737
  543.7 14.1 %collective-permute-start.70 = (bf16[4,64,1280]{2,1,0:T(8,128)(2,1)S(1)}, bf16[4,64,1280]{2,1,0:T(8,128)(2,1)S(1)}, u32[]{:S(2)}, u32[]{:S(2)}) collective-permute-start(bf16[4,64,1280]{2,1,0:T(8,128)(2,1)S(1)} %get-tuple-element.232), channel_id=1, source_target_pairs={{0,1},{1,0},{2,3},{3,2},{4,5},{5,4},{6,7},{7,6},{8,9},{9,8},{10,11... | collective-permute-start | bytes 1966088 | tf_op jit(solution)/shard_map/ppermute | solution.py:737
  560.5 19.0 %collective-permute-start.76 = (bf16[2,2,64,1280]{3,2,1,0:T(8,128)(2,1)S(1)}, bf16[2,2,64,1280]{3,2,1,0:T(8,128)(2,1)S(1)}, u32[]{:S(2)}, u32[]{:S(2)}) collective-permute-start(bf16[2,2,64,1280]{3,2,1,0:T(8,128)(2,1)S(1)} %get-tuple-element.252), channel_id=1, source_target_pairs={{0,2},{1,3},{2,0},{3,1},{4,6},{5,7},{6,4},{7,5},{8,10},{9,11},{10,... | collective-permute-start | bytes 1966088 | tf_op jit(solution)/shard_map/ppermute | solution.py:737
  562.9 32.0 %collective-permute-start.75 = (bf16[64,2432]{1,0:T(8,128)(2,1)}, bf16[64,2432]{1,0:T(8,128)(2,1)S(1)}, u32[]{:S(2)}, u32[]{:S(2)}) collective-permute-start(bf16[64,2432]{1,0:T(8,128)(2,1)} %slice_bitcast_fusion.3), channel_id=1, source_target_pairs={{0,16},{4,20},{8,24},{12,28},{16,0},{20,4},{24,8},{28,12},{1,17},{... | collective-permute-start | bytes 933896 | tf_op jit(solution)/shard_map/ppermute | solution.py:750
  565.8 29.2 %collective-permute-start.73 = (bf16[64,2432]{1,0:T(8,128)(2,1)}, bf16[64,2432]{1,0:T(8,128)(2,1)S(1)}, u32[]{:S(2)}, u32[]{:S(2)}) collective-permute-start(bf16[64,2432]{1,0:T(8,128)(2,1)} %get-tuple-element.265), channel_id=1, source_target_pairs={{0,8},{4,12},{8,16},{12,20},{16,24},{20,28},{24,0},{28,4},{1,9},{5... | collective-permute-start | bytes 933896 | tf_op jit(solution)/shard_map/ppermute | solution.py:750
  567.1 28.4 %collective-permute-start.74 = (bf16[64,2432]{1,0:T(8,128)(2,1)}, bf16[64,2432]{1,0:T(8,128)(2,1)}, u32[]{:S(2)}, u32[]{:S(2)}) collective-permute-start(bf16[64,2432]{1,0:T(8,128)(2,1)} %get-tuple-element.266), channel_id=1, source_target_pairs={{0,24},{4,28},{8,0},{12,4},{16,8},{20,12},{24,16},{28,20},{1,25},{... | collective-permute-start | bytes 933896 | tf_op jit(solution)/shard_map/ppermute | solution.py:750
  580.4 35.8 %collective-permute-start.77 = (bf16[2,2,64,1280]{3,2,1,0:T(8,128)(2,1)}, bf16[2,2,64,1280]{3,2,1,0:T(8,128)(2,1)S(1)}, u32[]{:S(2)}, u32[]{:S(2)}) collective-permute-start(bf16[2,2,64,1280]{3,2,1,0:T(8,128)(2,1)} %get-tuple-element.250), channel_id=1, source_target_pairs={{0,4},{4,0},{8,12},{12,8},{16,20},{20,16},{24,28},{28,24},{1,5},{5... | collective-permute-start | bytes 1966088 | tf_op jit(solution)/shard_map/ppermute | solution.py:733
  (108 other events, 944.7 us)
Sparse Core Ops, SparseCore 0:
  72.3 55.5 all-gather.2
  129.5 96.8 all-gather.4
  480.1 134.3 reduce-scatter.1
